TPU v7x, 32 devices: a whole 2x2x4 slice. The times are simulated.
32 devices in a mesh: dp: 16 (over z, x, core), mp: 2 (over y).
Axes of the slice: x: 2, y: 2, z: 4, core: 2. Of those that a mesh axis runs over, the one named last changes fastest.
Arguments:
- hidden: bfloat16 [16, 780, 1536], P('dp', 'mp'), may hold values from -6 to 6
- text_states: bfloat16 [16, 512, 1536], P('dp', 'mp'), may hold values from -6 to 6
- time_emb: float32 [16, 6, 1536], P('dp'), may hold values from -1.2 to 1.2
- lengths: int32 [16], replicated, may hold values from 702 to 780
- positions: int32 [16, 3, 780], P('dp'), may hold values from 0 to 38, as said below
- teacher: bfloat16 [16, 780, 1536], P('dp', 'mp'), may hold values from -14 to 14
- modulation: float32 [6, 1536], P(None, ('dp', 'mp')), may hold values from -0.9 to 0.9
- out_bias: float32 [4, 1536], P(None, ('dp', 'mp')), may hold values from -0.4 to 0.4
- norm3_gain: float32 [1536], P(('dp', 'mp')), may hold values from 0.5 to 1.5
- self_qkv: bfloat16 [3, 1536, 1536], P(None, 'dp', 'mp'), may hold values from -0.15625 to 0.15625
- self_out: bfloat16 [1536, 1536], P('mp', 'dp'), may hold values from -1 to 1
- cross_qkv: bfloat16 [3, 1536, 1536], P(None, 'dp', 'mp'), may hold values from -0.15625 to 0.15625
- cross_out: bfloat16 [1536, 1536], P('mp', 'dp'), may hold values from -0.875 to 0.875
- ffn_in: bfloat16 [1536, 8960], P('dp', 'mp'), may hold values from -0.15625 to 0.15625
- ffn_out: bfloat16 [8960, 1536], P('mp', 'dp'), may hold values from -0.0625 to 0.0625
- head_bias: bfloat16 [2, 3, 12, 128], P(None, None, 'mp', 'dp'), may hold values from -0.15917969 to 0.15917969
- qk_gain: bfloat16 [2, 2, 12, 128], P(None, None, 'mp', 'dp'), may hold values from 1.1484375 to 1.4453125
- ffn_bias: bfloat16 [70, 128], P('mp', 'dp'), may hold values from -2 to 2
Outputs:
- layer_out: bfloat16 [16, 780, 1536], P('dp', 'mp')
- mean_loss: float32 [], replicated
- hidden_grad: float32 [16, 780, 1536], P('dp', 'mp')
- text_grad: float32 [16, 512, 1536], P('dp', 'mp')
- modulation_grad: float32 [6, 1536], P(None, ('dp', 'mp'))
- out_bias_grad: float32 [4, 1536], P(None, ('dp', 'mp'))
- norm3_grad: float32 [1536], P(('dp', 'mp'))
- self_qkv_grad: float32 [3, 1536, 1536], P(None, 'dp', 'mp')
- self_out_grad: float32 [1536, 1536], P('mp', 'dp')
- cross_qkv_grad: float32 [3, 1536, 1536], P(None, 'dp', 'mp')
- cross_out_grad: float32 [1536, 1536], P('mp', 'dp')
- ffn_in_grad: float32 [1536, 8960], P('dp', 'mp')
- ffn_out_grad: float32 [8960, 1536], P('mp', 'dp')
- head_bias_grad: float32 [2, 3, 12, 128], P(None, None, 'mp', 'dp')
- qk_gain_grad: float32 [2, 2, 12, 128], P(None, None, 'mp', 'dp')
- ffn_bias_grad: float32 [70, 128], P('mp', 'dp')
Inputs may be any that keep to these rules, and one draw needn't show every extreme that they name: The valid slots of clip c are its first lengths[c] slots; later slots are padding. `positions`: slot s of a clip holds frame s // (R W), row (s // W) mod R and column s mod W of a grid whose W (16 to 39) and R (8 to 19) are drawn for each clip; the first clip has W = 39.
All inputs are finite; a program needn't handle non-finite values.
Results may differ from a plain program's by a relative error of at most 0.025.
Values may be sent and summed in bfloat16 or wider, within the bound.
A program may use at most 320 MiB of HBM per device.

v0:
```python
from functools import partial
import math

import jax
import jax.numpy as jnp
from jax import lax
from jax.sharding import PartitionSpec as P

D = 1536
HD = 128
LEN = 780


EPS = 1e-06


def rope_tables(positions):
    pair_count = HD // 2
    third_count = pair_count // 3
    counts = [pair_count - 2 * third_count, third_count, third_count]
    pieces = []
    for axis_id in range(3):
        rank_steps = jnp.arange(counts[axis_id], dtype=jnp.float32) / counts[axis_id]
        freq_rates = jnp.exp(-math.log(10000.0) * rank_steps)
        pieces.append(positions[axis_id].astype(jnp.float32)[:, None] * freq_rates[None, :])
    angles = jnp.repeat(jnp.concatenate(pieces, axis=1), 2, axis=1)
    return (jnp.cos(angles), jnp.sin(angles))


def pair_turn(values):
    next_value = jnp.roll(values, -1, axis=-1)
    prev_value = jnp.roll(values, 1, axis=-1)
    parity = jnp.arange(values.shape[-1]) % 2 == 0
    return jnp.where(parity, -next_value, prev_value)


def turn_heads(values, tables, direction):
    shape_in = values.shape
    grouped = values.reshape(shape_in[0], shape_in[1], -1, HD)
    turned = grouped * tables[0] + direction * pair_turn(grouped) * tables[1]
    return turned.reshape(shape_in)


def layer_norm(values):
    center = values - jnp.mean(values, axis=-1, keepdims=True)
    spread = jnp.mean(center * center, axis=-1, keepdims=True)
    return center * lax.rsqrt(spread + EPS)


def modulate(values, shift_vec, scale_vec):
    return layer_norm(values) * (1.0 + scale_vec) + shift_vec


def affine_norm(values, gain_vec, bias_vec):
    return layer_norm(values) * gain_vec + bias_vec


def matmul(left, right):
    return jnp.einsum("crd,dk->crk", left, right, preferred_element_type=jnp.float32)


def matmul_back(left, right):
    return jnp.einsum("crk,dk->crd", left, right, preferred_element_type=jnp.float32)


def weight_grad(left, right):
    return jnp.einsum("crd,crk->dk", left, right, preferred_element_type=jnp.float32)


def row_sums(values):
    return jnp.sum(values, axis=(0, 1), dtype=jnp.float32)


def collect(values):
    return lax.all_gather(values, "mp", axis=1, tiled=True)


def spread_back(values):
    return lax.psum_scatter(values, "mp", scatter_dimension=1, tiled=True)


def feature_sums(pair_values):
    return lax.psum((pair_values[0], pair_values[1]), "mp")


def project_heads(rows_query, rows_keys, weights, biases, gain_pair, tables):
    query_pre = matmul(rows_query, weights[0]) + biases[0]
    key_pre = matmul(rows_keys, weights[1]) + biases[1]
    value_all = (matmul(rows_keys, weights[2]) + biases[2]).astype(jnp.bfloat16)
    query_sq, key_sq = feature_sums(
        (jnp.sum(query_pre * query_pre, axis=-1), jnp.sum(key_pre * key_pre, axis=-1))
    )
    query_scale = lax.rsqrt(query_sq / D + EPS)[..., None]
    key_scale = lax.rsqrt(key_sq / D + EPS)[..., None]
    query_norm = query_pre * query_scale * gain_pair[0]
    key_norm = key_pre * key_scale * gain_pair[1]
    if tables is not None:
        query_norm = turn_heads(query_norm, tables, 1.0)
        key_norm = turn_heads(key_norm, tables, 1.0)
    return {
        "query_pre": query_pre,
        "key_pre": key_pre,
        "query_scale": query_scale,
        "key_scale": key_scale,
        "query": query_norm.astype(jnp.bfloat16),
        "key": key_norm.astype(jnp.bfloat16),
        "value": value_all,
    }


def split_heads(values):
    return values.reshape(values.shape[0], values.shape[1], -1, HD)


def masked_scores(query_heads, key_heads, key_valid):
    scores = jnp.einsum(
        "cqhd,ckhd->chqk", query_heads, key_heads, preferred_element_type=jnp.float32
    ) * HD ** (-0.5)
    if key_valid is not None:
        scores = jnp.where(key_valid[:, None, None, :], scores, -1e30)
    return scores


def attend_forward(kept_heads, key_valid):
    query_heads = split_heads(kept_heads["query"])
    scores = masked_scores(query_heads, split_heads(kept_heads["key"]), key_valid)
    row_top = jnp.max(scores, axis=-1, keepdims=True)
    weights = jnp.exp(scores - row_top)
    row_total = jnp.sum(weights, axis=-1, keepdims=True)
    probabilities = (weights / row_total).astype(jnp.bfloat16)
    mixed_rows = jnp.einsum(
        "chqk,ckhd->cqhd",
        probabilities,
        split_heads(kept_heads["value"]),
        preferred_element_type=jnp.float32,
    )
    return (
        mixed_rows.astype(jnp.bfloat16).reshape(kept_heads["query"].shape),
        row_top + jnp.log(row_total),
    )


def attend_backward(kept_heads, key_valid, log_total, mixed_grad):
    query_heads = split_heads(kept_heads["query"])
    key_heads = split_heads(kept_heads["key"])
    value_heads = split_heads(kept_heads["value"])
    probabilities = jnp.exp(masked_scores(query_heads, key_heads, key_valid) - log_total)
    grad_heads = split_heads(mixed_grad)
    probs_grad = jnp.einsum(
        "cqhd,ckhd->chqk", grad_heads, value_heads, preferred_element_type=jnp.float32
    )
    row_inner = jnp.sum(probs_grad * probabilities, axis=-1, keepdims=True)
    score_grad = (probabilities * (probs_grad - row_inner)).astype(jnp.bfloat16)
    value_grad = jnp.einsum(
        "chqk,cqhd->ckhd",
        probabilities.astype(jnp.bfloat16),
        grad_heads,
        preferred_element_type=jnp.float32,
    ).astype(jnp.bfloat16)
    query_grad = jnp.einsum(
        "chqk,ckhd->cqhd", score_grad, key_heads, preferred_element_type=jnp.float32
    ) * HD ** (-0.5)
    key_grad = jnp.einsum(
        "chqk,cqhd->ckhd", score_grad, query_heads, preferred_element_type=jnp.float32
    ) * HD ** (-0.5)
    return (
        query_grad.reshape(kept_heads["query"].shape),
        key_grad.reshape(kept_heads["key"].shape),
        value_grad.reshape(kept_heads["value"].shape),
    )


def heads_back(kept_heads, query_grad, key_grad, gain_pair, tables):
    if tables is not None:
        query_grad = turn_heads(query_grad, tables, -1.0)
        key_grad = turn_heads(key_grad, tables, -1.0)
    query_weighted = query_grad * gain_pair[0]
    key_weighted = key_grad * gain_pair[1]
    query_dot, key_dot = feature_sums(
        (
            jnp.sum(query_weighted * kept_heads["query_pre"], axis=-1),
            jnp.sum(key_weighted * kept_heads["key_pre"], axis=-1),
        )
    )
    query_scale = kept_heads["query_scale"]
    key_scale = kept_heads["key_scale"]
    query_pre_grad = (
        query_weighted * query_scale
        - kept_heads["query_pre"] * query_scale**3 * query_dot[..., None] / D
    ).astype(jnp.bfloat16)
    key_pre_grad = (
        key_weighted * key_scale - kept_heads["key_pre"] * key_scale**3 * key_dot[..., None] / D
    ).astype(jnp.bfloat16)
    gain_grads = jnp.stack(
        [
            row_sums(query_grad * kept_heads["query_pre"] * query_scale),
            row_sums(key_grad * kept_heads["key_pre"] * key_scale),
        ]
    )
    return (query_pre_grad, key_pre_grad, gain_grads)


def weights_back(rows_query, rows_keys, weights, query_pre_grad, key_pre_grad, value_grad):
    matrix_grads = jnp.stack(
        [
            weight_grad(rows_query, query_pre_grad),
            weight_grad(rows_keys, key_pre_grad),
            weight_grad(rows_keys, value_grad),
        ]
    )
    bias_grads = jnp.stack([row_sums(query_pre_grad), row_sums(key_pre_grad), row_sums(value_grad)])
    query_back = matmul_back(query_pre_grad, weights[0])
    keys_back = matmul_back(key_pre_grad, weights[1]) + matmul_back(value_grad, weights[2])
    return (matrix_grads, bias_grads, query_back, keys_back)


def local(
    hidden,
    text_states,
    time_emb,
    lengths,
    positions,
    teacher,
    modulation,
    out_bias,
    norm3_gain,
    self_qkv,
    self_out,
    cross_qkv,
    cross_out,
    ffn_in,
    ffn_out,
    head_bias,
    qk_gain,
    ffn_bias,
):
    clip_count, half_len = (hidden.shape[0], hidden.shape[1])
    modulation_full, out_bias_full, norm3_full = (
        lax.all_gather(modulation, ("dp", "mp"), axis=1, tiled=True),
        lax.all_gather(out_bias, ("dp", "mp"), axis=1, tiled=True),
        lax.all_gather(norm3_gain, ("dp", "mp"), axis=0, tiled=True),
    )
    (
        self_qkv_w,
        self_out_w,
        cross_qkv_w,
        cross_out_w,
        head_bias_w,
        qk_gain_w,
        ffn_in_w,
        ffn_out_w,
        ffn_bias_w,
    ) = (
        lax.all_gather(self_qkv, "dp", axis=1, tiled=True),
        lax.all_gather(self_out, "dp", axis=1, tiled=True),
        lax.all_gather(cross_qkv, "dp", axis=1, tiled=True),
        lax.all_gather(cross_out, "dp", axis=1, tiled=True),
        lax.all_gather(head_bias, "dp", axis=3, tiled=True),
        lax.all_gather(qk_gain, "dp", axis=3, tiled=True),
        lax.all_gather(ffn_in, "dp", axis=0, tiled=True),
        lax.all_gather(ffn_out, "dp", axis=1, tiled=True),
        lax.all_gather(ffn_bias, "dp", axis=1, tiled=True),
    )
    self_bias = head_bias_w[0].astype(jnp.float32).reshape(3, -1)
    cross_bias = head_bias_w[1].astype(jnp.float32).reshape(3, -1)
    self_gain = qk_gain_w[0].astype(jnp.float32).reshape(2, -1)
    cross_gain = qk_gain_w[1].astype(jnp.float32).reshape(2, -1)
    signals = modulation_full[None] + time_emb
    shift_attn = signals[:, 0:1]
    scale_attn = signals[:, 1:2]
    gate_attn = signals[:, 2:3]
    shift_ffn = signals[:, 3:4]
    scale_ffn = signals[:, 4:5]
    gate_ffn = signals[:, 5:6]
    residual = hidden.astype(jnp.float32)
    first_clip = lax.axis_index("dp") * clip_count
    clip_lengths = lax.dynamic_slice_in_dim(lengths, first_clip, clip_count)
    key_valid = jnp.arange(LEN)[None, :] < clip_lengths[:, None]
    row_index = lax.axis_index("mp") * half_len + jnp.arange(half_len)
    row_valid = (row_index[None, :] < clip_lengths[:, None]).astype(jnp.float32)[:, :, None]
    cosine, sine_table = jax.vmap(rope_tables)(positions)
    tables = (cosine[:, :, None, :], sine_table[:, :, None, :])
    attn_rows = collect(modulate(residual, shift_attn, scale_attn).astype(jnp.bfloat16))
    self_kept = project_heads(attn_rows, attn_rows, self_qkv_w, self_bias, self_gain, tables)
    self_mixed, self_lse = attend_forward(self_kept, key_valid)
    self_branch = spread_back(matmul(self_mixed, self_out_w)) + out_bias_full[1]
    after_self = residual + gate_attn * self_branch
    text_rows = lax.all_gather(text_states, "mp", axis=1, tiled=True)
    cross_rows = collect(affine_norm(after_self, norm3_full, out_bias_full[0]).astype(jnp.bfloat16))
    cross_kept = project_heads(cross_rows, text_rows, cross_qkv_w, cross_bias, cross_gain, None)
    cross_mixed, cross_lse = attend_forward(cross_kept, None)
    cross_branch = spread_back(matmul(cross_mixed, cross_out_w)) + out_bias_full[2]
    after_cross = after_self + cross_branch
    ffn_rows = collect(modulate(after_cross, shift_ffn, scale_ffn).astype(jnp.bfloat16))
    inner_act = matmul(ffn_rows, ffn_in_w) + ffn_bias_w.astype(jnp.float32).reshape(-1)
    gelu_value, gelu_back = jax.vjp(partial(jax.nn.gelu, approximate=True), inner_act)
    activated = gelu_value.astype(jnp.bfloat16)
    ffn_branch = spread_back(matmul(activated, ffn_out_w)) + out_bias_full[3]
    result = after_cross + gate_ffn * ffn_branch
    error_rows = (result - teacher.astype(jnp.float32)) * row_valid
    squares = lax.psum(jnp.sum(error_rows * error_rows), ("dp", "mp"))
    valid_count = jnp.sum(lengths).astype(jnp.float32)
    mean_loss = squares / (valid_count * D)
    grad_gate_ffn = jnp.sum(ffn_branch * error_rows, axis=1, keepdims=True)
    ffn_branch_grad = (gate_ffn * error_rows).astype(jnp.bfloat16)
    bias_grad_ffn = row_sums(ffn_branch_grad)
    grad_rows = collect(ffn_branch_grad)
    ffn_out_grad = weight_grad(activated, grad_rows)
    act_grad = matmul_back(grad_rows, ffn_out_w)
    inner_grad = gelu_back(act_grad)[0].astype(jnp.bfloat16)
    ffn_bias_grad = row_sums(inner_grad).reshape(ffn_bias_w.shape)
    ffn_in_grad = weight_grad(ffn_rows, inner_grad)
    rows_back = spread_back(matmul_back(inner_grad, ffn_in_w))
    mod_value, mod_back = jax.vjp(modulate, after_cross, shift_ffn, scale_ffn)
    cross_state_grad, grad_shift_ffn, grad_scale_ffn = mod_back(rows_back)
    state_grad = error_rows + cross_state_grad
    cross_branch_grad = state_grad.astype(jnp.bfloat16)
    bias_grad_cross = row_sums(cross_branch_grad)
    grad_rows = collect(cross_branch_grad)
    cross_out_grad = weight_grad(cross_mixed, grad_rows)
    mixed_grad = matmul_back(grad_rows, cross_out_w).astype(jnp.bfloat16)
    query_grad, key_grad, value_grad = attend_backward(cross_kept, None, cross_lse, mixed_grad)
    query_pre_grad, key_pre_grad, cross_gain_grad = heads_back(
        cross_kept, query_grad, key_grad, cross_gain, None
    )
    cross_qkv_grad, cross_bias_grad, query_back, keys_back = weights_back(
        cross_rows, text_rows, cross_qkv_w, query_pre_grad, key_pre_grad, value_grad
    )
    text_grad = lax.psum_scatter(
        keys_back.astype(jnp.bfloat16), "mp", scatter_dimension=1, tiled=True
    ).astype(jnp.float32)
    rows_back = spread_back(query_back)
    norm_value, norm_back = jax.vjp(affine_norm, after_self, norm3_full, out_bias_full[0])
    self_state_grad, norm3_grad, norm_bias_grad = norm_back(rows_back)
    state_grad = state_grad + self_state_grad
    grad_gate_attn = jnp.sum(self_branch * state_grad, axis=1, keepdims=True)
    self_branch_grad = (gate_attn * state_grad).astype(jnp.bfloat16)
    bias_grad_self = row_sums(self_branch_grad)
    grad_rows = collect(self_branch_grad)
    self_out_grad = weight_grad(self_mixed, grad_rows)
    mixed_grad = matmul_back(grad_rows, self_out_w).astype(jnp.bfloat16)
    query_grad, key_grad, value_grad = attend_backward(self_kept, key_valid, self_lse, mixed_grad)
    query_pre_grad, key_pre_grad, self_gain_grad = heads_back(
        self_kept, query_grad, key_grad, self_gain, tables
    )
    self_qkv_grad, self_bias_grad, query_back, keys_back = weights_back(
        attn_rows, attn_rows, self_qkv_w, query_pre_grad, key_pre_grad, value_grad
    )
    rows_back = spread_back(query_back + keys_back)
    first_value, first_back = jax.vjp(modulate, residual, shift_attn, scale_attn)
    input_grad, grad_shift_attn, grad_scale_attn = first_back(rows_back)
    hidden_grad = state_grad + input_grad
    modulation_grad = jnp.sum(
        jnp.concatenate(
            [
                grad_shift_attn,
                grad_scale_attn,
                grad_gate_attn,
                grad_shift_ffn,
                grad_scale_ffn,
                grad_gate_ffn,
            ],
            axis=1,
        ),
        axis=0,
    )
    out_bias_grad = jnp.stack([norm_bias_grad, bias_grad_self, bias_grad_cross, bias_grad_ffn])
    modulation_grad, out_bias_grad, norm3_grad = (
        lax.psum_scatter(modulation_grad, ("dp", "mp"), scatter_dimension=1, tiled=True),
        lax.psum_scatter(out_bias_grad, ("dp", "mp"), scatter_dimension=1, tiled=True),
        lax.psum_scatter(norm3_grad, ("dp", "mp"), scatter_dimension=0, tiled=True),
    )
    head_bias_grad = jnp.stack([self_bias_grad, cross_bias_grad]).reshape(head_bias_w.shape)
    qk_gain_grad = jnp.stack([self_gain_grad, cross_gain_grad]).reshape(qk_gain_w.shape)
    (
        self_qkv_grad,
        self_out_grad,
        cross_qkv_grad,
        cross_out_grad,
        head_bias_grad,
        qk_gain_grad,
        ffn_in_grad,
        ffn_out_grad,
        ffn_bias_grad,
    ) = (
        lax.psum_scatter(self_qkv_grad, "dp", scatter_dimension=1, tiled=True),
        lax.psum_scatter(self_out_grad, "dp", scatter_dimension=1, tiled=True),
        lax.psum_scatter(cross_qkv_grad, "dp", scatter_dimension=1, tiled=True),
        lax.psum_scatter(cross_out_grad, "dp", scatter_dimension=1, tiled=True),
        lax.psum_scatter(head_bias_grad, "dp", scatter_dimension=3, tiled=True),
        lax.psum_scatter(qk_gain_grad, "dp", scatter_dimension=3, tiled=True),
        lax.psum_scatter(ffn_in_grad, "dp", scatter_dimension=0, tiled=True),
        lax.psum_scatter(ffn_out_grad, "dp", scatter_dimension=1, tiled=True),
        lax.psum_scatter(ffn_bias_grad, "dp", scatter_dimension=1, tiled=True),
    )
    return (
        result.astype(jnp.bfloat16),
        mean_loss,
        hidden_grad,
        text_grad,
        modulation_grad,
        out_bias_grad,
        norm3_grad,
        self_qkv_grad,
        self_out_grad,
        cross_qkv_grad,
        cross_out_grad,
        ffn_in_grad,
        ffn_out_grad,
        head_bias_grad,
        qk_gain_grad,
        ffn_bias_grad,
    )


def solution(mesh):
    in_specs = (
        P("dp", "mp", None),
        P("dp", "mp", None),
        P("dp", None, None),
        P(),
        P("dp", None, None),
        P("dp", "mp", None),
        P(None, ("dp", "mp")),
        P(None, ("dp", "mp")),
        P(("dp", "mp")),
        P(None, "dp", "mp"),
        P("mp", "dp"),
        P(None, "dp", "mp"),
        P("mp", "dp"),
        P("dp", "mp"),
        P("mp", "dp"),
        P(None, None, "mp", "dp"),
        P(None, None, "mp", "dp"),
        P("mp", "dp"),
    )
    out_specs = (
        P("dp", "mp", None),
        P(),
        P("dp", "mp", None),
        P("dp", "mp", None),
        P(None, ("dp", "mp")),
        P(None, ("dp", "mp")),
        P(("dp", "mp")),
        P(None, "dp", "mp"),
        P("mp", "dp"),
        P(None, "dp", "mp"),
        P("mp", "dp"),
        P("dp", "mp"),
        P("mp", "dp"),
        P(None, None, "mp", "dp"),
        P(None, None, "mp", "dp"),
        P("mp", "dp"),
    )
    return jax.shard_map(local, mesh=mesh, in_specs=in_specs, out_specs=out_specs, check_vma=False)
```

profile of v0, /device:TPU:0, one launch (start us, length us, event | category | flops | bytes accessed | tf_op | source)
XLA Modules:
  0.0 3298.5 jit_solution(16150969279984866461)
XLA Ops:
  7.2 70.7 %all-gather = f32[32,48,6]{1,2,0:T(8,128)S(1)} all-gather(f32[1,48,6]{1,2,0:T(8,128)} %bitcast.382), channel_id=1, replica_groups=mesh['dp'=16,'mp'=2] {'dp','mp'}, dimensions={0}, use_global_device_ids=true | all-gather | bytes 38016 | tf_op jit(solution)/shard_map/all_gather | solution.py:239
  115.9 19.7 all_gather.61
  157.4 66.0 %all-gather.18.cloned.1.call-done = bf16[3,1536,768]{2,1,0:T(8,128)(2,1)} async-done(((bf16[3,96,768]{2,1,0:T(8,128)(2,1)}), bf16[3,1536,768]{2,1,0:T(8,128)(2,1)}) %all-gather.18.cloned.1.call-update) | async-done | bytes 7077904 | tf_op jit(solution)/shard_map/all_gather | solution.py:254
  318.3 66.7 %all-gather.1 = f32[32,48,4]{1,2,0:T(4,128)S(1)} all-gather(f32[1,48,4]{1,2,0:T(4,128)S(1)} %bitcast.383), channel_id=1, replica_groups=mesh['dp'=16,'mp'=2] {'dp','mp'}, dimensions={0}, use_global_device_ids=true | all-gather | bytes 25344 | tf_op jit(solution)/shard_map/all_gather | solution.py:240
  386.7 37.7 %all-reduce = f32[1536]{0:T(1024)S(1)} all-reduce(f32[1536]{0:T(1024)S(1)} %dynamic-update-slice), channel_id=1, replica_groups=mesh['dp'=16,'mp'=2] {'dp','mp'}, use_global_device_ids=true, to_apply=%add | all-reduce | flops 1536 | bytes 12288
  467.8 69.1 %all-gather.24.cloned.1.call-done = bf16[3,1536,768]{2,1,0:T(8,128)(2,1)} async-done(((bf16[3,96,768]{2,1,0:T(8,128)(2,1)}), bf16[3,1536,768]{2,1,0:T(8,128)(2,1)}) %all-gather.24.cloned.1.call-update) | async-done | bytes 7077904 | tf_op jit(solution)/shard_map/all_gather | solution.py:256
  545.4 55.1 %all-gather.26.cloned.1.call-done = bf16[1,780,1536]{2,0,1:T(2,128)(2,1)} async-done(((bf16[1,390,1536]{2,0,1:T(2,128)(2,1)}), bf16[1,780,1536]{2,0,1:T(2,128)(2,1)}) %all-gather.26.cloned.1.call-update) | async-done | bytes 2396176 | tf_op jit(solution)/shard_map/all_gather | solution.py:75
  662.1 118.9 %all-reduce.25.cloned.1.call-done = f32[1,780,1536]{2,0,1:T(1,128)} async-done(((f32[1,780,1536]{2,0,1:T(1,128)}), f32[1,780,1536]{2,0,1:T(1,128)}) %all-reduce.25.cloned.1.call-update) | async-done | bytes 4792336
  796.3 22.1 all_gather.71
  818.5 73.4 %all-gather.32.cloned.1.call-done = bf16[1536,4480]{1,0:T(8,128)(2,1)} async-done(((bf16[96,4480]{1,0:T(8,128)(2,1)}), bf16[1536,4480]{1,0:T(8,128)(2,1)}) %all-gather.32.cloned.1.call-update) | async-done | bytes 13762576 | tf_op jit(solution)/shard_map/all_gather | solution.py:260
  892.0 63.2 %all-gather.30.cloned.1.call-done = bf16[1,780,1536]{2,0,1:T(2,128)(2,1)} async-done(((bf16[1,390,1536]{2,0,1:T(2,128)(2,1)}), bf16[1,780,1536]{2,0,1:T(2,128)(2,1)}) %all-gather.30.cloned.1.call-update) | async-done | bytes 2396176 | tf_op jit(solution)/shard_map/all_gather | solution.py:75
  955.2 18.8 fusion.52
  974.0 91.5 %all-gather.34.cloned.1.call-done = bf16[4480,1536]{0,1:T(8,128)(2,1)} async-done(((bf16[4480,96]{0,1:T(8,128)(2,1)}), bf16[4480,1536]{0,1:T(8,128)(2,1)}) %all-gather.34.cloned.1.call-update) | async-done | bytes 13762576 | tf_op jit(solution)/shard_map/all_gather | solution.py:261
  1065.6 21.3 convolution_bitcast_fusion.1
  1097.1 118.4 %all-reduce.27.cloned.1.call-done = f32[1,780,1536]{2,0,1:T(1,128)} async-done(((f32[1,780,1536]{2,0,1:T(1,128)}), f32[1,780,1536]{2,0,1:T(1,128)}) %all-reduce.27.cloned.1.call-update) | async-done | bytes 4792336
  1231.7 64.1 %all-gather.36.cloned.1.call-done = bf16[1,780,1536]{2,0,1:T(2,128)(2,1)} async-done(((bf16[1,390,1536]{2,0,1:T(2,128)(2,1)}), bf16[1,780,1536]{2,0,1:T(2,128)(2,1)}) %all-gather.36.cloned.1.call-update) | async-done | bytes 2396176 | tf_op jit(solution)/shard_map/all_gather | solution.py:75
  1295.8 28.1 convert_reduce_fusion
  1351.0 120.9 %all-reduce.29.cloned.1.call-done = f32[1,780,1536]{2,0,1:T(1,128)} async-done(((f32[1,780,1536]{2,0,1:T(1,128)}), f32[1,780,1536]{2,0,1:T(1,128)}) %all-reduce.29.cloned.1.call-update) | async-done | bytes 4792336
  1503.3 63.6 %all-gather.38.cloned.1.call-done = bf16[1,780,1536]{2,0,1:T(2,128)(2,1)} async-done(((bf16[1,390,1536]{2,0,1:T(2,128)(2,1)}), bf16[1,780,1536]{2,0,1:T(2,128)(2,1)}) %all-gather.38.cloned.1.call-update) | async-done | bytes 2396176 | tf_op jit(solution)/shard_map/all_gather | solution.py:75
  1618.1 120.9 %all-reduce.31.cloned.1.call-done = f32[1,780,1536]{2,0,1:T(1,128)} async-done(((f32[1,780,1536]{2,0,1:T(1,128)}), f32[1,780,1536]{2,0,1:T(1,128)}) %all-reduce.31.cloned.1.call-update) | async-done | bytes 4792336
  1775.3 51.6 %all-gather.40.cloned.1.call-done = bf16[1,780,1536]{2,0,1:T(2,128)(2,1)} async-done(((bf16[1,390,1536]{2,0,1:T(2,128)(2,1)}), bf16[1,780,1536]{2,0,1:T(2,128)(2,1)}) %all-gather.40.cloned.1.call-update) | async-done | bytes 2396176 | tf_op jit(solution)/shard_map/all_gather | solution.py:75
  1963.9 103.8 %all-reduce.33.cloned.1.call-done = f32[1,780,1536]{2,0,1:T(1,128)} async-done(((f32[1,780,1536]{2,0,1:T(1,128)}), f32[1,780,1536]{2,0,1:T(1,128)}) %all-reduce.33.cloned.1.call-update) | async-done | bytes 4792336
  2164.2 22.6 fusion.50
  2187.6 23.5 fusion.44
  2215.5 40.0 %all-reduce.11 = (f32[]{:T(128)}, f32[1536]{0:T(1024)S(1)}) all-reduce(f32[]{:T(128)} %get-tuple-element.175, f32[1536]{0:T(1024)S(1)} %copy-done.114), channel_id=1, replica_groups=mesh['dp'=16,'mp'=2] {'dp','mp'}, use_global_device_ids=true, to_apply=%region_22.23 | all-reduce | flops 1537 | bytes 12296 | tf_op jit(solution)/shard_map/psum | solution.py:301
  2258.2 60.2 %all-reduce.12 = (f32[2,3,6,128]{3,2,1,0:T(8,128)S(1)}, f32[2,2,6,128]{3,2,1,0:T(8,128)S(1)}, f32[35,128]{1,0:T(8,128)S(1)}) all-reduce(f32[2,3,6,128]{3,2,1,0:T(8,128)S(1)} %maximum_maximum_fusion, f32[2,2,6,128]{3,2,1,0:T(8,128)S(1)} %maximum_maximum_fusion.1, ...), channel_id=18, replica_groups=mesh['dp'=16,'mp'=2] {'dp'}, use_global_device_ids=true, to_apply=%region_70.71.clone | all-reduce | flops 12160 | bytes 97280
  2324.5 53.3 %reduce-scatter.25.cloned.1.call-done = f32[768,96]{0,1:T(8,128)} async-done(((f32[768,1536]{0,1:T(8,128)}), f32[768,96]{0,1:T(8,128)}) %reduce-scatter.25.cloned.1.call-update) | async-done | bytes 294928 | tf_op jit(solution)/shard_map/reduce_scatter | solution.py:389
  2377.8 78.9 %reduce-scatter.21.cloned.1.call-done = f32[768,96]{0,1:T(8,128)} async-done(((f32[768,1536]{0,1:T(8,128)}), f32[768,96]{0,1:T(8,128)}) %reduce-scatter.21.cloned.1.call-update) | async-done | bytes 294928 | tf_op jit(solution)/shard_map/reduce_scatter | solution.py:387
  2456.7 150.0 %reduce-scatter.19.cloned.1.call-done = f32[3,96,768]{2,1,0:T(8,128)} async-done(((f32[3,1536,768]{2,1,0:T(8,128)}), f32[3,96,768]{2,1,0:T(8,128)}) %reduce-scatter.19.cloned.1.call-update) | async-done | bytes 884752 | tf_op jit(solution)/shard_map/reduce_scatter | solution.py:386
  2606.7 149.8 %reduce-scatter.23.cloned.1.call-done = f32[3,96,768]{2,1,0:T(8,128)} async-done(((f32[3,1536,768]{2,1,0:T(8,128)}), f32[3,96,768]{2,1,0:T(8,128)}) %reduce-scatter.23.cloned.1.call-update) | async-done | bytes 884752 | tf_op jit(solution)/shard_map/reduce_scatter | solution.py:388
  2756.6 267.1 %reduce-scatter.27.cloned.1.call-done = f32[96,4480]{1,0:T(8,128)} async-done(((f32[1536,4480]{1,0:T(8,128)}), f32[96,4480]{1,0:T(8,128)}) %reduce-scatter.27.cloned.1.call-update) | async-done | bytes 1720336 | tf_op jit(solution)/shard_map/reduce_scatter | solution.py:392
  3023.7 266.7 %reduce-scatter.29.cloned.1.call-done = f32[4480,96]{0,1:T(8,128)} async-done(((f32[4480,1536]{0,1:T(8,128)}), f32[4480,96]{0,1:T(8,128)}) %reduce-scatter.29.cloned.1.call-update) | async-done | bytes 1720336 | tf_op jit(solution)/shard_map/reduce_scatter | solution.py:393
  (590 shorter events, 700.2 us)
Async XLA Ops:
  7.2 147.2 %all-gather.16.cloned.1.call-start = ((), (), s32[]{:S(2)}) async-start(), calls=%async_computation.9 | async-start | bytes 7188480 | tf_op jit(solution)/shard_map/all_gather | solution.py:75
  94.9 128.5 %all-gather.18.cloned.1.call-start = ((), (), s32[]{:S(2)}) async-start(), calls=%async_computation.10 | async-start | bytes 7520256 | tf_op jit(solution)/shard_map/all_gather | solution.py:254
  95.7 205.1 %all-gather.20.cloned.1.call-start = ((), (), s32[]{:S(2)}) async-start(), calls=%async_computation.11 | async-start | bytes 2506752 | tf_op jit(solution)/shard_map/all_gather | solution.py:255
  96.4 342.4 %all-reduce.23.cloned.1.call-start = ((), (), s32[]{:S(2)}) async-start(), calls=%async_computation.31 | async-start | bytes 9584640
  317.0 150.8 %all-gather.22.cloned.1.call-start = ((), (), s32[]{:S(2)}) async-start(), calls=%async_computation.12 | async-start | bytes 2359296 | tf_op jit(solution)/shard_map/all_gather | solution.py:288
  317.6 219.3 %all-gather.24.cloned.1.call-start = ((), (), s32[]{:S(2)}) async-start(), calls=%async_computation.13 | async-start | bytes 7520256 | tf_op jit(solution)/shard_map/all_gather | solution.py:256
  318.2 282.3 %all-gather.26.cloned.1.call-start = ((), (), s32[]{:S(2)}) async-start(), calls=%async_computation.14 | async-start | bytes 7188480 | tf_op jit(solution)/shard_map/all_gather | solution.py:75
  459.0 186.4 %all-gather.28.cloned.1.call-start = ((), (), s32[]{:S(2)}) async-start(), calls=%async_computation.15 | async-start | bytes 2506752 | tf_op jit(solution)/shard_map/all_gather | solution.py:257
  459.8 321.2 %all-reduce.25.cloned.1.call-start = ((), (), s32[]{:S(2)}) async-start(), calls=%async_computation.32 | async-start | bytes 9584640
  460.4 150.5 %copy-start.99 = (f32[768]{0:T(1024)}, f32[768]{0:T(1024)S(1)}, u32[]{:S(2)}) copy-start(f32[768]{0:T(1024)S(1)} %get-tuple-element.188) | copy-start | bytes 9220
  460.5 150.4 %copy-start.101 = (f32[768]{0:T(1024)}, f32[768]{0:T(1024)S(1)}, u32[]{:S(2)}) copy-start(f32[768]{0:T(1024)S(1)} %get-tuple-element.194) | copy-start | bytes 9220
  460.5 154.2 %copy-start.89 = (f32[768]{0:T(1024)}, f32[768]{0:T(1024)S(1)}, u32[]{:S(2)}) copy-start(f32[768]{0:T(1024)S(1)} %get-tuple-element.193) | copy-start | bytes 9220
  661.2 230.8 %all-gather.32.cloned.1.call-start = ((), (), s32[]{:S(2)}) async-start(), calls=%async_computation.17 | async-start | bytes 14622720 | tf_op jit(solution)/shard_map/all_gather | solution.py:260
  661.8 293.4 %all-gather.30.cloned.1.call-start = ((), (), s32[]{:S(2)}) async-start(), calls=%async_computation.16 | async-start | bytes 7188480 | tf_op jit(solution)/shard_map/all_gather | solution.py:75
  795.7 269.9 %all-gather.34.cloned.1.call-start = ((), (), s32[]{:S(2)}) async-start(), calls=%async_computation.18 | async-start | bytes 14622720 | tf_op jit(solution)/shard_map/all_gather | solution.py:261
  796.3 419.2 %all-reduce.27.cloned.1.call-start = ((), (), s32[]{:S(2)}) async-start(), calls=%async_computation.33 | async-start | bytes 9584640
  818.5 477.3 %copy-start.119 = (f32[4480]{0:T(1024)}, f32[4480]{0:T(1024)S(1)}, u32[]{:S(2)}) copy-start(f32[4480]{0:T(1024)S(1)} %bitcast_convert_fusion) | copy-start | bytes 53764
  1096.4 199.4 %all-gather.36.cloned.1.call-start = ((), (), s32[]{:S(2)}) async-start(), calls=%async_computation.19 | async-start | bytes 7188480 | tf_op jit(solution)/shard_map/all_gather | solution.py:75
  1231.6 240.2 %all-reduce.29.cloned.1.call-start = ((), (), s32[]{:S(2)}) async-start(), calls=%async_computation.34 | async-start | bytes 9584640
  1350.9 216.1 %all-gather.38.cloned.1.call-start = ((), (), s32[]{:S(2)}) async-start(), calls=%async_computation.20 | async-start | bytes 7188480 | tf_op jit(solution)/shard_map/all_gather | solution.py:75
  1502.8 236.2 %all-reduce.31.cloned.1.call-start = ((), (), s32[]{:S(2)}) async-start(), calls=%async_computation.35 | async-start | bytes 9584640
  1618.0 208.9 %all-gather.40.cloned.1.call-start = ((), (), s32[]{:S(2)}) async-start(), calls=%async_computation.21 | async-start | bytes 7188480 | tf_op jit(solution)/shard_map/all_gather | solution.py:75
  1762.8 304.9 %all-reduce.33.cloned.1.call-start = ((), (), s32[]{:S(2)}) async-start(), calls=%async_computation.36 | async-start | bytes 9584640
  1945.6 311.2 %reduce-scatter.33.cloned.1.call-start = ((), (), s32[]{:S(2)}) async-start(), calls=%async_computation.30 | async-start | bytes 811008
  1955.2 365.4 %reduce-scatter.17.cloned.1.call-start = ((), (), s32[]{:S(2)}) async-start(), calls=%async_computation.22 | async-start | bytes 2359296 | tf_op jit(solution)/shard_map/reduce_scatter | solution.py:329
  1963.8 359.3 %reduce-scatter.31.cloned.1.call-start = ((), (), s32[]{:S(2)}) async-start(), calls=%async_computation.29 | async-start | bytes 811008
  2092.5 285.3 %reduce-scatter.25.cloned.1.call-start = ((), (), s32[]{:S(2)}) async-start(), calls=%async_computation.26 | async-start | bytes 5013504 | tf_op jit(solution)/shard_map/reduce_scatter | solution.py:389
  2100.3 356.4 %reduce-scatter.21.cloned.1.call-start = ((), (), s32[]{:S(2)}) async-start(), calls=%async_computation.24 | async-start | bytes 5013504 | tf_op jit(solution)/shard_map/reduce_scatter | solution.py:387
  2108.8 497.9 %reduce-scatter.19.cloned.1.call-start = ((), (), s32[]{:S(2)}) async-start(), calls=%async_computation.23 | async-start | bytes 15040512 | tf_op jit(solution)/shard_map/reduce_scatter | solution.py:386
  2136.0 620.6 %reduce-scatter.23.cloned.1.call-start = ((), (), s32[]{:S(2)}) async-start(), calls=%async_computation.25 | async-start | bytes 15040512 | tf_op jit(solution)/shard_map/reduce_scatter | solution.py:388
  2164.2 859.5 %reduce-scatter.27.cloned.1.call-start = ((), (), s32[]{:S(2)}) async-start(), calls=%async_computation.27 | async-start | bytes 29245440 | tf_op jit(solution)/shard_map/reduce_scatter | solution.py:392
  2186.9 1103.5 %reduce-scatter.29.cloned.1.call-start = ((), (), s32[]{:S(2)}) async-start(), calls=%async_computation.28 | async-start | bytes 29245440 | tf_op jit(solution)/shard_map/reduce_scatter | solution.py:393
  (151 other events, 3584.6 us)
Sparse Core Ops, SparseCore 0:
  95.0 59.3 all-gather.15
  156.7 66.6 all-gather.17
  225.7 40.7 all-gather.19
  317.2 121.6 all-reduce.22
  440.3 27.5 all-gather.21
  470.2 66.6 all-gather.23
  538.5 61.9 all-gather.25
  603.1 42.3 all-gather.27
  661.3 119.5 all-reduce.24
  783.1 108.8 all-gather.31
  893.5 61.6 all-gather.29
  957.4 108.1 all-gather.33
  1096.5 118.9 all-reduce.26
  1231.7 63.9 all-gather.35
  1351.0 120.7 all-reduce.28
  1502.9 63.9 all-gather.37
  1618.1 120.7 all-reduce.30
  1762.9 63.9 all-gather.39
  1945.7 121.9 all-reduce.32
  2072.7 95.9 reduce-scatter.32
  2171.5 25.0 reduce-scatter.16
  2202.6 95.6 reduce-scatter.30
  2303.2 74.5 reduce-scatter.24
  2382.1 74.5 reduce-scatter.20
  2462.0 144.6 reduce-scatter.18
  2611.9 144.6 reduce-scatter.22
  2761.7 261.9 reduce-scatter.26
  3028.4 261.9 reduce-scatter.28
where the time goes:
time: 3310 us; the launch traced here: 3300 us
  waiting for transfers between devices  2200 us (66%)
  blocking collectives  357 us (11%)
  matrix products  323 us (10%)
  other arithmetic  236 us (7%)
  local copies, waits for them, and re-layouts  156 us (5%)
    unnamed x36, waiting for transfers between devices  602 us
    all_gather x6, waiting for transfers between devices, collect(): return lax.all_gather(values, 'mp', axis=1, tiled=True)  312 us
    reduce_scatter x1, waiting for transfers between devices, local(): lax.psum_scatter(ffn_in_grad, 'dp', scatter_dimension=0, tiled=True)  267 us
    reduce_scatter x1, waiting for transfers between devices, local(): lax.psum_scatter(ffn_out_grad, 'dp', scatter_dimension=1, tiled=True)  267 us
    reduce_scatter x1, waiting for transfers between devices, local(): lax.psum_scatter(self_qkv_grad, 'dp', scatter_dimension=1, tiled=True)  150 us
    reduce_scatter x1, waiting for transfers between devices, local(): lax.psum_scatter(cross_qkv_grad, 'dp', scatter_dimension=1, tiled=True)  150 us
    unnamed x2, blocking collectives  97.9 us
    all_gather x1, waiting for transfers between devices, local(): lax.all_gather(ffn_out, 'dp', axis=1, tiled=True)  91.5 us
  transfers between devices with their start and end apart: 28, of which 24 were waited for; matrix products, arithmetic and copies ran while one was open for 10% of the time, Pallas kernels for 0%

commit v1 on v0

v1 whole, which is shorter than its diff:
```python
import functools
import math

import jax
import jax.numpy as jnp
import numpy as np
from jax import lax
from jax.experimental import pallas as pl
from jax.experimental.pallas import tpu as pltpu
from jax.sharding import PartitionSpec as P

D = 1536
HD = 128
EPS = 1e-06
SCALE = HD ** (-0.5)
BF = jnp.bfloat16
F32 = jnp.float32
NEG = -1e30
SWAP = [(0, 1), (1, 0)]
VMEM_BYTES = 48 * 1024 * 1024


def rope_rates():
    pair_count = HD // 2
    third = pair_count // 3
    counts = [pair_count - 2 * third, third, third]
    rates = np.zeros((3, HD), np.float32)
    start = 0
    for axis_id, count in enumerate(counts):
        steps = np.arange(count, dtype=np.float32) / np.float32(count)
        values = np.exp(np.float32(-math.log(10000.0)) * steps).astype(np.float32)
        rates[axis_id, 2 * start : 2 * (start + count)] = np.repeat(values, 2)
        start += count
    return rates


def dot_nn(a, b):
    return lax.dot_general(a, b, (((1,), (0,)), ((), ())), preferred_element_type=F32)


def dot_nt(a, b):
    return lax.dot_general(a, b, (((1,), (1,)), ((), ())), preferred_element_type=F32)


def dot_tn(a, b):
    return lax.dot_general(a, b, (((0,), (0,)), ((), ())), preferred_element_type=F32)


def cost(flops, nbytes, trans=0):
    return pl.CostEstimate(flops=int(flops), bytes_accessed=int(nbytes), transcendentals=int(trans))


def params():
    return pltpu.CompilerParams(vmem_limit_bytes=VMEM_BYTES)


def turn(values):
    lane = lax.broadcasted_iota(jnp.int32, values.shape, 1)
    after = pltpu.roll(values, HD - 1, 1)
    before = pltpu.roll(values, 1, 1)
    return jnp.where(lane % 2 == 0, after, before)


def prep_kernel(qp, kp, qs, ks, qg, kg, cos, sin, q_out, k_out):
    c = cos[...]
    s = sin[...]
    for pre, sq, gain, out in ((qp, qs, qg, q_out), (kp, ks, kg, k_out)):
        v = pre[...] * lax.rsqrt(sq[...] * (1.0 / D) + EPS) * gain[...]
        out[...] = (v * c + turn(v) * s).astype(BF)


def prep(qp, kp, qs, ks, qg, kg, cos, sin):
    rows, width = qp.shape
    head = pl.BlockSpec((rows, HD), lambda h: (0, h))
    col = pl.BlockSpec((rows, 1), lambda h: (0, 0))
    gain = pl.BlockSpec((1, HD), lambda h: (0, h))
    tab = pl.BlockSpec((rows, HD), lambda h: (0, 0))
    return pl.pallas_call(
        prep_kernel,
        grid=(width // HD,),
        in_specs=[head, head, col, col, gain, gain, tab, tab],
        out_specs=[head, head],
        out_shape=[jax.ShapeDtypeStruct((rows, width), BF)] * 2,
        compiler_params=params(),
        cost_estimate=cost(rows * width * 20, rows * width * 12),
        name="rope_prep",
    )(qp, kp, qs, ks, qg, kg, cos, sin)


def attend_kernel(masked, *refs):
    if masked:
        q, k, v, mask, out, lse = refs
    else:
        q, k, v, out, lse = refs
    st = dot_nt(k[...], q[...]) * SCALE
    if masked:
        st = st + mask[...]
    top = jnp.max(st, axis=0, keepdims=True)
    e = jnp.exp(st - top)
    total = jnp.sum(e, axis=0, keepdims=True)
    lse[0] = top + jnp.log(total)
    mixed = dot_tn(v[...], e.astype(BF)) * (1.0 / total)
    out[...] = mixed.T.astype(BF)


def attend(q, k, v, mask):
    nq, width = q.shape
    nk = k.shape[0]
    heads = width // HD
    qb = pl.BlockSpec((nq, HD), lambda h: (0, h))
    kb = pl.BlockSpec((nk, HD), lambda h: (0, h))
    ins = [qb, kb, kb]
    args = [q, k, v]
    if mask is not None:
        ins.append(pl.BlockSpec((nk, 1), lambda h: (0, 0)))
        args.append(mask)
    return pl.pallas_call(
        functools.partial(attend_kernel, mask is not None),
        grid=(heads,),
        in_specs=ins,
        out_specs=[qb, pl.BlockSpec((1, 1, nq), lambda h: (h, 0, 0))],
        out_shape=[
            jax.ShapeDtypeStruct((nq, width), BF),
            jax.ShapeDtypeStruct((heads, 1, nq), F32),
        ],
        compiler_params=params(),
        cost_estimate=cost(4 * nq * nk * width * 3, 4 * nq * width + 4 * nk * width, nq * nk * heads),
        name="attend_fwd",
    )(*args)


def attend_back_kernel(self_form, *refs):
    if self_form:
        (q, k, v, do, lse, mask, qp, kp, qs, ks, qg, kg, cos, sin,
         dq_out, dk_out, dv_out, qdot, kdot, qgain, kgain) = refs
    else:
        q, k, v, do, lse, qp, qs, qg, dq_out, dk_out, dv_out, qdot, qgain = refs
    st = dot_nt(k[...], q[...]) * SCALE
    if self_form:
        st = st + mask[...]
    p = jnp.exp(st - lse[0])
    dp = dot_nt(v[...], do[...])
    inner = jnp.sum(dp * p, axis=0, keepdims=True)
    ds = (p * (dp - inner)).astype(BF)
    dv_out[...] = dot_nn(p.astype(BF), do[...]).astype(dv_out.dtype)
    dk = dot_nn(ds, q[...]) * SCALE
    dq = dot_tn(k[...], ds).T * SCALE
    sides = [(dq, qp, qs, qg, dq_out, qdot, qgain)]
    if self_form:
        dq = dq * cos[...] - turn(dq) * sin[...]
        dk = dk * cos[...] - turn(dk) * sin[...]
        sides = [(dq, qp, qs, qg, dq_out, qdot, qgain), (dk, kp, ks, kg, dk_out, kdot, kgain)]
    else:
        dk_out[...] = dk
    for grad, pre, sq, gain, out, dots, gains in sides:
        p_rows = pre[...]
        weighted = grad * gain[...]
        out[...] = weighted
        part = jnp.sum(weighted * p_rows, axis=1, keepdims=True)

        @pl.when(pl.program_id(0) == 0)
        def _():
            dots[...] = part

        @pl.when(pl.program_id(0) > 0)
        def _():
            dots[...] += part

        scaled = p_rows * lax.rsqrt(sq[...] * (1.0 / D) + EPS)
        gains[...] = jnp.sum(grad * scaled, axis=0, keepdims=True)


def attend_back_self(q, k, v, do, lse, mask, qp, kp, qs, ks, qg, kg, cos, sin):
    n, width = q.shape
    heads = width // HD
    rows = pl.BlockSpec((n, HD), lambda h: (0, h))
    col = pl.BlockSpec((n, 1), lambda h: (0, 0))
    gain = pl.BlockSpec((1, HD), lambda h: (0, h))
    tab = pl.BlockSpec((n, HD), lambda h: (0, 0))
    lses = pl.BlockSpec((1, 1, n), lambda h: (h, 0, 0))
    full = jax.ShapeDtypeStruct((n, width), F32)
    cols = jax.ShapeDtypeStruct((n, 1), F32)
    gains = jax.ShapeDtypeStruct((1, width), F32)
    return pl.pallas_call(
        functools.partial(attend_back_kernel, True),
        grid=(heads,),
        in_specs=[rows, rows, rows, rows, lses, col, rows, rows, col, col, gain, gain, tab, tab],
        out_specs=[rows, rows, rows, col, col, gain, gain],
        out_shape=[full, full, jax.ShapeDtypeStruct((n, width), BF), cols, cols, gains, gains],
        compiler_params=params(),
        cost_estimate=cost(10 * n * n * width * 3, 26 * n * width, n * n * heads),
        name="attend_bwd_self",
    )(q, k, v, do, lse, mask, qp, kp, qs, ks, qg, kg, cos, sin)


def attend_back_cross(q, k, v, do, lse, qp, qs, qg):
    n, width = q.shape
    nk = k.shape[0]
    heads = width // HD
    rows = pl.BlockSpec((n, HD), lambda h: (0, h))
    keys = pl.BlockSpec((nk, HD), lambda h: (0, h))
    col = pl.BlockSpec((n, 1), lambda h: (0, 0))
    gain = pl.BlockSpec((1, HD), lambda h: (0, h))
    lses = pl.BlockSpec((1, 1, n), lambda h: (h, 0, 0))
    return pl.pallas_call(
        functools.partial(attend_back_kernel, False),
        grid=(heads,),
        in_specs=[rows, keys, keys, rows, lses, rows, col, gain],
        out_specs=[rows, keys, keys, col, gain],
        out_shape=[
            jax.ShapeDtypeStruct((n, width), F32),
            jax.ShapeDtypeStruct((nk, width), F32),
            jax.ShapeDtypeStruct((nk, width), F32),
            jax.ShapeDtypeStruct((n, 1), F32),
            jax.ShapeDtypeStruct((1, width), F32),
        ],
        compiler_params=params(),
        cost_estimate=cost(10 * n * nk * width * 3, 12 * n * width + 12 * nk * width, n * nk * heads),
        name="attend_bwd_cross",
    )(q, k, v, do, lse, qp, qs, qg)


def normal(values):
    center = values - jnp.mean(values, axis=-1, keepdims=True)
    scale = lax.rsqrt(jnp.mean(center * center, axis=-1, keepdims=True) + EPS)
    return center * scale, scale


def normal_back(grad, unit, scale):
    mean_g = jnp.mean(grad, axis=-1, keepdims=True)
    mean_gz = jnp.mean(grad * unit, axis=-1, keepdims=True)
    return scale * (grad - mean_g - unit * mean_gz)


def swap(values):
    return lax.ppermute(values, "mp", SWAP)


def collect(own):
    return jnp.concatenate([own, swap(own)], axis=0)


def spread(partial):
    half = partial.shape[0] // 2
    return partial[:half] + swap(partial[half:].astype(BF)).astype(F32)


def row_totals(own):
    half = own.shape[0] // 2
    return own + swap(jnp.concatenate([own[half:], own[:half]], axis=0))


def squares(values):
    return jnp.sum(values * values, axis=-1, keepdims=True)


def colsum(values):
    return jnp.sum(values, axis=0, dtype=F32)


def tie(*values):
    return lax.optimization_barrier(values)


def ring_order(chips):
    return list(range(0, chips, 2)) + list(range(chips - 1, 0, -2))


class Ring:
    def __init__(self, ndp, dp):
        self.chips = ndp // 2
        self.order = ring_order(self.chips)
        place = [self.order.index(i) for i in range(self.chips)]
        self.core = dp % 2
        self.place = jnp.asarray(place, jnp.int32)[dp // 2]
        self.way = 1 - 2 * self.core
        self.steps = []
        for i, chip in enumerate(self.order):
            after = self.order[(i + 1) % self.chips]
            self.steps.append((2 * chip, 2 * after))
            self.steps.append((2 * after + 1, 2 * chip + 1))
        self.pairs = [(i, i ^ 1) for i in range(ndp)]

    def chip_at(self, shift):
        spot = (self.place + self.way * shift) % self.chips
        return jnp.asarray(self.order, jnp.int32)[spot]

    def forward(self, values):
        return lax.ppermute(values, "dp", self.steps)

    def cross(self, values):
        return lax.ppermute(values, "dp", self.pairs)

    def gather(self, shard):
        k, r, n = shard.shape
        whole = jnp.zeros((k, 2 * self.chips, r, n), shard.dtype)
        piece = shard
        for step in range(self.chips):
            mine = 2 * self.chip_at(-step) + self.core
            theirs = 2 * self.chip_at(step) + 1 - self.core
            other = self.cross(piece)
            whole = lax.dynamic_update_slice(whole, piece[:, None], (0, mine, 0, 0))
            whole = lax.dynamic_update_slice(whole, other[:, None], (0, theirs, 0, 0))
            if step < self.chips - 1:
                piece = self.forward(piece)
        return whole

    def scatter_steps(self, full):
        k, rows, n = full.shape
        r = rows // (2 * self.chips)
        parts = full.astype(BF).reshape(k, self.chips, 2, r, n)
        mine = lax.dynamic_index_in_dim(parts, self.core, 2, False)
        theirs = lax.dynamic_index_in_dim(parts, 1 - self.core, 2, False)
        got = yield self.cross(theirs)
        total = None
        for step in range(self.chips):
            chip = self.chip_at(-1 - step)
            term = lax.dynamic_index_in_dim(mine, chip, 1, False).astype(F32)
            term = term + lax.dynamic_index_in_dim(got, chip, 1, False).astype(F32)
            total = term if total is None else total.astype(F32) + term
            if step < self.chips - 1:
                total = yield self.forward(total.astype(BF))
        yield total


class Steps:
    def __init__(self, ring, full):
        self.left = ring.chips
        self.work = ring.scatter_steps(full)
        self.piece = next(self.work)

    def step(self, *values):
        self.left -= 1
        *values, piece = tie(*values, self.piece)
        self.piece = self.work.send(piece)
        return values if len(values) > 1 else values[0]

    def finish(self):
        while self.left:
            self.left -= 1
            self.piece = self.work.send(self.piece)
        return self.piece


def partners(ndp, bit):
    return [(i, i ^ (1 << bit)) for i in range(ndp)]


def gather_small(flat, ndp, dp, mp):
    rows = flat[None]
    got = swap(rows)
    rows = jnp.where(mp == 0, jnp.concatenate([rows, got]), jnp.concatenate([got, rows]))
    for bit in range(ndp.bit_length() - 1):
        got = lax.ppermute(rows, "dp", partners(ndp, bit))
        low = (dp >> bit) % 2 == 0
        rows = jnp.where(low, jnp.concatenate([rows, got]), jnp.concatenate([got, rows]))
    return rows


def sum_small(values, ndp):
    for bit in range(ndp.bit_length() - 1):
        values = values + lax.ppermute(values, "dp", partners(ndp, bit))
    return values


def chunks_of(padded):
    first = (padded // 2 + 15) // 16 * 16
    return [(0, first), (first, padded)]


def local(
    hidden,
    text_states,
    time_emb,
    lengths,
    positions,
    teacher,
    modulation,
    out_bias,
    norm3_gain,
    self_qkv,
    self_out,
    cross_qkv,
    cross_out,
    ffn_in,
    ffn_out,
    head_bias,
    qk_gain,
    ffn_bias,
):
    ndp = lax.axis_size("dp")
    dp = lax.axis_index("dp")
    mp = lax.axis_index("mp")
    own_len = hidden.shape[1]
    length = 2 * own_len
    padded = (own_len + 15) // 16 * 16
    pad = padded - own_len
    cuts = chunks_of(padded)

    f32_part = jnp.concatenate([modulation, out_bias, norm3_gain[None]], axis=0)
    hb = head_bias.reshape(-1, head_bias.shape[-1])
    qg = qk_gain.reshape(-1, qk_gain.shape[-1])
    low_part = jnp.concatenate([hb, qg, ffn_bias], axis=0).astype(F32)
    n_f32, w_f32 = f32_part.shape
    n_low, w_low = low_part.shape
    flat = jnp.concatenate([f32_part.reshape(-1), low_part.reshape(-1)])
    n_flat = flat.shape[0]
    flat_all = gather_small(jnp.pad(flat, (0, -n_flat % 128)), ndp, dp, mp)[:, :n_flat]
    f32_all = flat_all[:, : n_f32 * w_f32].reshape(2 * ndp, n_f32, w_f32)
    f32_all = f32_all.transpose(1, 0, 2).reshape(n_f32, -1)
    low_all = flat_all[:, n_f32 * w_f32 :].reshape(ndp, 2, n_low, w_low)
    low_all = lax.dynamic_index_in_dim(low_all, mp, 1, False)
    low_all = low_all.transpose(1, 0, 2).reshape(n_low, -1)
    mod_full = f32_all[:6]
    out_bias_full = f32_all[6:10]
    norm3_full = f32_all[10]
    hb_full = low_all[: hb.shape[0]].reshape(2, 3, -1)
    qg_full = low_all[hb.shape[0] : hb.shape[0] + qg.shape[0]].reshape(2, 2, 1, -1)
    ffn_bias_full = low_all[hb.shape[0] + qg.shape[0] :].reshape(-1)

    ring = Ring(ndp, dp)
    def whole(shards):
        return lax.all_gather(shards, "dp", axis=1, tiled=True)

    heads_w = whole(jnp.concatenate([self_qkv, self_out.T[None], cross_qkv, cross_out.T[None]]))
    self_w = heads_w[:4]
    cross_w = heads_w[4:]
    ffn_w = whole(jnp.stack([ffn_in, ffn_out.T]))
    self_out_t = self_w[3]
    cross_out_t = cross_w[3]
    ffn_in_w = ffn_w[0]
    ffn_out_t = ffn_w[1]

    signals = mod_full + time_emb[0]
    shift_attn, scale_attn, gate_attn, shift_ffn, scale_ffn, gate_ffn = [
        signals[i : i + 1] for i in range(6)
    ]
    clip_length = lax.dynamic_index_in_dim(lengths, dp, 0, False)

    def own_chunks(array):
        full = jnp.pad(array, ((0, pad), (0, 0)))
        return [full[a:b] for a, b in cuts]

    hid = own_chunks(hidden[0])
    teach = own_chunks(teacher[0])
    index = jnp.arange(padded)
    pos_pad = jnp.pad(positions[0].reshape(3, 2, own_len), ((0, 0), (0, 0), (0, pad)))

    def both(own, other):
        return jnp.concatenate([x[a:b] for a, b in cuts for x in (own, other)], axis=0)

    def slot_valid(half):
        return (index < own_len) & (half * own_len + index < clip_length)

    own_valid = slot_valid(mp)
    key_valid = both(own_valid, slot_valid(1 - mp))
    key_mask = jnp.where(key_valid, 0.0, NEG).astype(F32)[:, None]
    row_valid = [own_valid.astype(F32)[a:b, None] for a, b in cuts]
    pos_own = lax.dynamic_index_in_dim(pos_pad, mp, 1, False)
    pos_other = lax.dynamic_index_in_dim(pos_pad, 1 - mp, 1, False)
    rates = rope_rates()
    angle = sum(
        both(pos_own[i], pos_other[i]).astype(F32)[:, None] * rates[i][None, :] for i in range(3)
    )
    even = np.arange(HD) % 2 == 0
    cos = jnp.cos(angle)
    sin = jnp.sin(angle) * np.where(even, -1.0, 1.0).astype(np.float32)
    ends = np.cumsum([0] + [2 * (b - a) for a, b in cuts])
    spans = [(int(ends[i]), int(ends[i + 1])) for i in range(len(cuts))]
    nc = len(cuts)

    text_rows = collect(text_states[0])
    cross_kp = dot_nn(text_rows, cross_w[1]) + hb_full[1, 1]
    cross_v = (dot_nn(text_rows, cross_w[2]) + hb_full[1, 2]).astype(BF)
    cross_ks = row_totals(squares(cross_kp))
    cross_kr = lax.rsqrt(cross_ks / D + EPS)
    cross_k = (cross_kp * cross_kr * qg_full[1, 1]).astype(BF)

    res0, unit0, scale0, rows0 = [], [], [], []
    qp, kp, vv, qs, ks = [], [], [], [], []
    for c in range(nc):
        r = hid[c].astype(F32)
        z, s = normal(r)
        x = (z * (1.0 + scale_attn) + shift_attn).astype(BF)
        rows = collect(x)
        qc = dot_nn(rows, self_w[0]) + hb_full[0, 0]
        kc = dot_nn(rows, self_w[1]) + hb_full[0, 1]
        vc = (dot_nn(rows, self_w[2]) + hb_full[0, 2]).astype(BF)
        tot = row_totals(jnp.concatenate([squares(qc), squares(kc)], axis=1))
        res0.append(r)
        unit0.append(z)
        scale0.append(s)
        rows0.append(rows)
        qp.append(qc)
        kp.append(kc)
        vv.append(vc)
        qs.append(tot[:, 0:1])
        ks.append(tot[:, 1:2])
    qp, kp, vv = [jnp.concatenate(x, axis=0) for x in (qp, kp, vv)]
    qs, ks = [jnp.concatenate(x, axis=0) for x in (qs, ks)]
    rows0 = jnp.concatenate(rows0, axis=0)
    self_q, self_k = prep(qp, kp, qs, ks, qg_full[0, 0], qg_full[0, 1], cos, sin)

    self_mixed, self_lse = [], []
    cross_mixed, cross_lse, cross_q, cross_qp, cross_qs = [], [], [], [], []
    rows1, rows2, branch0, unit1, scale1, unit2, scale2 = [], [], [], [], [], [], []
    acts, slopes, results, errors, d_ffn_all, grads2 = [], [], [], [], [], []
    gate_ffn_grad, err_sq = 0.0, 0.0
    for c in range(nc):
        a, b = spans[c]
        mixed, lse = attend(self_q[a:b], self_k, vv, key_mask)
        self_mixed.append(mixed)
        self_lse.append(lse)
        branch = spread(dot_nt(mixed, self_out_t)) + out_bias_full[1]
        after_self = res0[c] + gate_attn * branch
        branch0.append(branch)
        z, s = normal(after_self)
        unit1.append(z)
        scale1.append(s)
        rows = collect((z * norm3_full + out_bias_full[0]).astype(BF))
        rows1.append(rows)
        qc = dot_nn(rows, cross_w[0]) + hb_full[1, 0]
        tot = row_totals(squares(qc))
        qn = (qc * lax.rsqrt(tot / D + EPS) * qg_full[1, 0]).astype(BF)
        cross_qp.append(qc)
        cross_qs.append(tot)
        cross_q.append(qn)
        mixed, lse = attend(qn, cross_k, cross_v, None)
        cross_mixed.append(mixed)
        cross_lse.append(lse)
        after_cross = after_self + spread(dot_nt(mixed, cross_out_t)) + out_bias_full[2]
        z, s = normal(after_cross)
        unit2.append(z)
        scale2.append(s)
        rows = collect((z * (1.0 + scale_ffn) + shift_ffn).astype(BF))
        rows2.append(rows)
        inner = dot_nn(rows, ffn_in_w) + ffn_bias_full
        act, back = jax.vjp(functools.partial(jax.nn.gelu, approximate=True), inner)
        slope = back(jnp.ones_like(inner))[0]
        act = act.astype(BF)
        acts.append(act)
        slopes.append(slope.astype(BF))
        branch = spread(dot_nt(act, ffn_out_t)) + out_bias_full[3]
        result = after_cross + gate_ffn * branch
        results.append(result.astype(BF))
        error = (result - teach[c].astype(F32)) * row_valid[c]
        errors.append(error)
        err_sq = err_sq + jnp.sum(error * error)
        gate_ffn_grad = gate_ffn_grad + colsum(branch * error)
        d_ffn_all.append((gate_ffn * error).astype(BF))

    def cat(parts):
        return jnp.concatenate(parts, axis=0)

    bias3 = bias2 = bias0 = bias1 = shift2 = scale2_g = norm3_g = gate0_g = 0.0
    ffn_b_grad = cross_qb = cross_qgain = 0.0
    d_rows2, d_inners, d_rows1, d_qpres = [], [], [], []
    cross_dk = cross_dv = 0.0
    d_rows0, state, backs = [], [], []
    def reduce_rows(full):
        return lax.psum_scatter(full, "dp", scatter_dimension=1, tiled=True)

    for c in range(nc):
        bias3 = bias3 + colsum(d_ffn_all[c].astype(F32))
        d_rows2.append(collect(d_ffn_all[c]))
    g_out = dot_tn(cat(d_rows2), cat(acts)).astype(BF)
    d_rows2[-1], g_out = tie(d_rows2[-1], g_out)
    s_out = reduce_rows(g_out[None])
    for c in range(nc):
        rows = d_rows2[c]
        d_inner = (dot_nn(rows, ffn_out_t) * slopes[c].astype(F32)).astype(BF)
        d_inners.append(d_inner)
        ffn_b_grad = ffn_b_grad + colsum(d_inner.astype(F32))
        backs.append(spread(dot_nt(d_inner, ffn_in_w)))
    g_in = dot_tn(cat(rows2), cat(d_inners)).astype(BF)
    for c in range(nc):
        back = backs[c]
        shift2 = shift2 + colsum(back)
        scale2_g = scale2_g + colsum(back * unit2[c])
        d_after_cross = errors[c] + normal_back(back * (1.0 + scale_ffn), unit2[c], scale2[c])
        d_cross = d_after_cross.astype(BF)
        bias2 = bias2 + colsum(d_cross.astype(F32))
        rows = collect(d_cross)
        d_rows1.append(rows)
        d_mixed = dot_nn(rows, cross_out_t).astype(BF)
        if c == 0:
            d_mixed, g_in = tie(d_mixed, g_in)
        dqw, dk, dv, qdot, qgain = attend_back_cross(
            cross_q[c], cross_k, cross_v, d_mixed, cross_lse[c], cross_qp[c], cross_qs[c], qg_full[1, 0]
        )
        cross_dk = cross_dk + dk
        cross_dv = cross_dv + dv
        cross_qgain = cross_qgain + qgain[0]
        r = lax.rsqrt(cross_qs[c] / D + EPS)
        dot = row_totals(qdot)
        d_qpre = (dqw * r - cross_qp[c] * (r * r * r * dot / D)).astype(BF)
        d_qpres.append(d_qpre)
        cross_qb = cross_qb + colsum(d_qpre.astype(F32))
        back = spread(dot_nt(d_qpre, cross_w[0]))
        norm3_g = norm3_g + colsum(back * unit1[c])
        bias0 = bias0 + colsum(back)
        st = d_after_cross + normal_back(back * norm3_full, unit1[c], scale1[c])
        state.append(st)
        gate0_g = gate0_g + colsum(branch0[c] * st)
        d_self = (gate_attn * st).astype(BF)
        if c == nc - 1:
            d_self, s_out = tie(d_self, s_out)
            s_in = reduce_rows(g_in[None])
        bias1 = bias1 + colsum(d_self.astype(F32))
        d_rows0.append(collect(d_self))
    ffn_out_g = s_out[0].astype(F32).T

    cross_dkw = cross_dk * qg_full[1, 1]
    kdot = row_totals(jnp.sum(cross_dkw * cross_kp, axis=-1, keepdims=True))
    cross_kgain = colsum(cross_dk * cross_kp * cross_kr)
    d_kpre = (cross_dkw * cross_kr - cross_kp * (cross_kr**3 * kdot / D)).astype(BF)
    d_v = cross_dv.astype(BF)
    g_cross = jnp.stack(
        [
            dot_tn(cat(rows1), cat(d_qpres)).astype(BF),
            dot_tn(text_rows, d_kpre).astype(BF),
            dot_tn(text_rows, d_v).astype(BF),
            dot_tn(cat(d_rows1), cat(cross_mixed)).astype(BF),
        ]
    )
    text_g = spread(dot_nt(d_kpre, cross_w[1]) + dot_nt(d_v, cross_w[2]))
    cross_b = jnp.stack([cross_qb, colsum(d_kpre.astype(F32)), colsum(d_v.astype(F32))])

    d_rows0 = cat(d_rows0)
    d_mixed = dot_nn(d_rows0, self_out_t).astype(BF)
    g_self_out = dot_tn(d_rows0, cat(self_mixed)).astype(BF)
    d_mixed, g_self_out, g_cross = tie(d_mixed, g_self_out, g_cross)
    lse = jnp.concatenate(self_lse, axis=2)
    dqw, dkw, dv, qdot, kdot, self_qgain, self_kgain = attend_back_self(
        self_q, self_k, vv, d_mixed, lse, key_mask, qp, kp, qs, ks, qg_full[0, 0], qg_full[0, 1], cos, sin
    )
    dots = []
    for a, b in spans:
        dots.append(row_totals(jnp.concatenate([qdot[a:b], kdot[a:b]], axis=1)))
    g_vo = jnp.stack([dot_tn(rows0, dv).astype(BF), g_self_out])
    steps_vo = Steps(ring, g_vo)
    dots = steps_vo.step(cat(dots))
    rq = lax.rsqrt(qs / D + EPS)
    rk = lax.rsqrt(ks / D + EPS)
    d_q = (dqw * rq - qp * (rq**3 * dots[:, 0:1] / D)).astype(BF)
    d_k = (dkw * rk - kp * (rk**3 * dots[:, 1:2] / D)).astype(BF)
    d_q, d_k, s_in, g_cross = tie(d_q, d_k, s_in, g_cross)
    ffn_in_g = s_in[0].astype(F32)
    cross_g = reduce_rows(g_cross).astype(F32)
    cross_qkv_g = cross_g[:3]
    cross_out_g = cross_g[3].T
    backs = []
    for a, b in spans:
        backs.append(dot_nt(d_q[a:b], self_w[0]) + dot_nt(d_k[a:b], self_w[1]) + dot_nt(dv[a:b], self_w[2]))
    d_q, d_k, *backs = steps_vo.step(d_q, d_k, *backs)
    g_qk = jnp.stack([dot_tn(rows0, g).astype(BF) for g in (d_q, d_k)])
    backs = [spread(x) for x in backs]
    g_qk = steps_vo.step(g_qk)
    self_g = jnp.concatenate([Steps(ring, g_qk).finish(), steps_vo.finish()])
    self_qkv_g = self_g[:3]
    self_out_g = self_g[3].T
    self_b = jnp.stack([colsum(g.astype(F32)) for g in (d_q, d_k, dv)])
    shift0 = scale0_g = 0.0
    hidden_g = []
    for c in range(nc):
        back = backs[c]
        shift0 = shift0 + colsum(back)
        scale0_g = scale0_g + colsum(back * unit0[c])
        hidden_g.append(state[c] + normal_back(back * (1.0 + scale_attn), unit0[c], scale0[c]))

    wide = jnp.stack(
        [shift0, scale0_g, gate0_g, shift2, scale2_g, gate_ffn_grad, bias0, bias1, bias2, bias3, norm3_g]
        + [jnp.broadcast_to(err_sq, (D,))]
    )
    narrow = jnp.concatenate(
        [
            self_b.reshape(-1, HD),
            cross_b.reshape(-1, HD),
            jnp.stack([self_qgain[0], self_kgain[0], cross_qgain, cross_kgain]).reshape(-1, HD),
            ffn_b_grad.reshape(-1, HD),
        ],
        axis=0,
    )
    n_wide = wide.size // HD
    small = sum_small(jnp.concatenate([wide.reshape(-1, HD), narrow]), ndp)
    wide = (small[:n_wide] + swap(small[:n_wide])).reshape(-1, D)
    narrow = lax.dynamic_slice_in_dim(small[n_wide:], dp * w_low, w_low, 1)
    mine = lax.dynamic_slice_in_dim(wide, (dp * 2 + mp) * w_f32, w_f32, 1)
    mean_loss = wide[11, 0] / (jnp.sum(lengths).astype(F32) * D)
    nh = head_bias.size // head_bias.shape[-1]
    ng = qk_gain.size // qk_gain.shape[-1]
    return (
        cat(results)[None, :own_len],
        mean_loss,
        cat(hidden_g)[None, :own_len],
        text_g[None],
        mine[:6],
        mine[6:10],
        mine[10],
        self_qkv_g,
        self_out_g,
        cross_qkv_g,
        cross_out_g,
        ffn_in_g,
        ffn_out_g,
        narrow[:nh].reshape(head_bias.shape),
        narrow[nh : nh + ng].reshape(qk_gain.shape),
        narrow[nh + ng :].reshape(ffn_bias.shape),
    )


def solution(mesh):
    in_specs = (
        P("dp", "mp", None),
        P("dp", "mp", None),
        P("dp", None, None),
        P(),
        P("dp", None, None),
        P("dp", "mp", None),
        P(None, ("dp", "mp")),
        P(None, ("dp", "mp")),
        P(("dp", "mp")),
        P(None, "dp", "mp"),
        P("mp", "dp"),
        P(None, "dp", "mp"),
        P("mp", "dp"),
        P("dp", "mp"),
        P("mp", "dp"),
        P(None, None, "mp", "dp"),
        P(None, None, "mp", "dp"),
        P("mp", "dp"),
    )
    out_specs = (
        P("dp", "mp", None),
        P(),
        P("dp", "mp", None),
        P("dp", "mp", None),
        P(None, ("dp", "mp")),
        P(None, ("dp", "mp")),
        P(("dp", "mp")),
        P(None, "dp", "mp"),
        P("mp", "dp"),
        P(None, "dp", "mp"),
        P("mp", "dp"),
        P("dp", "mp"),
        P("mp", "dp"),
        P(None, None, "mp", "dp"),
        P(None, None, "mp", "dp"),
        P("mp", "dp"),
    )
    return jax.shard_map(local, mesh=mesh, in_specs=in_specs, out_specs=out_specs, check_vma=False)
```

time: 3310 us -> 874 us (0.26)
  waiting for transfers between devices: 2200 us -> 234 us
  blocking collectives: 357 us -> 0 us
  other arithmetic: 236 us -> 113 us
  local copies, waits for them, and re-layouts: 156 us -> 56.8 us
  Pallas kernels: 0 us -> 82.8 us
  starting transfers between devices: 3.63 us -> 84.7 us
  matrix products: 323 us -> 250 us
    reduce_scatter x7 -> x3, waiting for transfers between devices: 966 us -> 0.01 us  [reduce_rows(): return lax.psum_scatter(full, 'dp', scatter_dimension=1, tiled=True)]
    unnamed x36 -> x5, waiting for transfers between devices: 602 us -> 0.08 us
    all_gather x13 -> x2, waiting for transfers between devices: 634 us -> 49.2 us  [whole(): return lax.all_gather(shards, 'dp', axis=1, tiled=True)]
    all_gather x5 -> x0, blocking collectives: 197 us -> none  [the longest x1 70.7 us: local(): lax.all_gather(modulation, ('dp', 'mp'), axis=1, tiled=True)]
    ppermute x0 -> x62, waiting for transfers between devices: none -> 184 us  [the longest x38 132 us: swap(): return lax.ppermute(values, 'mp', SWAP)]
    reduce_sum x26 -> x34, other arithmetic: 151 us -> 35.2 us  [the longest x17 20.8 us: colsum(): return jnp.sum(values, axis=0, dtype=F32)]
    unnamed x2 -> x0, blocking collectives: 97.9 us -> none
    ppermute x0 -> x62, starting transfers between devices: none -> 84.5 us  [the longest x38 43.7 us: swap(): return lax.ppermute(values, 'mp', SWAP)]
  transfers between devices with their start and end apart: 28 -> 67, of which waited for: 24 -> 30; matrix products, arithmetic and copies ran while one was open for 10% -> 44% of each run, Pallas kernels for 0% -> 10%
where the time goes in v1:
time: 874 us; the launch traced here: 863 us
  matrix products  250 us (29%)
  waiting for transfers between devices  234 us (27%)
  other arithmetic  113 us (13%)
  starting transfers between devices  84.7 us (10%)
  Pallas kernels  82.8 us (9%)
  local copies, waits for them, and re-layouts  56.8 us (6%)
  between operations  42 us (5%)
    ppermute x38, waiting for transfers between devices, swap(): return lax.ppermute(values, 'mp', SWAP)  132 us
    dot_general x17, matrix products, dot_nn(): lax.dot_general(a, b, (((1,), (0,)), ((), ())), preferred_element_type=F32)  93.5 us
    dot_general x18, matrix products, dot_nt(): lax.dot_general(a, b, (((1,), (1,)), ((), ())), preferred_element_type=F32)  84.9 us
    dot_general x10, matrix products, dot_tn(): lax.dot_general(a, b, (((0,), (0,)), ((), ())), preferred_element_type=F32)  71.5 us
    all_gather x2, waiting for transfers between devices, whole(): return lax.all_gather(shards, 'dp', axis=1, tiled=True)  49.2 us
    ppermute x38, starting transfers between devices, swap(): return lax.ppermute(values, 'mp', SWAP)  43.7 us
    pallas_call x4, Pallas kernels, attend(): pl.pallas_call(functools.partial(attend_kernel, mask is not None), grid=(...  34.5 us
    ppermute x14, starting transfers between devices, forward(): return lax.ppermute(values, 'dp', self.steps)  32.8 us
  transfers between devices with their start and end apart: 67, of which 30 were waited for; matrix products, arithmetic and copies ran while one was open for 44% of the time, Pallas kernels for 10%

profile of v1, /device:TPU:0, one launch (start us, length us, event | category | flops | bytes accessed | tf_op | source)
XLA Modules:
  0.0 863.1 jit_solution(10162674425082357460)
XLA Ops:
  35.1 6.7 collective-permute-done.4
  53.2 12.3 %collective-permute-done.6 = bf16[192,1536]{1,0:T(8,128)(2,1)} collective-permute-done((bf16[192,1536]{1,0:T(8,128)(2,1)}, bf16[192,1536]{1,0:T(8,128)(2,1)}, u32[]{:S(2)}, u32[]{:S(2)}) %collective-permute-start.6) | collective-permute-done | bytes 589856 | tf_op jit(solution)/shard_map/ppermute | solution.py:236
  65.5 49.2 %all-gather.3.cloned.1.call-done = bf16[8,1536,768]{2,1,0:T(8,128)(2,1)} async-done(((bf16[8,96,768]{2,1,0:T(8,128)(2,1)}), bf16[8,1536,768]{2,1,0:T(8,128)(2,1)}) %all-gather.3.cloned.1.call-update) | async-done | bytes 18874384 | tf_op jit(solution)/shard_map/all_gather | solution.py:423
  144.3 7.2 rope_prep.1
  163.8 7.0 attend_fwd.4
  181.2 10.9 %collective-permute-done.9 = bf16[208,1536]{1,0:T(8,128)(2,1)S(1)} collective-permute-done((bf16[208,1536]{1,0:T(8,128)(2,1)S(1)}, bf16[208,1536]{1,0:T(8,128)(2,1)S(1)}, u32[]{:S(2)}, u32[]{:S(2)}) %collective-permute-start.9) | collective-permute-done | bytes 639008 | tf_op jit(solution)/shard_map/ppermute | solution.py:236
  193.0 10.6 %collective-permute-done.18 = bf16[192,1536]{1,0:T(8,128)(2,1)S(1)} collective-permute-done((bf16[192,1536]{1,0:T(8,128)(2,1)S(1)}, bf16[192,1536]{1,0:T(8,128)(2,1)S(1)}, u32[]{:S(2)}, u32[]{:S(2)}) %collective-permute-start.18) | collective-permute-done | bytes 589856 | tf_op jit(solution)/shard_map/ppermute | solution.py:236
  240.8 16.8 %attend_fwd.5 = (bf16[416,768]{1,0:T(8,128)(2,1)S(1)}, f32[6,1,416]{2,1,0:T(1,128)S(1)}) custom-call(bf16[416,768]{1,0:T(8,128)(2,1)S(1)} %multiply_convert_fusion.5.refs_0_, bf16[512,768]{1,0:T(8,128)(2,1)S(1)} %copy-done.13, bf16[512,768]{1,0:T(8,128)(2,1)S(1)} %copy-done.32), custom_call_target="tpu_custom_call" | custom-call | flops 1962934272 | bytes 2850816 | tf_op jit(solution)/shard_map/attend_fwd/pallas_call | solution.py:117
  265.1 13.2 %collective-permute-done.14 = bf16[208,1536]{1,0:T(8,128)(2,1)S(1)} collective-permute-done((bf16[208,1536]{1,0:T(8,128)(2,1)S(1)}, bf16[208,1536]{1,0:T(8,128)(2,1)S(1)}, u32[]{:S(2)}, u32[]{:S(2)}) %collective-permute-start.14) | collective-permute-done | bytes 639008 | tf_op jit(solution)/shard_map/ppermute | solution.py:236
  282.1 8.9 %collective-permute-done.21 = bf16[192,1536]{1,0:T(8,128)(2,1)} collective-permute-done((bf16[192,1536]{1,0:T(8,128)(2,1)S(1)}, bf16[192,1536]{1,0:T(8,128)(2,1)}, u32[]{:S(2)}, u32[]{:S(2)}) %collective-permute-start.21) | collective-permute-done | bytes 589856 | tf_op jit(solution)/shard_map/ppermute | solution.py:236
  291.0 11.7 %multiply_convert_fusion.1 = (bf16[384,4480]{1,0:T(8,128)(2,1)S(1)}, f32[384,4480]{1,0:T(8,128)}) fusion(f32[4480]{0:T(1024)} %add.1140, bf16[2,1536,4480]{2,1,0:T(8,128)(2,1)} %all-gather.5.cloned.1.call-done, bf16[192,1536]{1,0:T(8,128)(2,1)} %collective-permute-done.21, bf16[192,1536]{1,0:T(8,128)(2,1)S(1)} %add_convert_fusion.4), kind=kOutput, calls=%fused_computation.64 | convolution fusion | flops 5304385536 | bytes 25284608 | tf_op jit(solution)/shard_map/dot_general | solution.py:38
  302.8 10.1 %fusion.6 = f32[384,1536]{1,0:T(8,128)S(1)} fusion(bf16[384,4480]{1,0:T(8,128)(2,1)S(1)} %get-tuple-element.361, bf16[2,1536,4480]{2,1,0:T(8,128)(2,1)} %all-gather.5.cloned.1.call-done), kind=kOutput, calls=%fused_computation.33 | convolution fusion | flops 5284823040 | bytes 19562496 | tf_op jit(solution)/shard_map/dot_general | solution.py:42
  316.5 12.6 %multiply_convert_fusion = (bf16[416,4480]{1,0:T(8,128)(2,1)S(1)}, f32[416,4480]{1,0:T(8,128)}) fusion(f32[4480]{0:T(1024)S(1)} %copy-done.175, bf16[2,1536,4480]{2,1,0:T(8,128)(2,1)} %all-gather.5.cloned.1.call-done, bf16[208,1536]{1,0:T(8,128)(2,1)} %collective-permute-done.15, bf16[208,1536]{1,0:T(8,128)(2,1)} %add_convert_fusion.2), kind=kOutput, calls=%fused_computation.45 | convolution fusion | flops 5746417664 | bytes 26240512 | tf_op jit(solution)/shard_map/dot_general | solution.py:38
  329.1 10.3 %fusion.7 = f32[416,1536]{1,0:T(8,128)S(1)} fusion(bf16[416,4480]{1,0:T(8,128)(2,1)S(1)} %get-tuple-element.359, bf16[2,1536,4480]{2,1,0:T(8,128)(2,1)} %all-gather.5.cloned.1.call-done), kind=kOutput, calls=%fused_computation.34 | convolution fusion | flops 5725224960 | bytes 20045824 | tf_op jit(solution)/shard_map/dot_general | solution.py:42
  348.9 10.5 %collective-permute-done.16 = bf16[208,1536]{1,0:T(8,128)(2,1)} collective-permute-done((bf16[208,1536]{1,0:T(8,128)(2,1)}, bf16[208,1536]{1,0:T(8,128)(2,1)}, u32[]{:S(2)}, u32[]{:S(2)}) %collective-permute-start.16) | collective-permute-done | bytes 639008 | tf_op jit(solution)/shard_map/ppermute | solution.py:236
  377.1 17.4 %convolution_convert_fusion.1 = bf16[1536,4480]{1,0:T(8,128)(2,1)} fusion(bf16[384,4480]{1,0:T(8,128)(2,1)S(1)} %copy-done.234, bf16[416,4480]{1,0:T(8,128)(2,1)S(1)} %copy-done.232, bf16[192,1536]{1,0:T(8,128)(2,1)S(1)} %collective-permute-done.26, bf16[192,1536]{1,0:T(8,128)(2,1)S(1)} %get-tuple-element.256, ...), kind=kOutput, calls=%fused_computation.1 | convolution fusion | flops 11041095680 | bytes 23388160 | tf_op jit(solution)/shard_map/dot_general | solution.py:46
  394.6 15.0 %convert_reduce_fusion = (f32[4480]{0:T(1024)}, bf16[416,4480]{1,0:T(8,128)(2,1)S(1)}) fusion(f32[416,4480]{1,0:T(8,128)} %get-tuple-element.360, bf16[2,1536,4480]{2,1,0:T(8,128)(2,1)} %all-gather.5.cloned.1.call-done, bf16[208,1536]{1,0:T(8,128)(2,1)} %copy-done.225, bf16[208,1536]{1,0:T(8,128)(2,1)} %copy-done.116), kind=kOutput, calls=%fused_computation.44 | convolution fusion | flops 5770640896 | bytes 26240512 | tf_op jit(solution)/shard_map/dot_general | solution.py:38
  409.6 10.5 %fusion.1 = f32[416,1536]{1,0:T(8,128)S(1)} fusion(bf16[416,4480]{1,0:T(8,128)(2,1)S(1)} %get-tuple-element.364, bf16[2,1536,4480]{2,1,0:T(8,128)(2,1)} %all-gather.5.cloned.1.call-done), kind=kOutput, calls=%fused_computation.28 | convolution fusion | flops 5725224960 | bytes 20045824 | tf_op jit(solution)/shard_map/dot_general | solution.py:42
  421.7 14.6 %convert_reduce_fusion.1 = (f32[4480]{0:T(1024)}, bf16[384,4480]{1,0:T(8,128)(2,1)}) fusion(f32[384,4480]{1,0:T(8,128)} %get-tuple-element.362, bf16[384,1536]{1,0:T(8,128)(2,1)S(1)} %copy-done.105, bf16[2,1536,4480]{2,1,0:T(8,128)(2,1)} %all-gather.5.cloned.1.call-done), kind=kOutput, calls=%fused_computation.63 | convolution fusion | flops 5324385792 | bytes 25282048 | tf_op jit(solution)/shard_map/dot_general | solution.py:38
  442.4 20.0 %convolution_convert_fusion = bf16[1536,4480]{1,0:T(8,128)(2,1)} fusion(bf16[384,4480]{1,0:T(8,128)(2,1)} %get-tuple-element.366, bf16[416,4480]{1,0:T(8,128)(2,1)S(1)} %get-tuple-element.364, bf16[192,1536]{1,0:T(8,128)(2,1)} %collective-permute-done.21, bf16[192,1536]{1,0:T(8,128)(2,1)S(1)} %copy-done.120, bf16[208,1536]{1,0:T(8,128)(2,1)} %collective-permute-done.15, ...), kind=kOutput, calls=%fused_computation | convolution fusion | flops 11041095680 | bytes 23388160 | tf_op jit(solution)/shard_map/dot_general | solution.py:46
  466.4 10.1 %fusion = f32[384,1536]{1,0:T(8,128)S(1)} fusion(bf16[384,4480]{1,0:T(8,128)(2,1)} %get-tuple-element.366, bf16[2,1536,4480]{2,1,0:T(8,128)(2,1)} %all-gather.5.cloned.1.call-done), kind=kOutput, calls=%fused_computation.27 | convolution fusion | flops 5284823040 | bytes 19562496 | tf_op jit(solution)/shard_map/dot_general | solution.py:42
  478.0 9.9 %collective-permute-done.30 = bf16[192,1536]{1,0:T(8,128)(2,1)S(1)} collective-permute-done((bf16[192,1536]{1,0:T(8,128)(2,1)S(1)}, bf16[192,1536]{1,0:T(8,128)(2,1)S(1)}, u32[]{:S(2)}, u32[]{:S(2)}) %collective-permute-start.30) | collective-permute-done | bytes 589856 | tf_op jit(solution)/shard_map/ppermute | solution.py:236
  520.8 8.3 attend_bwd_cross.3
  543.0 9.8 %attend_bwd_cross.2 = (f32[416,768]{1,0:T(8,128)S(1)}, f32[512,768]{1,0:T(8,128)}, f32[512,768]{1,0:T(8,128)}, f32[416,1]{1,0:T(8,128)S(1)}, f32[1,768]{1,0:T(1,128)S(1)}) custom-call(bf16[416,768]{1,0:T(8,128)(2,1)S(1)} %copy-done.15, bf16[512,768]{1,0:T(8,128)(2,1)S(1)} %copy-done.13, bf16[512,768]{1,0:T(8,128)(2,1)S(1)} %copy-done.33, ...), custom_call_target="tpu_custom_call" | custom-call | flops 4907335680 | bytes 8552448 | tf_op jit(solution)/shard_map/attend_bwd_cross/pallas_call | solution.py:205
  601.8 9.3 %pad_maximum_fusion = bf16[4,1536,768]{2,1,0:T(8,128)(2,1)} fusion(bf16[1,1536,768]{2,1,0:T(8,128)(2,1)} %fusion.37, bf16[1,1536,768]{2,1,0:T(8,128)(2,1)} %fusion.35, bf16[1,1536,768]{2,1,0:T(8,128)(2,1)} %fusion.34, bf16[1,1536,768]{2,1,0:T(8,128)(2,1)} %fusion.36), kind=kLoop, calls=%fused_computation.26 | loop fusion | flops 14155776 | bytes 18874368 | tf_op jit(solution)/shard_map/stack | solution.py:618
  611.1 8.9 %collective-permute-done.29 = bf16[208,1536]{1,0:T(8,128)(2,1)} collective-permute-done((bf16[208,1536]{1,0:T(8,128)(2,1)S(1)}, bf16[208,1536]{1,0:T(8,128)(2,1)}, u32[]{:S(2)}, u32[]{:S(2)}) %collective-permute-start.29) | collective-permute-done | bytes 639008 | tf_op jit(solution)/shard_map/ppermute | solution.py:236
  636.4 22.9 %attend_bwd_self.1 = (f32[800,768]{1,0:T(8,128)}, f32[800,768]{1,0:T(8,128)}, bf16[800,768]{1,0:T(8,128)(2,1)S(1)}, f32[800,1]{1,0:T(8,128)S(1)}, f32[800,1]{1,0...) custom-call(bf16[800,768]{1,0:T(8,128)(2,1)S(1)} %copy-done.11, bf16[800,768]{1,0:T(8,128)(2,1)} %copy-done.22, ...), custom_call_target="tpu_custom_call" | custom-call | flops 14745600000 | bytes 15974400 | tf_op jit(solution)/shard_map/attend_bwd_self/pallas_call | solution.py:184
  738.1 7.5 collective-permute-done.57
  747.6 6.9 collective-permute-start.58
  769.9 8.8 %collective-permute-done.50 = bf16[2,96,768]{2,1,0:T(8,128)(2,1)} collective-permute-done((bf16[2,96,768]{2,1,0:T(8,128)(2,1)}, bf16[2,96,768]{2,1,0:T(8,128)(2,1)}, u32[]{:S(2)}, u32[]{:S(2)}) %collective-permute-start.50) | collective-permute-done | bytes 294944 | tf_op jit(solution)/shard_map/ppermute | solution.py:289
  795.9 11.0 %collective-permute-done.45 = f32[239,128]{1,0:T(8,128)S(1)} collective-permute-done((f32[239,128]{1,0:T(8,128)S(1)}, f32[239,128]{1,0:T(8,128)S(1)}, u32[]{:S(2)}, u32[]{:S(2)}) %collective-permute-start.45) | collective-permute-done | bytes 122400 | tf_op jit(solution)/shard_map/ppermute | solution.py:362
  808.8 8.4 collective-permute-start.53
  (933 shorter events, 423.8 us)
Async XLA Ops:
  7.2 107.5 %all-gather.3.cloned.1.call-start = ((), (), s32[]{:S(2)}) async-start(), calls=%async_computation.3 | async-start | bytes 20054016 | tf_op jit(solution)/shard_map/all_gather | solution.py:423
  9.8 281.3 %all-gather.5.cloned.1.call-start = ((), (), s32[]{:S(2)}) async-start(), calls=%async_computation.4 | async-start | bytes 29245440 | tf_op jit(solution)/shard_map/all_gather | solution.py:423
  12.6 588.2 %reduce-scatter.4.cloned.1.call-start = ((), (), s32[]{:S(2)}) async-start(), calls=%async_computation.5 | async-start | bytes 14622720 | tf_op jit(solution)/shard_map/reduce_scatter | solution.py:561
  16.6 111.7 %collective-permute-start.12 = (bf16[256,1536]{1,0:T(8,128)(2,1)}, bf16[256,1536]{1,0:T(8,128)(2,1)}, u32[]{:S(2)}, u32[]{:S(2)}) collective-permute-start(bf16[256,1536]{1,0:T(8,128)(2,1)} %bitcast.36), channel_id=1, source_target_pairs={{0,1},{1,0},{2,3},{3,2},{4,5},{5,4},{6,7},{7,6},{8,9},{9,8},{10,11... | collective-permute-start | bytes 2359304 | tf_op jit(solution)/shard_map/ppermute | solution.py:236
  51.0 73.1 %collective-permute-start.5 = (bf16[208,1536]{1,0:T(8,128)(2,1)S(1)}, bf16[208,1536]{1,0:T(8,128)(2,1)S(1)}, u32[]{:S(2)}, u32[]{:S(2)}) collective-permute-start(bf16[208,1536]{1,0:T(8,128)(2,1)S(1)} %fusion.123), channel_id=1, source_target_pairs={{0,1},{1,0},{2,3},{3,2},{4,5},{5,4},{6,7},{7,6},{8,9},{9,8},{10,11... | collective-permute-start | bytes 1916936 | tf_op jit(solution)/shard_map/ppermute | solution.py:236
  122.6 20.6 %collective-permute-start.8 = (f32[384,2]{0,1:T(2,128)S(1)}, f32[384,2]{0,1:T(2,128)S(1)}, u32[]{:S(2)}, u32[]{:S(2)}) collective-permute-start(f32[384,2]{0,1:T(2,128)S(1)} %pad_maximum_fusion.40), channel_id=1, source_target_pairs={{0,1},{1,0},{2,3},{3,2},{4,5},{5,4},{6,7},{7,6},{8,9},{9,8},{10,11... | collective-permute-start | bytes 9224 | tf_op jit(solution)/shard_map/ppermute | solution.py:236
  174.0 18.1 %collective-permute-start.9 = (bf16[208,1536]{1,0:T(8,128)(2,1)S(1)}, bf16[208,1536]{1,0:T(8,128)(2,1)S(1)}, u32[]{:S(2)}, u32[]{:S(2)}) collective-permute-start(bf16[208,1536]{1,0:T(8,128)(2,1)S(1)} %slice.1128), channel_id=1, source_target_pairs={{0,1},{1,0},{2,3},{3,2},{4,5},{5,4},{6,7},{7,6},{8,9},{9,8},{10,11... | collective-permute-start | bytes 1916936 | tf_op jit(solution)/shard_map/ppermute | solution.py:236
  179.5 24.1 %collective-permute-start.18 = (bf16[192,1536]{1,0:T(8,128)(2,1)S(1)}, bf16[192,1536]{1,0:T(8,128)(2,1)S(1)}, u32[]{:S(2)}, u32[]{:S(2)}) collective-permute-start(bf16[192,1536]{1,0:T(8,128)(2,1)S(1)} %add_convert_fusion.5), channel_id=1, source_target_pairs={{0,1},{1,0},{2,3},{3,2},{4,5},{5,4},{6,7},{7,6},{8,9},{9,8},{10,11... | collective-permute-start | bytes 1769480 | tf_op jit(solution)/shard_map/ppermute | solution.py:236
  237.5 24.7 %collective-permute-start.20 = (bf16[192,1536]{1,0:T(8,128)(2,1)}, bf16[192,1536]{1,0:T(8,128)(2,1)}, u32[]{:S(2)}, u32[]{:S(2)}) collective-permute-start(bf16[192,1536]{1,0:T(8,128)(2,1)} %slice.1133), channel_id=1, source_target_pairs={{0,1},{1,0},{2,3},{3,2},{4,5},{5,4},{6,7},{7,6},{8,9},{9,8},{10,11... | collective-permute-start | bytes 1769480 | tf_op jit(solution)/shard_map/ppermute | solution.py:236
  264.2 26.8 %collective-permute-start.21 = (bf16[192,1536]{1,0:T(8,128)(2,1)S(1)}, bf16[192,1536]{1,0:T(8,128)(2,1)}, u32[]{:S(2)}, u32[]{:S(2)}) collective-permute-start(bf16[192,1536]{1,0:T(8,128)(2,1)S(1)} %add_convert_fusion.4), channel_id=1, source_target_pairs={{0,1},{1,0},{2,3},{3,2},{4,5},{5,4},{6,7},{7,6},{8,9},{9,8},{10,11... | collective-permute-start | bytes 1769480 | tf_op jit(solution)/shard_map/ppermute | solution.py:236
  280.8 35.6 %collective-permute-start.15 = (bf16[208,1536]{1,0:T(8,128)(2,1)}, bf16[208,1536]{1,0:T(8,128)(2,1)}, u32[]{:S(2)}, u32[]{:S(2)}) collective-permute-start(bf16[208,1536]{1,0:T(8,128)(2,1)} %add_convert_fusion.2), channel_id=1, source_target_pairs={{0,1},{1,0},{2,3},{3,2},{4,5},{5,4},{6,7},{7,6},{8,9},{9,8},{10,11... | collective-permute-start | bytes 1916936 | tf_op jit(solution)/shard_map/ppermute | solution.py:236
  315.2 28.2 %collective-permute-start.22 = (bf16[192,1536]{1,0:T(8,128)(2,1)}, bf16[192,1536]{1,0:T(8,128)(2,1)S(1)}, u32[]{:S(2)}, u32[]{:S(2)}) collective-permute-start(bf16[192,1536]{1,0:T(8,128)(2,1)} %slice.1132), channel_id=1, source_target_pairs={{0,1},{1,0},{2,3},{3,2},{4,5},{5,4},{6,7},{7,6},{8,9},{9,8},{10,11... | collective-permute-start | bytes 1769480 | tf_op jit(solution)/shard_map/ppermute | solution.py:236
  341.7 17.6 %collective-permute-start.16 = (bf16[208,1536]{1,0:T(8,128)(2,1)}, bf16[208,1536]{1,0:T(8,128)(2,1)}, u32[]{:S(2)}, u32[]{:S(2)}) collective-permute-start(bf16[208,1536]{1,0:T(8,128)(2,1)} %slice.1126), channel_id=1, source_target_pairs={{0,1},{1,0},{2,3},{3,2},{4,5},{5,4},{6,7},{7,6},{8,9},{9,8},{10,11... | collective-permute-start | bytes 1916936 | tf_op jit(solution)/shard_map/ppermute | solution.py:236
  347.6 22.6 %collective-permute-start.26 = (bf16[192,1536]{1,0:T(8,128)(2,1)S(1)}, bf16[192,1536]{1,0:T(8,128)(2,1)S(1)}, u32[]{:S(2)}, u32[]{:S(2)}) collective-permute-start(bf16[192,1536]{1,0:T(8,128)(2,1)S(1)} %get-tuple-element.256), channel_id=1, source_target_pairs={{0,1},{1,0},{2,3},{3,2},{4,5},{5,4},{6,7},{7,6},{8,9},{9,8},{10,11... | collective-permute-start | bytes 1769480 | tf_op jit(solution)/shard_map/ppermute | solution.py:236
  394.6 294.0 %reduce-scatter.6.cloned.1.call-start = ((), (), s32[]{:S(2)}) async-start(), calls=%async_computation.6 | async-start | bytes 14622720 | tf_op jit(solution)/shard_map/reduce_scatter | solution.py:561
  441.7 20.7 %collective-permute-start.25 = (bf16[208,1536]{1,0:T(8,128)(2,1)S(1)}, bf16[208,1536]{1,0:T(8,128)(2,1)S(1)}, u32[]{:S(2)}, u32[]{:S(2)}) collective-permute-start(bf16[208,1536]{1,0:T(8,128)(2,1)S(1)} %get-tuple-element.291), channel_id=1, source_target_pairs={{0,1},{1,0},{2,3},{3,2},{4,5},{5,4},{6,7},{7,6},{8,9},{9,8},{10,11... | collective-permute-start | bytes 1916936 | tf_op jit(solution)/shard_map/ppermute | solution.py:236
  466.4 385.6 %reduce-scatter.8.cloned.1.call-start = ((), (), s32[]{:S(2)}) async-start(), calls=%async_computation.7 | async-start | bytes 10027008 | tf_op jit(solution)/shard_map/reduce_scatter | solution.py:561
  492.1 25.4 %collective-permute-start.31 = (bf16[192,1536]{1,0:T(8,128)(2,1)}, bf16[192,1536]{1,0:T(8,128)(2,1)S(1)}, u32[]{:S(2)}, u32[]{:S(2)}) collective-permute-start(bf16[192,1536]{1,0:T(8,128)(2,1)} %get-tuple-element.294), channel_id=1, source_target_pairs={{0,1},{1,0},{2,3},{3,2},{4,5},{5,4},{6,7},{7,6},{8,9},{9,8},{10,11... | collective-permute-start | bytes 1769480 | tf_op jit(solution)/shard_map/ppermute | solution.py:236
  541.9 50.9 %collective-permute-start.33 = (bf16[192,1536]{1,0:T(8,128)(2,1)}, bf16[192,1536]{1,0:T(8,128)(2,1)S(1)}, u32[]{:S(2)}, u32[]{:S(2)}) collective-permute-start(bf16[192,1536]{1,0:T(8,128)(2,1)} %slice.1130), channel_id=1, source_target_pairs={{0,1},{1,0},{2,3},{3,2},{4,5},{5,4},{6,7},{7,6},{8,9},{9,8},{10,11... | collective-permute-start | bytes 1769480 | tf_op jit(solution)/shard_map/ppermute | solution.py:236
  555.8 22.2 %collective-permute-start.35 = (f32[512,1]{0,1:T(1,128)S(1)}, f32[512,1]{0,1:T(1,128)S(1)}, u32[]{:S(2)}, u32[]{:S(2)}) collective-permute-start(f32[512,1]{0,1:T(1,128)S(1)} %pad_maximum_fusion.44), channel_id=1, source_target_pairs={{0,1},{1,0},{2,3},{3,2},{4,5},{5,4},{6,7},{7,6},{8,9},{9,8},{10,11... | collective-permute-start | bytes 6152 | tf_op jit(solution)/shard_map/ppermute | solution.py:236
  572.5 23.2 %collective-permute-start.28 = (bf16[208,1536]{1,0:T(8,128)(2,1)S(1)}, bf16[208,1536]{1,0:T(8,128)(2,1)S(1)}, u32[]{:S(2)}, u32[]{:S(2)}) collective-permute-start(bf16[208,1536]{1,0:T(8,128)(2,1)S(1)} %slice.1124), channel_id=1, source_target_pairs={{0,1},{1,0},{2,3},{3,2},{4,5},{5,4},{6,7},{7,6},{8,9},{9,8},{10,11... | collective-permute-start | bytes 1916936 | tf_op jit(solution)/shard_map/ppermute | solution.py:236
  587.3 87.0 %collective-permute-start.47 = (bf16[256,1536]{1,0:T(8,128)(2,1)}, bf16[256,1536]{1,0:T(8,128)(2,1)}, u32[]{:S(2)}, u32[]{:S(2)}) collective-permute-start(bf16[256,1536]{1,0:T(8,128)(2,1)} %slice.1122), channel_id=1, source_target_pairs={{0,1},{1,0},{2,3},{3,2},{4,5},{5,4},{6,7},{7,6},{8,9},{9,8},{10,11... | collective-permute-start | bytes 2359304 | tf_op jit(solution)/shard_map/ppermute | solution.py:236
  599.8 20.2 %collective-permute-start.29 = (bf16[208,1536]{1,0:T(8,128)(2,1)S(1)}, bf16[208,1536]{1,0:T(8,128)(2,1)}, u32[]{:S(2)}, u32[]{:S(2)}) collective-permute-start(bf16[208,1536]{1,0:T(8,128)(2,1)S(1)} %get-tuple-element.268), channel_id=1, source_target_pairs={{0,1},{1,0},{2,3},{3,2},{4,5},{5,4},{6,7},{7,6},{8,9},{9,8},{10,11... | collective-permute-start | bytes 1916936 | tf_op jit(solution)/shard_map/ppermute | solution.py:236
  600.8 25.5 %collective-permute-start.34 = (bf16[192,1536]{1,0:T(8,128)(2,1)S(1)}, bf16[192,1536]{1,0:T(8,128)(2,1)}, u32[]{:S(2)}, u32[]{:S(2)}) collective-permute-start(bf16[192,1536]{1,0:T(8,128)(2,1)S(1)} %multiply_convert_fusion.6), channel_id=1, source_target_pairs={{0,1},{1,0},{2,3},{3,2},{4,5},{5,4},{6,7},{7,6},{8,9},{9,8},{10,11... | collective-permute-start | bytes 1769480 | tf_op jit(solution)/shard_map/ppermute | solution.py:236
  665.5 17.5 %collective-permute-start.38 = (bf16[2,8,96,768]{3,2,0,1:T(8,128)(2,1)}, bf16[2,8,96,768]{3,2,0,1:T(8,128)(2,1)}, u32[]{:S(2)}, u32[]{:S(2)}) collective-permute-start(bf16[2,8,96,768]{3,2,0,1:T(8,128)(2,1)} %fusion.70), channel_id=1, source_target_pairs={{0,2},{2,0},{4,6},{6,4},{8,10},{10,8},{12,14},{14,12},{16,18},{18,... | collective-permute-start | bytes 7077896 | tf_op jit(solution)/shard_map/ppermute | solution.py:292
  692.5 21.6 %collective-permute-start.39 = (bf16[2,96,768]{2,1,0:T(8,128)(2,1)S(1)}, bf16[2,96,768]{2,1,0:T(8,128)(2,1)S(1)}, u32[]{:S(2)}, u32[]{:S(2)}) collective-permute-start(bf16[2,96,768]{2,1,0:T(8,128)(2,1)S(1)} %fusion.208), channel_id=1, source_target_pairs={{0,8},{10,2},{8,16},{18,10},{16,24},{26,18},{24,28},{30,26},{28,20... | collective-permute-start | bytes 884744 | tf_op jit(solution)/shard_map/ppermute | solution.py:289
  729.1 32.6 %collective-permute-start.49 = (bf16[2,8,96,768]{3,2,0,1:T(8,128)(2,1)}, bf16[2,8,96,768]{3,2,0,1:T(8,128)(2,1)}, u32[]{:S(2)}, u32[]{:S(2)}) collective-permute-start(bf16[2,8,96,768]{3,2,0,1:T(8,128)(2,1)} %copy_bitcast_fusion), channel_id=1, source_target_pairs={{0,2},{2,0},{4,6},{6,4},{8,10},{10,8},{12,14},{14,12},{16,18},{18,... | collective-permute-start | bytes 7077896 | tf_op jit(solution)/shard_map/ppermute | solution.py:292
  731.3 23.3 %collective-permute-start.41 = (bf16[192,1536]{1,0:T(8,128)(2,1)}, bf16[192,1536]{1,0:T(8,128)(2,1)S(1)}, u32[]{:S(2)}, u32[]{:S(2)}) collective-permute-start(bf16[192,1536]{1,0:T(8,128)(2,1)} %slice.1129), channel_id=1, source_target_pairs={{0,1},{1,0},{2,3},{3,2},{4,5},{5,4},{6,7},{7,6},{8,9},{9,8},{10,11... | collective-permute-start | bytes 1769480 | tf_op jit(solution)/shard_map/ppermute | solution.py:236
  736.6 24.3 %collective-permute-start.40 = (bf16[208,1536]{1,0:T(8,128)(2,1)S(1)}, bf16[208,1536]{1,0:T(8,128)(2,1)S(1)}, u32[]{:S(2)}, u32[]{:S(2)}) collective-permute-start(bf16[208,1536]{1,0:T(8,128)(2,1)S(1)} %slice.1123), channel_id=1, source_target_pairs={{0,1},{1,0},{2,3},{3,2},{4,5},{5,4},{6,7},{7,6},{8,9},{9,8},{10,11... | collective-permute-start | bytes 1916936 | tf_op jit(solution)/shard_map/ppermute | solution.py:236
  747.6 45.8 %collective-permute-start.58 = (bf16[2,96,768]{2,1,0:T(8,128)(2,1)}, bf16[2,96,768]{2,1,0:T(8,128)(2,1)}, u32[]{:S(2)}, u32[]{:S(2)}) collective-permute-start(bf16[2,96,768]{2,1,0:T(8,128)(2,1)} %fusion.189), channel_id=1, source_target_pairs={{0,8},{10,2},{8,16},{18,10},{16,24},{26,18},{24,28},{30,26},{28,20... | collective-permute-start | bytes 884744 | tf_op jit(solution)/shard_map/ppermute | solution.py:289
  787.9 19.0 %collective-permute-start.52 = (bf16[2,96,768]{2,1,0:T(8,128)(2,1)S(1)}, bf16[2,96,768]{2,1,0:T(8,128)(2,1)S(1)}, u32[]{:S(2)}, u32[]{:S(2)}) collective-permute-start(bf16[2,96,768]{2,1,0:T(8,128)(2,1)S(1)} %fusion.202), channel_id=1, source_target_pairs={{0,8},{10,2},{8,16},{18,10},{16,24},{26,18},{24,28},{30,26},{28,20... | collective-permute-start | bytes 884744 | tf_op jit(solution)/shard_map/ppermute | solution.py:289
  794.7 26.1 %collective-permute-start.59 = (bf16[2,96,768]{2,1,0:T(8,128)(2,1)S(1)}, bf16[2,96,768]{2,1,0:T(8,128)(2,1)S(1)}, u32[]{:S(2)}, u32[]{:S(2)}) collective-permute-start(bf16[2,96,768]{2,1,0:T(8,128)(2,1)S(1)} %fusion.187), channel_id=1, source_target_pairs={{0,8},{10,2},{8,16},{18,10},{16,24},{26,18},{24,28},{30,26},{28,20... | collective-permute-start | bytes 884744 | tf_op jit(solution)/shard_map/ppermute | solution.py:289
  (270 other events, 3665.8 us)
Sparse Core Ops, SparseCore 0:
  10.2 104.5 all-gather.2
  116.8 139.6 all-gather.4
  394.7 144.0 reduce-scatter.3
  543.3 142.1 reduce-scatter.5
  689.4 127.9 reduce-scatter.7

commit v2 on v1

--- a/solution.py
+++ b/solution.py
@@ -220,6 +220,327 @@
     )(q, k, v, do, lse, qp, qs, qg)
 
 
+def head_grads_kernel(plan, *refs):
+    out = refs[-1]
+    for i, terms in enumerate(plan):
+
+        @pl.when(pl.program_id(0) == i)
+        def _(terms=terms):
+            total = None
+            for a, b, lo, hi in terms:
+                term = dot_tn(refs[a][...], refs[b][lo:hi])
+                total = term if total is None else total + term
+            out[0] = total.astype(BF)
+
+
+def self_back_kernel(spans, *refs):
+    n = 2 * len(spans)
+    rows = refs[:n]
+    weights = refs[n]
+    heads = refs[n + 1 : n + 4]
+    grads, part, other, acc = refs[n + 4 :]
+    halves = [x for a, b in spans for x in ((a, (a + b) // 2), ((a + b) // 2, b))]
+    for i in range(3):
+
+        @pl.when(pl.program_id(0) == i)
+        def _(i=i):
+            total = None
+            for x, (a, b) in zip(rows, halves):
+                term = dot_tn(x[...], heads[i][a:b])
+                total = term if total is None else total + term
+            grads[0] = total.astype(BF)
+            back = dot_nt(heads[i][...], weights[0])
+            if i == 0:
+                acc[...] = back
+            elif i == 1:
+                acc[...] += back
+            else:
+                back = acc[...] + back
+                at = 0
+                for a, b in spans:
+                    half = (b - a) // 2
+                    part[at : at + half] = back[a : a + half]
+                    other[at : at + half] = back[a + half : b].astype(BF)
+                    at += half
+
+
+def self_back(rows, spans, weights, heads):
+    n, width = heads[0].shape
+    d = rows[0].shape[1]
+    once = lambda x: pl.BlockSpec(x.shape, lambda i: (0, 0), pipeline_mode=pl.Buffered(1))
+    return pl.pallas_call(
+        functools.partial(self_back_kernel, spans),
+        grid=(3,),
+        in_specs=[once(x) for x in rows]
+        + [pl.BlockSpec((1, d, width), lambda i: (i, 0, 0))]
+        + [once(x) for x in heads],
+        out_specs=[
+            pl.BlockSpec((1, d, width), lambda i: (i, 0, 0)),
+            pl.BlockSpec((n // 2, d), lambda i: (0, 0)),
+            pl.BlockSpec((n // 2, d), lambda i: (0, 0)),
+        ],
+        out_shape=[
+            jax.ShapeDtypeStruct((3, d, width), BF),
+            jax.ShapeDtypeStruct((n // 2, d), F32),
+            jax.ShapeDtypeStruct((n // 2, d), BF),
+        ],
+        scratch_shapes=[pltpu.VMEM((n, d), F32)],
+        compiler_params=params(),
+        cost_estimate=cost(12 * n * d * width, 30e6),
+        name="self_back",
+    )(*rows, weights, *heads)
+
+
+def head_grads(products):
+    arrays, plan = [], []
+
+    def place(x):
+        for i, y in enumerate(arrays):
+            if x is y:
+                return i
+        arrays.append(x)
+        return len(arrays) - 1
+
+    for pairs in products:
+        terms = []
+        for pieces, b in pairs:
+            at = 0
+            for a in pieces:
+                terms.append((place(a), place(b), at, at + a.shape[0]))
+                at += a.shape[0]
+        plan.append(terms)
+    m, n = products[0][0][0][0].shape[1], products[0][0][1].shape[1]
+    rows = sum(b.shape[0] for pairs in products for _, b in pairs)
+    return pl.pallas_call(
+        functools.partial(head_grads_kernel, plan),
+        grid=(len(products),),
+        in_specs=[
+            pl.BlockSpec(x.shape, lambda i: (0, 0), pipeline_mode=pl.Buffered(1)) for x in arrays
+        ],
+        out_specs=pl.BlockSpec((1, m, n), lambda i: (i, 0, 0)),
+        out_shape=jax.ShapeDtypeStruct((len(products), m, n), BF),
+        compiler_params=params(),
+        cost_estimate=cost(2 * rows * m * n, 2 * sum(x.size for x in arrays) + 2 * len(products) * m * n),
+        name="head_grads",
+    )(*arrays)
+
+
+def tail_kernel(ndp, counts, nc, *refs):
+    n = len(counts)
+    g = refs[:n]
+    state = refs[n : n + nc]
+    unit = refs[n + nc : n + 2 * nc]
+    (part, other, lns, ones, small, gsum, hgrad, small_out,
+     mine, got, send, slot, ybuf, pbuf, stbuf, ubuf, vals, inbox,
+     mine_sem, got_send, got_recv, ring_send, ring_recv, y_sem, load_sem, sum_send, sum_recv) = refs[n + 2 * nc :]
+    chips = ndp // 2
+    bits = ndp.bit_length() - 1
+    dp = lax.axis_index("dp")
+    mp = lax.axis_index("mp")
+    core = lax.rem(dp, 2)
+    chip = lax.div(dp, 2)
+    odd = lax.rem(chip, 2)
+    row = lax.div(chip, 2)
+    place = row * (1 - odd) + (chips - 1 - row) * odd
+    way = 1 - 2 * core
+
+    def chip_at(shift):
+        spot = lax.rem(place + way * shift + 2 * chips, chips)
+        back = lax.div(spot, chips // 2)
+        return 2 * spot * (1 - back) + (2 * (chips - 1 - spot) + 1) * back
+
+    after = 2 * chip_at(1) + core
+    before = 2 * chip_at(-1) + core
+    mates = [dp + (1 - 2 * lax.rem(lax.div(dp, 1 << b), 2)) * (1 << b) for b in range(bits)]
+    mesh_id = pl.DeviceIdType.MESH
+
+    barrier = pltpu.get_barrier_semaphore()
+    for device in (after, before, *mates):
+        pl.semaphore_signal(barrier, inc=1, device_id=(device, mp), device_id_type=mesh_id)
+    pl.semaphore_signal(barrier, inc=1, device_id=(dp, 1 - mp), device_id_type=mesh_id)
+    pl.semaphore_wait(barrier, 3 + bits)
+
+    def remote(src, dst, s_sem, r_sem, device):
+        return pltpu.make_async_remote_copy(
+            src_ref=src, dst_ref=dst, send_sem=s_sem, recv_sem=r_sem, device_id=device, device_id_type=mesh_id
+        )
+
+    starts = [sum(counts[:i]) for i in range(n)]
+    total = sum(counts)
+    cuts = [(0, (total + 1) // 2), ((total + 1) // 2, total)]
+
+    def to_mate(s, i):
+        return remote(
+            g[i].at[:, chip_at(1 + s), 1 - core],
+            got.at[s, pl.ds(starts[i], counts[i])],
+            got_send.at[i, s],
+            got_recv.at[i, s],
+            (mates[0], mp),
+        )
+
+    def to_self(s, i):
+        return pltpu.make_async_copy(
+            g[i].at[:, chip_at(-1 - s), core], mine.at[s, pl.ds(starts[i], counts[i])], mine_sem.at[i, s]
+        )
+
+    def along(s, half):
+        lo, hi = cuts[half]
+        return remote(
+            send.at[s, pl.ds(lo, hi - lo)],
+            slot.at[s, pl.ds(lo, hi - lo)],
+            ring_send.at[half, s],
+            ring_recv.at[half, s],
+            (after, mp),
+        )
+
+    def sum_copy(j):
+        if j < bits:
+            return remote(vals.at[j], inbox.at[j], sum_send.at[j], sum_recv.at[j], (mates[j], mp))
+        return remote(
+            vals.at[j, pl.ds(0, 16)], inbox.at[j, pl.ds(0, 16)], sum_send.at[j], sum_recv.at[j], (dp, 1 - mp)
+        )
+
+    y_copy = remote(other, ybuf, y_sem.at[0], y_sem.at[1], (dp, 1 - mp))
+    for s in range(chips):
+        for i in range(n):
+            to_mate(s, i).start()
+            to_self(s, i).start()
+        if s == 0:
+            y_copy.start()
+    pairs = [(part, pbuf)]
+    at = 0
+    for st, un in zip(state, unit):
+        span = pl.ds(at, st.shape[0])
+        pairs += [(st, stbuf.at[span]), (un, ubuf.at[span])]
+        at += st.shape[0]
+    loads = [pltpu.make_async_copy(src, dst, load_sem.at[i]) for i, (src, dst) in enumerate(pairs)]
+    for load in loads:
+        load.start()
+
+    def finish_rows():
+        for load in loads:
+            load.wait()
+        y_copy.wait_recv()
+        rows, width = pbuf.shape
+        block = 80 if rows % 80 == 0 else 16
+        gain = ones[...]
+
+        def body(i, sums):
+            at = pl.ds(pl.multiple_of(i * block, block), block)
+            back = pbuf[at, :] + ybuf[at, :].astype(F32)
+            z = ubuf[at, :]
+            grad = back * gain
+            mean_g = jnp.mean(grad, axis=1, keepdims=True)
+            mean_gz = jnp.mean(grad * z, axis=1, keepdims=True)
+            hgrad[at, :] = stbuf[at, :] + lns[at, :] * (grad - mean_g - z * mean_gz)
+            return (
+                sums[0] + jnp.sum(back, axis=0, keepdims=True),
+                sums[1] + jnp.sum(back * z, axis=0, keepdims=True),
+            )
+
+        zero = jnp.zeros((1, width), F32)
+        sums = lax.fori_loop(0, rows // block, body, (zero, zero))
+        vals[0] = small[...]
+        vals[0, 0:1, :] = sums[0]
+        vals[0, 1:2, :] = sums[1]
+        sum_copy(0).start()
+
+    def sum_step(j):
+        sum_copy(j).wait_recv()
+        if j < bits:
+            vals[j + 1] = vals[j] + inbox[j]
+            sum_copy(j + 1).start()
+        else:
+            small_out[...] = vals[j]
+            small_out[0:16, :] = vals[j, 0:16, :] + inbox[j, 0:16, :]
+
+    first = min(2, chips - 1)
+    done = 0
+    for s in range(chips):
+        for i in range(n):
+            to_self(s, i).wait()
+            to_mate(s, i).wait_recv()
+        for half in range(2):
+            lo, hi = cuts[half]
+            value = mine[s, lo:hi].astype(F32) + got[s, lo:hi].astype(F32)
+            if s > 0:
+                along(s - 1, half).wait_recv()
+                value = value + slot[s - 1, lo:hi].astype(F32)
+            if s < chips - 1:
+                send[s, lo:hi] = value.astype(BF)
+                along(s, half).start()
+            else:
+                gsum[lo:hi] = value
+        if s == first:
+            finish_rows()
+        elif s > first and done <= bits:
+            sum_step(done)
+            done += 1
+    while done <= bits:
+        sum_step(done)
+        done += 1
+    for s in range(chips):
+        for i in range(n):
+            to_mate(s, i).wait_send()
+        if s < chips - 1:
+            for half in range(2):
+                along(s, half).wait_send()
+    y_copy.wait_send()
+    for j in range(bits + 1):
+        sum_copy(j).wait_send()
+
+
+def tail(ndp, grads, part, other, state, unit, lns, ones, small):
+    chips = ndp // 2
+    bits = ndp.bit_length() - 1
+    split = [x.reshape(x.shape[0], chips, 2, x.shape[1] // ndp, x.shape[2]) for x in grads]
+    counts = tuple(x.shape[0] for x in grads)
+    total = sum(counts)
+    r, w = split[0].shape[3:]
+    rows, width = part.shape
+    n = len(grads)
+    nc = len(state)
+    hbm = pl.BlockSpec(memory_space=pl.ANY)
+    vmem = pl.BlockSpec(memory_space=pltpu.VMEM)
+    dma = pltpu.SemaphoreType.DMA
+    return pl.pallas_call(
+        functools.partial(tail_kernel, ndp, counts, nc),
+        in_specs=[hbm] * (n + 2 * nc) + [hbm, hbm, vmem, vmem, vmem],
+        out_specs=[vmem] * 3,
+        out_shape=[
+            jax.ShapeDtypeStruct((total, r, w), F32),
+            jax.ShapeDtypeStruct((rows, width), F32),
+            jax.ShapeDtypeStruct(small.shape, F32),
+        ],
+        scratch_shapes=[
+            pltpu.VMEM((chips, total, r, w), BF),
+            pltpu.VMEM((chips, total, r, w), BF),
+            pltpu.VMEM((chips - 1, total, r, w), BF),
+            pltpu.VMEM((chips - 1, total, r, w), BF),
+            pltpu.VMEM((rows, width), BF),
+            pltpu.VMEM((rows, width), F32),
+            pltpu.VMEM((rows, width), F32),
+            pltpu.VMEM((rows, width), F32),
+            pltpu.VMEM((bits + 1,) + small.shape, F32),
+            pltpu.VMEM((bits + 1,) + small.shape, F32),
+            dma((n, chips)),
+            dma((n, chips)),
+            dma((n, chips)),
+            dma((2, chips - 1)),
+            dma((2, chips - 1)),
+            dma((2,)),
+            dma((1 + 2 * nc,)),
+            dma((bits + 1,)),
+            dma((bits + 1,)),
+        ],
+        compiler_params=pltpu.CompilerParams(
+            vmem_limit_bytes=58 * 1024 * 1024, collective_id=0, has_side_effects=True
+        ),
+        cost_estimate=cost(1e6, 1e6),
+        name="tail_sums",
+    )(*split, *state, *unit, part, other, lns, ones, small)
+
+
 def normal(values):
     center = values - jnp.mean(values, axis=-1, keepdims=True)
     scale = lax.rsqrt(jnp.mean(center * center, axis=-1, keepdims=True) + EPS)
@@ -237,7 +558,8 @@
 
 
 def collect(own):
-    return jnp.concatenate([own, swap(own)], axis=0)
+    pieces = [own, swap(own)]
+    return jnp.concatenate(pieces, axis=0), pieces
 
 
 def spread(partial):
@@ -260,86 +582,6 @@
 
 def tie(*values):
     return lax.optimization_barrier(values)
-
-
-def ring_order(chips):
-    return list(range(0, chips, 2)) + list(range(chips - 1, 0, -2))
-
-
-class Ring:
-    def __init__(self, ndp, dp):
-        self.chips = ndp // 2
-        self.order = ring_order(self.chips)
-        place = [self.order.index(i) for i in range(self.chips)]
-        self.core = dp % 2
-        self.place = jnp.asarray(place, jnp.int32)[dp // 2]
-        self.way = 1 - 2 * self.core
-        self.steps = []
-        for i, chip in enumerate(self.order):
-            after = self.order[(i + 1) % self.chips]
-            self.steps.append((2 * chip, 2 * after))
-            self.steps.append((2 * after + 1, 2 * chip + 1))
-        self.pairs = [(i, i ^ 1) for i in range(ndp)]
-
-    def chip_at(self, shift):
-        spot = (self.place + self.way * shift) % self.chips
-        return jnp.asarray(self.order, jnp.int32)[spot]
-
-    def forward(self, values):
-        return lax.ppermute(values, "dp", self.steps)
-
-    def cross(self, values):
-        return lax.ppermute(values, "dp", self.pairs)
-
-    def gather(self, shard):
-        k, r, n = shard.shape
-        whole = jnp.zeros((k, 2 * self.chips, r, n), shard.dtype)
-        piece = shard
-        for step in range(self.chips):
-            mine = 2 * self.chip_at(-step) + self.core
-            theirs = 2 * self.chip_at(step) + 1 - self.core
-            other = self.cross(piece)
-            whole = lax.dynamic_update_slice(whole, piece[:, None], (0, mine, 0, 0))
-            whole = lax.dynamic_update_slice(whole, other[:, None], (0, theirs, 0, 0))
-            if step < self.chips - 1:
-                piece = self.forward(piece)
-        return whole
-
-    def scatter_steps(self, full):
-        k, rows, n = full.shape
-        r = rows // (2 * self.chips)
-        parts = full.astype(BF).reshape(k, self.chips, 2, r, n)
-        mine = lax.dynamic_index_in_dim(parts, self.core, 2, False)
-        theirs = lax.dynamic_index_in_dim(parts, 1 - self.core, 2, False)
-        got = yield self.cross(theirs)
-        total = None
-        for step in range(self.chips):
-            chip = self.chip_at(-1 - step)
-            term = lax.dynamic_index_in_dim(mine, chip, 1, False).astype(F32)
-            term = term + lax.dynamic_index_in_dim(got, chip, 1, False).astype(F32)
-            total = term if total is None else total.astype(F32) + term
-            if step < self.chips - 1:
-                total = yield self.forward(total.astype(BF))
-        yield total
-
-
-class Steps:
-    def __init__(self, ring, full):
-        self.left = ring.chips
-        self.work = ring.scatter_steps(full)
-        self.piece = next(self.work)
-
-    def step(self, *values):
-        self.left -= 1
-        *values, piece = tie(*values, self.piece)
-        self.piece = self.work.send(piece)
-        return values if len(values) > 1 else values[0]
-
-    def finish(self):
-        while self.left:
-            self.left -= 1
-            self.piece = self.work.send(self.piece)
-        return self.piece
 
 
 def partners(ndp, bit):
@@ -355,12 +597,6 @@
         low = (dp >> bit) % 2 == 0
         rows = jnp.where(low, jnp.concatenate([rows, got]), jnp.concatenate([got, rows]))
     return rows
-
-
-def sum_small(values, ndp):
-    for bit in range(ndp.bit_length() - 1):
-        values = values + lax.ppermute(values, "dp", partners(ndp, bit))
-    return values
 
 
 def chunks_of(padded):
@@ -418,7 +654,6 @@
     qg_full = low_all[hb.shape[0] : hb.shape[0] + qg.shape[0]].reshape(2, 2, 1, -1)
     ffn_bias_full = low_all[hb.shape[0] + qg.shape[0] :].reshape(-1)
 
-    ring = Ring(ndp, dp)
     def whole(shards):
         return lax.all_gather(shards, "dp", axis=1, tiled=True)
 
@@ -469,7 +704,7 @@
     spans = [(int(ends[i]), int(ends[i + 1])) for i in range(len(cuts))]
     nc = len(cuts)
 
-    text_rows = collect(text_states[0])
+    text_rows, text_pieces = collect(text_states[0])
     cross_kp = dot_nn(text_rows, cross_w[1]) + hb_full[1, 1]
     cross_v = (dot_nn(text_rows, cross_w[2]) + hb_full[1, 2]).astype(BF)
     cross_ks = row_totals(squares(cross_kp))
@@ -482,7 +717,7 @@
         r = hid[c].astype(F32)
         z, s = normal(r)
         x = (z * (1.0 + scale_attn) + shift_attn).astype(BF)
-        rows = collect(x)
+        rows, pieces = collect(x)
         qc = dot_nn(rows, self_w[0]) + hb_full[0, 0]
         kc = dot_nn(rows, self_w[1]) + hb_full[0, 1]
         vc = (dot_nn(rows, self_w[2]) + hb_full[0, 2]).astype(BF)
@@ -490,7 +725,7 @@
         res0.append(r)
         unit0.append(z)
         scale0.append(s)
-        rows0.append(rows)
+        rows0 += pieces
         qp.append(qc)
         kp.append(kc)
         vv.append(vc)
@@ -498,13 +733,12 @@
         ks.append(tot[:, 1:2])
     qp, kp, vv = [jnp.concatenate(x, axis=0) for x in (qp, kp, vv)]
     qs, ks = [jnp.concatenate(x, axis=0) for x in (qs, ks)]
-    rows0 = jnp.concatenate(rows0, axis=0)
     self_q, self_k = prep(qp, kp, qs, ks, qg_full[0, 0], qg_full[0, 1], cos, sin)
 
     self_mixed, self_lse = [], []
     cross_mixed, cross_lse, cross_q, cross_qp, cross_qs = [], [], [], [], []
     rows1, rows2, branch0, unit1, scale1, unit2, scale2 = [], [], [], [], [], [], []
-    acts, slopes, results, errors, d_ffn_all, grads2 = [], [], [], [], [], []
+    acts, slopes, results, errors, d_ffn_all, after = [], [], [], [], [], []
     gate_ffn_grad, err_sq = 0.0, 0.0
     for c in range(nc):
         a, b = spans[c]
@@ -517,8 +751,8 @@
         z, s = normal(after_self)
         unit1.append(z)
         scale1.append(s)
-        rows = collect((z * norm3_full + out_bias_full[0]).astype(BF))
-        rows1.append(rows)
+        rows, pieces = collect((z * norm3_full + out_bias_full[0]).astype(BF))
+        rows1.append(pieces)
         qc = dot_nn(rows, cross_w[0]) + hb_full[1, 0]
         tot = row_totals(squares(qc))
         qn = (qc * lax.rsqrt(tot / D + EPS) * qg_full[1, 0]).astype(BF)
@@ -532,16 +766,18 @@
         z, s = normal(after_cross)
         unit2.append(z)
         scale2.append(s)
-        rows = collect((z * (1.0 + scale_ffn) + shift_ffn).astype(BF))
+        rows, _ = collect((z * (1.0 + scale_ffn) + shift_ffn).astype(BF))
         rows2.append(rows)
         inner = dot_nn(rows, ffn_in_w) + ffn_bias_full
         act, back = jax.vjp(functools.partial(jax.nn.gelu, approximate=True), inner)
         slope = back(jnp.ones_like(inner))[0]
-        act = act.astype(BF)
-        acts.append(act)
+        acts.append(act.astype(BF))
         slopes.append(slope.astype(BF))
-        branch = spread(dot_nt(act, ffn_out_t)) + out_bias_full[3]
-        result = after_cross + gate_ffn * branch
+        after.append(after_cross)
+    acts = list(tie(*acts))
+    for c in range(nc):
+        branch = spread(dot_nt(acts[c], ffn_out_t)) + out_bias_full[3]
+        result = after[c] + gate_ffn * branch
         results.append(result.astype(BF))
         error = (result - teach[c].astype(F32)) * row_valid[c]
         errors.append(error)
@@ -562,29 +798,54 @@
 
     for c in range(nc):
         bias3 = bias3 + colsum(d_ffn_all[c].astype(F32))
-        d_rows2.append(collect(d_ffn_all[c]))
+        d_rows2.append(collect(d_ffn_all[c])[0])
+    def inner_only(c):
+        return (dot_nn(d_rows2[c], ffn_out_t) * slopes[c].astype(F32)).astype(BF)
+
+    def inner_back(c):
+        d_inner = inner_only(c)
+        return d_inner, dot_nt(d_inner, ffn_in_w)
+
+    def after_back(c, back):
+        d_after = errors[c] + normal_back(back * (1.0 + scale_ffn), unit2[c], scale2[c])
+        return d_after, d_after.astype(BF)
+
     g_out = dot_tn(cat(d_rows2), cat(acts)).astype(BF)
-    d_rows2[-1], g_out = tie(d_rows2[-1], g_out)
+    d_rows2[0], g_out = tie(d_rows2[0], g_out)
     s_out = reduce_rows(g_out[None])
-    for c in range(nc):
-        rows = d_rows2[c]
-        d_inner = (dot_nn(rows, ffn_out_t) * slopes[c].astype(F32)).astype(BF)
-        d_inners.append(d_inner)
-        ffn_b_grad = ffn_b_grad + colsum(d_inner.astype(F32))
-        backs.append(spread(dot_nt(d_inner, ffn_in_w)))
+    d_inner, back = inner_back(0)
+    d_inners.append(d_inner)
+    back = spread(back)
+    d_inner = inner_only(1)
+    back, d_inner = tie(back, d_inner)
+    backs.append(back)
+    d_after, d_cross = after_back(0, back)
+    d_afters, d_crosses = [d_after], [d_cross]
+    d_inner, d_crosses[0] = tie(d_inner, d_crosses[0])
+    cross_rows = [collect(d_crosses[0])]
+    back = dot_nt(d_inner, ffn_in_w)
+    cross_rows[0][1][1], d_inner, back = tie(cross_rows[0][1][1], d_inner, back)
+    d_inners.append(d_inner)
+    back = spread(back)
     g_in = dot_tn(cat(rows2), cat(d_inners)).astype(BF)
+    back, g_in = tie(back, g_in)
+    backs.append(back)
+    d_after, d_cross = after_back(1, back)
+    cross_rows[0][1][1], d_cross = tie(cross_rows[0][1][1], d_cross)
+    cross_rows[0] = (cat(cross_rows[0][1]), cross_rows[0][1])
+    d_afters.append(d_after)
+    d_crosses.append(d_cross)
+    cross_rows.append(collect(d_cross))
     for c in range(nc):
         back = backs[c]
+        ffn_b_grad = ffn_b_grad + colsum(d_inners[c].astype(F32))
         shift2 = shift2 + colsum(back)
         scale2_g = scale2_g + colsum(back * unit2[c])
-        d_after_cross = errors[c] + normal_back(back * (1.0 + scale_ffn), unit2[c], scale2[c])
-        d_cross = d_after_cross.astype(BF)
-        bias2 = bias2 + colsum(d_cross.astype(F32))
-        rows = collect(d_cross)
-        d_rows1.append(rows)
+        d_after_cross = d_afters[c]
+        bias2 = bias2 + colsum(d_crosses[c].astype(F32))
+        rows, pieces = cross_rows[c]
+        d_rows1.append(pieces)
         d_mixed = dot_nn(rows, cross_out_t).astype(BF)
-        if c == 0:
-            d_mixed, g_in = tie(d_mixed, g_in)
         dqw, dk, dv, qdot, qgain = attend_back_cross(
             cross_q[c], cross_k, cross_v, d_mixed, cross_lse[c], cross_qp[c], cross_qs[c], qg_full[1, 0]
         )
@@ -607,28 +868,28 @@
             d_self, s_out = tie(d_self, s_out)
             s_in = reduce_rows(g_in[None])
         bias1 = bias1 + colsum(d_self.astype(F32))
-        d_rows0.append(collect(d_self))
-    ffn_out_g = s_out[0].astype(F32).T
+        d_rows0.append(collect(d_self)[1])
 
     cross_dkw = cross_dk * qg_full[1, 1]
     kdot = row_totals(jnp.sum(cross_dkw * cross_kp, axis=-1, keepdims=True))
     cross_kgain = colsum(cross_dk * cross_kp * cross_kr)
     d_kpre = (cross_dkw * cross_kr - cross_kp * (cross_kr**3 * kdot / D)).astype(BF)
     d_v = cross_dv.astype(BF)
-    g_cross = jnp.stack(
+    g_cross = head_grads(
         [
-            dot_tn(cat(rows1), cat(d_qpres)).astype(BF),
-            dot_tn(text_rows, d_kpre).astype(BF),
-            dot_tn(text_rows, d_v).astype(BF),
-            dot_tn(cat(d_rows1), cat(cross_mixed)).astype(BF),
+            list(zip(rows1, d_qpres)),
+            [(text_pieces, d_kpre)],
+            [(text_pieces, d_v)],
+            list(zip(d_rows1, cross_mixed)),
         ]
     )
+    ffn_out_g = s_out[0].astype(F32).T
+    ffn_in_g = s_in[0].astype(F32)
     text_g = spread(dot_nt(d_kpre, cross_w[1]) + dot_nt(d_v, cross_w[2]))
     cross_b = jnp.stack([cross_qb, colsum(d_kpre.astype(F32)), colsum(d_v.astype(F32))])
 
-    d_rows0 = cat(d_rows0)
-    d_mixed = dot_nn(d_rows0, self_out_t).astype(BF)
-    g_self_out = dot_tn(d_rows0, cat(self_mixed)).astype(BF)
+    g_self_out = head_grads([list(zip(d_rows0, self_mixed))])
+    d_mixed = dot_nn(cat([x for pieces in d_rows0 for x in pieces]), self_out_t).astype(BF)
     d_mixed, g_self_out, g_cross = tie(d_mixed, g_self_out, g_cross)
     lse = jnp.concatenate(self_lse, axis=2)
     dqw, dkw, dv, qdot, kdot, self_qgain, self_kgain = attend_back_self(
@@ -637,40 +898,19 @@
     dots = []
     for a, b in spans:
         dots.append(row_totals(jnp.concatenate([qdot[a:b], kdot[a:b]], axis=1)))
-    g_vo = jnp.stack([dot_tn(rows0, dv).astype(BF), g_self_out])
-    steps_vo = Steps(ring, g_vo)
-    dots = steps_vo.step(cat(dots))
+    dots = cat(dots)
     rq = lax.rsqrt(qs / D + EPS)
     rk = lax.rsqrt(ks / D + EPS)
     d_q = (dqw * rq - qp * (rq**3 * dots[:, 0:1] / D)).astype(BF)
     d_k = (dkw * rk - kp * (rk**3 * dots[:, 1:2] / D)).astype(BF)
-    d_q, d_k, s_in, g_cross = tie(d_q, d_k, s_in, g_cross)
-    ffn_in_g = s_in[0].astype(F32)
-    cross_g = reduce_rows(g_cross).astype(F32)
-    cross_qkv_g = cross_g[:3]
-    cross_out_g = cross_g[3].T
-    backs = []
-    for a, b in spans:
-        backs.append(dot_nt(d_q[a:b], self_w[0]) + dot_nt(d_k[a:b], self_w[1]) + dot_nt(dv[a:b], self_w[2]))
-    d_q, d_k, *backs = steps_vo.step(d_q, d_k, *backs)
-    g_qk = jnp.stack([dot_tn(rows0, g).astype(BF) for g in (d_q, d_k)])
-    backs = [spread(x) for x in backs]
-    g_qk = steps_vo.step(g_qk)
-    self_g = jnp.concatenate([Steps(ring, g_qk).finish(), steps_vo.finish()])
-    self_qkv_g = self_g[:3]
-    self_out_g = self_g[3].T
+    g_self, part, other = self_back(rows0, spans, heads_w, [d_q, d_k, dv])
     self_b = jnp.stack([colsum(g.astype(F32)) for g in (d_q, d_k, dv)])
-    shift0 = scale0_g = 0.0
-    hidden_g = []
-    for c in range(nc):
-        back = backs[c]
-        shift0 = shift0 + colsum(back)
-        scale0_g = scale0_g + colsum(back * unit0[c])
-        hidden_g.append(state[c] + normal_back(back * (1.0 + scale_attn), unit0[c], scale0[c]))
-
+
+    blank = jnp.zeros((D,), F32)
     wide = jnp.stack(
-        [shift0, scale0_g, gate0_g, shift2, scale2_g, gate_ffn_grad, bias0, bias1, bias2, bias3, norm3_g]
+        [blank, blank, gate0_g, shift2, scale2_g, gate_ffn_grad, bias0, bias1, bias2, bias3, norm3_g]
         + [jnp.broadcast_to(err_sq, (D,))]
+        + [blank] * 4
     )
     narrow = jnp.concatenate(
         [
@@ -681,10 +921,26 @@
         ],
         axis=0,
     )
-    n_wide = wide.size // HD
-    small = sum_small(jnp.concatenate([wide.reshape(-1, HD), narrow]), ndp)
-    wide = (small[:n_wide] + swap(small[:n_wide])).reshape(-1, D)
-    narrow = lax.dynamic_slice_in_dim(small[n_wide:], dp * w_low, w_low, 1)
+    n_narrow = narrow.shape[0]
+    narrow = jnp.pad(narrow.reshape(-1), (0, -narrow.size % (8 * D))).reshape(-1, D)
+    sums, hidden_g, small = tail(
+        ndp,
+        [g_self, g_self_out, g_cross],
+        part,
+        other,
+        state,
+        unit0,
+        cat(scale0),
+        1.0 + scale_attn,
+        jnp.concatenate([wide, narrow]),
+    )
+    self_qkv_g = sums[:3]
+    self_out_g = sums[3].T
+    cross_qkv_g = sums[4:7]
+    cross_out_g = sums[7].T
+    wide = small[:16]
+    narrow = small[16:].reshape(-1)[: n_narrow * HD].reshape(n_narrow, HD)
+    narrow = lax.dynamic_slice_in_dim(narrow, dp * w_low, w_low, 1)
     mine = lax.dynamic_slice_in_dim(wide, (dp * 2 + mp) * w_f32, w_f32, 1)
     mean_loss = wide[11, 0] / (jnp.sum(lengths).astype(F32) * D)
     nh = head_bias.size // head_bias.shape[-1]
@@ -692,7 +948,7 @@
     return (
         cat(results)[None, :own_len],
         mean_loss,
-        cat(hidden_g)[None, :own_len],
+        hidden_g[None, :own_len],
         text_g[None],
         mine[:6],
         mine[6:10],

time: 874 us -> 808 us (0.924)
  Pallas kernels: 82.8 us -> 212 us
  waiting for transfers between devices: 234 us -> 175 us
  matrix products: 250 us -> 194 us
  starting transfers between devices: 84.7 us -> 44.3 us
  other arithmetic: 113 us -> 78.9 us
  between operations: 42 us -> 20.8 us
  local copies, waits for them, and re-layouts: 56.8 us -> 71 us
    pallas_call x0 -> x4, Pallas kernels: none -> 141 us  [the longest x1 106 us: tail(): pl.pallas_call(functools.partial(tail_kernel, ndp, counts, nc), in_specs=...]
    ppermute x20 -> x0, waiting for transfers between devices: 39.2 us -> none  [the longest x14 26.9 us: forward(): return lax.ppermute(values, 'dp', self.steps)]
    ppermute x20 -> x0, starting transfers between devices: 34.4 us -> none  [the longest x14 32.8 us: forward(): return lax.ppermute(values, 'dp', self.steps)]
    dot_general x10 -> x2, matrix products: 71.5 us -> 37.3 us  [dot_tn(): lax.dot_general(a, b, (((0,), (0,)), ((), ())), preferred_element_type=F32)]
    convert_element_type x23 -> x4, other arithmetic: 33.2 us -> 3.04 us  [the longest x2 2.46 us: local(): rows, _ = collect((z * (1.0 + scale_ffn) + shift_ffn).astype(BF))]
    dot_general x18 -> x12, matrix products: 84.9 us -> 63.6 us  [dot_nt(): lax.dot_general(a, b, (((1,), (1,)), ((), ())), preferred_element_type=F32)]
    ppermute x38 -> x35, waiting for transfers between devices: 132 us -> 117 us  [swap(): return lax.ppermute(values, 'mp', SWAP)]
    pallas_call x4, Pallas kernels: 34.5 us -> 23.3 us  [attend(): pl.pallas_call(functools.partial(attend_kernel, mask is not None), grid=(...]
  transfers between devices with their start and end apart: 67 -> 43, of which waited for: 30 -> 25; matrix products, arithmetic and copies ran while one was open for 44% -> 34% of each run, Pallas kernels for 10% -> 27%
where the time goes in v2:
time: 808 us; the launch traced here: 796 us
  Pallas kernels  212 us (26%)
  matrix products  194 us (24%)
  waiting for transfers between devices  175 us (22%)
  other arithmetic  78.9 us (10%)
  local copies, waits for them, and re-layouts  71 us (9%)
  starting transfers between devices  44.3 us (5%)
  between operations  20.8 us (3%)
    ppermute x35, waiting for transfers between devices, swap(): return lax.ppermute(values, 'mp', SWAP)  117 us
    pallas_call x1, Pallas kernels, tail(): pl.pallas_call(functools.partial(tail_kernel, ndp, counts, nc), in_specs=...  106 us
    dot_general x17, matrix products, dot_nn(): lax.dot_general(a, b, (((1,), (0,)), ((), ())), preferred_element_type=F32)  92.7 us
    dot_general x12, matrix products, dot_nt(): lax.dot_general(a, b, (((1,), (1,)), ((), ())), preferred_element_type=F32)  63.6 us
    all_gather x2, waiting for transfers between devices, whole(): return lax.all_gather(shards, 'dp', axis=1, tiled=True)  45 us
    ppermute x35, starting transfers between devices, swap(): return lax.ppermute(values, 'mp', SWAP)  37.8 us
    dot_general x2, matrix products, dot_tn(): lax.dot_general(a, b, (((0,), (0,)), ((), ())), preferred_element_type=F32)  37.3 us
    unnamed x422, local copies, waits for them, and re-layouts  34.5 us
  transfers between devices with their start and end apart: 43, of which 25 were waited for; matrix products, arithmetic and copies ran while one was open for 34% of the time, Pallas kernels for 27%

profile of v2, /device:TPU:0, one launch (start us, length us, event | category | flops | bytes accessed | tf_op | source)
XLA Modules:
  0.0 795.8 jit_solution(14270655278577245130)
XLA Ops:
  35.6 6.7 collective-permute-done.4
  62.7 7.0 collective-permute-done.5.refs_1_
  69.7 45.0 %all-gather.3.cloned.1.call-done.refs_4_ = bf16[8,1536,768]{2,1,0:T(8,128)(2,1)} async-done(((bf16[8,96,768]{2,1,0:T(8,128)(2,1)}), bf16[8,1536,768]{2,1,0:T(8,128)(2,1)}) %all-gather.3.cloned.1.call-update) | async-done | bytes 18874384 | tf_op jit(solution)/shard_map/all_gather | solution.py:658
  146.6 6.8 rope_prep.1
  154.8 6.1 attend_fwd.6
  164.9 7.0 attend_fwd.4
  182.6 11.1 %collective-permute-done.9 = bf16[208,1536]{1,0:T(8,128)(2,1)S(1)} collective-permute-done((bf16[208,1536]{1,0:T(8,128)(2,1)S(1)}, bf16[208,1536]{1,0:T(8,128)(2,1)S(1)}, u32[]{:S(2)}, u32[]{:S(2)}) %collective-permute-start.9) | collective-permute-done | bytes 639008 | tf_op jit(solution)/shard_map/ppermute | solution.py:557
  194.8 10.2 %collective-permute-done.17.refs_5_ = bf16[192,1536]{1,0:T(8,128)(2,1)S(1)} collective-permute-done((bf16[192,1536]{1,0:T(8,128)(2,1)S(1)}, bf16[192,1536]{1,0:T(8,128)(2,1)S(1)}, u32[]{:S(2)}, u32[]{:S(2)}) %collective-permute-start.17) | collective-permute-done | bytes 589856 | tf_op jit(solution)/shard_map/ppermute | solution.py:557
  221.6 6.5 collective-permute-done.10.refs_2_
  240.7 5.6 attend_fwd.5
  257.4 10.3 %collective-permute-done.14 = bf16[208,1536]{1,0:T(8,128)(2,1)S(1)} collective-permute-done((bf16[208,1536]{1,0:T(8,128)(2,1)S(1)}, bf16[208,1536]{1,0:T(8,128)(2,1)S(1)}, u32[]{:S(2)}, u32[]{:S(2)}) %collective-permute-start.14) | collective-permute-done | bytes 639008 | tf_op jit(solution)/shard_map/ppermute | solution.py:557
  270.7 9.7 %collective-permute-done.20 = bf16[192,1536]{1,0:T(8,128)(2,1)} collective-permute-done((bf16[192,1536]{1,0:T(8,128)(2,1)S(1)}, bf16[192,1536]{1,0:T(8,128)(2,1)}, u32[]{:S(2)}, u32[]{:S(2)}) %collective-permute-start.20) | collective-permute-done | bytes 589856 | tf_op jit(solution)/shard_map/ppermute | solution.py:557
  280.5 11.7 %multiply_convert_fusion.1 = (bf16[384,4480]{1,0:T(8,128)(2,1)S(1)}, f32[384,4480]{1,0:T(8,128)}) fusion(f32[4480]{0:T(1024)S(1)} %add.736, bf16[2,1536,4480]{2,1,0:T(8,128)(2,1)} %all-gather.5.cloned.1.call-done, bf16[192,1536]{1,0:T(8,128)(2,1)} %collective-permute-done.20, bf16[192,1536]{1,0:T(8,128)(2,1)S(1)} %add_convert_fusion.5), kind=kOutput, calls=%fused_computation.45 | convolution fusion | flops 5304385536 | bytes 25282048 | tf_op jit(solution)/shard_map/dot_general | solution.py:38
  292.2 13.6 %multiply_convert_fusion = (bf16[416,4480]{1,0:T(8,128)(2,1)S(1)}, f32[416,4480]{1,0:T(8,128)}) fusion(f32[4480]{0:T(1024)S(1)} %add.736, bf16[2,1536,4480]{2,1,0:T(8,128)(2,1)} %all-gather.5.cloned.1.call-done, bf16[208,1536]{1,0:T(8,128)(2,1)} %collective-permute-done.15, bf16[208,1536]{1,0:T(8,128)(2,1)S(1)} %add_convert_fusion.2), kind=kOutput, calls=%fused_computation.26 | convolution fusion | flops 5746417664 | bytes 26240512 | tf_op jit(solution)/shard_map/dot_general | solution.py:38
  305.8 10.3 %fusion.7 = f32[416,1536]{1,0:T(8,128)S(1)} fusion(bf16[416,4480]{1,0:T(8,128)(2,1)S(1)} %get-tuple-element.75, bf16[2,1536,4480]{2,1,0:T(8,128)(2,1)} %all-gather.5.cloned.1.call-done), kind=kOutput, calls=%fused_computation.15 | convolution fusion | flops 5725224960 | bytes 20045824 | tf_op jit(solution)/shard_map/dot_general | solution.py:42
  317.7 9.2 %fusion.6 = f32[384,1536]{1,0:T(8,128)S(1)} fusion(bf16[384,4480]{1,0:T(8,128)(2,1)S(1)} %get-tuple-element.76, bf16[2,1536,4480]{2,1,0:T(8,128)(2,1)} %all-gather.5.cloned.1.call-done), kind=kOutput, calls=%fused_computation.14 | convolution fusion | flops 5284823040 | bytes 19562496 | tf_op jit(solution)/shard_map/dot_general | solution.py:42
  337.9 7.9 collective-permute-done.22
  349.6 9.7 %collective-permute-done.23 = bf16[208,1536]{1,0:T(8,128)(2,1)S(1)} collective-permute-done((bf16[208,1536]{1,0:T(8,128)(2,1)S(1)}, bf16[208,1536]{1,0:T(8,128)(2,1)S(1)}, u32[]{:S(2)}, u32[]{:S(2)}) %collective-permute-start.23) | collective-permute-done | bytes 639008 | tf_op jit(solution)/shard_map/ppermute | solution.py:557
  360.5 8.9 %collective-permute-done.24 = bf16[192,1536]{1,0:T(8,128)(2,1)S(1)} collective-permute-done((bf16[192,1536]{1,0:T(8,128)(2,1)S(1)}, bf16[192,1536]{1,0:T(8,128)(2,1)S(1)}, u32[]{:S(2)}, u32[]{:S(2)}) %collective-permute-start.24) | collective-permute-done | bytes 589856 | tf_op jit(solution)/shard_map/ppermute | solution.py:557
  369.4 17.4 %convolution_convert_fusion.1 = bf16[1536,4480]{1,0:T(8,128)(2,1)} fusion(bf16[384,4480]{1,0:T(8,128)(2,1)S(1)} %copy-done.207, bf16[416,4480]{1,0:T(8,128)(2,1)S(1)} %copy-done.205, bf16[192,1536]{1,0:T(8,128)(2,1)S(1)} %collective-permute-done.24, bf16[192,1536]{1,0:T(8,128)(2,1)S(1)} %get-tuple-element.260, ...), kind=kOutput, calls=%fused_computation.1 | convolution fusion | flops 11041095680 | bytes 23388160 | tf_op jit(solution)/shard_map/dot_general | solution.py:46
  392.9 15.3 %convert_reduce_fusion = (f32[4480]{0:T(1024)S(1)}, bf16[416,4480]{1,0:T(8,128)(2,1)S(1)}) fusion(f32[416,4480]{1,0:T(8,128)} %get-tuple-element.359, bf16[416,1536]{1,0:T(8,128)(2,1)S(1)} %copy-done.123, bf16[2,1536,4480]{2,1,0:T(8,128)(2,1)} %all-gather.5.cloned.1.call-done), kind=kOutput, calls=%fused_computation.25 | convolution fusion | flops 5768084992 | bytes 26240512 | tf_op jit(solution)/shard_map/dot_general | solution.py:38
  410.2 9.3 %fusion.1 = f32[416,1536]{1,0:T(8,128)S(1)} fusion(bf16[416,4480]{1,0:T(8,128)(2,1)S(1)} %get-tuple-element.363, bf16[2,1536,4480]{2,1,0:T(8,128)(2,1)} %all-gather.5.cloned.1.call-done), kind=kOutput, calls=%fused_computation.9 | convolution fusion | flops 5725224960 | bytes 20045824 | tf_op jit(solution)/shard_map/dot_general | solution.py:42
  419.8 13.4 %fusion.26 = bf16[384,4480]{1,0:T(8,128)(2,1)S(1)} fusion(bf16[2,1536,4480]{2,1,0:T(8,128)(2,1)} %all-gather.5.cloned.1.call-done, f32[384,4480]{1,0:T(8,128)} %get-tuple-element.361, bf16[192,1536]{1,0:T(8,128)(2,1)S(1)} %copy-done.200, bf16[192,1536]{1,0:T(8,128)(2,1)S(1)} %copy-done.132), kind=kOutput, calls=%fused_computation.36 | convolution fusion | flops 5323309056 | bytes 25264128 | tf_op jit(solution)/shard_map/dot_general | solution.py:38
  442.5 9.0 %fusion = f32[384,1536]{1,0:T(8,128)S(1)} fusion(bf16[384,4480]{1,0:T(8,128)(2,1)S(1)} %fusion.26, bf16[2,1536,4480]{2,1,0:T(8,128)(2,1)} %all-gather.5.cloned.1.call-done), kind=kOutput, calls=%fused_computation.8 | convolution fusion | flops 5284823040 | bytes 19562496 | tf_op jit(solution)/shard_map/dot_general | solution.py:42
  456.9 19.9 %convolution_convert_fusion = bf16[1536,4480]{1,0:T(8,128)(2,1)} fusion(bf16[384,4480]{1,0:T(8,128)(2,1)S(1)} %fusion.26, bf16[416,4480]{1,0:T(8,128)(2,1)} %copy-done.203, bf16[192,1536]{1,0:T(8,128)(2,1)} %collective-permute-done.20, bf16[192,1536]{1,0:T(8,128)(2,1)S(1)} %copy-done.130, bf16[208,1536]{1,0:T(8,128)(2,1)} %collective-permute-done.15, ...), kind=kOutput, calls=%fused_computation | convolution fusion | flops 11041095680 | bytes 23388160 | tf_op jit(solution)/shard_map/dot_general | solution.py:46
  489.2 9.8 %attend_bwd_cross.2 = (f32[416,768]{1,0:T(8,128)S(1)}, f32[512,768]{1,0:T(8,128)}, f32[512,768]{1,0:T(8,128)}, f32[416,1]{1,0:T(8,128)S(1)}, f32[1,768]{1,0:T(1,128)S(1)}) custom-call(bf16[416,768]{1,0:T(8,128)(2,1)S(1)} %copy-done.25, bf16[512,768]{1,0:T(8,128)(2,1)S(1)} %copy-done.18, bf16[512,768]{1,0:T(8,128)(2,1)S(1)} %copy-done.58, ...), custom_call_target="tpu_custom_call" | custom-call | flops 4907335680 | bytes 8552448 | tf_op jit(solution)/shard_map/attend_bwd_cross/pallas_call | solution.py:205
  517.6 8.3 %attend_bwd_cross.3 = (f32[384,768]{1,0:T(8,128)S(1)}, f32[512,768]{1,0:T(8,128)}, f32[512,768]{1,0:T(8,128)}, f32[384,1]{1,0:T(8,128)S(1)}, f32[1,768]{1,0:T(1,128)S(1)}) custom-call(bf16[384,768]{1,0:T(8,128)(2,1)S(1)} %copy-done.33, bf16[512,768]{1,0:T(8,128)(2,1)S(1)} %copy-done.19, bf16[512,768]{1,0:T(8,128)(2,1)S(1)} %copy-done.59, ...), custom_call_target="tpu_custom_call" | custom-call | flops 4529848320 | bytes 8257536 | tf_op jit(solution)/shard_map/attend_bwd_cross/pallas_call | solution.py:205
  556.3 13.5 %head_grads.3 = bf16[4,1536,768]{2,1,0:T(8,128)(2,1)} custom-call(bf16[208,1536]{1,0:T(8,128)(2,1)S(1)} %copy-done.23, bf16[416,768]{1,0:T(8,128)(2,1)S(1)} %copy-done.21, bf16[208,1536]{1,0:T(8,128)(2,1)S(1)} %copy-done.46, bf16[192,1536]{1,0:T(8,128)(2,1)S(1)} %copy-done.31, bf16[384,768]{1,0:T(8,128)(2,1)S(1)} %copy-done.35, ...), custom_call_target="tpu_custom_call" | custom-call | flops 6190792704 | bytes 19955712 | tf_op jit(solution)/shard_map/head_grads/pallas_call | solution.py:314
  588.9 8.0 %collective-permute-done.34.refs_5_ = bf16[192,1536]{1,0:T(8,128)(2,1)S(1)} collective-permute-done((bf16[192,1536]{1,0:T(8,128)(2,1)S(1)}, bf16[192,1536]{1,0:T(8,128)(2,1)S(1)}, u32[]{:S(2)}, u32[]{:S(2)}) %collective-permute-start.34) | collective-permute-done | bytes 589856 | tf_op jit(solution)/shard_map/ppermute | solution.py:557
  606.0 22.4 %attend_bwd_self.1 = (f32[800,768]{1,0:T(8,128)}, f32[800,768]{1,0:T(8,128)}, bf16[800,768]{1,0:T(8,128)(2,1)S(1)}, f32[800,1]{1,0:T(8,128)S(1)}, f32[800,1]{1,0...) custom-call(bf16[800,768]{1,0:T(8,128)(2,1)S(1)} %copy-done.13, bf16[800,768]{1,0:T(8,128)(2,1)} %copy-done.42, ...), custom_call_target="tpu_custom_call" | custom-call | flops 14745600000 | bytes 15974400 | tf_op jit(solution)/shard_map/attend_bwd_self/pallas_call | solution.py:184
  644.0 19.0 %self_back.1 = (bf16[3,1536,768]{2,1,0:T(8,128)(2,1)}, f32[400,1536]{1,0:T(8,128)}, bf16[400,1536]{1,0:T(8,128)(2,1)S(1)}) custom-call(bf16[208,1536]{1,0:T(8,128)(2,1)S(1)} %copy-done.27, bf16[208,1536]{1,0:T(8,128)(2,1)S(1)} %copy-done.44, bf16[192,1536]{1,0:T(8,128)(2,1)S(1)} %copy-done.29, bf16[192,1536]{1,0:T(8,128)(2,1)} %collective-permute-done.6.refs_3_, ...), custom_call_target="tpu_custom_call" | custom-call | flops 11324620800 | bytes 30000000 | tf_op jit(solution)/shard_map/self_back/pallas_call | solution.py:271
  664.1 105.9 %tail_sums.1 = (f32[8,96,768]{2,1,0:T(8,128)}, f32[400,1536]{1,0:T(8,128)}, f32[24,1536]{1,0:T(8,128)}) custom-call(bf16[3,8,2,96,768]{4,3,2,1,0:T(8,128)(2,1)} %bitcast.251, bf16[1,8,2,96,768]{4,3,2,1,0:T(8,128)(2,1)} %bitcast.243, bf16[4,8,2,96,768]{4,3,2,1,0:T(8,128)(2,1)} %bitcast.250, f32[208,1536]{1,0:T(8,128)} %copy-done.75, f32[192,1536]{1,0:T(8,128)} %copy-done.76, ...), custom_call_target="tpu_custom_call" | custom-call | flops 1000000 | bytes 1000000 | tf_op jit(solution)/shard_map/tail_sums/pallas_call | solution.py:506
  (784 shorter events, 300.3 us)
Async XLA Ops:
  7.2 107.5 %all-gather.3.cloned.1.call-start = ((), (), s32[]{:S(2)}) async-start(), calls=%async_computation.2 | async-start | bytes 20054016 | tf_op jit(solution)/shard_map/all_gather | solution.py:658
  9.8 270.6 %all-gather.5.cloned.1.call-start = ((), (), s32[]{:S(2)}) async-start(), calls=%async_computation.3 | async-start | bytes 29245440 | tf_op jit(solution)/shard_map/all_gather | solution.py:658
  11.4 572.7 %reduce-scatter.3.cloned.1.call-start = ((), (), s32[]{:S(2)}) async-start(), calls=%async_computation.4 | async-start | bytes 14622720 | tf_op jit(solution)/shard_map/reduce_scatter | solution.py:797
  15.9 113.9 %collective-permute-start.12 = (bf16[256,1536]{1,0:T(8,128)(2,1)}, bf16[256,1536]{1,0:T(8,128)(2,1)}, u32[]{:S(2)}, u32[]{:S(2)}) collective-permute-start(bf16[256,1536]{1,0:T(8,128)(2,1)} %bitcast.300), channel_id=1, source_target_pairs={{0,1},{1,0},{2,3},{3,2},{4,5},{5,4},{6,7},{7,6},{8,9},{9,8},{10,11... | collective-permute-start | bytes 2359304 | tf_op jit(solution)/shard_map/ppermute | solution.py:557
  52.4 17.3 %collective-permute-start.5 = (bf16[208,1536]{1,0:T(8,128)(2,1)S(1)}, bf16[208,1536]{1,0:T(8,128)(2,1)S(1)}, u32[]{:S(2)}, u32[]{:S(2)}) collective-permute-start(bf16[208,1536]{1,0:T(8,128)(2,1)S(1)} %get-tuple-element.299.refs_0_), channel_id=1, source_target_pairs={{0,1},{1,0},{2,3},{3,2},{4,5},{5,4},{6,7},{7,6},{8,9},{9,8},{10,11... | collective-permute-start | bytes 1916936 | tf_op jit(solution)/shard_map/ppermute | solution.py:557
  57.3 66.3 %collective-permute-start.6 = (bf16[192,1536]{1,0:T(8,128)(2,1)S(1)}, bf16[192,1536]{1,0:T(8,128)(2,1)}, u32[]{:S(2)}, u32[]{:S(2)}) collective-permute-start(bf16[192,1536]{1,0:T(8,128)(2,1)S(1)} %get-tuple-element.297.refs_2_), channel_id=1, source_target_pairs={{0,1},{1,0},{2,3},{3,2},{4,5},{5,4},{6,7},{7,6},{8,9},{9,8},{10,11... | collective-permute-start | bytes 1769480 | tf_op jit(solution)/shard_map/ppermute | solution.py:557
  122.1 22.7 %collective-permute-start.7 = (f32[416,2]{0,1:T(2,128)S(1)}, f32[416,2]{0,1:T(2,128)S(1)}, u32[]{:S(2)}, u32[]{:S(2)}) collective-permute-start(f32[416,2]{0,1:T(2,128)S(1)} %pad_maximum_fusion.27), channel_id=1, source_target_pairs={{0,1},{1,0},{2,3},{3,2},{4,5},{5,4},{6,7},{7,6},{8,9},{9,8},{10,11... | collective-permute-start | bytes 9992 | tf_op jit(solution)/shard_map/ppermute | solution.py:557
  128.8 16.0 %collective-permute-start.8 = (f32[384,2]{0,1:T(2,128)S(1)}, f32[384,2]{0,1:T(2,128)S(1)}, u32[]{:S(2)}, u32[]{:S(2)}) collective-permute-start(f32[384,2]{0,1:T(2,128)S(1)} %pad_maximum_fusion.34), channel_id=1, source_target_pairs={{0,1},{1,0},{2,3},{3,2},{4,5},{5,4},{6,7},{7,6},{8,9},{9,8},{10,11... | collective-permute-start | bytes 9224 | tf_op jit(solution)/shard_map/ppermute | solution.py:557
  132.4 11.0 %collective-permute-start.13 = (f32[512,1]{0,1:T(1,128)S(1)}, f32[512,1]{0,1:T(1,128)S(1)}, u32[]{:S(2)}, u32[]{:S(2)}) collective-permute-start(f32[512,1]{0,1:T(1,128)S(1)} %pad_maximum_fusion.37), channel_id=1, source_target_pairs={{0,1},{1,0},{2,3},{3,2},{4,5},{5,4},{6,7},{7,6},{8,9},{9,8},{10,11... | collective-permute-start | bytes 6152 | tf_op jit(solution)/shard_map/ppermute | solution.py:557
  164.0 16.0 %collective-permute-start.16 = (bf16[192,1536]{1,0:T(8,128)(2,1)S(1)}, bf16[192,1536]{1,0:T(8,128)(2,1)S(1)}, u32[]{:S(2)}, u32[]{:S(2)}) collective-permute-start(bf16[192,1536]{1,0:T(8,128)(2,1)S(1)} %slice.1025), channel_id=1, source_target_pairs={{0,1},{1,0},{2,3},{3,2},{4,5},{5,4},{6,7},{7,6},{8,9},{9,8},{10,11... | collective-permute-start | bytes 1769480 | tf_op jit(solution)/shard_map/ppermute | solution.py:557
  175.2 18.4 %collective-permute-start.9 = (bf16[208,1536]{1,0:T(8,128)(2,1)S(1)}, bf16[208,1536]{1,0:T(8,128)(2,1)S(1)}, u32[]{:S(2)}, u32[]{:S(2)}) collective-permute-start(bf16[208,1536]{1,0:T(8,128)(2,1)S(1)} %slice.1020), channel_id=1, source_target_pairs={{0,1},{1,0},{2,3},{3,2},{4,5},{5,4},{6,7},{7,6},{8,9},{9,8},{10,11... | collective-permute-start | bytes 1916936 | tf_op jit(solution)/shard_map/ppermute | solution.py:557
  181.4 23.7 %collective-permute-start.17 = (bf16[192,1536]{1,0:T(8,128)(2,1)S(1)}, bf16[192,1536]{1,0:T(8,128)(2,1)S(1)}, u32[]{:S(2)}, u32[]{:S(2)}) collective-permute-start(bf16[192,1536]{1,0:T(8,128)(2,1)S(1)} %add_convert_fusion.6.refs_3_), channel_id=1, source_target_pairs={{0,1},{1,0},{2,3},{3,2},{4,5},{5,4},{6,7},{7,6},{8,9},{9,8},{10,11... | collective-permute-start | bytes 1769480 | tf_op jit(solution)/shard_map/ppermute | solution.py:557
  210.1 18.0 %collective-permute-start.10 = (bf16[208,1536]{1,0:T(8,128)(2,1)S(1)}, bf16[208,1536]{1,0:T(8,128)(2,1)S(1)}, u32[]{:S(2)}, u32[]{:S(2)}) collective-permute-start(bf16[208,1536]{1,0:T(8,128)(2,1)S(1)} %add_convert_fusion.3.refs_0_), channel_id=1, source_target_pairs={{0,1},{1,0},{2,3},{3,2},{4,5},{5,4},{6,7},{7,6},{8,9},{9,8},{10,11... | collective-permute-start | bytes 1916936 | tf_op jit(solution)/shard_map/ppermute | solution.py:557
  238.3 15.8 %collective-permute-start.19 = (bf16[192,1536]{1,0:T(8,128)(2,1)}, bf16[192,1536]{1,0:T(8,128)(2,1)}, u32[]{:S(2)}, u32[]{:S(2)}) collective-permute-start(bf16[192,1536]{1,0:T(8,128)(2,1)} %slice.1024), channel_id=1, source_target_pairs={{0,1},{1,0},{2,3},{3,2},{4,5},{5,4},{6,7},{7,6},{8,9},{9,8},{10,11... | collective-permute-start | bytes 1769480 | tf_op jit(solution)/shard_map/ppermute | solution.py:557
  249.6 18.1 %collective-permute-start.14 = (bf16[208,1536]{1,0:T(8,128)(2,1)S(1)}, bf16[208,1536]{1,0:T(8,128)(2,1)S(1)}, u32[]{:S(2)}, u32[]{:S(2)}) collective-permute-start(bf16[208,1536]{1,0:T(8,128)(2,1)S(1)} %slice.1019), channel_id=1, source_target_pairs={{0,1},{1,0},{2,3},{3,2},{4,5},{5,4},{6,7},{7,6},{8,9},{9,8},{10,11... | collective-permute-start | bytes 1916936 | tf_op jit(solution)/shard_map/ppermute | solution.py:557
  257.3 23.2 %collective-permute-start.20 = (bf16[192,1536]{1,0:T(8,128)(2,1)S(1)}, bf16[192,1536]{1,0:T(8,128)(2,1)}, u32[]{:S(2)}, u32[]{:S(2)}) collective-permute-start(bf16[192,1536]{1,0:T(8,128)(2,1)S(1)} %add_convert_fusion.5), channel_id=1, source_target_pairs={{0,1},{1,0},{2,3},{3,2},{4,5},{5,4},{6,7},{7,6},{8,9},{9,8},{10,11... | collective-permute-start | bytes 1769480 | tf_op jit(solution)/shard_map/ppermute | solution.py:557
  270.1 22.0 %collective-permute-start.15 = (bf16[208,1536]{1,0:T(8,128)(2,1)S(1)}, bf16[208,1536]{1,0:T(8,128)(2,1)}, u32[]{:S(2)}, u32[]{:S(2)}) collective-permute-start(bf16[208,1536]{1,0:T(8,128)(2,1)S(1)} %add_convert_fusion.2), channel_id=1, source_target_pairs={{0,1},{1,0},{2,3},{3,2},{4,5},{5,4},{6,7},{7,6},{8,9},{9,8},{10,11... | collective-permute-start | bytes 1916936 | tf_op jit(solution)/shard_map/ppermute | solution.py:557
  317.1 15.9 %collective-permute-start.21 = (bf16[208,1536]{1,0:T(8,128)(2,1)}, bf16[208,1536]{1,0:T(8,128)(2,1)S(1)}, u32[]{:S(2)}, u32[]{:S(2)}) collective-permute-start(bf16[208,1536]{1,0:T(8,128)(2,1)} %slice.1018), channel_id=1, source_target_pairs={{0,1},{1,0},{2,3},{3,2},{4,5},{5,4},{6,7},{7,6},{8,9},{9,8},{10,11... | collective-permute-start | bytes 1916936 | tf_op jit(solution)/shard_map/ppermute | solution.py:557
  328.5 17.2 %collective-permute-start.22 = (bf16[192,1536]{1,0:T(8,128)(2,1)}, bf16[192,1536]{1,0:T(8,128)(2,1)}, u32[]{:S(2)}, u32[]{:S(2)}) collective-permute-start(bf16[192,1536]{1,0:T(8,128)(2,1)} %slice.1023), channel_id=1, source_target_pairs={{0,1},{1,0},{2,3},{3,2},{4,5},{5,4},{6,7},{7,6},{8,9},{9,8},{10,11... | collective-permute-start | bytes 1769480 | tf_op jit(solution)/shard_map/ppermute | solution.py:557
  337.9 21.5 %collective-permute-start.23 = (bf16[208,1536]{1,0:T(8,128)(2,1)S(1)}, bf16[208,1536]{1,0:T(8,128)(2,1)S(1)}, u32[]{:S(2)}, u32[]{:S(2)}) collective-permute-start(bf16[208,1536]{1,0:T(8,128)(2,1)S(1)} %get-tuple-element.263), channel_id=1, source_target_pairs={{0,1},{1,0},{2,3},{3,2},{4,5},{5,4},{6,7},{7,6},{8,9},{9,8},{10,11... | collective-permute-start | bytes 1916936 | tf_op jit(solution)/shard_map/ppermute | solution.py:557
  348.8 20.6 %collective-permute-start.24 = (bf16[192,1536]{1,0:T(8,128)(2,1)S(1)}, bf16[192,1536]{1,0:T(8,128)(2,1)S(1)}, u32[]{:S(2)}, u32[]{:S(2)}) collective-permute-start(bf16[192,1536]{1,0:T(8,128)(2,1)S(1)} %get-tuple-element.260), channel_id=1, source_target_pairs={{0,1},{1,0},{2,3},{3,2},{4,5},{5,4},{6,7},{7,6},{8,9},{9,8},{10,11... | collective-permute-start | bytes 1769480 | tf_op jit(solution)/shard_map/ppermute | solution.py:557
  386.9 398.6 %reduce-scatter.5.cloned.1.call-start = ((), (), s32[]{:S(2)}) async-start(), calls=%async_computation.5 | async-start | bytes 14622720 | tf_op jit(solution)/shard_map/reduce_scatter | solution.py:797
  419.5 14.1 %collective-permute-start.25 = (bf16[208,1536]{1,0:T(8,128)(2,1)S(1)}, bf16[208,1536]{1,0:T(8,128)(2,1)S(1)}, u32[]{:S(2)}, u32[]{:S(2)}) collective-permute-start(bf16[208,1536]{1,0:T(8,128)(2,1)S(1)} %slice.1017), channel_id=1, source_target_pairs={{0,1},{1,0},{2,3},{3,2},{4,5},{5,4},{6,7},{7,6},{8,9},{9,8},{10,11... | collective-permute-start | bytes 1916936 | tf_op jit(solution)/shard_map/ppermute | solution.py:557
  440.7 13.4 %collective-permute-start.26 = (bf16[208,1536]{1,0:T(8,128)(2,1)S(1)}, bf16[208,1536]{1,0:T(8,128)(2,1)S(1)}, u32[]{:S(2)}, u32[]{:S(2)}) collective-permute-start(bf16[208,1536]{1,0:T(8,128)(2,1)S(1)} %get-tuple-element.80.refs_10_), channel_id=1, source_target_pairs={{0,1},{1,0},{2,3},{3,2},{4,5},{5,4},{6,7},{7,6},{8,9},{9,8},{10,11... | collective-permute-start | bytes 1916936 | tf_op jit(solution)/shard_map/ppermute | solution.py:557
  455.0 21.8 %collective-permute-start.27 = (bf16[192,1536]{1,0:T(8,128)(2,1)S(1)}, bf16[192,1536]{1,0:T(8,128)(2,1)S(1)}, u32[]{:S(2)}, u32[]{:S(2)}) collective-permute-start(bf16[192,1536]{1,0:T(8,128)(2,1)S(1)} %slice.1022), channel_id=1, source_target_pairs={{0,1},{1,0},{2,3},{3,2},{4,5},{5,4},{6,7},{7,6},{8,9},{9,8},{10,11... | collective-permute-start | bytes 1769480 | tf_op jit(solution)/shard_map/ppermute | solution.py:557
  486.1 28.4 %collective-permute-start.31 = (bf16[192,1536]{1,0:T(8,128)(2,1)S(1)}, bf16[192,1536]{1,0:T(8,128)(2,1)}, u32[]{:S(2)}, u32[]{:S(2)}) collective-permute-start(bf16[192,1536]{1,0:T(8,128)(2,1)S(1)} %get-tuple-element.90.refs_13_), channel_id=1, source_target_pairs={{0,1},{1,0},{2,3},{3,2},{4,5},{5,4},{6,7},{7,6},{8,9},{9,8},{10,11... | collective-permute-start | bytes 1769480 | tf_op jit(solution)/shard_map/ppermute | solution.py:557
  512.7 57.2 %collective-permute-start.29 = (bf16[208,1536]{1,0:T(8,128)(2,1)}, bf16[208,1536]{1,0:T(8,128)(2,1)}, u32[]{:S(2)}, u32[]{:S(2)}) collective-permute-start(bf16[208,1536]{1,0:T(8,128)(2,1)} %slice.1016), channel_id=1, source_target_pairs={{0,1},{1,0},{2,3},{3,2},{4,5},{5,4},{6,7},{7,6},{8,9},{9,8},{10,11... | collective-permute-start | bytes 1916936 | tf_op jit(solution)/shard_map/ppermute | solution.py:557
  528.1 12.3 %collective-permute-start.35 = (f32[512,1]{0,1:T(1,128)S(1)}, f32[512,1]{0,1:T(1,128)S(1)}, u32[]{:S(2)}, u32[]{:S(2)}) collective-permute-start(f32[512,1]{0,1:T(1,128)S(1)} %pad_maximum_fusion.38), channel_id=1, source_target_pairs={{0,1},{1,0},{2,3},{3,2},{4,5},{5,4},{6,7},{7,6},{8,9},{9,8},{10,11... | collective-permute-start | bytes 6152 | tf_op jit(solution)/shard_map/ppermute | solution.py:557
  538.9 36.6 %collective-permute-start.33 = (bf16[192,1536]{1,0:T(8,128)(2,1)}, bf16[192,1536]{1,0:T(8,128)(2,1)}, u32[]{:S(2)}, u32[]{:S(2)}) collective-permute-start(bf16[192,1536]{1,0:T(8,128)(2,1)} %slice.1021), channel_id=1, source_target_pairs={{0,1},{1,0},{2,3},{3,2},{4,5},{5,4},{6,7},{7,6},{8,9},{9,8},{10,11... | collective-permute-start | bytes 1769480 | tf_op jit(solution)/shard_map/ppermute | solution.py:557
  550.9 29.8 %collective-permute-start.38 = (bf16[256,1536]{1,0:T(8,128)(2,1)}, bf16[256,1536]{1,0:T(8,128)(2,1)}, u32[]{:S(2)}, u32[]{:S(2)}) collective-permute-start(bf16[256,1536]{1,0:T(8,128)(2,1)} %slice.1015), channel_id=1, source_target_pairs={{0,1},{1,0},{2,3},{3,2},{4,5},{5,4},{6,7},{7,6},{8,9},{9,8},{10,11... | collective-permute-start | bytes 2359304 | tf_op jit(solution)/shard_map/ppermute | solution.py:557
  573.7 15.1 %collective-permute-start.30 = (bf16[208,1536]{1,0:T(8,128)(2,1)S(1)}, bf16[208,1536]{1,0:T(8,128)(2,1)S(1)}, u32[]{:S(2)}, u32[]{:S(2)}) collective-permute-start(bf16[208,1536]{1,0:T(8,128)(2,1)S(1)} %get-tuple-element.266.refs_0_), channel_id=1, source_target_pairs={{0,1},{1,0},{2,3},{3,2},{4,5},{5,4},{6,7},{7,6},{8,9},{9,8},{10,11... | collective-permute-start | bytes 1916936 | tf_op jit(solution)/shard_map/ppermute | solution.py:557
  584.1 12.8 %collective-permute-start.34 = (bf16[192,1536]{1,0:T(8,128)(2,1)S(1)}, bf16[192,1536]{1,0:T(8,128)(2,1)S(1)}, u32[]{:S(2)}, u32[]{:S(2)}) collective-permute-start(bf16[192,1536]{1,0:T(8,128)(2,1)S(1)} %multiply_convert_fusion.6.refs_3_), channel_id=1, source_target_pairs={{0,1},{1,0},{2,3},{3,2},{4,5},{5,4},{6,7},{7,6},{8,9},{9,8},{10,11... | collective-permute-start | bytes 1769480 | tf_op jit(solution)/shard_map/ppermute | solution.py:557
  (219 other events, 2700.4 us)
Sparse Core Ops, SparseCore 0:
  10.1 104.5 all-gather.2
  116.8 139.6 all-gather.4
  387.0 141.8 reduce-scatter.2
  533.5 142.2 reduce-scatter.4

commit v3 on v2

--- a/solution.py
+++ b/solution.py
@@ -64,8 +64,8 @@
 def prep_kernel(qp, kp, qs, ks, qg, kg, cos, sin, q_out, k_out):
     c = cos[...]
     s = sin[...]
-    for pre, sq, gain, out in ((qp, qs, qg, q_out), (kp, ks, kg, k_out)):
-        v = pre[...] * lax.rsqrt(sq[...] * (1.0 / D) + EPS) * gain[...]
+    for pre, scale, gain, out in ((qp, qs, qg, q_out), (kp, ks, kg, k_out)):
+        v = pre[...] * scale[...] * gain[...]
         out[...] = (v * c + turn(v) * s).astype(BF)
 
 
@@ -89,9 +89,9 @@
 
 def attend_kernel(masked, *refs):
     if masked:
-        q, k, v, mask, out, lse = refs
+        q, k, v, w, mask, out, lse, own, other = refs
     else:
-        q, k, v, out, lse = refs
+        q, k, v, w, out, lse, own, other = refs
     st = dot_nt(k[...], q[...]) * SCALE
     if masked:
         st = st + mask[...]
@@ -100,17 +100,25 @@
     total = jnp.sum(e, axis=0, keepdims=True)
     lse[0] = top + jnp.log(total)
     mixed = dot_tn(v[...], e.astype(BF)) * (1.0 / total)
-    out[...] = mixed.T.astype(BF)
-
-
-def attend(q, k, v, mask):
+    h = pl.program_id(0)
+    out[:, pl.ds(pl.multiple_of(h * HD, HD), HD)] = mixed.T.astype(BF)
+
+    @pl.when(h == pl.num_programs(0) - 1)
+    def _():
+        half = out.shape[0] // 2
+        own[...] = dot_nt(out[:half], w[0])
+        other[...] = dot_nt(out[half:], w[0]).astype(BF)
+
+
+def attend(q, k, v, mask, weights, slab):
     nq, width = q.shape
     nk = k.shape[0]
+    d = weights.shape[1]
     heads = width // HD
     qb = pl.BlockSpec((nq, HD), lambda h: (0, h))
     kb = pl.BlockSpec((nk, HD), lambda h: (0, h))
-    ins = [qb, kb, kb]
-    args = [q, k, v]
+    ins = [qb, kb, kb, pl.BlockSpec((1, d, width), lambda h: (slab, 0, 0), pipeline_mode=pl.Buffered(1))]
+    args = [q, k, v, weights]
     if mask is not None:
         ins.append(pl.BlockSpec((nk, 1), lambda h: (0, 0)))
         args.append(mask)
@@ -118,10 +126,17 @@
         functools.partial(attend_kernel, mask is not None),
         grid=(heads,),
         in_specs=ins,
-        out_specs=[qb, pl.BlockSpec((1, 1, nq), lambda h: (h, 0, 0))],
+        out_specs=[
+            pl.BlockSpec((nq, width), lambda h: (0, 0)),
+            pl.BlockSpec((1, 1, nq), lambda h: (h, 0, 0)),
+            pl.BlockSpec((nq // 2, d), lambda h: (0, 0)),
+            pl.BlockSpec((nq // 2, d), lambda h: (0, 0)),
+        ],
         out_shape=[
             jax.ShapeDtypeStruct((nq, width), BF),
             jax.ShapeDtypeStruct((heads, 1, nq), F32),
+            jax.ShapeDtypeStruct((nq // 2, d), F32),
+            jax.ShapeDtypeStruct((nq // 2, d), BF),
         ],
         compiler_params=params(),
         cost_estimate=cost(4 * nq * nk * width * 3, 4 * nq * width + 4 * nk * width, nq * nk * heads),
@@ -152,7 +167,7 @@
         sides = [(dq, qp, qs, qg, dq_out, qdot, qgain), (dk, kp, ks, kg, dk_out, kdot, kgain)]
     else:
         dk_out[...] = dk
-    for grad, pre, sq, gain, out, dots, gains in sides:
+    for grad, pre, scale, gain, out, dots, gains in sides:
         p_rows = pre[...]
         weighted = grad * gain[...]
         out[...] = weighted
@@ -166,8 +181,7 @@
         def _():
             dots[...] += part
 
-        scaled = p_rows * lax.rsqrt(sq[...] * (1.0 / D) + EPS)
-        gains[...] = jnp.sum(grad * scaled, axis=0, keepdims=True)
+        gains[...] = jnp.sum(grad * (p_rows * scale[...]), axis=0, keepdims=True)
 
 
 def attend_back_self(q, k, v, do, lse, mask, qp, kp, qs, ks, qg, kg, cos, sin):
@@ -567,6 +581,11 @@
     return partial[:half] + swap(partial[half:].astype(BF)).astype(F32)
 
 
+def halves(partial):
+    half = partial.shape[0] // 2
+    return partial[:half], swap(partial[half:].astype(BF))
+
+
 def row_totals(own):
     half = own.shape[0] // 2
     return own + swap(jnp.concatenate([own[half:], own[:half]], axis=0))
@@ -729,146 +748,185 @@
         qp.append(qc)
         kp.append(kc)
         vv.append(vc)
-        qs.append(tot[:, 0:1])
-        ks.append(tot[:, 1:2])
+        scales = lax.rsqrt(tot / D + EPS)
+        qs.append(scales[:, 0:1])
+        ks.append(scales[:, 1:2])
     qp, kp, vv = [jnp.concatenate(x, axis=0) for x in (qp, kp, vv)]
     qs, ks = [jnp.concatenate(x, axis=0) for x in (qs, ks)]
     self_q, self_k = prep(qp, kp, qs, ks, qg_full[0, 0], qg_full[0, 1], cos, sin)
 
-    self_mixed, self_lse = [], []
-    cross_mixed, cross_lse, cross_q, cross_qp, cross_qs = [], [], [], [], []
-    rows1, rows2, branch0, unit1, scale1, unit2, scale2 = [], [], [], [], [], [], []
-    acts, slopes, results, errors, d_ffn_all, after = [], [], [], [], [], []
-    gate_ffn_grad, err_sq = 0.0, 0.0
-    for c in range(nc):
+    none = [None] * nc
+    f, g = nc - 1, 0
+    self_mixed, self_lse, branch0, unit1, scale1, after_self = [list(none) for _ in range(6)]
+    cross_mixed, cross_lse, cross_q, cross_qp, cross_qs = [list(none) for _ in range(5)]
+    rows1, rows2, unit2, scale2, after = [list(none) for _ in range(5)]
+
+    def self_rows(c):
         a, b = spans[c]
-        mixed, lse = attend(self_q[a:b], self_k, vv, key_mask)
-        self_mixed.append(mixed)
-        self_lse.append(lse)
-        branch = spread(dot_nt(mixed, self_out_t)) + out_bias_full[1]
-        after_self = res0[c] + gate_attn * branch
-        branch0.append(branch)
-        z, s = normal(after_self)
-        unit1.append(z)
-        scale1.append(s)
-        rows, pieces = collect((z * norm3_full + out_bias_full[0]).astype(BF))
-        rows1.append(pieces)
-        qc = dot_nn(rows, cross_w[0]) + hb_full[1, 0]
-        tot = row_totals(squares(qc))
-        qn = (qc * lax.rsqrt(tot / D + EPS) * qg_full[1, 0]).astype(BF)
-        cross_qp.append(qc)
-        cross_qs.append(tot)
-        cross_q.append(qn)
-        mixed, lse = attend(qn, cross_k, cross_v, None)
-        cross_mixed.append(mixed)
-        cross_lse.append(lse)
-        after_cross = after_self + spread(dot_nt(mixed, cross_out_t)) + out_bias_full[2]
-        z, s = normal(after_cross)
-        unit2.append(z)
-        scale2.append(s)
-        rows, _ = collect((z * (1.0 + scale_ffn) + shift_ffn).astype(BF))
-        rows2.append(rows)
-        inner = dot_nn(rows, ffn_in_w) + ffn_bias_full
-        act, back = jax.vjp(functools.partial(jax.nn.gelu, approximate=True), inner)
-        slope = back(jnp.ones_like(inner))[0]
-        acts.append(act.astype(BF))
-        slopes.append(slope.astype(BF))
-        after.append(after_cross)
-    acts = list(tie(*acts))
-    for c in range(nc):
-        branch = spread(dot_nt(acts[c], ffn_out_t)) + out_bias_full[3]
-        result = after[c] + gate_ffn * branch
-        results.append(result.astype(BF))
-        error = (result - teach[c].astype(F32)) * row_valid[c]
-        errors.append(error)
-        err_sq = err_sq + jnp.sum(error * error)
-        gate_ffn_grad = gate_ffn_grad + colsum(branch * error)
-        d_ffn_all.append((gate_ffn * error).astype(BF))
+        self_mixed[c], self_lse[c], own, other = attend(self_q[a:b], self_k, vv, key_mask, heads_w, 3)
+        return own, swap(other)
+
+    def cross_query(c, own, got):
+        branch0[c] = own + got.astype(F32) + out_bias_full[1]
+        after_self[c] = res0[c] + gate_attn * branch0[c]
+        unit1[c], scale1[c] = normal(after_self[c])
+        x = (unit1[c] * norm3_full + out_bias_full[0]).astype(BF)
+        rows1[c] = [x, swap(x)]
+
+    def cross_prepare(c, got=None):
+        qc = dot_nn(jnp.concatenate(rows1[c], axis=0), heads_w[4]) + hb_full[1, 0]
+        if got is not None:
+            qc, got = tie(qc, got)
+        cross_qp[c] = qc
+        cross_qs[c] = lax.rsqrt(row_totals(squares(qc)) / D + EPS)
+        cross_q[c] = (qc * cross_qs[c] * qg_full[1, 0]).astype(BF)
+        return got
+
+    def cross_attend(c):
+        cross_mixed[c], cross_lse[c], own, other = attend(cross_q[c], cross_k, cross_v, None, heads_w, 7)
+        return own, other
+
+    def ffn_input(c, own, got):
+        after[c] = after_self[c] + own + got.astype(F32) + out_bias_full[2]
+        unit2[c], scale2[c] = normal(after[c])
+        return (unit2[c] * (1.0 + scale_ffn) + shift_ffn).astype(BF)
+
+    own_f, got_f = self_rows(f)
+    own_g, got_g = self_rows(g)
+    got_f, own_g = tie(got_f, own_g)
+    cross_query(f, own_f, got_f)
+    cross_query(g, own_g, got_g)
+    cross_prepare(f)
+    own_f, other_f = cross_attend(f)
+    rows1[g][1], other_f = tie(rows1[g][1], other_f)
+    got_f = swap(other_f)
+    got_f = cross_prepare(g, got_f)
+    x_f = ffn_input(f, own_f, got_f)
+    cross_q[g], x_f = tie(cross_q[g], x_f)
+    y_f = swap(x_f)
+    own_g, other_g = cross_attend(g)
+    y_f, own_g, other_g = tie(y_f, own_g, other_g)
+    rows2[f] = jnp.concatenate([x_f, y_f], axis=0)
+    got_g = swap(other_g)
 
     def cat(parts):
         return jnp.concatenate(parts, axis=0)
 
-    bias3 = bias2 = bias0 = bias1 = shift2 = scale2_g = norm3_g = gate0_g = 0.0
-    ffn_b_grad = cross_qb = cross_qgain = 0.0
-    d_rows2, d_inners, d_rows1, d_qpres = [], [], [], []
-    cross_dk = cross_dv = 0.0
-    d_rows0, state, backs = [], [], []
     def reduce_rows(full):
         return lax.psum_scatter(full, "dp", scatter_dimension=1, tiled=True)
 
-    for c in range(nc):
-        bias3 = bias3 + colsum(d_ffn_all[c].astype(F32))
-        d_rows2.append(collect(d_ffn_all[c])[0])
-    def inner_only(c):
-        return (dot_nn(d_rows2[c], ffn_out_t) * slopes[c].astype(F32)).astype(BF)
-
-    def inner_back(c):
-        d_inner = inner_only(c)
-        return d_inner, dot_nt(d_inner, ffn_in_w)
-
-    def after_back(c, back):
-        d_after = errors[c] + normal_back(back * (1.0 + scale_ffn), unit2[c], scale2[c])
-        return d_after, d_after.astype(BF)
-
-    g_out = dot_tn(cat(d_rows2), cat(acts)).astype(BF)
-    d_rows2[0], g_out = tie(d_rows2[0], g_out)
+    acts, slopes, results, errors, d_ffn, d_inners, d_afters, d_crosses = [list(none) for _ in range(8)]
+    squares_of, gate_grads, ffn_backs = [list(none) for _ in range(3)]
+
+    def inner_of(c):
+        inner = dot_nn(rows2[c], ffn_in_w) + ffn_bias_full
+        act, back = jax.vjp(functools.partial(jax.nn.gelu, approximate=True), inner)
+        acts[c] = act.astype(BF)
+        slopes[c] = back(jnp.ones_like(inner))[0].astype(BF)
+
+    def loss_of(c, own, got):
+        branch = own + got.astype(F32) + out_bias_full[3]
+        result = after[c] + gate_ffn * branch
+        results[c] = result.astype(BF)
+        errors[c] = (result - teach[c].astype(F32)) * row_valid[c]
+        d_ffn[c] = (gate_ffn * errors[c]).astype(BF)
+        squares_of[c] = jnp.sum(errors[c] * errors[c])
+        gate_grads[c] = colsum(branch * errors[c])
+
+    def inner_back(c, rows):
+        d_inners[c] = (dot_nn(rows, ffn_out_t) * slopes[c].astype(F32)).astype(BF)
+
+    def after_back(c, own, got):
+        back = own + got.astype(F32)
+        ffn_backs[c] = back
+        d_afters[c] = errors[c] + normal_back(back * (1.0 + scale_ffn), unit2[c], scale2[c])
+        d_crosses[c] = d_afters[c].astype(BF)
+
+    inner_of(f)
+    got_g, acts[f] = tie(got_g, acts[f])
+    x_g = ffn_input(g, own_g, got_g)
+    acts[f], x_g = tie(acts[f], x_g)
+    y_g = swap(x_g)
+    branch_f = dot_nt(acts[f], ffn_out_t)
+    y_g, branch_f = tie(y_g, branch_f)
+    rows2[g] = jnp.concatenate([x_g, y_g], axis=0)
+    own_f, got_f = halves(branch_f)
+    inner_of(g)
+    got_f, acts[g] = tie(got_f, acts[g])
+    loss_of(f, own_f, got_f)
+    acts[g], d_ffn[f] = tie(acts[g], d_ffn[f])
+    d_f = swap(d_ffn[f])
+    branch_g = dot_nt(acts[g], ffn_out_t)
+    d_f, branch_g = tie(d_f, branch_g)
+    own_g, got_g = halves(branch_g)
+    d_f = cat([d_ffn[f], d_f])
+    inner_back(f, d_f)
+    d_inners[f], got_g = tie(d_inners[f], got_g)
+    loss_of(g, own_g, got_g)
+    d_inners[f], d_ffn[g] = tie(d_inners[f], d_ffn[g])
+    d_g = swap(d_ffn[g])
+    back_f = dot_nt(d_inners[f], ffn_in_w)
+    d_g, back_f = tie(d_g, back_f)
+    own_f, got_f = halves(back_f)
+    d_g = cat([d_ffn[g], d_g])
+    g_out = dot_tn(cat([d_f, d_g]), cat([acts[f], acts[g]])).astype(BF)
+    got_f, d_g, g_out = tie(got_f, d_g, g_out)
     s_out = reduce_rows(g_out[None])
-    d_inner, back = inner_back(0)
-    d_inners.append(d_inner)
-    back = spread(back)
-    d_inner = inner_only(1)
-    back, d_inner = tie(back, d_inner)
-    backs.append(back)
-    d_after, d_cross = after_back(0, back)
-    d_afters, d_crosses = [d_after], [d_cross]
-    d_inner, d_crosses[0] = tie(d_inner, d_crosses[0])
-    cross_rows = [collect(d_crosses[0])]
-    back = dot_nt(d_inner, ffn_in_w)
-    cross_rows[0][1][1], d_inner, back = tie(cross_rows[0][1][1], d_inner, back)
-    d_inners.append(d_inner)
-    back = spread(back)
-    g_in = dot_tn(cat(rows2), cat(d_inners)).astype(BF)
-    back, g_in = tie(back, g_in)
-    backs.append(back)
-    d_after, d_cross = after_back(1, back)
-    cross_rows[0][1][1], d_cross = tie(cross_rows[0][1][1], d_cross)
-    cross_rows[0] = (cat(cross_rows[0][1]), cross_rows[0][1])
-    d_afters.append(d_after)
-    d_crosses.append(d_cross)
-    cross_rows.append(collect(d_cross))
-    for c in range(nc):
-        back = backs[c]
-        ffn_b_grad = ffn_b_grad + colsum(d_inners[c].astype(F32))
-        shift2 = shift2 + colsum(back)
-        scale2_g = scale2_g + colsum(back * unit2[c])
-        d_after_cross = d_afters[c]
-        bias2 = bias2 + colsum(d_crosses[c].astype(F32))
-        rows, pieces = cross_rows[c]
-        d_rows1.append(pieces)
-        d_mixed = dot_nn(rows, cross_out_t).astype(BF)
+    inner_back(g, d_g)
+    after_back(f, own_f, got_f)
+    d_inners[g], d_crosses[f] = tie(d_inners[g], d_crosses[f])
+    c_f = swap(d_crosses[f])
+    back_g = dot_nt(d_inners[g], ffn_in_w)
+    c_f, d_inners[g], back_g = tie(c_f, d_inners[g], back_g)
+    own_g, got_g = halves(back_g)
+    g_in = dot_tn(cat([rows2[f], rows2[g]]), cat([d_inners[f], d_inners[g]])).astype(BF)
+    got_g, g_in = tie(got_g, g_in)
+    after_back(g, own_g, got_g)
+    c_f, d_crosses[g] = tie(c_f, d_crosses[g])
+    c_g = swap(d_crosses[g])
+    d_rows1 = list(none)
+    d_rows1[f] = [d_crosses[f], c_f]
+    d_rows1[g] = [d_crosses[g], c_g]
+    err_sq = sum(squares_of)
+    gate_ffn_grad = sum(gate_grads)
+    bias3 = sum(colsum(x.astype(F32)) for x in d_ffn)
+    bias2 = sum(colsum(x.astype(F32)) for x in d_crosses)
+    ffn_b_grad = sum(colsum(x.astype(F32)) for x in d_inners)
+    shift2 = sum(colsum(x) for x in ffn_backs)
+    scale2_g = sum(colsum(x * z) for x, z in zip(ffn_backs, unit2))
+
+    bias0 = bias1 = norm3_g = gate0_g = cross_qb = cross_qgain = cross_dk = cross_dv = 0.0
+    d_qpres, d_rows0, state = [list(none) for _ in range(3)]
+    for c in (f, g):
+        d_mixed = dot_nn(cat(d_rows1[c]), cross_out_t).astype(BF)
+        if c == g:
+            d_mixed, q_back = tie(d_mixed, q_back)
+            own_q, got_q = halves(q_back)
         dqw, dk, dv, qdot, qgain = attend_back_cross(
             cross_q[c], cross_k, cross_v, d_mixed, cross_lse[c], cross_qp[c], cross_qs[c], qg_full[1, 0]
         )
+        if c == f:
+            d_rows1[g][1], dqw, qdot = tie(d_rows1[g][1], dqw, qdot)
+        else:
+            got_q, dqw, qdot = tie(got_q, dqw, qdot)
         cross_dk = cross_dk + dk
         cross_dv = cross_dv + dv
         cross_qgain = cross_qgain + qgain[0]
-        r = lax.rsqrt(cross_qs[c] / D + EPS)
+        r = cross_qs[c]
         dot = row_totals(qdot)
-        d_qpre = (dqw * r - cross_qp[c] * (r * r * r * dot / D)).astype(BF)
-        d_qpres.append(d_qpre)
-        cross_qb = cross_qb + colsum(d_qpre.astype(F32))
-        back = spread(dot_nt(d_qpre, cross_w[0]))
+        d_qpres[c] = (dqw * r - cross_qp[c] * (r * r * r * dot / D)).astype(BF)
+        cross_qb = cross_qb + colsum(d_qpres[c].astype(F32))
+        q_back = dot_nt(d_qpres[c], cross_w[0])
+    backs = {f: own_q + got_q.astype(F32), g: spread(q_back)}
+    for c in (f, g):
+        back = backs[c]
         norm3_g = norm3_g + colsum(back * unit1[c])
         bias0 = bias0 + colsum(back)
-        st = d_after_cross + normal_back(back * norm3_full, unit1[c], scale1[c])
-        state.append(st)
-        gate0_g = gate0_g + colsum(branch0[c] * st)
-        d_self = (gate_attn * st).astype(BF)
-        if c == nc - 1:
-            d_self, s_out = tie(d_self, s_out)
-            s_in = reduce_rows(g_in[None])
+        state[c] = d_afters[c] + normal_back(back * norm3_full, unit1[c], scale1[c])
+        gate0_g = gate0_g + colsum(branch0[c] * state[c])
+        d_self = (gate_attn * state[c]).astype(BF)
         bias1 = bias1 + colsum(d_self.astype(F32))
-        d_rows0.append(collect(d_self)[1])
+        d_rows0[c] = [d_self, swap(d_self)]
 
     cross_dkw = cross_dk * qg_full[1, 1]
     kdot = row_totals(jnp.sum(cross_dkw * cross_kp, axis=-1, keepdims=True))
@@ -883,14 +941,15 @@
             list(zip(d_rows1, cross_mixed)),
         ]
     )
+    own_text, got_text = halves(dot_nt(d_kpre, cross_w[1]) + dot_nt(d_v, cross_w[2]))
+    cross_b = jnp.stack([cross_qb, colsum(d_kpre.astype(F32)), colsum(d_v.astype(F32))])
+
+    g_self_out = head_grads([list(zip(d_rows0, self_mixed))])
+    d_mixed = dot_nn(cat([x for pieces in d_rows0 for x in pieces]), self_out_t).astype(BF)
+    d_mixed, g_self_out, g_cross, s_out, g_in = tie(d_mixed, g_self_out, g_cross, s_out, g_in)
+    s_in = reduce_rows(g_in[None])
     ffn_out_g = s_out[0].astype(F32).T
     ffn_in_g = s_in[0].astype(F32)
-    text_g = spread(dot_nt(d_kpre, cross_w[1]) + dot_nt(d_v, cross_w[2]))
-    cross_b = jnp.stack([cross_qb, colsum(d_kpre.astype(F32)), colsum(d_v.astype(F32))])
-
-    g_self_out = head_grads([list(zip(d_rows0, self_mixed))])
-    d_mixed = dot_nn(cat([x for pieces in d_rows0 for x in pieces]), self_out_t).astype(BF)
-    d_mixed, g_self_out, g_cross = tie(d_mixed, g_self_out, g_cross)
     lse = jnp.concatenate(self_lse, axis=2)
     dqw, dkw, dv, qdot, kdot, self_qgain, self_kgain = attend_back_self(
         self_q, self_k, vv, d_mixed, lse, key_mask, qp, kp, qs, ks, qg_full[0, 0], qg_full[0, 1], cos, sin
@@ -899,10 +958,10 @@
     for a, b in spans:
         dots.append(row_totals(jnp.concatenate([qdot[a:b], kdot[a:b]], axis=1)))
     dots = cat(dots)
-    rq = lax.rsqrt(qs / D + EPS)
-    rk = lax.rsqrt(ks / D + EPS)
-    d_q = (dqw * rq - qp * (rq**3 * dots[:, 0:1] / D)).astype(BF)
-    d_k = (dkw * rk - kp * (rk**3 * dots[:, 1:2] / D)).astype(BF)
+    d_q = (dqw * qs - qp * (qs**3 * dots[:, 0:1] / D)).astype(BF)
+    d_k = (dkw * ks - kp * (ks**3 * dots[:, 1:2] / D)).astype(BF)
+    d_q, got_text = tie(d_q, got_text)
+    text_g = own_text + got_text.astype(F32)
     g_self, part, other = self_back(rows0, spans, heads_w, [d_q, d_k, dv])
     self_b = jnp.stack([colsum(g.astype(F32)) for g in (d_q, d_k, dv)])
 

time: 808 us -> 800 us (0.990)
  Pallas kernels: 212 us -> 260 us
  waiting for transfers between devices: 175 us -> 140 us
  matrix products: 194 us -> 185 us
    ppermute x35, waiting for transfers between devices: 117 us -> 74.1 us  [swap(): return lax.ppermute(values, 'mp', SWAP)]
    pallas_call x1, Pallas kernels: 106 us -> 140 us  [tail(): pl.pallas_call(functools.partial(tail_kernel, ndp, counts, nc), in_specs=...]
    pallas_call x4, Pallas kernels: 23.3 us -> 38.5 us  [attend(): pl.pallas_call(functools.partial(attend_kernel, mask is not None), grid=(...]
    dot_general x12 -> x8, matrix products: 63.6 us -> 51.1 us  [dot_nt(): lax.dot_general(a, b, (((1,), (1,)), ((), ())), preferred_element_type=F32)]
    all_gather x2, waiting for transfers between devices: 45 us -> 53.1 us  [whole(): return lax.all_gather(shards, 'dp', axis=1, tiled=True)]
    reduce_sum x21 -> x22, other arithmetic: 28.9 us -> 23.6 us  [colsum(): return jnp.sum(values, axis=0, dtype=F32)]
    unnamed x422 -> x394, local copies, waits for them, and re-layouts: 34.5 us -> 29.5 us
  transfers between devices with their start and end apart: 43 -> 43, of which waited for: 25 -> 22; matrix products, arithmetic and copies ran while one was open for 34% -> 37% of each run, Pallas kernels for 27% -> 33%
where the time goes in v3:
time: 800 us; the launch traced here: 790 us
  Pallas kernels  260 us (32%)
  matrix products  185 us (23%)
  waiting for transfers between devices  140 us (18%)
  other arithmetic  75.8 us (9%)
  local copies, waits for them, and re-layouts  63.9 us (8%)
  starting transfers between devices  43.6 us (5%)
  between operations  20.6 us (3%)
    pallas_call x1, Pallas kernels, tail(): pl.pallas_call(functools.partial(tail_kernel, ndp, counts, nc), in_specs=...  140 us
    dot_general x17, matrix products, dot_nn(): lax.dot_general(a, b, (((1,), (0,)), ((), ())), preferred_element_type=F32)  91.3 us
    ppermute x35, waiting for transfers between devices, swap(): return lax.ppermute(values, 'mp', SWAP)  74.1 us
    all_gather x2, waiting for transfers between devices, whole(): return lax.all_gather(shards, 'dp', axis=1, tiled=True)  53.1 us
    dot_general x8, matrix products, dot_nt(): lax.dot_general(a, b, (((1,), (1,)), ((), ())), preferred_element_type=F32)  51.1 us
    dot_general x2, matrix products, dot_tn(): lax.dot_general(a, b, (((0,), (0,)), ((), ())), preferred_element_type=F32)  43.1 us
    pallas_call x4, Pallas kernels, attend(): pl.pallas_call(functools.partial(attend_kernel, mask is not None), grid=(...  38.5 us
    ppermute x35, starting transfers between devices, swap(): return lax.ppermute(values, 'mp', SWAP)  37.1 us
  transfers between devices with their start and end apart: 43, of which 22 were waited for; matrix products, arithmetic and copies ran while one was open for 37% of the time, Pallas kernels for 33%

profile of v3, /device:TPU:0, one launch (start us, length us, event | category | flops | bytes accessed | tf_op | source)
XLA Modules:
  0.0 789.7 jit_solution(15130428265877958587)
XLA Ops:
  35.5 6.2 collective-permute-done.4
  55.8 5.8 collective-permute-done.5.refs_1_
  61.6 53.1 %all-gather.3.cloned.1.call-done.refs_3_.refs_4_ = bf16[8,1536,768]{2,1,0:T(8,128)(2,1)} async-done(((bf16[8,96,768]{2,1,0:T(8,128)(2,1)}), bf16[8,1536,768]{2,1,0:T(8,128)(2,1)}) %all-gather.3.cloned.1.call-update) | async-done | bytes 18874384 | tf_op jit(solution)/shard_map/all_gather | solution.py:677
  147.7 6.8 rope_prep.1
  154.7 10.1 %attend_fwd.4 = (bf16[384,768]{1,0:T(8,128)(2,1)S(1)}, f32[6,1,384]{2,1,0:T(1,128)S(1)}, f32[192,1536]{1,0:T(8,128)S(1)}, bf16[192,1536]{1,0:T(8,128)(2,1)S(1)}) custom-call(bf16[384,768]{1,0:T(8,128)(2,1)S(1)} %slice.527.refs_0_, bf16[800,768]{1,0:T(8,128)(2,1)S(1)} %get-tuple-element.114.refs_1_, bf16[800,768]{1,0:T(8,128)(2,1)S(1)} %pad_maximum_fusion.6.refs_2_, ...), custom_call_target="tpu_custom_call" | custom-call | flops 2831155200 | bytes 3637248 | tf_op jit(solution)/shard_map/attend_fwd/pallas_call | solution.py:125
  166.6 10.1 %attend_fwd.5 = (bf16[416,768]{1,0:T(8,128)(2,1)S(1)}, f32[6,1,416]{2,1,0:T(1,128)S(1)}, f32[208,1536]{1,0:T(8,128)S(1)}, bf16[208,1536]{1,0:T(8,128)(2,1)S(1)}) custom-call(bf16[416,768]{1,0:T(8,128)(2,1)S(1)} %slice.534.refs_0_, bf16[800,768]{1,0:T(8,128)(2,1)S(1)} %get-tuple-element.114.refs_1_, bf16[800,768]{1,0:T(8,128)(2,1)S(1)} %pad_maximum_fusion.6.refs_2_, ...), custom_call_target="tpu_custom_call" | custom-call | flops 3067084800 | bytes 3735552 | tf_op jit(solution)/shard_map/attend_fwd/pallas_call | solution.py:125
  183.9 10.2 %collective-permute-done.10 = bf16[208,1536]{1,0:T(8,128)(2,1)S(1)} collective-permute-done((bf16[208,1536]{1,0:T(8,128)(2,1)S(1)}, bf16[208,1536]{1,0:T(8,128)(2,1)S(1)}, u32[]{:S(2)}, u32[]{:S(2)}) %collective-permute-start.10) | collective-permute-done | bytes 639008 | tf_op jit(solution)/shard_map/ppermute | solution.py:571
  195.3 10.6 %collective-permute-done.12.refs_5_ = bf16[192,1536]{1,0:T(8,128)(2,1)S(1)} collective-permute-done((bf16[192,1536]{1,0:T(8,128)(2,1)S(1)}, bf16[192,1536]{1,0:T(8,128)(2,1)S(1)}, u32[]{:S(2)}, u32[]{:S(2)}) %collective-permute-start.12) | collective-permute-done | bytes 589856 | tf_op jit(solution)/shard_map/ppermute | solution.py:571
  219.1 8.9 %attend_fwd.6 = (bf16[384,768]{1,0:T(8,128)(2,1)S(1)}, f32[6,1,384]{2,1,0:T(1,128)S(1)}, f32[192,1536]{1,0:T(8,128)S(1)}, bf16[192,1536]{1,0:T(8,128)(2,1)}) custom-call(bf16[384,768]{1,0:T(8,128)(2,1)S(1)} %multiply_convert_fusion.8.refs_0_, bf16[512,768]{1,0:T(8,128)(2,1)S(1)} %multiply_convert_fusion.2.refs_1_, ...), custom_call_target="tpu_custom_call" | custom-call | flops 1811939328 | bytes 2752512 | tf_op jit(solution)/shard_map/attend_fwd/pallas_call | solution.py:125
  235.4 9.6 %collective-permute-done.16 = bf16[192,1536]{1,0:T(8,128)(2,1)} collective-permute-done((bf16[192,1536]{1,0:T(8,128)(2,1)}, bf16[192,1536]{1,0:T(8,128)(2,1)}, u32[]{:S(2)}, u32[]{:S(2)}) %collective-permute-start.16) | collective-permute-done | bytes 589856 | tf_op jit(solution)/shard_map/ppermute | solution.py:571
  262.8 9.4 %attend_fwd.7 = (bf16[416,768]{1,0:T(8,128)(2,1)S(1)}, f32[6,1,416]{2,1,0:T(1,128)S(1)}, f32[208,1536]{1,0:T(8,128)S(1)}, bf16[208,1536]{1,0:T(8,128)(2,1)}) custom-call(bf16[416,768]{1,0:T(8,128)(2,1)S(1)} %copy-done.10, bf16[512,768]{1,0:T(8,128)(2,1)S(1)} %multiply_convert_fusion.2.refs_1_, bf16[512,768]{1,0:T(8,128)(2,1)S(1)} %add_convert_fusion.1.refs_2_, ...), custom_call_target="tpu_custom_call" | custom-call | flops 1962934272 | bytes 2850816 | tf_op jit(solution)/shard_map/attend_fwd/pallas_call | solution.py:125
  275.4 12.0 %multiply_convert_fusion.1 = (bf16[384,4480]{1,0:T(8,128)(2,1)S(1)}, f32[384,4480]{1,0:T(8,128)}) fusion(f32[4480]{0:T(1024)} %add.738, bf16[2,1536,4480]{2,1,0:T(8,128)(2,1)} %all-gather.5.cloned.1.call-done, bf16[192,1536]{1,0:T(8,128)(2,1)} %collective-permute-done.18, bf16[192,1536]{1,0:T(8,128)(2,1)} %add_convert_fusion.5), kind=kOutput, calls=%fused_computation.45 | convolution fusion | flops 5304385536 | bytes 25284608 | tf_op jit(solution)/shard_map/dot_general | solution.py:38
  291.4 8.8 %fusion.7 = f32[384,1536]{1,0:T(8,128)S(1)} fusion(bf16[384,4480]{1,0:T(8,128)(2,1)S(1)} %get-tuple-element.137, bf16[2,1536,4480]{2,1,0:T(8,128)(2,1)} %all-gather.5.cloned.1.call-done), kind=kOutput, calls=%fused_computation.15 | convolution fusion | flops 5284823040 | bytes 19562496 | tf_op jit(solution)/shard_map/dot_general | solution.py:42
  300.3 4.5 collective-permute-done.20
  306.0 13.2 %multiply_convert_fusion = (bf16[416,4480]{1,0:T(8,128)(2,1)}, f32[416,4480]{1,0:T(8,128)}) fusion(f32[4480]{0:T(1024)S(1)} %copy-done.149, bf16[2,1536,4480]{2,1,0:T(8,128)(2,1)} %all-gather.5.cloned.1.call-done, bf16[208,1536]{1,0:T(8,128)(2,1)S(1)} %collective-permute-done.20, bf16[208,1536]{1,0:T(8,128)(2,1)S(1)} %add_convert_fusion.2), kind=kOutput, calls=%fused_computation.26 | convolution fusion | flops 5746417664 | bytes 26240512 | tf_op jit(solution)/shard_map/dot_general | solution.py:38
  322.5 10.1 %fusion.6 = f32[416,1536]{1,0:T(8,128)S(1)} fusion(bf16[416,4480]{1,0:T(8,128)(2,1)} %get-tuple-element.143, bf16[2,1536,4480]{2,1,0:T(8,128)(2,1)} %all-gather.5.cloned.1.call-done), kind=kOutput, calls=%fused_computation.14 | convolution fusion | flops 5725224960 | bytes 20045824 | tf_op jit(solution)/shard_map/dot_general | solution.py:42
  335.6 12.3 %fusion.26 = bf16[384,4480]{1,0:T(8,128)(2,1)S(1)} fusion(bf16[2,1536,4480]{2,1,0:T(8,128)(2,1)} %all-gather.5.cloned.1.call-done, f32[384,4480]{1,0:T(8,128)} %get-tuple-element.436, bf16[192,1536]{1,0:T(8,128)(2,1)S(1)} %collective-permute-done.22, bf16[192,1536]{1,0:T(8,128)(2,1)S(1)} %multiply_convert_fusion.7), kind=kOutput, calls=%fused_computation.36 | convolution fusion | flops 5323309056 | bytes 25264128 | tf_op jit(solution)/shard_map/dot_general | solution.py:38
  351.7 8.8 %fusion.1 = f32[384,1536]{1,0:T(8,128)S(1)} fusion(bf16[384,4480]{1,0:T(8,128)(2,1)S(1)} %fusion.26, bf16[2,1536,4480]{2,1,0:T(8,128)(2,1)} %all-gather.5.cloned.1.call-done), kind=kOutput, calls=%fused_computation.9 | convolution fusion | flops 5284823040 | bytes 19562496 | tf_op jit(solution)/shard_map/dot_general | solution.py:42
  360.6 6.6 collective-permute-done.24
  368.3 20.8 %convolution_convert_fusion.1 = bf16[1536,4480]{1,0:T(8,128)(2,1)} fusion(bf16[416,4480]{1,0:T(8,128)(2,1)} %get-tuple-element.143, bf16[384,4480]{1,0:T(8,128)(2,1)} %copy-done.193, bf16[208,1536]{1,0:T(8,128)(2,1)S(1)} %collective-permute-done.24, bf16[208,1536]{1,0:T(8,128)(2,1)S(1)} %multiply_convert_fusion.4, ...), kind=kOutput, calls=%fused_computation.1 | convolution fusion | flops 11041095680 | bytes 23388160 | tf_op jit(solution)/shard_map/dot_general | solution.py:46
  395.7 14.8 %fusion.25 = bf16[416,4480]{1,0:T(8,128)(2,1)S(1)} fusion(bf16[416,1536]{1,0:T(8,128)(2,1)S(1)} %copy-done.110, bf16[2,1536,4480]{2,1,0:T(8,128)(2,1)} %all-gather.5.cloned.1.call-done, f32[416,4480]{1,0:T(8,128)} %get-tuple-element.438), kind=kOutput, calls=%fused_computation.35 | convolution fusion | flops 5764362240 | bytes 26222592 | tf_op jit(solution)/shard_map/dot_general | solution.py:38
  411.4 10.4 %fusion = f32[416,1536]{1,0:T(8,128)S(1)} fusion(bf16[416,4480]{1,0:T(8,128)(2,1)S(1)} %fusion.25, bf16[2,1536,4480]{2,1,0:T(8,128)(2,1)} %all-gather.5.cloned.1.call-done), kind=kOutput, calls=%fused_computation.8 | convolution fusion | flops 5725224960 | bytes 20045824 | tf_op jit(solution)/shard_map/dot_general | solution.py:42
  423.1 22.2 %convolution_convert_fusion = bf16[1536,4480]{1,0:T(8,128)(2,1)} fusion(bf16[416,4480]{1,0:T(8,128)(2,1)} %copy-done.91, bf16[384,4480]{1,0:T(8,128)(2,1)} %copy-done.96, bf16[208,1536]{1,0:T(8,128)(2,1)S(1)} %copy-done.190, bf16[208,1536]{1,0:T(8,128)(2,1)S(1)} %copy-done.118, bf16[192,1536]{1,0:T(8,128)(2,1)} %collective-permute-done.18, ...), kind=kOutput, calls=%fused_computation | convolution fusion | flops 11041095680 | bytes 23388160 | tf_op jit(solution)/shard_map/dot_general | solution.py:46
  450.8 8.3 %attend_bwd_cross.2 = (f32[384,768]{1,0:T(8,128)S(1)}, f32[512,768]{1,0:T(8,128)}, f32[512,768]{1,0:T(8,128)}, f32[384,1]{1,0:T(8,128)S(1)}, f32[1,768]{1,0:T(1,128)S(1)}) custom-call(bf16[384,768]{1,0:T(8,128)(2,1)S(1)} %copy-done.16, bf16[512,768]{1,0:T(8,128)(2,1)S(1)} %multiply_convert_fusion.2.refs_1_, bf16[512,768]{1,0:T(8,128)(2,1)S(1)} %add_convert_fusion.1.refs_2_, ...), custom_call_target="tpu_custom_call" | custom-call | flops 4529848320 | bytes 8257536 | tf_op jit(solution)/shard_map/attend_bwd_cross/pallas_call | solution.py:219
  471.6 9.6 %attend_bwd_cross.3 = (f32[416,768]{1,0:T(8,128)S(1)}, f32[512,768]{1,0:T(8,128)}, f32[512,768]{1,0:T(8,128)}, f32[416,1]{1,0:T(8,128)S(1)}, f32[1,768]{1,0:T(1,128)S(1)}) custom-call(bf16[416,768]{1,0:T(8,128)(2,1)S(1)} %copy-done.11, bf16[512,768]{1,0:T(8,128)(2,1)S(1)} %multiply_convert_fusion.2.refs_1_, bf16[512,768]{1,0:T(8,128)(2,1)S(1)} %add_convert_fusion.1.refs_2_, ...), custom_call_target="tpu_custom_call" | custom-call | flops 4907335680 | bytes 8552448 | tf_op jit(solution)/shard_map/attend_bwd_cross/pallas_call | solution.py:219
  490.1 6.1 collective-permute-done.31
  503.4 6.9 collective-permute-done.32
  516.0 13.0 %head_grads.3 = bf16[4,1536,768]{2,1,0:T(8,128)(2,1)} custom-call(bf16[208,1536]{1,0:T(8,128)(2,1)S(1)} %copy-done.34, bf16[416,768]{1,0:T(8,128)(2,1)S(1)} %get-tuple-element.338.refs_1_, bf16[208,1536]{1,0:T(8,128)(2,1)S(1)} %copy-done.50, bf16[192,1536]{1,0:T(8,128)(2,1)S(1)} %copy-done.40, bf16[384,768]{1,0:T(8,128)(2,1)S(1)} %get-tuple-element.340.refs_4_, ...), custom_call_target="tpu_custom_call" | custom-call | flops 6190792704 | bytes 19955712 | tf_op jit(solution)/shard_map/head_grads/pallas_call | solution.py:328
  533.2 4.8 fusion.70.refs_3_
  563.2 22.4 %attend_bwd_self.1 = (f32[800,768]{1,0:T(8,128)}, f32[800,768]{1,0:T(8,128)}, bf16[800,768]{1,0:T(8,128)(2,1)S(1)}, f32[800,1]{1,0:T(8,128)S(1)}, f32[800,1]{1,0...) custom-call(bf16[800,768]{1,0:T(8,128)(2,1)S(1)} %copy-done.28, bf16[800,768]{1,0:T(8,128)(2,1)} %copy-done.3, ...), custom_call_target="tpu_custom_call" | custom-call | flops 14745600000 | bytes 15974400 | tf_op jit(solution)/shard_map/attend_bwd_self/pallas_call | solution.py:198
  600.1 18.7 %self_back.1 = (bf16[3,1536,768]{2,1,0:T(8,128)(2,1)}, f32[400,1536]{1,0:T(8,128)}, bf16[400,1536]{1,0:T(8,128)(2,1)S(1)}) custom-call(bf16[208,1536]{1,0:T(8,128)(2,1)S(1)} %copy-done.36, bf16[208,1536]{1,0:T(8,128)(2,1)S(1)} %copy-done.46, bf16[192,1536]{1,0:T(8,128)(2,1)S(1)} %copy-done.38, bf16[192,1536]{1,0:T(8,128)(2,1)} %collective-permute-done.6.refs_3_, ...), custom_call_target="tpu_custom_call" | custom-call | flops 11324620800 | bytes 30000000 | tf_op jit(solution)/shard_map/self_back/pallas_call | solution.py:285
  619.8 140.3 %tail_sums.1 = (f32[8,96,768]{2,1,0:T(8,128)}, f32[400,1536]{1,0:T(8,128)}, f32[24,1536]{1,0:T(8,128)}) custom-call(bf16[3,8,2,96,768]{4,3,2,1,0:T(8,128)(2,1)} %bitcast.237, bf16[1,8,2,96,768]{4,3,2,1,0:T(8,128)(2,1)} %bitcast.229, bf16[4,8,2,96,768]{4,3,2,1,0:T(8,128)(2,1)} %bitcast.236, f32[208,1536]{1,0:T(8,128)} %get-tuple-element.347.refs_3_, ...), custom_call_target="tpu_custom_call" | custom-call | flops 1000000 | bytes 1000000 | tf_op jit(solution)/shard_map/tail_sums/pallas_call | solution.py:520
  (751 shorter events, 253.5 us)
Async XLA Ops:
  7.2 107.5 %all-gather.3.cloned.1.call-start = ((), (), s32[]{:S(2)}) async-start(), calls=%async_computation.2 | async-start | bytes 20054016 | tf_op jit(solution)/shard_map/all_gather | solution.py:677
  9.8 265.6 %all-gather.5.cloned.1.call-start = ((), (), s32[]{:S(2)}) async-start(), calls=%async_computation.3 | async-start | bytes 29245440 | tf_op jit(solution)/shard_map/all_gather | solution.py:677
  11.4 526.5 %reduce-scatter.3.cloned.1.call-start = ((), (), s32[]{:S(2)}) async-start(), calls=%async_computation.4 | async-start | bytes 14622720 | tf_op jit(solution)/shard_map/reduce_scatter | solution.py:816
  15.9 113.9 %collective-permute-start.14 = (bf16[256,1536]{1,0:T(8,128)(2,1)}, bf16[256,1536]{1,0:T(8,128)(2,1)}, u32[]{:S(2)}, u32[]{:S(2)}) collective-permute-start(bf16[256,1536]{1,0:T(8,128)(2,1)} %bitcast.286), channel_id=1, source_target_pairs={{0,1},{1,0},{2,3},{3,2},{4,5},{5,4},{6,7},{7,6},{8,9},{9,8},{10,11... | collective-permute-start | bytes 2359304 | tf_op jit(solution)/shard_map/ppermute | solution.py:571
  32.4 9.4 %collective-permute-start.4 = (f32[16,1408]{1,0:T(8,128)S(1)}, f32[16,1408]{1,0:T(8,128)S(1)}, u32[]{:S(2)}, u32[]{:S(2)}) collective-permute-start(f32[16,1408]{1,0:T(8,128)S(1)} %maximum_select_fusion.1), channel_id=1, source_target_pairs={{0,16},{2,18},{4,20},{6,22},{8,24},{10,26},{12,28},{14,30},{16,0},... | collective-permute-start | bytes 270344 | tf_op jit(solution)/shard_map/ppermute | solution.py:615
  44.3 17.3 %collective-permute-start.5 = (bf16[208,1536]{1,0:T(8,128)(2,1)S(1)}, bf16[208,1536]{1,0:T(8,128)(2,1)S(1)}, u32[]{:S(2)}, u32[]{:S(2)}) collective-permute-start(bf16[208,1536]{1,0:T(8,128)(2,1)S(1)} %get-tuple-element.380.refs_0_), channel_id=1, source_target_pairs={{0,1},{1,0},{2,3},{3,2},{4,5},{5,4},{6,7},{7,6},{8,9},{9,8},{10,11... | collective-permute-start | bytes 1916936 | tf_op jit(solution)/shard_map/ppermute | solution.py:571
  52.8 70.8 %collective-permute-start.6 = (bf16[192,1536]{1,0:T(8,128)(2,1)S(1)}, bf16[192,1536]{1,0:T(8,128)(2,1)}, u32[]{:S(2)}, u32[]{:S(2)}) collective-permute-start(bf16[192,1536]{1,0:T(8,128)(2,1)S(1)} %get-tuple-element.378.refs_2_), channel_id=1, source_target_pairs={{0,1},{1,0},{2,3},{3,2},{4,5},{5,4},{6,7},{7,6},{8,9},{9,8},{10,11... | collective-permute-start | bytes 1769480 | tf_op jit(solution)/shard_map/ppermute | solution.py:571
  122.1 21.5 %collective-permute-start.7 = (f32[416,2]{0,1:T(2,128)S(1)}, f32[416,2]{0,1:T(2,128)S(1)}, u32[]{:S(2)}, u32[]{:S(2)}) collective-permute-start(f32[416,2]{0,1:T(2,128)S(1)} %pad_maximum_fusion.27), channel_id=1, source_target_pairs={{0,1},{1,0},{2,3},{3,2},{4,5},{5,4},{6,7},{7,6},{8,9},{9,8},{10,11... | collective-permute-start | bytes 9992 | tf_op jit(solution)/shard_map/ppermute | solution.py:571
  128.8 14.8 %collective-permute-start.8 = (f32[384,2]{0,1:T(2,128)S(1)}, f32[384,2]{0,1:T(2,128)S(1)}, u32[]{:S(2)}, u32[]{:S(2)}) collective-permute-start(f32[384,2]{0,1:T(2,128)S(1)} %pad_maximum_fusion.34), channel_id=1, source_target_pairs={{0,1},{1,0},{2,3},{3,2},{4,5},{5,4},{6,7},{7,6},{8,9},{9,8},{10,11... | collective-permute-start | bytes 9224 | tf_op jit(solution)/shard_map/ppermute | solution.py:571
  133.4 32.5 %collective-permute-start.15 = (f32[512,1]{0,1:T(1,128)S(1)}, f32[512,1]{0,1:T(1,128)S(1)}, u32[]{:S(2)}, u32[]{:S(2)}) collective-permute-start(f32[512,1]{0,1:T(1,128)S(1)} %pad_maximum_fusion.36), channel_id=1, source_target_pairs={{0,1},{1,0},{2,3},{3,2},{4,5},{5,4},{6,7},{7,6},{8,9},{9,8},{10,11... | collective-permute-start | bytes 6152 | tf_op jit(solution)/shard_map/ppermute | solution.py:571
  164.8 15.5 %collective-permute-start.9 = (bf16[192,1536]{1,0:T(8,128)(2,1)S(1)}, bf16[192,1536]{1,0:T(8,128)(2,1)S(1)}, u32[]{:S(2)}, u32[]{:S(2)}) collective-permute-start(bf16[192,1536]{1,0:T(8,128)(2,1)S(1)} %get-tuple-element.115), channel_id=1, source_target_pairs={{0,1},{1,0},{2,3},{3,2},{4,5},{5,4},{6,7},{7,6},{8,9},{9,8},{10,11... | collective-permute-start | bytes 1769480 | tf_op jit(solution)/shard_map/ppermute | solution.py:571
  176.8 17.4 %collective-permute-start.10 = (bf16[208,1536]{1,0:T(8,128)(2,1)S(1)}, bf16[208,1536]{1,0:T(8,128)(2,1)S(1)}, u32[]{:S(2)}, u32[]{:S(2)}) collective-permute-start(bf16[208,1536]{1,0:T(8,128)(2,1)S(1)} %get-tuple-element.118), channel_id=1, source_target_pairs={{0,1},{1,0},{2,3},{3,2},{4,5},{5,4},{6,7},{7,6},{8,9},{9,8},{10,11... | collective-permute-start | bytes 1916936 | tf_op jit(solution)/shard_map/ppermute | solution.py:571
  182.1 23.8 %collective-permute-start.12 = (bf16[192,1536]{1,0:T(8,128)(2,1)S(1)}, bf16[192,1536]{1,0:T(8,128)(2,1)S(1)}, u32[]{:S(2)}, u32[]{:S(2)}) collective-permute-start(bf16[192,1536]{1,0:T(8,128)(2,1)S(1)} %add_convert_fusion.6.refs_3_), channel_id=1, source_target_pairs={{0,1},{1,0},{2,3},{3,2},{4,5},{5,4},{6,7},{7,6},{8,9},{9,8},{10,11... | collective-permute-start | bytes 1769480 | tf_op jit(solution)/shard_map/ppermute | solution.py:571
  213.0 17.1 %collective-permute-start.11 = (bf16[208,1536]{1,0:T(8,128)(2,1)S(1)}, bf16[208,1536]{1,0:T(8,128)(2,1)S(1)}, u32[]{:S(2)}, u32[]{:S(2)}) collective-permute-start(bf16[208,1536]{1,0:T(8,128)(2,1)S(1)} %add_convert_fusion.3.refs_0_), channel_id=1, source_target_pairs={{0,1},{1,0},{2,3},{3,2},{4,5},{5,4},{6,7},{7,6},{8,9},{9,8},{10,11... | collective-permute-start | bytes 1916936 | tf_op jit(solution)/shard_map/ppermute | solution.py:571
  231.0 14.1 %collective-permute-start.16 = (bf16[192,1536]{1,0:T(8,128)(2,1)}, bf16[192,1536]{1,0:T(8,128)(2,1)}, u32[]{:S(2)}, u32[]{:S(2)}) collective-permute-start(bf16[192,1536]{1,0:T(8,128)(2,1)} %get-tuple-element.123), channel_id=1, source_target_pairs={{0,1},{1,0},{2,3},{3,2},{4,5},{5,4},{6,7},{7,6},{8,9},{9,8},{10,11... | collective-permute-start | bytes 1769480 | tf_op jit(solution)/shard_map/ppermute | solution.py:571
  254.3 19.9 %collective-permute-start.18 = (bf16[192,1536]{1,0:T(8,128)(2,1)}, bf16[192,1536]{1,0:T(8,128)(2,1)}, u32[]{:S(2)}, u32[]{:S(2)}) collective-permute-start(bf16[192,1536]{1,0:T(8,128)(2,1)} %add_convert_fusion.5), channel_id=1, source_target_pairs={{0,1},{1,0},{2,3},{3,2},{4,5},{5,4},{6,7},{7,6},{8,9},{9,8},{10,11... | collective-permute-start | bytes 1769480 | tf_op jit(solution)/shard_map/ppermute | solution.py:571
  274.1 13.4 %collective-permute-start.19 = (bf16[208,1536]{1,0:T(8,128)(2,1)}, bf16[208,1536]{1,0:T(8,128)(2,1)}, u32[]{:S(2)}, u32[]{:S(2)}) collective-permute-start(bf16[208,1536]{1,0:T(8,128)(2,1)} %get-tuple-element.132), channel_id=1, source_target_pairs={{0,1},{1,0},{2,3},{3,2},{4,5},{5,4},{6,7},{7,6},{8,9},{9,8},{10,11... | collective-permute-start | bytes 1916936 | tf_op jit(solution)/shard_map/ppermute | solution.py:571
  290.4 14.4 %collective-permute-start.20 = (bf16[208,1536]{1,0:T(8,128)(2,1)S(1)}, bf16[208,1536]{1,0:T(8,128)(2,1)S(1)}, u32[]{:S(2)}, u32[]{:S(2)}) collective-permute-start(bf16[208,1536]{1,0:T(8,128)(2,1)S(1)} %add_convert_fusion.2), channel_id=1, source_target_pairs={{0,1},{1,0},{2,3},{3,2},{4,5},{5,4},{6,7},{7,6},{8,9},{9,8},{10,11... | collective-permute-start | bytes 1916936 | tf_op jit(solution)/shard_map/ppermute | solution.py:571
  304.9 14.3 %collective-permute-start.21 = (bf16[192,1536]{1,0:T(8,128)(2,1)S(1)}, bf16[192,1536]{1,0:T(8,128)(2,1)S(1)}, u32[]{:S(2)}, u32[]{:S(2)}) collective-permute-start(bf16[192,1536]{1,0:T(8,128)(2,1)S(1)} %slice.955), channel_id=1, source_target_pairs={{0,1},{1,0},{2,3},{3,2},{4,5},{5,4},{6,7},{7,6},{8,9},{9,8},{10,11... | collective-permute-start | bytes 1769480 | tf_op jit(solution)/shard_map/ppermute | solution.py:571
  321.4 13.1 %collective-permute-start.22 = (bf16[192,1536]{1,0:T(8,128)(2,1)S(1)}, bf16[192,1536]{1,0:T(8,128)(2,1)S(1)}, u32[]{:S(2)}, u32[]{:S(2)}) collective-permute-start(bf16[192,1536]{1,0:T(8,128)(2,1)S(1)} %multiply_convert_fusion.7), channel_id=1, source_target_pairs={{0,1},{1,0},{2,3},{3,2},{4,5},{5,4},{6,7},{7,6},{8,9},{9,8},{10,11... | collective-permute-start | bytes 1769480 | tf_op jit(solution)/shard_map/ppermute | solution.py:571
  334.5 13.4 %collective-permute-start.23 = (bf16[208,1536]{1,0:T(8,128)(2,1)S(1)}, bf16[208,1536]{1,0:T(8,128)(2,1)S(1)}, u32[]{:S(2)}, u32[]{:S(2)}) collective-permute-start(bf16[208,1536]{1,0:T(8,128)(2,1)S(1)} %slice.952), channel_id=1, source_target_pairs={{0,1},{1,0},{2,3},{3,2},{4,5},{5,4},{6,7},{7,6},{8,9},{9,8},{10,11... | collective-permute-start | bytes 1916936 | tf_op jit(solution)/shard_map/ppermute | solution.py:571
  350.6 16.6 %collective-permute-start.24 = (bf16[208,1536]{1,0:T(8,128)(2,1)S(1)}, bf16[208,1536]{1,0:T(8,128)(2,1)S(1)}, u32[]{:S(2)}, u32[]{:S(2)}) collective-permute-start(bf16[208,1536]{1,0:T(8,128)(2,1)S(1)} %multiply_convert_fusion.4), channel_id=1, source_target_pairs={{0,1},{1,0},{2,3},{3,2},{4,5},{5,4},{6,7},{7,6},{8,9},{9,8},{10,11... | collective-permute-start | bytes 1916936 | tf_op jit(solution)/shard_map/ppermute | solution.py:571
  367.3 23.1 %collective-permute-start.25 = (bf16[192,1536]{1,0:T(8,128)(2,1)S(1)}, bf16[192,1536]{1,0:T(8,128)(2,1)}, u32[]{:S(2)}, u32[]{:S(2)}) collective-permute-start(bf16[192,1536]{1,0:T(8,128)(2,1)S(1)} %slice.954), channel_id=1, source_target_pairs={{0,1},{1,0},{2,3},{3,2},{4,5},{5,4},{6,7},{7,6},{8,9},{9,8},{10,11... | collective-permute-start | bytes 1769480 | tf_op jit(solution)/shard_map/ppermute | solution.py:571
  390.4 389.0 %reduce-scatter.5.cloned.1.call-start = ((), (), s32[]{:S(2)}) async-start(), calls=%async_computation.5 | async-start | bytes 14622720 | tf_op jit(solution)/shard_map/reduce_scatter | solution.py:816
  410.5 11.3 %collective-permute-start.26 = (bf16[192,1536]{1,0:T(8,128)(2,1)S(1)}, bf16[192,1536]{1,0:T(8,128)(2,1)S(1)}, u32[]{:S(2)}, u32[]{:S(2)}) collective-permute-start(bf16[192,1536]{1,0:T(8,128)(2,1)S(1)} %get-tuple-element.154.refs_13_), channel_id=1, source_target_pairs={{0,1},{1,0},{2,3},{3,2},{4,5},{5,4},{6,7},{7,6},{8,9},{9,8},{10,11... | collective-permute-start | bytes 1769480 | tf_op jit(solution)/shard_map/ppermute | solution.py:571
  421.9 23.4 %collective-permute-start.27 = (bf16[208,1536]{1,0:T(8,128)(2,1)S(1)}, bf16[208,1536]{1,0:T(8,128)(2,1)S(1)}, u32[]{:S(2)}, u32[]{:S(2)}) collective-permute-start(bf16[208,1536]{1,0:T(8,128)(2,1)S(1)} %slice.951), channel_id=1, source_target_pairs={{0,1},{1,0},{2,3},{3,2},{4,5},{5,4},{6,7},{7,6},{8,9},{9,8},{10,11... | collective-permute-start | bytes 1916936 | tf_op jit(solution)/shard_map/ppermute | solution.py:571
  447.3 12.5 %collective-permute-start.28 = (bf16[208,1536]{1,0:T(8,128)(2,1)S(1)}, bf16[208,1536]{1,0:T(8,128)(2,1)S(1)}, u32[]{:S(2)}, u32[]{:S(2)}) collective-permute-start(bf16[208,1536]{1,0:T(8,128)(2,1)S(1)} %get-tuple-element.160.refs_10_), channel_id=1, source_target_pairs={{0,1},{1,0},{2,3},{3,2},{4,5},{5,4},{6,7},{7,6},{8,9},{9,8},{10,11... | collective-permute-start | bytes 1916936 | tf_op jit(solution)/shard_map/ppermute | solution.py:571
  471.0 16.8 %collective-permute-start.30 = (bf16[192,1536]{1,0:T(8,128)(2,1)}, bf16[192,1536]{1,0:T(8,128)(2,1)S(1)}, u32[]{:S(2)}, u32[]{:S(2)}) collective-permute-start(bf16[192,1536]{1,0:T(8,128)(2,1)} %slice.953), channel_id=1, source_target_pairs={{0,1},{1,0},{2,3},{3,2},{4,5},{5,4},{6,7},{7,6},{8,9},{9,8},{10,11... | collective-permute-start | bytes 1769480 | tf_op jit(solution)/shard_map/ppermute | solution.py:571
  499.6 10.7 %collective-permute-start.32 = (bf16[208,1536]{1,0:T(8,128)(2,1)S(1)}, bf16[208,1536]{1,0:T(8,128)(2,1)S(1)}, u32[]{:S(2)}, u32[]{:S(2)}) collective-permute-start(bf16[208,1536]{1,0:T(8,128)(2,1)S(1)} %slice.950), channel_id=1, source_target_pairs={{0,1},{1,0},{2,3},{3,2},{4,5},{5,4},{6,7},{7,6},{8,9},{9,8},{10,11... | collective-permute-start | bytes 1916936 | tf_op jit(solution)/shard_map/ppermute | solution.py:571
  502.7 26.3 %collective-permute-start.34 = (bf16[192,1536]{1,0:T(8,128)(2,1)S(1)}, bf16[192,1536]{1,0:T(8,128)(2,1)S(1)}, u32[]{:S(2)}, u32[]{:S(2)}) collective-permute-start(bf16[192,1536]{1,0:T(8,128)(2,1)S(1)} %get-tuple-element.349.refs_3_), channel_id=1, source_target_pairs={{0,1},{1,0},{2,3},{3,2},{4,5},{5,4},{6,7},{7,6},{8,9},{9,8},{10,11... | collective-permute-start | bytes 1769480 | tf_op jit(solution)/shard_map/ppermute | solution.py:571
  512.7 16.3 %collective-permute-start.33 = (bf16[208,1536]{1,0:T(8,128)(2,1)S(1)}, bf16[208,1536]{1,0:T(8,128)(2,1)S(1)}, u32[]{:S(2)}, u32[]{:S(2)}) collective-permute-start(bf16[208,1536]{1,0:T(8,128)(2,1)S(1)} %get-tuple-element.346.refs_0_), channel_id=1, source_target_pairs={{0,1},{1,0},{2,3},{3,2},{4,5},{5,4},{6,7},{7,6},{8,9},{9,8},{10,11... | collective-permute-start | bytes 1916936 | tf_op jit(solution)/shard_map/ppermute | solution.py:571
  557.3 36.9 %collective-permute-start.38 = (bf16[256,1536]{1,0:T(8,128)(2,1)}, bf16[256,1536]{1,0:T(8,128)(2,1)}, u32[]{:S(2)}, u32[]{:S(2)}) collective-permute-start(bf16[256,1536]{1,0:T(8,128)(2,1)} %slice.949), channel_id=1, source_target_pairs={{0,1},{1,0},{2,3},{3,2},{4,5},{5,4},{6,7},{7,6},{8,9},{9,8},{10,11... | collective-permute-start | bytes 2359304 | tf_op jit(solution)/shard_map/ppermute | solution.py:571
  (205 other events, 2859.4 us)
Sparse Core Ops, SparseCore 0:
  10.1 104.5 all-gather.2
  116.8 139.6 all-gather.4
  390.5 142.6 reduce-scatter.2
  538.1 159.7 reduce-scatter.4

commit v4 on v3

--- a/solution.py
+++ b/solution.py
@@ -723,9 +723,23 @@
     spans = [(int(ends[i]), int(ends[i + 1])) for i in range(len(cuts))]
     nc = len(cuts)
 
+    out_rows = [out_bias_full[i : i + 1] for i in range(4)]
+    norm3_row = norm3_full[None]
+    ffn_bias_row = ffn_bias_full[None]
+    bias_rows = [hb_full[i, j][None] for i in range(2) for j in range(3)]
+    late = [gate_attn, shift_ffn, scale_ffn, gate_ffn, norm3_row, ffn_bias_row, key_mask, cos, sin]
+    late += out_rows + bias_rows + row_valid
+    heads_w, *late = tie(heads_w, *late)
+    gate_attn, shift_ffn, scale_ffn, gate_ffn, norm3_row, ffn_bias_row, key_mask, cos, sin = late[:9]
+    out_rows, bias_rows, row_valid = late[9:13], late[13:19], late[19:]
+    self_w = heads_w[:4]
+    cross_w = heads_w[4:]
+    self_out_t = heads_w[3]
+    cross_out_t = heads_w[7]
+
     text_rows, text_pieces = collect(text_states[0])
-    cross_kp = dot_nn(text_rows, cross_w[1]) + hb_full[1, 1]
-    cross_v = (dot_nn(text_rows, cross_w[2]) + hb_full[1, 2]).astype(BF)
+    cross_kp = dot_nn(text_rows, cross_w[1]) + bias_rows[4]
+    cross_v = (dot_nn(text_rows, cross_w[2]) + bias_rows[5]).astype(BF)
     cross_ks = row_totals(squares(cross_kp))
     cross_kr = lax.rsqrt(cross_ks / D + EPS)
     cross_k = (cross_kp * cross_kr * qg_full[1, 1]).astype(BF)
@@ -737,9 +751,9 @@
         z, s = normal(r)
         x = (z * (1.0 + scale_attn) + shift_attn).astype(BF)
         rows, pieces = collect(x)
-        qc = dot_nn(rows, self_w[0]) + hb_full[0, 0]
-        kc = dot_nn(rows, self_w[1]) + hb_full[0, 1]
-        vc = (dot_nn(rows, self_w[2]) + hb_full[0, 2]).astype(BF)
+        qc = dot_nn(rows, self_w[0]) + bias_rows[0]
+        kc = dot_nn(rows, self_w[1]) + bias_rows[1]
+        vc = (dot_nn(rows, self_w[2]) + bias_rows[2]).astype(BF)
         tot = row_totals(jnp.concatenate([squares(qc), squares(kc)], axis=1))
         res0.append(r)
         unit0.append(z)
@@ -767,18 +781,19 @@
         return own, swap(other)
 
     def cross_query(c, own, got):
-        branch0[c] = own + got.astype(F32) + out_bias_full[1]
+        branch0[c] = own + got.astype(F32) + out_rows[1]
         after_self[c] = res0[c] + gate_attn * branch0[c]
         unit1[c], scale1[c] = normal(after_self[c])
-        x = (unit1[c] * norm3_full + out_bias_full[0]).astype(BF)
+        x = (unit1[c] * norm3_row + out_rows[0]).astype(BF)
         rows1[c] = [x, swap(x)]
 
     def cross_prepare(c, got=None):
-        qc = dot_nn(jnp.concatenate(rows1[c], axis=0), heads_w[4]) + hb_full[1, 0]
+        qc = dot_nn(jnp.concatenate(rows1[c], axis=0), heads_w[4]) + bias_rows[3]
+        total = row_totals(squares(qc))
         if got is not None:
             qc, got = tie(qc, got)
         cross_qp[c] = qc
-        cross_qs[c] = lax.rsqrt(row_totals(squares(qc)) / D + EPS)
+        cross_qs[c] = lax.rsqrt(total / D + EPS)
         cross_q[c] = (qc * cross_qs[c] * qg_full[1, 0]).astype(BF)
         return got
 
@@ -787,7 +802,7 @@
         return own, other
 
     def ffn_input(c, own, got):
-        after[c] = after_self[c] + own + got.astype(F32) + out_bias_full[2]
+        after[c] = after_self[c] + own + got.astype(F32) + out_rows[2]
         unit2[c], scale2[c] = normal(after[c])
         return (unit2[c] * (1.0 + scale_ffn) + shift_ffn).astype(BF)
 
@@ -819,13 +834,13 @@
     squares_of, gate_grads, ffn_backs = [list(none) for _ in range(3)]
 
     def inner_of(c):
-        inner = dot_nn(rows2[c], ffn_in_w) + ffn_bias_full
+        inner = dot_nn(rows2[c], ffn_in_w) + ffn_bias_row
         act, back = jax.vjp(functools.partial(jax.nn.gelu, approximate=True), inner)
         acts[c] = act.astype(BF)
         slopes[c] = back(jnp.ones_like(inner))[0].astype(BF)
 
     def loss_of(c, own, got):
-        branch = own + got.astype(F32) + out_bias_full[3]
+        branch = own + got.astype(F32) + out_rows[3]
         result = after[c] + gate_ffn * branch
         results[c] = result.astype(BF)
         errors[c] = (result - teach[c].astype(F32)) * row_valid[c]
@@ -922,7 +937,7 @@
         back = backs[c]
         norm3_g = norm3_g + colsum(back * unit1[c])
         bias0 = bias0 + colsum(back)
-        state[c] = d_afters[c] + normal_back(back * norm3_full, unit1[c], scale1[c])
+        state[c] = d_afters[c] + normal_back(back * norm3_row, unit1[c], scale1[c])
         gate0_g = gate0_g + colsum(branch0[c] * state[c])
         d_self = (gate_attn * state[c]).astype(BF)
         bias1 = bias1 + colsum(d_self.astype(F32))
@@ -962,6 +977,7 @@
     d_k = (dkw * ks - kp * (ks**3 * dots[:, 1:2] / D)).astype(BF)
     d_q, got_text = tie(d_q, got_text)
     text_g = own_text + got_text.astype(F32)
+    text_g, d_k = tie(text_g, d_k)
     g_self, part, other = self_back(rows0, spans, heads_w, [d_q, d_k, dv])
     self_b = jnp.stack([colsum(g.astype(F32)) for g in (d_q, d_k, dv)])
 

time: 800 us -> 799 us (level)
    dot_general x17, matrix products: 91.3 us -> 99.6 us  [dot_nn(): lax.dot_general(a, b, (((1,), (0,)), ((), ())), preferred_element_type=F32)]
    unnamed x394 -> x398, local copies, waits for them, and re-layouts: 29.5 us -> 29 us
  transfers between devices with their start and end apart: 43 -> 43, of which waited for: 22 -> 22; matrix products, arithmetic and copies ran while one was open for 37% -> 37% of each run, Pallas kernels for 33% -> 32%
where the time goes in v4:
time: 799 us; the launch traced here: 795 us
  Pallas kernels  257 us (32%)
  matrix products  191 us (24%)
  waiting for transfers between devices  144 us (18%)
  other arithmetic  79.2 us (10%)
  local copies, waits for them, and re-layouts  56.7 us (7%)
  starting transfers between devices  45.4 us (6%)
  between operations  20.7 us (3%)
    pallas_call x1, Pallas kernels, tail(): pl.pallas_call(functools.partial(tail_kernel, ndp, counts, nc), in_specs=...  137 us
    dot_general x17, matrix products, dot_nn(): lax.dot_general(a, b, (((1,), (0,)), ((), ())), preferred_element_type=F32)  99.6 us
    ppermute x35, waiting for transfers between devices, swap(): return lax.ppermute(values, 'mp', SWAP)  74.4 us
    all_gather x2, waiting for transfers between devices, whole(): return lax.all_gather(shards, 'dp', axis=1, tiled=True)  57.6 us
    dot_general x8, matrix products, dot_nt(): lax.dot_general(a, b, (((1,), (1,)), ((), ())), preferred_element_type=F32)  50.5 us
    dot_general x2, matrix products, dot_tn(): lax.dot_general(a, b, (((0,), (0,)), ((), ())), preferred_element_type=F32)  41 us
    ppermute x35, starting transfers between devices, swap(): return lax.ppermute(values, 'mp', SWAP)  38.9 us
    pallas_call x4, Pallas kernels, attend(): pl.pallas_call(functools.partial(attend_kernel, mask is not None), grid=(...  38.9 us
  transfers between devices with their start and end apart: 43, of which 22 were waited for; matrix products, arithmetic and copies ran while one was open for 37% of the time, Pallas kernels for 32%

profile of v4, /device:TPU:0, one launch (start us, length us, event | category | flops | bytes accessed | tf_op | source)
XLA Modules:
  0.0 794.8 jit_solution(15868226734349435034)
XLA Ops:
  37.2 5.5 collective-permute-done.4
  57.2 57.6 %all-gather.3.cloned.1.call-done.refs_3_.refs_4_ = bf16[8,1536,768]{2,1,0:T(8,128)(2,1)} async-done(((bf16[8,96,768]{2,1,0:T(8,128)(2,1)}), bf16[8,1536,768]{2,1,0:T(8,128)(2,1)}) %all-gather.3.cloned.1.call-update) | async-done | bytes 18874384 | tf_op jit(solution)/shard_map/all_gather | solution.py:677
  114.8 4.7 multiply_reduce_fusion.2
  160.0 6.9 rope_prep.1
  167.1 10.1 %attend_fwd.4 = (bf16[384,768]{1,0:T(8,128)(2,1)S(1)}, f32[6,1,384]{2,1,0:T(1,128)S(1)}, f32[192,1536]{1,0:T(8,128)S(1)}, bf16[192,1536]{1,0:T(8,128)(2,1)S(1)}) custom-call(bf16[384,768]{1,0:T(8,128)(2,1)S(1)} %slice.551.refs_0_, bf16[800,768]{1,0:T(8,128)(2,1)S(1)} %get-tuple-element.144.refs_1_, bf16[800,768]{1,0:T(8,128)(2,1)S(1)} %pad_maximum_fusion.6.refs_2_, ...), custom_call_target="tpu_custom_call" | custom-call | flops 2831155200 | bytes 3637248 | tf_op jit(solution)/shard_map/attend_fwd/pallas_call | solution.py:125
  179.7 10.1 %attend_fwd.5 = (bf16[416,768]{1,0:T(8,128)(2,1)S(1)}, f32[6,1,416]{2,1,0:T(1,128)S(1)}, f32[208,1536]{1,0:T(8,128)S(1)}, bf16[208,1536]{1,0:T(8,128)(2,1)S(1)}) custom-call(bf16[416,768]{1,0:T(8,128)(2,1)S(1)} %slice.553.refs_0_, bf16[800,768]{1,0:T(8,128)(2,1)S(1)} %get-tuple-element.144.refs_1_, bf16[800,768]{1,0:T(8,128)(2,1)S(1)} %pad_maximum_fusion.6.refs_2_, ...), custom_call_target="tpu_custom_call" | custom-call | flops 3067084800 | bytes 3735552 | tf_op jit(solution)/shard_map/attend_fwd/pallas_call | solution.py:125
  197.0 10.4 %collective-permute-done.10 = bf16[208,1536]{1,0:T(8,128)(2,1)S(1)} collective-permute-done((bf16[208,1536]{1,0:T(8,128)(2,1)S(1)}, bf16[208,1536]{1,0:T(8,128)(2,1)S(1)}, u32[]{:S(2)}, u32[]{:S(2)}) %collective-permute-start.10) | collective-permute-done | bytes 639008 | tf_op jit(solution)/shard_map/ppermute | solution.py:571
  208.6 10.5 %collective-permute-done.12.refs_5_ = bf16[192,1536]{1,0:T(8,128)(2,1)S(1)} collective-permute-done((bf16[192,1536]{1,0:T(8,128)(2,1)S(1)}, bf16[192,1536]{1,0:T(8,128)(2,1)S(1)}, u32[]{:S(2)}, u32[]{:S(2)}) %collective-permute-start.12) | collective-permute-done | bytes 589856 | tf_op jit(solution)/shard_map/ppermute | solution.py:571
  231.4 9.3 %attend_fwd.6 = (bf16[384,768]{1,0:T(8,128)(2,1)S(1)}, f32[6,1,384]{2,1,0:T(1,128)S(1)}, f32[192,1536]{1,0:T(8,128)S(1)}, bf16[192,1536]{1,0:T(8,128)(2,1)}) custom-call(bf16[384,768]{1,0:T(8,128)(2,1)S(1)} %multiply_convert_fusion.8.refs_0_, bf16[512,768]{1,0:T(8,128)(2,1)S(1)} %multiply_convert_fusion.2.refs_1_, ...), custom_call_target="tpu_custom_call" | custom-call | flops 1811939328 | bytes 2752512 | tf_op jit(solution)/shard_map/attend_fwd/pallas_call | solution.py:125
  248.8 12.3 %collective-permute-done.17 = f32[416,1]{1,0:T(8,128)} collective-permute-done((f32[416,1]{1,0:T(8,128)S(1)}, f32[416,1]{1,0:T(8,128)}, u32[]{:S(2)}, u32[]{:S(2)}) %collective-permute-start.17) | collective-permute-done | bytes 1696 | tf_op jit(solution)/shard_map/ppermute | solution.py:571
  271.5 9.4 %attend_fwd.7 = (bf16[416,768]{1,0:T(8,128)(2,1)S(1)}, f32[6,1,416]{2,1,0:T(1,128)S(1)}, f32[208,1536]{1,0:T(8,128)S(1)}, bf16[208,1536]{1,0:T(8,128)(2,1)}) custom-call(bf16[416,768]{1,0:T(8,128)(2,1)S(1)} %copy-done.13, bf16[512,768]{1,0:T(8,128)(2,1)S(1)} %multiply_convert_fusion.2.refs_1_, bf16[512,768]{1,0:T(8,128)(2,1)S(1)} %copy-done.9, ...), custom_call_target="tpu_custom_call" | custom-call | flops 1962934272 | bytes 2850816 | tf_op jit(solution)/shard_map/attend_fwd/pallas_call | solution.py:125
  283.9 12.1 %multiply_convert_fusion.1 = (bf16[384,4480]{1,0:T(8,128)(2,1)S(1)}, f32[384,4480]{1,0:T(8,128)}) fusion(f32[4480]{0:T(1024)} %reduce.26, bf16[2,1536,4480]{2,1,0:T(8,128)(2,1)} %all-gather.5.cloned.1.call-done, bf16[192,1536]{1,0:T(8,128)(2,1)} %collective-permute-done.18, bf16[192,1536]{1,0:T(8,128)(2,1)} %add_convert_fusion.5), kind=kOutput, calls=%fused_computation.45 | convolution fusion | flops 5304385536 | bytes 25284608 | tf_op jit(solution)/shard_map/dot_general | solution.py:38
  300.5 8.8 %fusion.7 = f32[384,1536]{1,0:T(8,128)S(1)} fusion(bf16[384,4480]{1,0:T(8,128)(2,1)S(1)} %get-tuple-element.180, bf16[2,1536,4480]{2,1,0:T(8,128)(2,1)} %all-gather.5.cloned.1.call-done), kind=kOutput, calls=%fused_computation.15 | convolution fusion | flops 5284823040 | bytes 19562496 | tf_op jit(solution)/shard_map/dot_general | solution.py:42
  309.3 4.6 collective-permute-done.20
  315.0 13.1 %multiply_convert_fusion = (bf16[416,4480]{1,0:T(8,128)(2,1)}, f32[416,4480]{1,0:T(8,128)}) fusion(f32[4480]{0:T(1024)S(1)} %copy-done.152, bf16[2,1536,4480]{2,1,0:T(8,128)(2,1)} %all-gather.5.cloned.1.call-done, bf16[208,1536]{1,0:T(8,128)(2,1)S(1)} %collective-permute-done.20, bf16[208,1536]{1,0:T(8,128)(2,1)S(1)} %add_convert_fusion.2), kind=kOutput, calls=%fused_computation.26 | convolution fusion | flops 5746417664 | bytes 26240512 | tf_op jit(solution)/shard_map/dot_general | solution.py:38
  331.4 10.1 %fusion.6 = f32[416,1536]{1,0:T(8,128)S(1)} fusion(bf16[416,4480]{1,0:T(8,128)(2,1)} %get-tuple-element.188, bf16[2,1536,4480]{2,1,0:T(8,128)(2,1)} %all-gather.5.cloned.1.call-done), kind=kOutput, calls=%fused_computation.14 | convolution fusion | flops 5725224960 | bytes 20045824 | tf_op jit(solution)/shard_map/dot_general | solution.py:42
  343.9 12.3 %fusion.26 = bf16[384,4480]{1,0:T(8,128)(2,1)S(1)} fusion(bf16[2,1536,4480]{2,1,0:T(8,128)(2,1)} %all-gather.5.cloned.1.call-done, f32[384,4480]{1,0:T(8,128)} %get-tuple-element.484, bf16[192,1536]{1,0:T(8,128)(2,1)S(1)} %collective-permute-done.22, bf16[192,1536]{1,0:T(8,128)(2,1)S(1)} %multiply_convert_fusion.7), kind=kOutput, calls=%fused_computation.36 | convolution fusion | flops 5323309056 | bytes 25264128 | tf_op jit(solution)/shard_map/dot_general | solution.py:38
  359.9 8.8 %fusion.1 = f32[384,1536]{1,0:T(8,128)S(1)} fusion(bf16[384,4480]{1,0:T(8,128)(2,1)S(1)} %fusion.26, bf16[2,1536,4480]{2,1,0:T(8,128)(2,1)} %all-gather.5.cloned.1.call-done), kind=kOutput, calls=%fused_computation.9 | convolution fusion | flops 5284823040 | bytes 19562496 | tf_op jit(solution)/shard_map/dot_general | solution.py:42
  368.7 5.3 collective-permute-done.24
  374.9 20.8 %convolution_convert_fusion.1 = bf16[1536,4480]{1,0:T(8,128)(2,1)} fusion(bf16[416,4480]{1,0:T(8,128)(2,1)} %get-tuple-element.188, bf16[384,4480]{1,0:T(8,128)(2,1)} %copy-done.195, bf16[208,1536]{1,0:T(8,128)(2,1)S(1)} %collective-permute-done.24, bf16[208,1536]{1,0:T(8,128)(2,1)S(1)} %multiply_convert_fusion.4, ...), kind=kOutput, calls=%fused_computation.1 | convolution fusion | flops 11041095680 | bytes 23388160 | tf_op jit(solution)/shard_map/dot_general | solution.py:46
  403.3 15.2 %fusion.25 = bf16[416,4480]{1,0:T(8,128)(2,1)S(1)} fusion(bf16[416,1536]{1,0:T(8,128)(2,1)S(1)} %copy-done.114, bf16[2,1536,4480]{2,1,0:T(8,128)(2,1)} %all-gather.5.cloned.1.call-done, f32[416,4480]{1,0:T(8,128)} %get-tuple-element.486), kind=kOutput, calls=%fused_computation.35 | convolution fusion | flops 5764362240 | bytes 26222592 | tf_op jit(solution)/shard_map/dot_general | solution.py:38
  419.7 9.9 %fusion = f32[416,1536]{1,0:T(8,128)S(1)} fusion(bf16[416,4480]{1,0:T(8,128)(2,1)S(1)} %fusion.25, bf16[2,1536,4480]{2,1,0:T(8,128)(2,1)} %all-gather.5.cloned.1.call-done), kind=kOutput, calls=%fused_computation.8 | convolution fusion | flops 5725224960 | bytes 20045824 | tf_op jit(solution)/shard_map/dot_general | solution.py:42
  433.8 20.3 %convolution_convert_fusion = bf16[1536,4480]{1,0:T(8,128)(2,1)} fusion(bf16[416,4480]{1,0:T(8,128)(2,1)S(1)} %fusion.25, bf16[384,4480]{1,0:T(8,128)(2,1)} %copy-done.99, bf16[208,1536]{1,0:T(8,128)(2,1)S(1)} %copy-done.192, bf16[208,1536]{1,0:T(8,128)(2,1)S(1)} %copy-done.121, bf16[192,1536]{1,0:T(8,128)(2,1)} %collective-permute-done.18, ...), kind=kOutput, calls=%fused_computation | convolution fusion | flops 11041095680 | bytes 23388160 | tf_op jit(solution)/shard_map/dot_general | solution.py:46
  460.9 8.3 %attend_bwd_cross.2 = (f32[384,768]{1,0:T(8,128)S(1)}, f32[512,768]{1,0:T(8,128)}, f32[512,768]{1,0:T(8,128)}, f32[384,1]{1,0:T(8,128)S(1)}, f32[1,768]{1,0:T(1,128)S(1)}) custom-call(bf16[384,768]{1,0:T(8,128)(2,1)S(1)} %copy-done.19, bf16[512,768]{1,0:T(8,128)(2,1)S(1)} %multiply_convert_fusion.2.refs_1_, bf16[512,768]{1,0:T(8,128)(2,1)S(1)} %copy-done.10, ...), custom_call_target="tpu_custom_call" | custom-call | flops 4529848320 | bytes 8257536 | tf_op jit(solution)/shard_map/attend_bwd_cross/pallas_call | solution.py:219
  480.6 9.6 %attend_bwd_cross.3 = (f32[416,768]{1,0:T(8,128)S(1)}, f32[512,768]{1,0:T(8,128)}, f32[512,768]{1,0:T(8,128)}, f32[416,1]{1,0:T(8,128)S(1)}, f32[1,768]{1,0:T(1,128)S(1)}) custom-call(bf16[416,768]{1,0:T(8,128)(2,1)S(1)} %copy-done.14, bf16[512,768]{1,0:T(8,128)(2,1)S(1)} %multiply_convert_fusion.2.refs_1_, bf16[512,768]{1,0:T(8,128)(2,1)S(1)} %copy-done.10, ...), custom_call_target="tpu_custom_call" | custom-call | flops 4907335680 | bytes 8552448 | tf_op jit(solution)/shard_map/attend_bwd_cross/pallas_call | solution.py:219
  498.5 5.9 collective-permute-done.31
  512.0 6.9 collective-permute-done.32
  524.5 12.9 %head_grads.3 = bf16[4,1536,768]{2,1,0:T(8,128)(2,1)} custom-call(bf16[208,1536]{1,0:T(8,128)(2,1)S(1)} %copy-done.37, bf16[416,768]{1,0:T(8,128)(2,1)S(1)} %get-tuple-element.374.refs_1_, bf16[208,1536]{1,0:T(8,128)(2,1)S(1)} %copy-done.53, bf16[192,1536]{1,0:T(8,128)(2,1)S(1)} %copy-done.43, bf16[384,768]{1,0:T(8,128)(2,1)S(1)} %get-tuple-element.376.refs_4_, ...), custom_call_target="tpu_custom_call" | custom-call | flops 6190792704 | bytes 19955712 | tf_op jit(solution)/shard_map/head_grads/pallas_call | solution.py:328
  541.5 4.8 fusion.103.refs_3_
  571.1 22.7 %attend_bwd_self.1 = (f32[800,768]{1,0:T(8,128)}, f32[800,768]{1,0:T(8,128)}, bf16[800,768]{1,0:T(8,128)(2,1)S(1)}, f32[800,1]{1,0:T(8,128)S(1)}, f32[800,1]{1,0...) custom-call(bf16[800,768]{1,0:T(8,128)(2,1)S(1)} %copy-done.31, bf16[800,768]{1,0:T(8,128)(2,1)} %copy-done.3, ...), custom_call_target="tpu_custom_call" | custom-call | flops 14745600000 | bytes 15974400 | tf_op jit(solution)/shard_map/attend_bwd_self/pallas_call | solution.py:198
  612.3 18.8 %self_back.1 = (bf16[3,1536,768]{2,1,0:T(8,128)(2,1)}, f32[400,1536]{1,0:T(8,128)}, bf16[400,1536]{1,0:T(8,128)(2,1)S(1)}) custom-call(bf16[208,1536]{1,0:T(8,128)(2,1)S(1)} %copy-done.39, bf16[208,1536]{1,0:T(8,128)(2,1)S(1)} %copy-done.49, bf16[192,1536]{1,0:T(8,128)(2,1)S(1)} %copy-done.41, bf16[192,1536]{1,0:T(8,128)(2,1)} %collective-permute-done.6.refs_3_, ...), custom_call_target="tpu_custom_call" | custom-call | flops 11324620800 | bytes 30000000 | tf_op jit(solution)/shard_map/self_back/pallas_call | solution.py:285
  632.1 136.8 %tail_sums.1 = (f32[8,96,768]{2,1,0:T(8,128)}, f32[400,1536]{1,0:T(8,128)}, f32[24,1536]{1,0:T(8,128)}) custom-call(bf16[3,8,2,96,768]{4,3,2,1,0:T(8,128)(2,1)} %bitcast.263, bf16[1,8,2,96,768]{4,3,2,1,0:T(8,128)(2,1)} %bitcast.255, bf16[4,8,2,96,768]{4,3,2,1,0:T(8,128)(2,1)} %bitcast.262, f32[208,1536]{1,0:T(8,128)} %get-tuple-element.383.refs_3_, ...), custom_call_target="tpu_custom_call" | custom-call | flops 1000000 | bytes 1000000 | tf_op jit(solution)/shard_map/tail_sums/pallas_call | solution.py:520
  (774 shorter events, 259.3 us)
Async XLA Ops:
  7.2 107.6 %all-gather.3.cloned.1.call-start = ((), (), s32[]{:S(2)}) async-start(), calls=%async_computation.2 | async-start | bytes 20054016 | tf_op jit(solution)/shard_map/all_gather | solution.py:677
  9.8 274.0 %all-gather.5.cloned.1.call-start = ((), (), s32[]{:S(2)}) async-start(), calls=%async_computation.3 | async-start | bytes 29245440 | tf_op jit(solution)/shard_map/all_gather | solution.py:677
  11.4 534.9 %reduce-scatter.3.cloned.1.call-start = ((), (), s32[]{:S(2)}) async-start(), calls=%async_computation.4 | async-start | bytes 14622720 | tf_op jit(solution)/shard_map/reduce_scatter | solution.py:831
  15.9 99.0 %collective-permute-start.14 = (bf16[256,1536]{1,0:T(8,128)(2,1)}, bf16[256,1536]{1,0:T(8,128)(2,1)}, u32[]{:S(2)}, u32[]{:S(2)}) collective-permute-start(bf16[256,1536]{1,0:T(8,128)(2,1)} %bitcast.42.refs_6_), channel_id=1, source_target_pairs={{0,1},{1,0},{2,3},{3,2},{4,5},{5,4},{6,7},{7,6},{8,9},{9,8},{10,11... | collective-permute-start | bytes 2359304 | tf_op jit(solution)/shard_map/ppermute | solution.py:571
  53.7 67.3 %collective-permute-start.5 = (bf16[208,1536]{1,0:T(8,128)(2,1)S(1)}, bf16[208,1536]{1,0:T(8,128)(2,1)S(1)}, u32[]{:S(2)}, u32[]{:S(2)}) collective-permute-start(bf16[208,1536]{1,0:T(8,128)(2,1)S(1)} %get-tuple-element.416.refs_0_), channel_id=1, source_target_pairs={{0,1},{1,0},{2,3},{3,2},{4,5},{5,4},{6,7},{7,6},{8,9},{9,8},{10,11... | collective-permute-start | bytes 1916936 | tf_op jit(solution)/shard_map/ppermute | solution.py:571
  56.8 73.3 %collective-permute-start.6 = (bf16[192,1536]{1,0:T(8,128)(2,1)S(1)}, bf16[192,1536]{1,0:T(8,128)(2,1)}, u32[]{:S(2)}, u32[]{:S(2)}) collective-permute-start(bf16[192,1536]{1,0:T(8,128)(2,1)S(1)} %get-tuple-element.414.refs_2_), channel_id=1, source_target_pairs={{0,1},{1,0},{2,3},{3,2},{4,5},{5,4},{6,7},{7,6},{8,9},{9,8},{10,11... | collective-permute-start | bytes 1769480 | tf_op jit(solution)/shard_map/ppermute | solution.py:571
  119.5 59.6 %collective-permute-start.15 = (f32[512,1]{0,1:T(1,128)S(1)}, f32[512,1]{0,1:T(1,128)S(1)}, u32[]{:S(2)}, u32[]{:S(2)}) collective-permute-start(f32[512,1]{0,1:T(1,128)S(1)} %pad_maximum_fusion.36), channel_id=1, source_target_pairs={{0,1},{1,0},{2,3},{3,2},{4,5},{5,4},{6,7},{7,6},{8,9},{9,8},{10,11... | collective-permute-start | bytes 6152 | tf_op jit(solution)/shard_map/ppermute | solution.py:571
  129.2 25.6 %collective-permute-start.7 = (f32[416,2]{0,1:T(2,128)S(1)}, f32[416,2]{0,1:T(2,128)S(1)}, u32[]{:S(2)}, u32[]{:S(2)}) collective-permute-start(f32[416,2]{0,1:T(2,128)S(1)} %pad_maximum_fusion.27), channel_id=1, source_target_pairs={{0,1},{1,0},{2,3},{3,2},{4,5},{5,4},{6,7},{7,6},{8,9},{9,8},{10,11... | collective-permute-start | bytes 9992 | tf_op jit(solution)/shard_map/ppermute | solution.py:571
  138.5 16.3 %collective-permute-start.8 = (f32[384,2]{0,1:T(2,128)S(1)}, f32[384,2]{0,1:T(2,128)S(1)}, u32[]{:S(2)}, u32[]{:S(2)}) collective-permute-start(f32[384,2]{0,1:T(2,128)S(1)} %pad_maximum_fusion.34), channel_id=1, source_target_pairs={{0,1},{1,0},{2,3},{3,2},{4,5},{5,4},{6,7},{7,6},{8,9},{9,8},{10,11... | collective-permute-start | bytes 9224 | tf_op jit(solution)/shard_map/ppermute | solution.py:571
  178.1 15.6 %collective-permute-start.9 = (bf16[192,1536]{1,0:T(8,128)(2,1)S(1)}, bf16[192,1536]{1,0:T(8,128)(2,1)S(1)}, u32[]{:S(2)}, u32[]{:S(2)}) collective-permute-start(bf16[192,1536]{1,0:T(8,128)(2,1)S(1)} %get-tuple-element.147), channel_id=1, source_target_pairs={{0,1},{1,0},{2,3},{3,2},{4,5},{5,4},{6,7},{7,6},{8,9},{9,8},{10,11... | collective-permute-start | bytes 1769480 | tf_op jit(solution)/shard_map/ppermute | solution.py:571
  189.8 17.5 %collective-permute-start.10 = (bf16[208,1536]{1,0:T(8,128)(2,1)S(1)}, bf16[208,1536]{1,0:T(8,128)(2,1)S(1)}, u32[]{:S(2)}, u32[]{:S(2)}) collective-permute-start(bf16[208,1536]{1,0:T(8,128)(2,1)S(1)} %get-tuple-element.150), channel_id=1, source_target_pairs={{0,1},{1,0},{2,3},{3,2},{4,5},{5,4},{6,7},{7,6},{8,9},{9,8},{10,11... | collective-permute-start | bytes 1916936 | tf_op jit(solution)/shard_map/ppermute | solution.py:571
  195.4 23.7 %collective-permute-start.12 = (bf16[192,1536]{1,0:T(8,128)(2,1)S(1)}, bf16[192,1536]{1,0:T(8,128)(2,1)S(1)}, u32[]{:S(2)}, u32[]{:S(2)}) collective-permute-start(bf16[192,1536]{1,0:T(8,128)(2,1)S(1)} %add_convert_fusion.6.refs_3_), channel_id=1, source_target_pairs={{0,1},{1,0},{2,3},{3,2},{4,5},{5,4},{6,7},{7,6},{8,9},{9,8},{10,11... | collective-permute-start | bytes 1769480 | tf_op jit(solution)/shard_map/ppermute | solution.py:571
  225.4 17.0 %collective-permute-start.11 = (bf16[208,1536]{1,0:T(8,128)(2,1)S(1)}, bf16[208,1536]{1,0:T(8,128)(2,1)S(1)}, u32[]{:S(2)}, u32[]{:S(2)}) collective-permute-start(bf16[208,1536]{1,0:T(8,128)(2,1)S(1)} %add_convert_fusion.3.refs_0_), channel_id=1, source_target_pairs={{0,1},{1,0},{2,3},{3,2},{4,5},{5,4},{6,7},{7,6},{8,9},{9,8},{10,11... | collective-permute-start | bytes 1916936 | tf_op jit(solution)/shard_map/ppermute | solution.py:571
  242.4 19.9 %collective-permute-start.16 = (bf16[192,1536]{1,0:T(8,128)(2,1)}, bf16[192,1536]{1,0:T(8,128)(2,1)}, u32[]{:S(2)}, u32[]{:S(2)}) collective-permute-start(bf16[192,1536]{1,0:T(8,128)(2,1)} %get-tuple-element.161), channel_id=1, source_target_pairs={{0,1},{1,0},{2,3},{3,2},{4,5},{5,4},{6,7},{7,6},{8,9},{9,8},{10,11... | collective-permute-start | bytes 1769480 | tf_op jit(solution)/shard_map/ppermute | solution.py:571
  246.6 14.5 %collective-permute-start.17 = (f32[416,1]{1,0:T(8,128)S(1)}, f32[416,1]{1,0:T(8,128)}, u32[]{:S(2)}, u32[]{:S(2)}) collective-permute-start(f32[416,1]{1,0:T(8,128)S(1)} %copy.138), channel_id=1, source_target_pairs={{0,1},{1,0},{2,3},{3,2},{4,5},{5,4},{6,7},{7,6},{8,9},{9,8},{10,11... | collective-permute-start | bytes 5000 | tf_op jit(solution)/shard_map/ppermute | solution.py:571
  266.9 15.9 %collective-permute-start.18 = (bf16[192,1536]{1,0:T(8,128)(2,1)}, bf16[192,1536]{1,0:T(8,128)(2,1)}, u32[]{:S(2)}, u32[]{:S(2)}) collective-permute-start(bf16[192,1536]{1,0:T(8,128)(2,1)} %add_convert_fusion.5), channel_id=1, source_target_pairs={{0,1},{1,0},{2,3},{3,2},{4,5},{5,4},{6,7},{7,6},{8,9},{9,8},{10,11... | collective-permute-start | bytes 1769480 | tf_op jit(solution)/shard_map/ppermute | solution.py:571
  282.8 13.9 %collective-permute-start.19 = (bf16[208,1536]{1,0:T(8,128)(2,1)}, bf16[208,1536]{1,0:T(8,128)(2,1)}, u32[]{:S(2)}, u32[]{:S(2)}) collective-permute-start(bf16[208,1536]{1,0:T(8,128)(2,1)} %get-tuple-element.173), channel_id=1, source_target_pairs={{0,1},{1,0},{2,3},{3,2},{4,5},{5,4},{6,7},{7,6},{8,9},{9,8},{10,11... | collective-permute-start | bytes 1916936 | tf_op jit(solution)/shard_map/ppermute | solution.py:571
  299.5 14.4 %collective-permute-start.20 = (bf16[208,1536]{1,0:T(8,128)(2,1)S(1)}, bf16[208,1536]{1,0:T(8,128)(2,1)S(1)}, u32[]{:S(2)}, u32[]{:S(2)}) collective-permute-start(bf16[208,1536]{1,0:T(8,128)(2,1)S(1)} %add_convert_fusion.2), channel_id=1, source_target_pairs={{0,1},{1,0},{2,3},{3,2},{4,5},{5,4},{6,7},{7,6},{8,9},{9,8},{10,11... | collective-permute-start | bytes 1916936 | tf_op jit(solution)/shard_map/ppermute | solution.py:571
  314.0 14.1 %collective-permute-start.21 = (bf16[192,1536]{1,0:T(8,128)(2,1)S(1)}, bf16[192,1536]{1,0:T(8,128)(2,1)S(1)}, u32[]{:S(2)}, u32[]{:S(2)}) collective-permute-start(bf16[192,1536]{1,0:T(8,128)(2,1)S(1)} %slice.987), channel_id=1, source_target_pairs={{0,1},{1,0},{2,3},{3,2},{4,5},{5,4},{6,7},{7,6},{8,9},{9,8},{10,11... | collective-permute-start | bytes 1769480 | tf_op jit(solution)/shard_map/ppermute | solution.py:571
  330.3 12.4 %collective-permute-start.22 = (bf16[192,1536]{1,0:T(8,128)(2,1)S(1)}, bf16[192,1536]{1,0:T(8,128)(2,1)S(1)}, u32[]{:S(2)}, u32[]{:S(2)}) collective-permute-start(bf16[192,1536]{1,0:T(8,128)(2,1)S(1)} %multiply_convert_fusion.7), channel_id=1, source_target_pairs={{0,1},{1,0},{2,3},{3,2},{4,5},{5,4},{6,7},{7,6},{8,9},{9,8},{10,11... | collective-permute-start | bytes 1769480 | tf_op jit(solution)/shard_map/ppermute | solution.py:571
  342.7 13.5 %collective-permute-start.23 = (bf16[208,1536]{1,0:T(8,128)(2,1)S(1)}, bf16[208,1536]{1,0:T(8,128)(2,1)S(1)}, u32[]{:S(2)}, u32[]{:S(2)}) collective-permute-start(bf16[208,1536]{1,0:T(8,128)(2,1)S(1)} %slice.984), channel_id=1, source_target_pairs={{0,1},{1,0},{2,3},{3,2},{4,5},{5,4},{6,7},{7,6},{8,9},{9,8},{10,11... | collective-permute-start | bytes 1916936 | tf_op jit(solution)/shard_map/ppermute | solution.py:571
  358.9 15.1 %collective-permute-start.24 = (bf16[208,1536]{1,0:T(8,128)(2,1)S(1)}, bf16[208,1536]{1,0:T(8,128)(2,1)S(1)}, u32[]{:S(2)}, u32[]{:S(2)}) collective-permute-start(bf16[208,1536]{1,0:T(8,128)(2,1)S(1)} %multiply_convert_fusion.4), channel_id=1, source_target_pairs={{0,1},{1,0},{2,3},{3,2},{4,5},{5,4},{6,7},{7,6},{8,9},{9,8},{10,11... | collective-permute-start | bytes 1916936 | tf_op jit(solution)/shard_map/ppermute | solution.py:571
  374.1 22.8 %collective-permute-start.25 = (bf16[192,1536]{1,0:T(8,128)(2,1)S(1)}, bf16[192,1536]{1,0:T(8,128)(2,1)}, u32[]{:S(2)}, u32[]{:S(2)}) collective-permute-start(bf16[192,1536]{1,0:T(8,128)(2,1)S(1)} %slice.986), channel_id=1, source_target_pairs={{0,1},{1,0},{2,3},{3,2},{4,5},{5,4},{6,7},{7,6},{8,9},{9,8},{10,11... | collective-permute-start | bytes 1769480 | tf_op jit(solution)/shard_map/ppermute | solution.py:571
  396.9 387.5 %reduce-scatter.5.cloned.1.call-start = ((), (), s32[]{:S(2)}) async-start(), calls=%async_computation.5 | async-start | bytes 14622720 | tf_op jit(solution)/shard_map/reduce_scatter | solution.py:831
  418.6 14.1 %collective-permute-start.26 = (bf16[192,1536]{1,0:T(8,128)(2,1)S(1)}, bf16[192,1536]{1,0:T(8,128)(2,1)S(1)}, u32[]{:S(2)}, u32[]{:S(2)}) collective-permute-start(bf16[192,1536]{1,0:T(8,128)(2,1)S(1)} %get-tuple-element.200.refs_13_), channel_id=1, source_target_pairs={{0,1},{1,0},{2,3},{3,2},{4,5},{5,4},{6,7},{7,6},{8,9},{9,8},{10,11... | collective-permute-start | bytes 1769480 | tf_op jit(solution)/shard_map/ppermute | solution.py:571
  432.7 21.3 %collective-permute-start.27 = (bf16[208,1536]{1,0:T(8,128)(2,1)S(1)}, bf16[208,1536]{1,0:T(8,128)(2,1)S(1)}, u32[]{:S(2)}, u32[]{:S(2)}) collective-permute-start(bf16[208,1536]{1,0:T(8,128)(2,1)S(1)} %slice.983), channel_id=1, source_target_pairs={{0,1},{1,0},{2,3},{3,2},{4,5},{5,4},{6,7},{7,6},{8,9},{9,8},{10,11... | collective-permute-start | bytes 1916936 | tf_op jit(solution)/shard_map/ppermute | solution.py:571
  457.0 13.0 %collective-permute-start.28 = (bf16[208,1536]{1,0:T(8,128)(2,1)S(1)}, bf16[208,1536]{1,0:T(8,128)(2,1)S(1)}, u32[]{:S(2)}, u32[]{:S(2)}) collective-permute-start(bf16[208,1536]{1,0:T(8,128)(2,1)S(1)} %get-tuple-element.206.refs_10_), channel_id=1, source_target_pairs={{0,1},{1,0},{2,3},{3,2},{4,5},{5,4},{6,7},{7,6},{8,9},{9,8},{10,11... | collective-permute-start | bytes 1916936 | tf_op jit(solution)/shard_map/ppermute | solution.py:571
  479.2 16.8 %collective-permute-start.30 = (bf16[192,1536]{1,0:T(8,128)(2,1)S(1)}, bf16[192,1536]{1,0:T(8,128)(2,1)S(1)}, u32[]{:S(2)}, u32[]{:S(2)}) collective-permute-start(bf16[192,1536]{1,0:T(8,128)(2,1)S(1)} %slice.985), channel_id=1, source_target_pairs={{0,1},{1,0},{2,3},{3,2},{4,5},{5,4},{6,7},{7,6},{8,9},{9,8},{10,11... | collective-permute-start | bytes 1769480 | tf_op jit(solution)/shard_map/ppermute | solution.py:571
  507.8 11.1 %collective-permute-start.32 = (bf16[208,1536]{1,0:T(8,128)(2,1)S(1)}, bf16[208,1536]{1,0:T(8,128)(2,1)S(1)}, u32[]{:S(2)}, u32[]{:S(2)}) collective-permute-start(bf16[208,1536]{1,0:T(8,128)(2,1)S(1)} %slice.982), channel_id=1, source_target_pairs={{0,1},{1,0},{2,3},{3,2},{4,5},{5,4},{6,7},{7,6},{8,9},{9,8},{10,11... | collective-permute-start | bytes 1916936 | tf_op jit(solution)/shard_map/ppermute | solution.py:571
  510.7 26.6 %collective-permute-start.34 = (bf16[192,1536]{1,0:T(8,128)(2,1)S(1)}, bf16[192,1536]{1,0:T(8,128)(2,1)S(1)}, u32[]{:S(2)}, u32[]{:S(2)}) collective-permute-start(bf16[192,1536]{1,0:T(8,128)(2,1)S(1)} %get-tuple-element.385.refs_3_), channel_id=1, source_target_pairs={{0,1},{1,0},{2,3},{3,2},{4,5},{5,4},{6,7},{7,6},{8,9},{9,8},{10,11... | collective-permute-start | bytes 1769480 | tf_op jit(solution)/shard_map/ppermute | solution.py:571
  521.3 16.0 %collective-permute-start.33 = (bf16[208,1536]{1,0:T(8,128)(2,1)S(1)}, bf16[208,1536]{1,0:T(8,128)(2,1)S(1)}, u32[]{:S(2)}, u32[]{:S(2)}) collective-permute-start(bf16[208,1536]{1,0:T(8,128)(2,1)S(1)} %get-tuple-element.382.refs_0_), channel_id=1, source_target_pairs={{0,1},{1,0},{2,3},{3,2},{4,5},{5,4},{6,7},{7,6},{8,9},{9,8},{10,11... | collective-permute-start | bytes 1916936 | tf_op jit(solution)/shard_map/ppermute | solution.py:571
  565.4 36.8 %collective-permute-start.38 = (bf16[256,1536]{1,0:T(8,128)(2,1)}, bf16[256,1536]{1,0:T(8,128)(2,1)}, u32[]{:S(2)}, u32[]{:S(2)}) collective-permute-start(bf16[256,1536]{1,0:T(8,128)(2,1)} %slice.981), channel_id=1, source_target_pairs={{0,1},{1,0},{2,3},{3,2},{4,5},{5,4},{6,7},{7,6},{8,9},{9,8},{10,11... | collective-permute-start | bytes 2359304 | tf_op jit(solution)/shard_map/ppermute | solution.py:571
  (208 other events, 2522.8 us)
Sparse Core Ops, SparseCore 0:
  10.1 104.6 all-gather.2
  116.9 139.6 all-gather.4
  397.0 142.7 reduce-scatter.2
  546.4 158.1 reduce-scatter.4

commit v5 on v4

--- a/solution.py
+++ b/solution.py
@@ -738,11 +738,6 @@
     cross_out_t = heads_w[7]
 
     text_rows, text_pieces = collect(text_states[0])
-    cross_kp = dot_nn(text_rows, cross_w[1]) + bias_rows[4]
-    cross_v = (dot_nn(text_rows, cross_w[2]) + bias_rows[5]).astype(BF)
-    cross_ks = row_totals(squares(cross_kp))
-    cross_kr = lax.rsqrt(cross_ks / D + EPS)
-    cross_k = (cross_kp * cross_kr * qg_full[1, 1]).astype(BF)
 
     res0, unit0, scale0, rows0 = [], [], [], []
     qp, kp, vv, qs, ks = [], [], [], [], []
@@ -789,11 +784,10 @@
 
     def cross_prepare(c, got=None):
         qc = dot_nn(jnp.concatenate(rows1[c], axis=0), heads_w[4]) + bias_rows[3]
-        total = row_totals(squares(qc))
         if got is not None:
             qc, got = tie(qc, got)
         cross_qp[c] = qc
-        cross_qs[c] = lax.rsqrt(total / D + EPS)
+        cross_qs[c] = lax.rsqrt(row_totals(squares(qc)) / D + EPS)
         cross_q[c] = (qc * cross_qs[c] * qg_full[1, 0]).astype(BF)
         return got
 
@@ -810,7 +804,14 @@
     own_g, got_g = self_rows(g)
     got_f, own_g = tie(got_f, own_g)
     cross_query(f, own_f, got_f)
+    rows1[f][0], text_rows = tie(rows1[f][0], text_rows)
     cross_query(g, own_g, got_g)
+    cross_kp = dot_nn(text_rows, cross_w[1]) + bias_rows[4]
+    cross_v = (dot_nn(text_rows, cross_w[2]) + bias_rows[5]).astype(BF)
+    rows1[f][1], cross_kp, cross_v = tie(rows1[f][1], cross_kp, cross_v)
+    cross_ks = row_totals(squares(cross_kp))
+    cross_kr = lax.rsqrt(cross_ks / D + EPS)
+    cross_k = (cross_kp * cross_kr * qg_full[1, 1]).astype(BF)
     cross_prepare(f)
     own_f, other_f = cross_attend(f)
     rows1[g][1], other_f = tie(rows1[g][1], other_f)

time: 799 us -> 804 us (level); the launches traced: 795 us -> 789 us
  waiting for transfers between devices: 144 us -> 131 us
  local copies, waits for them, and re-layouts: 56.7 us -> 67.8 us
    ppermute x35, waiting for transfers between devices: 74.4 us -> 63.1 us  [swap(): return lax.ppermute(values, 'mp', SWAP)]
    dot_general x17, matrix products: 99.6 us -> 90 us  [dot_nn(): lax.dot_general(a, b, (((1,), (0,)), ((), ())), preferred_element_type=F32)]
    unnamed x398 -> x436, local copies, waits for them, and re-layouts: 29 us -> 33.1 us
  transfers between devices with their start and end apart: 43 -> 43, of which waited for: 22 -> 19; matrix products, arithmetic and copies ran while one was open for 37% -> 38% of each run, Pallas kernels for 32% -> 32%
where the time goes in v5:
time: 804 us; the launch traced here: 789 us
  Pallas kernels  254 us (32%)
  matrix products  183 us (23%)
  waiting for transfers between devices  131 us (16%)
  other arithmetic  86.6 us (11%)
  local copies, waits for them, and re-layouts  67.8 us (8%)
  starting transfers between devices  45.6 us (6%)
  between operations  21 us (3%)
    pallas_call x1, Pallas kernels, tail(): pl.pallas_call(functools.partial(tail_kernel, ndp, counts, nc), in_specs=...  134 us
    dot_general x17, matrix products, dot_nn(): lax.dot_general(a, b, (((1,), (0,)), ((), ())), preferred_element_type=F32)  90 us
    ppermute x35, waiting for transfers between devices, swap(): return lax.ppermute(values, 'mp', SWAP)  63.1 us
    all_gather x2, waiting for transfers between devices, whole(): return lax.all_gather(shards, 'dp', axis=1, tiled=True)  56.2 us
    dot_general x8, matrix products, dot_nt(): lax.dot_general(a, b, (((1,), (1,)), ((), ())), preferred_element_type=F32)  52 us
    dot_general x2, matrix products, dot_tn(): lax.dot_general(a, b, (((0,), (0,)), ((), ())), preferred_element_type=F32)  40.9 us
    ppermute x35, starting transfers between devices, swap(): return lax.ppermute(values, 'mp', SWAP)  39.2 us
    pallas_call x4, Pallas kernels, attend(): pl.pallas_call(functools.partial(attend_kernel, mask is not None), grid=(...  38.7 us
  transfers between devices with their start and end apart: 43, of which 19 were waited for; matrix products, arithmetic and copies ran while one was open for 38% of the time, Pallas kernels for 32%

profile of v5, /device:TPU:0, one launch (start us, length us, event | category | flops | bytes accessed | tf_op | source)
XLA Modules:
  0.0 789.3 jit_solution(7043017684029888168)
XLA Ops:
  37.0 5.5 collective-permute-done.4
  58.6 56.2 %all-gather.3.cloned.1.call-done.refs_3_.refs_4_ = bf16[8,1536,768]{2,1,0:T(8,128)(2,1)} async-done(((bf16[8,96,768]{2,1,0:T(8,128)(2,1)}), bf16[8,1536,768]{2,1,0:T(8,128)(2,1)}) %all-gather.3.cloned.1.call-update) | async-done | bytes 18874384 | tf_op jit(solution)/shard_map/all_gather | solution.py:677
  138.6 6.8 rope_prep.1
  146.6 10.2 %attend_fwd.4 = (bf16[384,768]{1,0:T(8,128)(2,1)S(1)}, f32[6,1,384]{2,1,0:T(1,128)S(1)}, f32[192,1536]{1,0:T(8,128)S(1)}, bf16[192,1536]{1,0:T(8,128)(2,1)}) custom-call(bf16[384,768]{1,0:T(8,128)(2,1)S(1)} %slice.551.refs_0_, bf16[800,768]{1,0:T(8,128)(2,1)S(1)} %get-tuple-element.149.refs_1_, bf16[800,768]{1,0:T(8,128)(2,1)S(1)} %pad_maximum_fusion.6.refs_2_, ...), custom_call_target="tpu_custom_call" | custom-call | flops 2831155200 | bytes 3637248 | tf_op jit(solution)/shard_map/attend_fwd/pallas_call | solution.py:125
  163.3 10.2 %attend_fwd.5 = (bf16[416,768]{1,0:T(8,128)(2,1)S(1)}, f32[6,1,416]{2,1,0:T(1,128)S(1)}, f32[208,1536]{1,0:T(8,128)S(1)}, bf16[208,1536]{1,0:T(8,128)(2,1)S(1)}) custom-call(bf16[416,768]{1,0:T(8,128)(2,1)S(1)} %slice.553.refs_0_, bf16[800,768]{1,0:T(8,128)(2,1)S(1)} %get-tuple-element.149.refs_1_, bf16[800,768]{1,0:T(8,128)(2,1)S(1)} %pad_maximum_fusion.6.refs_2_, ...), custom_call_target="tpu_custom_call" | custom-call | flops 3067084800 | bytes 3735552 | tf_op jit(solution)/shard_map/attend_fwd/pallas_call | solution.py:125
  186.6 4.3 collective-permute-done.10
  194.2 9.3 %collective-permute-done.13.refs_5_ = bf16[192,1536]{1,0:T(8,128)(2,1)S(1)} collective-permute-done((bf16[192,1536]{1,0:T(8,128)(2,1)S(1)}, bf16[192,1536]{1,0:T(8,128)(2,1)S(1)}, u32[]{:S(2)}, u32[]{:S(2)}) %collective-permute-start.13) | collective-permute-done | bytes 589856 | tf_op jit(solution)/shard_map/ppermute | solution.py:571
  210.7 9.4 %collective-permute-done.14 = f32[384,1]{1,0:T(8,128)S(1)} collective-permute-done((f32[384,1]{1,0:T(8,128)S(1)}, f32[384,1]{1,0:T(8,128)S(1)}, u32[]{:S(2)}, u32[]{:S(2)}) %collective-permute-start.14) | collective-permute-done | bytes 1568 | tf_op jit(solution)/shard_map/ppermute | solution.py:571
  221.9 9.0 %attend_fwd.6 = (bf16[384,768]{1,0:T(8,128)(2,1)S(1)}, f32[6,1,384]{2,1,0:T(1,128)S(1)}, f32[192,1536]{1,0:T(8,128)S(1)}, bf16[192,1536]{1,0:T(8,128)(2,1)}) custom-call(bf16[384,768]{1,0:T(8,128)(2,1)S(1)} %multiply_convert_fusion.8.refs_0_, bf16[512,768]{1,0:T(8,128)(2,1)S(1)} %multiply_convert_fusion.2.refs_1_, bf16[512,768]{1,0:T(8,128)(2,1)S(1)} %copy-done.9, ...), custom_call_target="tpu_custom_call" | custom-call | flops 1811939328 | bytes 2752512 | tf_op jit(solution)/shard_map/attend_fwd/pallas_call | solution.py:125
  237.3 9.8 %collective-permute-done.16 = bf16[192,1536]{1,0:T(8,128)(2,1)} collective-permute-done((bf16[192,1536]{1,0:T(8,128)(2,1)}, bf16[192,1536]{1,0:T(8,128)(2,1)}, u32[]{:S(2)}, u32[]{:S(2)}) %collective-permute-start.16) | collective-permute-done | bytes 589856 | tf_op jit(solution)/shard_map/ppermute | solution.py:571
  260.7 9.4 %attend_fwd.7 = (bf16[416,768]{1,0:T(8,128)(2,1)S(1)}, f32[6,1,416]{2,1,0:T(1,128)S(1)}, f32[208,1536]{1,0:T(8,128)S(1)}, bf16[208,1536]{1,0:T(8,128)(2,1)}) custom-call(bf16[416,768]{1,0:T(8,128)(2,1)S(1)} %multiply_convert_fusion.5.refs_0_, bf16[512,768]{1,0:T(8,128)(2,1)S(1)} %multiply_convert_fusion.2.refs_1_, bf16[512,768]{1,0:T(8,128)(2,1)S(1)} %copy-done.10, ...), custom_call_target="tpu_custom_call" | custom-call | flops 1962934272 | bytes 2850816 | tf_op jit(solution)/shard_map/attend_fwd/pallas_call | solution.py:125
  273.3 12.0 %multiply_convert_fusion.1 = (bf16[384,4480]{1,0:T(8,128)(2,1)S(1)}, f32[384,4480]{1,0:T(8,128)}) fusion(f32[4480]{0:T(1024)} %reduce.26, bf16[2,1536,4480]{2,1,0:T(8,128)(2,1)} %all-gather.5.cloned.1.call-done, bf16[192,1536]{1,0:T(8,128)(2,1)} %collective-permute-done.18, bf16[192,1536]{1,0:T(8,128)(2,1)} %add_convert_fusion.5), kind=kOutput, calls=%fused_computation.45 | convolution fusion | flops 5304385536 | bytes 25284608 | tf_op jit(solution)/shard_map/dot_general | solution.py:38
  289.1 8.8 %fusion.7 = f32[384,1536]{1,0:T(8,128)S(1)} fusion(bf16[384,4480]{1,0:T(8,128)(2,1)S(1)} %get-tuple-element.190, bf16[2,1536,4480]{2,1,0:T(8,128)(2,1)} %all-gather.5.cloned.1.call-done), kind=kOutput, calls=%fused_computation.15 | convolution fusion | flops 5284823040 | bytes 19562496 | tf_op jit(solution)/shard_map/dot_general | solution.py:42
  297.9 4.7 collective-permute-done.20
  303.6 13.1 %multiply_convert_fusion = (bf16[416,4480]{1,0:T(8,128)(2,1)}, f32[416,4480]{1,0:T(8,128)}) fusion(f32[4480]{0:T(1024)S(1)} %copy-done.170, bf16[2,1536,4480]{2,1,0:T(8,128)(2,1)} %all-gather.5.cloned.1.call-done, bf16[208,1536]{1,0:T(8,128)(2,1)S(1)} %collective-permute-done.20, bf16[208,1536]{1,0:T(8,128)(2,1)S(1)} %add_convert_fusion.2), kind=kOutput, calls=%fused_computation.26 | convolution fusion | flops 5746417664 | bytes 26240512 | tf_op jit(solution)/shard_map/dot_general | solution.py:38
  320.2 10.1 %fusion.6 = f32[416,1536]{1,0:T(8,128)S(1)} fusion(bf16[416,4480]{1,0:T(8,128)(2,1)} %get-tuple-element.198, bf16[2,1536,4480]{2,1,0:T(8,128)(2,1)} %all-gather.5.cloned.1.call-done), kind=kOutput, calls=%fused_computation.14 | convolution fusion | flops 5725224960 | bytes 20045824 | tf_op jit(solution)/shard_map/dot_general | solution.py:42
  332.9 12.4 %fusion.26 = bf16[384,4480]{1,0:T(8,128)(2,1)S(1)} fusion(bf16[2,1536,4480]{2,1,0:T(8,128)(2,1)} %all-gather.5.cloned.1.call-done, f32[384,4480]{1,0:T(8,128)} %get-tuple-element.490, bf16[192,1536]{1,0:T(8,128)(2,1)S(1)} %collective-permute-done.22, bf16[192,1536]{1,0:T(8,128)(2,1)S(1)} %multiply_convert_fusion.7), kind=kOutput, calls=%fused_computation.36 | convolution fusion | flops 5323309056 | bytes 25264128 | tf_op jit(solution)/shard_map/dot_general | solution.py:38
  349.0 8.8 %fusion.1 = f32[384,1536]{1,0:T(8,128)S(1)} fusion(bf16[384,4480]{1,0:T(8,128)(2,1)S(1)} %fusion.26, bf16[2,1536,4480]{2,1,0:T(8,128)(2,1)} %all-gather.5.cloned.1.call-done), kind=kOutput, calls=%fused_computation.9 | convolution fusion | flops 5284823040 | bytes 19562496 | tf_op jit(solution)/shard_map/dot_general | solution.py:42
  357.9 5.7 collective-permute-done.24
  364.4 20.8 %convolution_convert_fusion.1 = bf16[1536,4480]{1,0:T(8,128)(2,1)} fusion(bf16[416,4480]{1,0:T(8,128)(2,1)} %get-tuple-element.198, bf16[384,4480]{1,0:T(8,128)(2,1)} %copy-done.214, bf16[208,1536]{1,0:T(8,128)(2,1)S(1)} %collective-permute-done.24, bf16[208,1536]{1,0:T(8,128)(2,1)S(1)} %multiply_convert_fusion.4, ...), kind=kOutput, calls=%fused_computation.1 | convolution fusion | flops 11041095680 | bytes 23388160 | tf_op jit(solution)/shard_map/dot_general | solution.py:46
  392.3 16.0 %fusion.25 = bf16[416,4480]{1,0:T(8,128)(2,1)} fusion(bf16[416,1536]{1,0:T(8,128)(2,1)S(1)} %copy-done.115, bf16[2,1536,4480]{2,1,0:T(8,128)(2,1)} %all-gather.5.cloned.1.call-done, f32[416,4480]{1,0:T(8,128)} %get-tuple-element.492), kind=kOutput, calls=%fused_computation.35 | convolution fusion | flops 5764362240 | bytes 26222592 | tf_op jit(solution)/shard_map/dot_general | solution.py:38
  409.6 10.9 %fusion = f32[416,1536]{1,0:T(8,128)S(1)} fusion(bf16[416,4480]{1,0:T(8,128)(2,1)} %fusion.25, bf16[2,1536,4480]{2,1,0:T(8,128)(2,1)} %all-gather.5.cloned.1.call-done), kind=kOutput, calls=%fused_computation.8 | convolution fusion | flops 5725224960 | bytes 20045824 | tf_op jit(solution)/shard_map/dot_general | solution.py:42
  425.0 20.2 %convolution_convert_fusion = bf16[1536,4480]{1,0:T(8,128)(2,1)} fusion(bf16[416,4480]{1,0:T(8,128)(2,1)} %fusion.25, bf16[384,4480]{1,0:T(8,128)(2,1)S(1)} %copy-done.102, bf16[208,1536]{1,0:T(8,128)(2,1)S(1)} %copy-done.211, bf16[208,1536]{1,0:T(8,128)(2,1)S(1)} %copy-done.120, bf16[192,1536]{1,0:T(8,128)(2,1)} %collective-permute-done.18, ...), kind=kOutput, calls=%fused_computation | convolution fusion | flops 11041095680 | bytes 23388160 | tf_op jit(solution)/shard_map/dot_general | solution.py:46
  452.0 8.3 %attend_bwd_cross.2 = (f32[384,768]{1,0:T(8,128)S(1)}, f32[512,768]{1,0:T(8,128)}, f32[512,768]{1,0:T(8,128)}, f32[384,1]{1,0:T(8,128)S(1)}, f32[1,768]{1,0:T(1,128)S(1)}) custom-call(bf16[384,768]{1,0:T(8,128)(2,1)S(1)} %copy-done.18, bf16[512,768]{1,0:T(8,128)(2,1)S(1)} %multiply_convert_fusion.2.refs_1_, bf16[512,768]{1,0:T(8,128)(2,1)S(1)} %copy-done.11, ...), custom_call_target="tpu_custom_call" | custom-call | flops 4529848320 | bytes 8257536 | tf_op jit(solution)/shard_map/attend_bwd_cross/pallas_call | solution.py:219
  473.0 9.6 %attend_bwd_cross.3 = (f32[416,768]{1,0:T(8,128)S(1)}, f32[512,768]{1,0:T(8,128)}, f32[512,768]{1,0:T(8,128)}, f32[416,1]{1,0:T(8,128)S(1)}, f32[1,768]{1,0:T(1,128)S(1)}) custom-call(bf16[416,768]{1,0:T(8,128)(2,1)S(1)} %copy-done.13, bf16[512,768]{1,0:T(8,128)(2,1)S(1)} %multiply_convert_fusion.2.refs_1_, bf16[512,768]{1,0:T(8,128)(2,1)S(1)} %copy-done.11, ...), custom_call_target="tpu_custom_call" | custom-call | flops 4907335680 | bytes 8552448 | tf_op jit(solution)/shard_map/attend_bwd_cross/pallas_call | solution.py:219
  492.4 4.6 collective-permute-done.31
  505.8 5.7 collective-permute-done.32
  516.9 13.2 %head_grads.3 = bf16[4,1536,768]{2,1,0:T(8,128)(2,1)} custom-call(bf16[208,1536]{1,0:T(8,128)(2,1)S(1)} %copy-done.35, bf16[416,768]{1,0:T(8,128)(2,1)S(1)} %get-tuple-element.384.refs_1_, bf16[208,1536]{1,0:T(8,128)(2,1)} %collective-permute-done.11.refs_2_, bf16[192,1536]{1,0:T(8,128)(2,1)S(1)} %copy-done.41, ...), custom_call_target="tpu_custom_call" | custom-call | flops 6190792704 | bytes 19955712 | tf_op jit(solution)/shard_map/head_grads/pallas_call | solution.py:328
  534.2 4.8 fusion.103.refs_3_
  567.5 22.4 %attend_bwd_self.1 = (f32[800,768]{1,0:T(8,128)}, f32[800,768]{1,0:T(8,128)}, bf16[800,768]{1,0:T(8,128)(2,1)S(1)}, f32[800,1]{1,0:T(8,128)S(1)}, f32[800,1]{1,0...) custom-call(bf16[800,768]{1,0:T(8,128)(2,1)S(1)} %copy-done.30, bf16[800,768]{1,0:T(8,128)(2,1)} %copy-done.3, ...), custom_call_target="tpu_custom_call" | custom-call | flops 14745600000 | bytes 15974400 | tf_op jit(solution)/shard_map/attend_bwd_self/pallas_call | solution.py:198
  609.9 18.6 %self_back.1 = (bf16[3,1536,768]{2,1,0:T(8,128)(2,1)}, f32[400,1536]{1,0:T(8,128)}, bf16[400,1536]{1,0:T(8,128)(2,1)S(1)}) custom-call(bf16[208,1536]{1,0:T(8,128)(2,1)S(1)} %copy-done.37, bf16[208,1536]{1,0:T(8,128)(2,1)S(1)} %copy-done.47, bf16[192,1536]{1,0:T(8,128)(2,1)S(1)} %copy-done.39, bf16[192,1536]{1,0:T(8,128)(2,1)S(1)} %copy-done.52, ...), custom_call_target="tpu_custom_call" | custom-call | flops 11324620800 | bytes 30000000 | tf_op jit(solution)/shard_map/self_back/pallas_call | solution.py:285
  629.6 133.7 %tail_sums.1 = (f32[8,96,768]{2,1,0:T(8,128)}, f32[400,1536]{1,0:T(8,128)}, f32[24,1536]{1,0:T(8,128)}) custom-call(bf16[3,8,2,96,768]{4,3,2,1,0:T(8,128)(2,1)} %bitcast.261, bf16[1,8,2,96,768]{4,3,2,1,0:T(8,128)(2,1)} %bitcast.253, bf16[4,8,2,96,768]{4,3,2,1,0:T(8,128)(2,1)} %bitcast.260, f32[208,1536]{1,0:T(8,128)} %get-tuple-element.393.refs_3_, ...), custom_call_target="tpu_custom_call" | custom-call | flops 1000000 | bytes 1000000 | tf_op jit(solution)/shard_map/tail_sums/pallas_call | solution.py:520
  (814 shorter events, 264.0 us)
Async XLA Ops:
  7.2 107.6 %all-gather.3.cloned.1.call-start = ((), (), s32[]{:S(2)}) async-start(), calls=%async_computation.2 | async-start | bytes 20054016 | tf_op jit(solution)/shard_map/all_gather | solution.py:677
  9.8 263.5 %all-gather.5.cloned.1.call-start = ((), (), s32[]{:S(2)}) async-start(), calls=%async_computation.3 | async-start | bytes 29245440 | tf_op jit(solution)/shard_map/all_gather | solution.py:677
  11.4 527.6 %reduce-scatter.3.cloned.1.call-start = ((), (), s32[]{:S(2)}) async-start(), calls=%async_computation.4 | async-start | bytes 14622720 | tf_op jit(solution)/shard_map/reduce_scatter | solution.py:832
  12.9 9.5 %collective-permute-start = (f32[1,1408]{1,0:T(1,128)S(1)}, f32[1,1408]{1,0:T(1,128)S(1)}, u32[]{:S(2)}, u32[]{:S(2)}) collective-permute-start(f32[1,1408]{1,0:T(1,128)S(1)} %broadcast_in_dim.93), channel_id=1, source_target_pairs={{0,1},{1,0},{2,3},{3,2},{4,5},{5,4},{6,7},{7,6},{8,9},{9,8},{10,11... | collective-permute-start | bytes 16904 | tf_op jit(solution)/shard_map/ppermute | solution.py:571
  15.9 143.4 %collective-permute-start.12 = (bf16[256,1536]{1,0:T(8,128)(2,1)}, bf16[256,1536]{1,0:T(8,128)(2,1)}, u32[]{:S(2)}, u32[]{:S(2)}) collective-permute-start(bf16[256,1536]{1,0:T(8,128)(2,1)} %bitcast.39.refs_6_), channel_id=1, source_target_pairs={{0,1},{1,0},{2,3},{3,2},{4,5},{5,4},{6,7},{7,6},{8,9},{9,8},{10,11... | collective-permute-start | bytes 2359304 | tf_op jit(solution)/shard_map/ppermute | solution.py:571
  49.4 65.5 %collective-permute-start.5 = (bf16[208,1536]{1,0:T(8,128)(2,1)S(1)}, bf16[208,1536]{1,0:T(8,128)(2,1)S(1)}, u32[]{:S(2)}, u32[]{:S(2)}) collective-permute-start(bf16[208,1536]{1,0:T(8,128)(2,1)S(1)} %get-tuple-element.426.refs_0_), channel_id=1, source_target_pairs={{0,1},{1,0},{2,3},{3,2},{4,5},{5,4},{6,7},{7,6},{8,9},{9,8},{10,11... | collective-permute-start | bytes 1916936 | tf_op jit(solution)/shard_map/ppermute | solution.py:571
  57.1 66.7 %collective-permute-start.6 = (bf16[192,1536]{1,0:T(8,128)(2,1)S(1)}, bf16[192,1536]{1,0:T(8,128)(2,1)S(1)}, u32[]{:S(2)}, u32[]{:S(2)}) collective-permute-start(bf16[192,1536]{1,0:T(8,128)(2,1)S(1)} %get-tuple-element.424.refs_2_), channel_id=1, source_target_pairs={{0,1},{1,0},{2,3},{3,2},{4,5},{5,4},{6,7},{7,6},{8,9},{9,8},{10,11... | collective-permute-start | bytes 1769480 | tf_op jit(solution)/shard_map/ppermute | solution.py:571
  122.4 10.9 %collective-permute-start.7 = (f32[416,2]{0,1:T(2,128)S(1)}, f32[416,2]{0,1:T(2,128)S(1)}, u32[]{:S(2)}, u32[]{:S(2)}) collective-permute-start(f32[416,2]{0,1:T(2,128)S(1)} %pad_maximum_fusion.25), channel_id=1, source_target_pairs={{0,1},{1,0},{2,3},{3,2},{4,5},{5,4},{6,7},{7,6},{8,9},{9,8},{10,11... | collective-permute-start | bytes 9992 | tf_op jit(solution)/shard_map/ppermute | solution.py:571
  158.6 16.4 %collective-permute-start.9 = (bf16[192,1536]{1,0:T(8,128)(2,1)}, bf16[192,1536]{1,0:T(8,128)(2,1)}, u32[]{:S(2)}, u32[]{:S(2)}) collective-permute-start(bf16[192,1536]{1,0:T(8,128)(2,1)} %get-tuple-element.152), channel_id=1, source_target_pairs={{0,1},{1,0},{2,3},{3,2},{4,5},{5,4},{6,7},{7,6},{8,9},{9,8},{10,11... | collective-permute-start | bytes 1769480 | tf_op jit(solution)/shard_map/ppermute | solution.py:571
  173.5 17.4 %collective-permute-start.10 = (bf16[208,1536]{1,0:T(8,128)(2,1)S(1)}, bf16[208,1536]{1,0:T(8,128)(2,1)S(1)}, u32[]{:S(2)}, u32[]{:S(2)}) collective-permute-start(bf16[208,1536]{1,0:T(8,128)(2,1)S(1)} %get-tuple-element.155), channel_id=1, source_target_pairs={{0,1},{1,0},{2,3},{3,2},{4,5},{5,4},{6,7},{7,6},{8,9},{9,8},{10,11... | collective-permute-start | bytes 1916936 | tf_op jit(solution)/shard_map/ppermute | solution.py:571
  177.4 26.1 %collective-permute-start.13 = (bf16[192,1536]{1,0:T(8,128)(2,1)S(1)}, bf16[192,1536]{1,0:T(8,128)(2,1)S(1)}, u32[]{:S(2)}, u32[]{:S(2)}) collective-permute-start(bf16[192,1536]{1,0:T(8,128)(2,1)S(1)} %add_convert_fusion.6.refs_3_), channel_id=1, source_target_pairs={{0,1},{1,0},{2,3},{3,2},{4,5},{5,4},{6,7},{7,6},{8,9},{9,8},{10,11... | collective-permute-start | bytes 1769480 | tf_op jit(solution)/shard_map/ppermute | solution.py:571
  192.8 39.9 %collective-permute-start.11 = (bf16[208,1536]{1,0:T(8,128)(2,1)S(1)}, bf16[208,1536]{1,0:T(8,128)(2,1)}, u32[]{:S(2)}, u32[]{:S(2)}) collective-permute-start(bf16[208,1536]{1,0:T(8,128)(2,1)S(1)} %add_convert_fusion.3.refs_0_), channel_id=1, source_target_pairs={{0,1},{1,0},{2,3},{3,2},{4,5},{5,4},{6,7},{7,6},{8,9},{9,8},{10,11... | collective-permute-start | bytes 1916936 | tf_op jit(solution)/shard_map/ppermute | solution.py:571
  206.9 13.2 %collective-permute-start.14 = (f32[384,1]{1,0:T(8,128)S(1)}, f32[384,1]{1,0:T(8,128)S(1)}, u32[]{:S(2)}, u32[]{:S(2)}) collective-permute-start(f32[384,1]{1,0:T(8,128)S(1)} %copy.136), channel_id=1, source_target_pairs={{0,1},{1,0},{2,3},{3,2},{4,5},{5,4},{6,7},{7,6},{8,9},{9,8},{10,11... | collective-permute-start | bytes 4616 | tf_op jit(solution)/shard_map/ppermute | solution.py:571
  210.0 10.6 %collective-permute-start.15 = (f32[512,1]{0,1:T(1,128)S(1)}, f32[512,1]{0,1:T(1,128)S(1)}, u32[]{:S(2)}, u32[]{:S(2)}) collective-permute-start(f32[512,1]{0,1:T(1,128)S(1)} %pad_maximum_fusion.34), channel_id=1, source_target_pairs={{0,1},{1,0},{2,3},{3,2},{4,5},{5,4},{6,7},{7,6},{8,9},{9,8},{10,11... | collective-permute-start | bytes 6152 | tf_op jit(solution)/shard_map/ppermute | solution.py:571
  232.8 14.4 %collective-permute-start.16 = (bf16[192,1536]{1,0:T(8,128)(2,1)}, bf16[192,1536]{1,0:T(8,128)(2,1)}, u32[]{:S(2)}, u32[]{:S(2)}) collective-permute-start(bf16[192,1536]{1,0:T(8,128)(2,1)} %get-tuple-element.171), channel_id=1, source_target_pairs={{0,1},{1,0},{2,3},{3,2},{4,5},{5,4},{6,7},{7,6},{8,9},{9,8},{10,11... | collective-permute-start | bytes 1769480 | tf_op jit(solution)/shard_map/ppermute | solution.py:571
  254.3 18.3 %collective-permute-start.18 = (bf16[192,1536]{1,0:T(8,128)(2,1)}, bf16[192,1536]{1,0:T(8,128)(2,1)}, u32[]{:S(2)}, u32[]{:S(2)}) collective-permute-start(bf16[192,1536]{1,0:T(8,128)(2,1)} %add_convert_fusion.5), channel_id=1, source_target_pairs={{0,1},{1,0},{2,3},{3,2},{4,5},{5,4},{6,7},{7,6},{8,9},{9,8},{10,11... | collective-permute-start | bytes 1769480 | tf_op jit(solution)/shard_map/ppermute | solution.py:571
  272.6 13.3 %collective-permute-start.19 = (bf16[208,1536]{1,0:T(8,128)(2,1)}, bf16[208,1536]{1,0:T(8,128)(2,1)S(1)}, u32[]{:S(2)}, u32[]{:S(2)}) collective-permute-start(bf16[208,1536]{1,0:T(8,128)(2,1)} %get-tuple-element.183), channel_id=1, source_target_pairs={{0,1},{1,0},{2,3},{3,2},{4,5},{5,4},{6,7},{7,6},{8,9},{9,8},{10,11... | collective-permute-start | bytes 1916936 | tf_op jit(solution)/shard_map/ppermute | solution.py:571
  288.3 14.3 %collective-permute-start.20 = (bf16[208,1536]{1,0:T(8,128)(2,1)S(1)}, bf16[208,1536]{1,0:T(8,128)(2,1)S(1)}, u32[]{:S(2)}, u32[]{:S(2)}) collective-permute-start(bf16[208,1536]{1,0:T(8,128)(2,1)S(1)} %add_convert_fusion.2), channel_id=1, source_target_pairs={{0,1},{1,0},{2,3},{3,2},{4,5},{5,4},{6,7},{7,6},{8,9},{9,8},{10,11... | collective-permute-start | bytes 1916936 | tf_op jit(solution)/shard_map/ppermute | solution.py:571
  302.7 14.0 %collective-permute-start.21 = (bf16[192,1536]{1,0:T(8,128)(2,1)S(1)}, bf16[192,1536]{1,0:T(8,128)(2,1)S(1)}, u32[]{:S(2)}, u32[]{:S(2)}) collective-permute-start(bf16[192,1536]{1,0:T(8,128)(2,1)S(1)} %slice.987), channel_id=1, source_target_pairs={{0,1},{1,0},{2,3},{3,2},{4,5},{5,4},{6,7},{7,6},{8,9},{9,8},{10,11... | collective-permute-start | bytes 1769480 | tf_op jit(solution)/shard_map/ppermute | solution.py:571
  319.0 12.7 %collective-permute-start.22 = (bf16[192,1536]{1,0:T(8,128)(2,1)S(1)}, bf16[192,1536]{1,0:T(8,128)(2,1)S(1)}, u32[]{:S(2)}, u32[]{:S(2)}) collective-permute-start(bf16[192,1536]{1,0:T(8,128)(2,1)S(1)} %multiply_convert_fusion.7), channel_id=1, source_target_pairs={{0,1},{1,0},{2,3},{3,2},{4,5},{5,4},{6,7},{7,6},{8,9},{9,8},{10,11... | collective-permute-start | bytes 1769480 | tf_op jit(solution)/shard_map/ppermute | solution.py:571
  331.7 13.6 %collective-permute-start.23 = (bf16[208,1536]{1,0:T(8,128)(2,1)S(1)}, bf16[208,1536]{1,0:T(8,128)(2,1)S(1)}, u32[]{:S(2)}, u32[]{:S(2)}) collective-permute-start(bf16[208,1536]{1,0:T(8,128)(2,1)S(1)} %slice.984), channel_id=1, source_target_pairs={{0,1},{1,0},{2,3},{3,2},{4,5},{5,4},{6,7},{7,6},{8,9},{9,8},{10,11... | collective-permute-start | bytes 1916936 | tf_op jit(solution)/shard_map/ppermute | solution.py:571
  348.0 15.6 %collective-permute-start.24 = (bf16[208,1536]{1,0:T(8,128)(2,1)S(1)}, bf16[208,1536]{1,0:T(8,128)(2,1)S(1)}, u32[]{:S(2)}, u32[]{:S(2)}) collective-permute-start(bf16[208,1536]{1,0:T(8,128)(2,1)S(1)} %multiply_convert_fusion.4), channel_id=1, source_target_pairs={{0,1},{1,0},{2,3},{3,2},{4,5},{5,4},{6,7},{7,6},{8,9},{9,8},{10,11... | collective-permute-start | bytes 1916936 | tf_op jit(solution)/shard_map/ppermute | solution.py:571
  363.6 22.7 %collective-permute-start.25 = (bf16[192,1536]{1,0:T(8,128)(2,1)S(1)}, bf16[192,1536]{1,0:T(8,128)(2,1)}, u32[]{:S(2)}, u32[]{:S(2)}) collective-permute-start(bf16[192,1536]{1,0:T(8,128)(2,1)S(1)} %slice.986), channel_id=1, source_target_pairs={{0,1},{1,0},{2,3},{3,2},{4,5},{5,4},{6,7},{7,6},{8,9},{9,8},{10,11... | collective-permute-start | bytes 1769480 | tf_op jit(solution)/shard_map/ppermute | solution.py:571
  386.4 392.4 %reduce-scatter.5.cloned.1.call-start = ((), (), s32[]{:S(2)}) async-start(), calls=%async_computation.5 | async-start | bytes 14622720 | tf_op jit(solution)/shard_map/reduce_scatter | solution.py:832
  408.3 15.2 %collective-permute-start.26 = (bf16[192,1536]{1,0:T(8,128)(2,1)S(1)}, bf16[192,1536]{1,0:T(8,128)(2,1)S(1)}, u32[]{:S(2)}, u32[]{:S(2)}) collective-permute-start(bf16[192,1536]{1,0:T(8,128)(2,1)S(1)} %get-tuple-element.210.refs_13_), channel_id=1, source_target_pairs={{0,1},{1,0},{2,3},{3,2},{4,5},{5,4},{6,7},{7,6},{8,9},{9,8},{10,11... | collective-permute-start | bytes 1769480 | tf_op jit(solution)/shard_map/ppermute | solution.py:571
  423.6 21.6 %collective-permute-start.27 = (bf16[208,1536]{1,0:T(8,128)(2,1)S(1)}, bf16[208,1536]{1,0:T(8,128)(2,1)S(1)}, u32[]{:S(2)}, u32[]{:S(2)}) collective-permute-start(bf16[208,1536]{1,0:T(8,128)(2,1)S(1)} %slice.983), channel_id=1, source_target_pairs={{0,1},{1,0},{2,3},{3,2},{4,5},{5,4},{6,7},{7,6},{8,9},{9,8},{10,11... | collective-permute-start | bytes 1916936 | tf_op jit(solution)/shard_map/ppermute | solution.py:571
  448.4 11.9 %collective-permute-start.28 = (bf16[208,1536]{1,0:T(8,128)(2,1)S(1)}, bf16[208,1536]{1,0:T(8,128)(2,1)S(1)}, u32[]{:S(2)}, u32[]{:S(2)}) collective-permute-start(bf16[208,1536]{1,0:T(8,128)(2,1)S(1)} %get-tuple-element.216.refs_10_), channel_id=1, source_target_pairs={{0,1},{1,0},{2,3},{3,2},{4,5},{5,4},{6,7},{7,6},{8,9},{9,8},{10,11... | collective-permute-start | bytes 1916936 | tf_op jit(solution)/shard_map/ppermute | solution.py:571
  472.2 16.5 %collective-permute-start.30 = (bf16[192,1536]{1,0:T(8,128)(2,1)}, bf16[192,1536]{1,0:T(8,128)(2,1)}, u32[]{:S(2)}, u32[]{:S(2)}) collective-permute-start(bf16[192,1536]{1,0:T(8,128)(2,1)} %slice.985), channel_id=1, source_target_pairs={{0,1},{1,0},{2,3},{3,2},{4,5},{5,4},{6,7},{7,6},{8,9},{9,8},{10,11... | collective-permute-start | bytes 1769480 | tf_op jit(solution)/shard_map/ppermute | solution.py:571
  500.8 10.6 %collective-permute-start.32 = (bf16[208,1536]{1,0:T(8,128)(2,1)S(1)}, bf16[208,1536]{1,0:T(8,128)(2,1)S(1)}, u32[]{:S(2)}, u32[]{:S(2)}) collective-permute-start(bf16[208,1536]{1,0:T(8,128)(2,1)S(1)} %slice.982), channel_id=1, source_target_pairs={{0,1},{1,0},{2,3},{3,2},{4,5},{5,4},{6,7},{7,6},{8,9},{9,8},{10,11... | collective-permute-start | bytes 1916936 | tf_op jit(solution)/shard_map/ppermute | solution.py:571
  504.9 25.1 %collective-permute-start.34 = (bf16[192,1536]{1,0:T(8,128)(2,1)S(1)}, bf16[192,1536]{1,0:T(8,128)(2,1)S(1)}, u32[]{:S(2)}, u32[]{:S(2)}) collective-permute-start(bf16[192,1536]{1,0:T(8,128)(2,1)S(1)} %get-tuple-element.395.refs_3_), channel_id=1, source_target_pairs={{0,1},{1,0},{2,3},{3,2},{4,5},{5,4},{6,7},{7,6},{8,9},{9,8},{10,11... | collective-permute-start | bytes 1769480 | tf_op jit(solution)/shard_map/ppermute | solution.py:571
  513.9 16.2 %collective-permute-start.33 = (bf16[208,1536]{1,0:T(8,128)(2,1)S(1)}, bf16[208,1536]{1,0:T(8,128)(2,1)S(1)}, u32[]{:S(2)}, u32[]{:S(2)}) collective-permute-start(bf16[208,1536]{1,0:T(8,128)(2,1)S(1)} %get-tuple-element.392.refs_0_), channel_id=1, source_target_pairs={{0,1},{1,0},{2,3},{3,2},{4,5},{5,4},{6,7},{7,6},{8,9},{9,8},{10,11... | collective-permute-start | bytes 1916936 | tf_op jit(solution)/shard_map/ppermute | solution.py:571
  560.3 38.3 %collective-permute-start.38 = (bf16[256,1536]{1,0:T(8,128)(2,1)}, bf16[256,1536]{1,0:T(8,128)(2,1)}, u32[]{:S(2)}, u32[]{:S(2)}) collective-permute-start(bf16[256,1536]{1,0:T(8,128)(2,1)} %slice.981), channel_id=1, source_target_pairs={{0,1},{1,0},{2,3},{3,2},{4,5},{5,4},{6,7},{7,6},{8,9},{9,8},{10,11... | collective-permute-start | bytes 2359304 | tf_op jit(solution)/shard_map/ppermute | solution.py:571
  (226 other events, 2350.0 us)
Sparse Core Ops, SparseCore 0:
  10.1 104.6 all-gather.2
  116.9 139.6 all-gather.4
  386.5 143.5 reduce-scatter.2
  539.1 156.1 reduce-scatter.4

commit v6 on v5

--- a/solution.py
+++ b/solution.py
@@ -439,21 +439,26 @@
         block = 80 if rows % 80 == 0 else 16
         gain = ones[...]
 
-        def body(i, sums):
-            at = pl.ds(pl.multiple_of(i * block, block), block)
+        def piece(at, sums):
             back = pbuf[at, :] + ybuf[at, :].astype(F32)
             z = ubuf[at, :]
             grad = back * gain
             mean_g = jnp.mean(grad, axis=1, keepdims=True)
             mean_gz = jnp.mean(grad * z, axis=1, keepdims=True)
-            hgrad[at, :] = stbuf[at, :] + lns[at, :] * (grad - mean_g - z * mean_gz)
+            hgrad[at, 0, :] = stbuf[at, :] + lns[at, :] * (grad - mean_g - z * mean_gz)
             return (
                 sums[0] + jnp.sum(back, axis=0, keepdims=True),
                 sums[1] + jnp.sum(back * z, axis=0, keepdims=True),
             )
 
+        def body(i, sums):
+            return piece(pl.ds(pl.multiple_of(i * block, block), block), sums)
+
+        kept = hgrad.shape[0]
         zero = jnp.zeros((1, width), F32)
-        sums = lax.fori_loop(0, rows // block, body, (zero, zero))
+        sums = lax.fori_loop(0, kept // block, body, (zero, zero))
+        if kept % block:
+            sums = piece(pl.ds(kept // block * block, kept % block), sums)
         vals[0] = small[...]
         vals[0, 0:1, :] = sums[0]
         vals[0, 1:2, :] = sums[1]
@@ -504,7 +509,7 @@
         sum_copy(j).wait_send()
 
 
-def tail(ndp, grads, part, other, state, unit, lns, ones, small):
+def tail(ndp, grads, part, other, state, unit, lns, ones, small, kept):
     chips = ndp // 2
     bits = ndp.bit_length() - 1
     split = [x.reshape(x.shape[0], chips, 2, x.shape[1] // ndp, x.shape[2]) for x in grads]
@@ -523,7 +528,7 @@
         out_specs=[vmem] * 3,
         out_shape=[
             jax.ShapeDtypeStruct((total, r, w), F32),
-            jax.ShapeDtypeStruct((rows, width), F32),
+            jax.ShapeDtypeStruct((kept, 1, width), F32),
             jax.ShapeDtypeStruct(small.shape, F32),
         ],
         scratch_shapes=[
@@ -962,7 +967,8 @@
 
     g_self_out = head_grads([list(zip(d_rows0, self_mixed))])
     d_mixed = dot_nn(cat([x for pieces in d_rows0 for x in pieces]), self_out_t).astype(BF)
-    d_mixed, g_self_out, g_cross, s_out, g_in = tie(d_mixed, g_self_out, g_cross, s_out, g_in)
+    g_self_out, g_cross, s_out, g_in = tie(g_self_out, g_cross, s_out, g_in)
+    d_mixed, g_self_out = tie(d_mixed, g_self_out)
     s_in = reduce_rows(g_in[None])
     ffn_out_g = s_out[0].astype(F32).T
     ffn_in_g = s_in[0].astype(F32)
@@ -1009,6 +1015,7 @@
         cat(scale0),
         1.0 + scale_attn,
         jnp.concatenate([wide, narrow]),
+        own_len,
     )
     self_qkv_g = sums[:3]
     self_out_g = sums[3].T
@@ -1024,7 +1031,7 @@
     return (
         cat(results)[None, :own_len],
         mean_loss,
-        hidden_g[None, :own_len],
+        hidden_g.transpose(1, 0, 2),
         text_g[None],
         mine[:6],
         mine[6:10],

time: 804 us -> 804 us (level)
    unnamed x436 -> x452, local copies, waits for them, and re-layouts: 33.1 us -> 32.6 us
  transfers between devices with their start and end apart: 43 -> 43, of which waited for: 19 -> 19; matrix products, arithmetic and copies ran while one was open for 38% -> 37% of each run, Pallas kernels for 32% -> 32%
where the time goes in v6:
time: 804 us; the launch traced here: 790 us
  Pallas kernels  254 us (32%)
  matrix products  183 us (23%)
  waiting for transfers between devices  132 us (16%)
  other arithmetic  86.8 us (11%)
  local copies, waits for them, and re-layouts  67.9 us (8%)
  starting transfers between devices  45.5 us (6%)
  between operations  20.9 us (3%)
    pallas_call x1, Pallas kernels, tail(): pl.pallas_call(functools.partial(tail_kernel, ndp, counts, nc), in_specs=...  134 us
    dot_general x17, matrix products, dot_nn(): lax.dot_general(a, b, (((1,), (0,)), ((), ())), preferred_element_type=F32)  90.3 us
    ppermute x35, waiting for transfers between devices, swap(): return lax.ppermute(values, 'mp', SWAP)  63.3 us
    all_gather x2, waiting for transfers between devices, whole(): return lax.all_gather(shards, 'dp', axis=1, tiled=True)  56.2 us
    dot_general x8, matrix products, dot_nt(): lax.dot_general(a, b, (((1,), (1,)), ((), ())), preferred_element_type=F32)  51.7 us
    dot_general x2, matrix products, dot_tn(): lax.dot_general(a, b, (((0,), (0,)), ((), ())), preferred_element_type=F32)  40.9 us
    ppermute x35, starting transfers between devices, swap(): return lax.ppermute(values, 'mp', SWAP)  39 us
    pallas_call x4, Pallas kernels, attend(): pl.pallas_call(functools.partial(attend_kernel, mask is not None), grid=(...  38.7 us
  transfers between devices with their start and end apart: 43, of which 19 were waited for; matrix products, arithmetic and copies ran while one was open for 37% of the time, Pallas kernels for 32%

profile of v6, /device:TPU:0, one launch (start us, length us, event | category | flops | bytes accessed | tf_op | source)
XLA Modules:
  0.0 789.7 jit_solution(18199404226510895974)
XLA Ops:
  37.0 5.5 collective-permute-done.4
  58.6 56.2 %all-gather.3.cloned.1.call-done.refs_3_.refs_4_ = bf16[8,1536,768]{2,1,0:T(8,128)(2,1)} async-done(((bf16[8,96,768]{2,1,0:T(8,128)(2,1)}), bf16[8,1536,768]{2,1,0:T(8,128)(2,1)}) %all-gather.3.cloned.1.call-update) | async-done | bytes 18874384 | tf_op jit(solution)/shard_map/all_gather | solution.py:682
  138.7 6.8 rope_prep.1
  146.6 10.2 %attend_fwd.4 = (bf16[384,768]{1,0:T(8,128)(2,1)S(1)}, f32[6,1,384]{2,1,0:T(1,128)S(1)}, f32[192,1536]{1,0:T(8,128)S(1)}, bf16[192,1536]{1,0:T(8,128)(2,1)}) custom-call(bf16[384,768]{1,0:T(8,128)(2,1)S(1)} %slice.548.refs_0_, bf16[800,768]{1,0:T(8,128)(2,1)S(1)} %get-tuple-element.150.refs_1_, bf16[800,768]{1,0:T(8,128)(2,1)S(1)} %pad_maximum_fusion.6.refs_2_, ...), custom_call_target="tpu_custom_call" | custom-call | flops 2831155200 | bytes 3637248 | tf_op jit(solution)/shard_map/attend_fwd/pallas_call | solution.py:125
  163.3 10.2 %attend_fwd.5 = (bf16[416,768]{1,0:T(8,128)(2,1)S(1)}, f32[6,1,416]{2,1,0:T(1,128)S(1)}, f32[208,1536]{1,0:T(8,128)S(1)}, bf16[208,1536]{1,0:T(8,128)(2,1)S(1)}) custom-call(bf16[416,768]{1,0:T(8,128)(2,1)S(1)} %slice.550.refs_0_, bf16[800,768]{1,0:T(8,128)(2,1)S(1)} %get-tuple-element.150.refs_1_, bf16[800,768]{1,0:T(8,128)(2,1)S(1)} %pad_maximum_fusion.6.refs_2_, ...), custom_call_target="tpu_custom_call" | custom-call | flops 3067084800 | bytes 3735552 | tf_op jit(solution)/shard_map/attend_fwd/pallas_call | solution.py:125
  186.6 4.3 collective-permute-done.10
  194.2 9.3 %collective-permute-done.13.refs_5_ = bf16[192,1536]{1,0:T(8,128)(2,1)S(1)} collective-permute-done((bf16[192,1536]{1,0:T(8,128)(2,1)S(1)}, bf16[192,1536]{1,0:T(8,128)(2,1)S(1)}, u32[]{:S(2)}, u32[]{:S(2)}) %collective-permute-start.13) | collective-permute-done | bytes 589856 | tf_op jit(solution)/shard_map/ppermute | solution.py:576
  210.7 9.4 %collective-permute-done.14 = f32[384,1]{1,0:T(8,128)S(1)} collective-permute-done((f32[384,1]{1,0:T(8,128)S(1)}, f32[384,1]{1,0:T(8,128)S(1)}, u32[]{:S(2)}, u32[]{:S(2)}) %collective-permute-start.14) | collective-permute-done | bytes 1568 | tf_op jit(solution)/shard_map/ppermute | solution.py:576
  221.9 9.0 %attend_fwd.6 = (bf16[384,768]{1,0:T(8,128)(2,1)S(1)}, f32[6,1,384]{2,1,0:T(1,128)S(1)}, f32[192,1536]{1,0:T(8,128)S(1)}, bf16[192,1536]{1,0:T(8,128)(2,1)}) custom-call(bf16[384,768]{1,0:T(8,128)(2,1)S(1)} %multiply_convert_fusion.8.refs_0_, bf16[512,768]{1,0:T(8,128)(2,1)S(1)} %multiply_convert_fusion.2.refs_1_, bf16[512,768]{1,0:T(8,128)(2,1)S(1)} %copy-done.9, ...), custom_call_target="tpu_custom_call" | custom-call | flops 1811939328 | bytes 2752512 | tf_op jit(solution)/shard_map/attend_fwd/pallas_call | solution.py:125
  237.3 9.9 %collective-permute-done.16 = bf16[192,1536]{1,0:T(8,128)(2,1)} collective-permute-done((bf16[192,1536]{1,0:T(8,128)(2,1)}, bf16[192,1536]{1,0:T(8,128)(2,1)}, u32[]{:S(2)}, u32[]{:S(2)}) %collective-permute-start.16) | collective-permute-done | bytes 589856 | tf_op jit(solution)/shard_map/ppermute | solution.py:576
  260.7 9.4 %attend_fwd.7 = (bf16[416,768]{1,0:T(8,128)(2,1)S(1)}, f32[6,1,416]{2,1,0:T(1,128)S(1)}, f32[208,1536]{1,0:T(8,128)S(1)}, bf16[208,1536]{1,0:T(8,128)(2,1)}) custom-call(bf16[416,768]{1,0:T(8,128)(2,1)S(1)} %multiply_convert_fusion.5.refs_0_, bf16[512,768]{1,0:T(8,128)(2,1)S(1)} %multiply_convert_fusion.2.refs_1_, bf16[512,768]{1,0:T(8,128)(2,1)S(1)} %copy-done.10, ...), custom_call_target="tpu_custom_call" | custom-call | flops 1962934272 | bytes 2850816 | tf_op jit(solution)/shard_map/attend_fwd/pallas_call | solution.py:125
  273.3 12.0 %multiply_convert_fusion.1 = (bf16[384,4480]{1,0:T(8,128)(2,1)S(1)}, f32[384,4480]{1,0:T(8,128)}) fusion(f32[4480]{0:T(1024)} %reduce.26, bf16[2,1536,4480]{2,1,0:T(8,128)(2,1)} %all-gather.5.cloned.1.call-done, bf16[192,1536]{1,0:T(8,128)(2,1)} %collective-permute-done.18, bf16[192,1536]{1,0:T(8,128)(2,1)} %add_convert_fusion.5), kind=kOutput, calls=%fused_computation.45 | convolution fusion | flops 5304385536 | bytes 25284608 | tf_op jit(solution)/shard_map/dot_general | solution.py:38
  289.1 8.8 %fusion.7 = f32[384,1536]{1,0:T(8,128)S(1)} fusion(bf16[384,4480]{1,0:T(8,128)(2,1)S(1)} %get-tuple-element.191, bf16[2,1536,4480]{2,1,0:T(8,128)(2,1)} %all-gather.5.cloned.1.call-done), kind=kOutput, calls=%fused_computation.15 | convolution fusion | flops 5284823040 | bytes 19562496 | tf_op jit(solution)/shard_map/dot_general | solution.py:42
  298.0 4.7 collective-permute-done.20
  303.6 13.2 %multiply_convert_fusion = (bf16[416,4480]{1,0:T(8,128)(2,1)}, f32[416,4480]{1,0:T(8,128)}) fusion(f32[4480]{0:T(1024)S(1)} %copy-done.178, bf16[2,1536,4480]{2,1,0:T(8,128)(2,1)} %all-gather.5.cloned.1.call-done, bf16[208,1536]{1,0:T(8,128)(2,1)S(1)} %collective-permute-done.20, bf16[208,1536]{1,0:T(8,128)(2,1)S(1)} %add_convert_fusion.2), kind=kOutput, calls=%fused_computation.26 | convolution fusion | flops 5746417664 | bytes 26240512 | tf_op jit(solution)/shard_map/dot_general | solution.py:38
  320.3 10.1 %fusion.6 = f32[416,1536]{1,0:T(8,128)S(1)} fusion(bf16[416,4480]{1,0:T(8,128)(2,1)} %get-tuple-element.199, bf16[2,1536,4480]{2,1,0:T(8,128)(2,1)} %all-gather.5.cloned.1.call-done), kind=kOutput, calls=%fused_computation.14 | convolution fusion | flops 5725224960 | bytes 20045824 | tf_op jit(solution)/shard_map/dot_general | solution.py:42
  333.0 12.3 %fusion.26 = bf16[384,4480]{1,0:T(8,128)(2,1)S(1)} fusion(bf16[2,1536,4480]{2,1,0:T(8,128)(2,1)} %all-gather.5.cloned.1.call-done, f32[384,4480]{1,0:T(8,128)} %get-tuple-element.476, bf16[192,1536]{1,0:T(8,128)(2,1)S(1)} %collective-permute-done.22, bf16[192,1536]{1,0:T(8,128)(2,1)S(1)} %multiply_convert_fusion.7), kind=kOutput, calls=%fused_computation.36 | convolution fusion | flops 5323309056 | bytes 25264128 | tf_op jit(solution)/shard_map/dot_general | solution.py:38
  349.0 8.8 %fusion.1 = f32[384,1536]{1,0:T(8,128)S(1)} fusion(bf16[384,4480]{1,0:T(8,128)(2,1)S(1)} %fusion.26, bf16[2,1536,4480]{2,1,0:T(8,128)(2,1)} %all-gather.5.cloned.1.call-done), kind=kOutput, calls=%fused_computation.9 | convolution fusion | flops 5284823040 | bytes 19562496 | tf_op jit(solution)/shard_map/dot_general | solution.py:42
  357.8 5.9 collective-permute-done.24
  364.4 20.8 %convolution_convert_fusion.1 = bf16[1536,4480]{1,0:T(8,128)(2,1)} fusion(bf16[416,4480]{1,0:T(8,128)(2,1)} %get-tuple-element.199, bf16[384,4480]{1,0:T(8,128)(2,1)} %copy-done.222, bf16[208,1536]{1,0:T(8,128)(2,1)S(1)} %collective-permute-done.24, bf16[208,1536]{1,0:T(8,128)(2,1)S(1)} %multiply_convert_fusion.4, ...), kind=kOutput, calls=%fused_computation.1 | convolution fusion | flops 11041095680 | bytes 23388160 | tf_op jit(solution)/shard_map/dot_general | solution.py:46
  392.4 16.1 %fusion.25 = bf16[416,4480]{1,0:T(8,128)(2,1)} fusion(bf16[416,1536]{1,0:T(8,128)(2,1)S(1)} %copy-done.123, bf16[2,1536,4480]{2,1,0:T(8,128)(2,1)} %all-gather.5.cloned.1.call-done, f32[416,4480]{1,0:T(8,128)} %get-tuple-element.478), kind=kOutput, calls=%fused_computation.35 | convolution fusion | flops 5764362240 | bytes 26222592 | tf_op jit(solution)/shard_map/dot_general | solution.py:38
  409.9 10.8 %fusion = f32[416,1536]{1,0:T(8,128)S(1)} fusion(bf16[416,4480]{1,0:T(8,128)(2,1)} %fusion.25, bf16[2,1536,4480]{2,1,0:T(8,128)(2,1)} %all-gather.5.cloned.1.call-done), kind=kOutput, calls=%fused_computation.8 | convolution fusion | flops 5725224960 | bytes 20045824 | tf_op jit(solution)/shard_map/dot_general | solution.py:42
  424.8 20.2 %convolution_convert_fusion = bf16[1536,4480]{1,0:T(8,128)(2,1)} fusion(bf16[416,4480]{1,0:T(8,128)(2,1)} %fusion.25, bf16[384,4480]{1,0:T(8,128)(2,1)S(1)} %copy-done.110, bf16[208,1536]{1,0:T(8,128)(2,1)S(1)} %copy-done.219, bf16[208,1536]{1,0:T(8,128)(2,1)S(1)} %copy-done.128, bf16[192,1536]{1,0:T(8,128)(2,1)} %collective-permute-done.18, ...), kind=kOutput, calls=%fused_computation | convolution fusion | flops 11041095680 | bytes 23388160 | tf_op jit(solution)/shard_map/dot_general | solution.py:46
  451.8 8.3 %attend_bwd_cross.2 = (f32[384,768]{1,0:T(8,128)S(1)}, f32[512,768]{1,0:T(8,128)}, f32[512,768]{1,0:T(8,128)}, f32[384,1]{1,0:T(8,128)S(1)}, f32[1,768]{1,0:T(1,128)S(1)}) custom-call(bf16[384,768]{1,0:T(8,128)(2,1)S(1)} %copy-done.18, bf16[512,768]{1,0:T(8,128)(2,1)S(1)} %multiply_convert_fusion.2.refs_1_, bf16[512,768]{1,0:T(8,128)(2,1)S(1)} %copy-done.11, ...), custom_call_target="tpu_custom_call" | custom-call | flops 4529848320 | bytes 8257536 | tf_op jit(solution)/shard_map/attend_bwd_cross/pallas_call | solution.py:219
  472.9 9.6 %attend_bwd_cross.3 = (f32[416,768]{1,0:T(8,128)S(1)}, f32[512,768]{1,0:T(8,128)}, f32[512,768]{1,0:T(8,128)}, f32[416,1]{1,0:T(8,128)S(1)}, f32[1,768]{1,0:T(1,128)S(1)}) custom-call(bf16[416,768]{1,0:T(8,128)(2,1)S(1)} %copy-done.13, bf16[512,768]{1,0:T(8,128)(2,1)S(1)} %multiply_convert_fusion.2.refs_1_, bf16[512,768]{1,0:T(8,128)(2,1)S(1)} %copy-done.11, ...), custom_call_target="tpu_custom_call" | custom-call | flops 4907335680 | bytes 8552448 | tf_op jit(solution)/shard_map/attend_bwd_cross/pallas_call | solution.py:219
  492.2 4.6 collective-permute-done.31
  505.5 5.7 collective-permute-done.32
  516.8 13.2 %head_grads.3 = bf16[4,1536,768]{2,1,0:T(8,128)(2,1)} custom-call(bf16[208,1536]{1,0:T(8,128)(2,1)S(1)} %copy-done.35, bf16[416,768]{1,0:T(8,128)(2,1)S(1)} %get-tuple-element.370.refs_1_, bf16[208,1536]{1,0:T(8,128)(2,1)} %collective-permute-done.11.refs_2_, bf16[192,1536]{1,0:T(8,128)(2,1)S(1)} %copy-done.45, ...), custom_call_target="tpu_custom_call" | custom-call | flops 6190792704 | bytes 19955712 | tf_op jit(solution)/shard_map/head_grads/pallas_call | solution.py:328
  564.5 4.9 fusion.103.refs_3_
  569.4 22.4 %attend_bwd_self.1 = (f32[800,768]{1,0:T(8,128)}, f32[800,768]{1,0:T(8,128)}, bf16[800,768]{1,0:T(8,128)(2,1)S(1)}, f32[800,1]{1,0:T(8,128)S(1)}, f32[800,1]{1,0...) custom-call(bf16[800,768]{1,0:T(8,128)(2,1)S(1)} %copy-done.30, bf16[800,768]{1,0:T(8,128)(2,1)} %copy-done.3, ...), custom_call_target="tpu_custom_call" | custom-call | flops 14745600000 | bytes 15974400 | tf_op jit(solution)/shard_map/attend_bwd_self/pallas_call | solution.py:198
  611.9 18.6 %self_back.1 = (bf16[3,1536,768]{2,1,0:T(8,128)(2,1)}, f32[400,1536]{1,0:T(8,128)}, bf16[400,1536]{1,0:T(8,128)(2,1)S(1)}) custom-call(bf16[208,1536]{1,0:T(8,128)(2,1)S(1)} %copy-done.37, bf16[208,1536]{1,0:T(8,128)(2,1)S(1)} %copy-done.51, bf16[192,1536]{1,0:T(8,128)(2,1)S(1)} %copy-done.43, bf16[192,1536]{1,0:T(8,128)(2,1)S(1)} %copy-done.58, ...), custom_call_target="tpu_custom_call" | custom-call | flops 11324620800 | bytes 30000000 | tf_op jit(solution)/shard_map/self_back/pallas_call | solution.py:285
  631.6 133.9 %tail_sums.1 = (f32[8,96,768]{2,1,0:T(8,128)}, f32[390,1,1536]{2,1,0:T(1,128)}, f32[24,1536]{1,0:T(8,128)}) custom-call(bf16[3,8,2,96,768]{4,3,2,1,0:T(8,128)(2,1)} %bitcast.260, bf16[1,8,2,96,768]{4,3,2,1,0:T(8,128)(2,1)} %bitcast.252, bf16[4,8,2,96,768]{4,3,2,1,0:T(8,128)(2,1)} %bitcast.259, f32[208,1536]{1,0:T(8,128)} %get-tuple-element.379.refs_3_, ...), custom_call_target="tpu_custom_call" | custom-call | flops 1000000 | bytes 1000000 | tf_op jit(solution)/shard_map/tail_sums/pallas_call | solution.py:525
  (829 shorter events, 263.7 us)
Async XLA Ops:
  7.2 107.6 %all-gather.3.cloned.1.call-start = ((), (), s32[]{:S(2)}) async-start(), calls=%async_computation.2 | async-start | bytes 20054016 | tf_op jit(solution)/shard_map/all_gather | solution.py:682
  9.8 263.4 %all-gather.5.cloned.1.call-start = ((), (), s32[]{:S(2)}) async-start(), calls=%async_computation.3 | async-start | bytes 29245440 | tf_op jit(solution)/shard_map/all_gather | solution.py:682
  11.4 524.5 %reduce-scatter.3.cloned.1.call-start = ((), (), s32[]{:S(2)}) async-start(), calls=%async_computation.4 | async-start | bytes 14622720 | tf_op jit(solution)/shard_map/reduce_scatter | solution.py:837
  12.9 9.5 %collective-permute-start = (f32[1,1408]{1,0:T(1,128)S(1)}, f32[1,1408]{1,0:T(1,128)S(1)}, u32[]{:S(2)}, u32[]{:S(2)}) collective-permute-start(f32[1,1408]{1,0:T(1,128)S(1)} %broadcast_in_dim.90), channel_id=1, source_target_pairs={{0,1},{1,0},{2,3},{3,2},{4,5},{5,4},{6,7},{7,6},{8,9},{9,8},{10,11... | collective-permute-start | bytes 16904 | tf_op jit(solution)/shard_map/ppermute | solution.py:576
  15.9 143.4 %collective-permute-start.12 = (bf16[256,1536]{1,0:T(8,128)(2,1)}, bf16[256,1536]{1,0:T(8,128)(2,1)}, u32[]{:S(2)}, u32[]{:S(2)}) collective-permute-start(bf16[256,1536]{1,0:T(8,128)(2,1)} %bitcast.39.refs_6_), channel_id=1, source_target_pairs={{0,1},{1,0},{2,3},{3,2},{4,5},{5,4},{6,7},{7,6},{8,9},{9,8},{10,11... | collective-permute-start | bytes 2359304 | tf_op jit(solution)/shard_map/ppermute | solution.py:576
  49.4 65.5 %collective-permute-start.5 = (bf16[208,1536]{1,0:T(8,128)(2,1)S(1)}, bf16[208,1536]{1,0:T(8,128)(2,1)S(1)}, u32[]{:S(2)}, u32[]{:S(2)}) collective-permute-start(bf16[208,1536]{1,0:T(8,128)(2,1)S(1)} %get-tuple-element.412.refs_0_), channel_id=1, source_target_pairs={{0,1},{1,0},{2,3},{3,2},{4,5},{5,4},{6,7},{7,6},{8,9},{9,8},{10,11... | collective-permute-start | bytes 1916936 | tf_op jit(solution)/shard_map/ppermute | solution.py:576
  57.1 66.7 %collective-permute-start.6 = (bf16[192,1536]{1,0:T(8,128)(2,1)S(1)}, bf16[192,1536]{1,0:T(8,128)(2,1)S(1)}, u32[]{:S(2)}, u32[]{:S(2)}) collective-permute-start(bf16[192,1536]{1,0:T(8,128)(2,1)S(1)} %get-tuple-element.410.refs_2_), channel_id=1, source_target_pairs={{0,1},{1,0},{2,3},{3,2},{4,5},{5,4},{6,7},{7,6},{8,9},{9,8},{10,11... | collective-permute-start | bytes 1769480 | tf_op jit(solution)/shard_map/ppermute | solution.py:576
  122.4 10.9 %collective-permute-start.7 = (f32[416,2]{0,1:T(2,128)S(1)}, f32[416,2]{0,1:T(2,128)S(1)}, u32[]{:S(2)}, u32[]{:S(2)}) collective-permute-start(f32[416,2]{0,1:T(2,128)S(1)} %pad_maximum_fusion.25), channel_id=1, source_target_pairs={{0,1},{1,0},{2,3},{3,2},{4,5},{5,4},{6,7},{7,6},{8,9},{9,8},{10,11... | collective-permute-start | bytes 9992 | tf_op jit(solution)/shard_map/ppermute | solution.py:576
  158.5 16.4 %collective-permute-start.9 = (bf16[192,1536]{1,0:T(8,128)(2,1)}, bf16[192,1536]{1,0:T(8,128)(2,1)}, u32[]{:S(2)}, u32[]{:S(2)}) collective-permute-start(bf16[192,1536]{1,0:T(8,128)(2,1)} %get-tuple-element.153), channel_id=1, source_target_pairs={{0,1},{1,0},{2,3},{3,2},{4,5},{5,4},{6,7},{7,6},{8,9},{9,8},{10,11... | collective-permute-start | bytes 1769480 | tf_op jit(solution)/shard_map/ppermute | solution.py:576
  173.5 17.4 %collective-permute-start.10 = (bf16[208,1536]{1,0:T(8,128)(2,1)S(1)}, bf16[208,1536]{1,0:T(8,128)(2,1)S(1)}, u32[]{:S(2)}, u32[]{:S(2)}) collective-permute-start(bf16[208,1536]{1,0:T(8,128)(2,1)S(1)} %get-tuple-element.156), channel_id=1, source_target_pairs={{0,1},{1,0},{2,3},{3,2},{4,5},{5,4},{6,7},{7,6},{8,9},{9,8},{10,11... | collective-permute-start | bytes 1916936 | tf_op jit(solution)/shard_map/ppermute | solution.py:576
  177.4 26.1 %collective-permute-start.13 = (bf16[192,1536]{1,0:T(8,128)(2,1)S(1)}, bf16[192,1536]{1,0:T(8,128)(2,1)S(1)}, u32[]{:S(2)}, u32[]{:S(2)}) collective-permute-start(bf16[192,1536]{1,0:T(8,128)(2,1)S(1)} %add_convert_fusion.6.refs_3_), channel_id=1, source_target_pairs={{0,1},{1,0},{2,3},{3,2},{4,5},{5,4},{6,7},{7,6},{8,9},{9,8},{10,11... | collective-permute-start | bytes 1769480 | tf_op jit(solution)/shard_map/ppermute | solution.py:576
  192.8 39.9 %collective-permute-start.11 = (bf16[208,1536]{1,0:T(8,128)(2,1)S(1)}, bf16[208,1536]{1,0:T(8,128)(2,1)}, u32[]{:S(2)}, u32[]{:S(2)}) collective-permute-start(bf16[208,1536]{1,0:T(8,128)(2,1)S(1)} %add_convert_fusion.3.refs_0_), channel_id=1, source_target_pairs={{0,1},{1,0},{2,3},{3,2},{4,5},{5,4},{6,7},{7,6},{8,9},{9,8},{10,11... | collective-permute-start | bytes 1916936 | tf_op jit(solution)/shard_map/ppermute | solution.py:576
  206.9 13.2 %collective-permute-start.14 = (f32[384,1]{1,0:T(8,128)S(1)}, f32[384,1]{1,0:T(8,128)S(1)}, u32[]{:S(2)}, u32[]{:S(2)}) collective-permute-start(f32[384,1]{1,0:T(8,128)S(1)} %copy.132), channel_id=1, source_target_pairs={{0,1},{1,0},{2,3},{3,2},{4,5},{5,4},{6,7},{7,6},{8,9},{9,8},{10,11... | collective-permute-start | bytes 4616 | tf_op jit(solution)/shard_map/ppermute | solution.py:576
  210.0 10.6 %collective-permute-start.15 = (f32[512,1]{0,1:T(1,128)S(1)}, f32[512,1]{0,1:T(1,128)S(1)}, u32[]{:S(2)}, u32[]{:S(2)}) collective-permute-start(f32[512,1]{0,1:T(1,128)S(1)} %pad_maximum_fusion.34), channel_id=1, source_target_pairs={{0,1},{1,0},{2,3},{3,2},{4,5},{5,4},{6,7},{7,6},{8,9},{9,8},{10,11... | collective-permute-start | bytes 6152 | tf_op jit(solution)/shard_map/ppermute | solution.py:576
  232.7 14.4 %collective-permute-start.16 = (bf16[192,1536]{1,0:T(8,128)(2,1)}, bf16[192,1536]{1,0:T(8,128)(2,1)}, u32[]{:S(2)}, u32[]{:S(2)}) collective-permute-start(bf16[192,1536]{1,0:T(8,128)(2,1)} %get-tuple-element.172), channel_id=1, source_target_pairs={{0,1},{1,0},{2,3},{3,2},{4,5},{5,4},{6,7},{7,6},{8,9},{9,8},{10,11... | collective-permute-start | bytes 1769480 | tf_op jit(solution)/shard_map/ppermute | solution.py:576
  254.3 18.3 %collective-permute-start.18 = (bf16[192,1536]{1,0:T(8,128)(2,1)}, bf16[192,1536]{1,0:T(8,128)(2,1)}, u32[]{:S(2)}, u32[]{:S(2)}) collective-permute-start(bf16[192,1536]{1,0:T(8,128)(2,1)} %add_convert_fusion.5), channel_id=1, source_target_pairs={{0,1},{1,0},{2,3},{3,2},{4,5},{5,4},{6,7},{7,6},{8,9},{9,8},{10,11... | collective-permute-start | bytes 1769480 | tf_op jit(solution)/shard_map/ppermute | solution.py:576
  272.5 13.3 %collective-permute-start.19 = (bf16[208,1536]{1,0:T(8,128)(2,1)}, bf16[208,1536]{1,0:T(8,128)(2,1)S(1)}, u32[]{:S(2)}, u32[]{:S(2)}) collective-permute-start(bf16[208,1536]{1,0:T(8,128)(2,1)} %get-tuple-element.184), channel_id=1, source_target_pairs={{0,1},{1,0},{2,3},{3,2},{4,5},{5,4},{6,7},{7,6},{8,9},{9,8},{10,11... | collective-permute-start | bytes 1916936 | tf_op jit(solution)/shard_map/ppermute | solution.py:576
  288.3 14.3 %collective-permute-start.20 = (bf16[208,1536]{1,0:T(8,128)(2,1)S(1)}, bf16[208,1536]{1,0:T(8,128)(2,1)S(1)}, u32[]{:S(2)}, u32[]{:S(2)}) collective-permute-start(bf16[208,1536]{1,0:T(8,128)(2,1)S(1)} %add_convert_fusion.2), channel_id=1, source_target_pairs={{0,1},{1,0},{2,3},{3,2},{4,5},{5,4},{6,7},{7,6},{8,9},{9,8},{10,11... | collective-permute-start | bytes 1916936 | tf_op jit(solution)/shard_map/ppermute | solution.py:576
  302.8 14.1 %collective-permute-start.21 = (bf16[192,1536]{1,0:T(8,128)(2,1)S(1)}, bf16[192,1536]{1,0:T(8,128)(2,1)S(1)}, u32[]{:S(2)}, u32[]{:S(2)}) collective-permute-start(bf16[192,1536]{1,0:T(8,128)(2,1)S(1)} %slice.982), channel_id=1, source_target_pairs={{0,1},{1,0},{2,3},{3,2},{4,5},{5,4},{6,7},{7,6},{8,9},{9,8},{10,11... | collective-permute-start | bytes 1769480 | tf_op jit(solution)/shard_map/ppermute | solution.py:576
  319.0 12.7 %collective-permute-start.22 = (bf16[192,1536]{1,0:T(8,128)(2,1)S(1)}, bf16[192,1536]{1,0:T(8,128)(2,1)S(1)}, u32[]{:S(2)}, u32[]{:S(2)}) collective-permute-start(bf16[192,1536]{1,0:T(8,128)(2,1)S(1)} %multiply_convert_fusion.7), channel_id=1, source_target_pairs={{0,1},{1,0},{2,3},{3,2},{4,5},{5,4},{6,7},{7,6},{8,9},{9,8},{10,11... | collective-permute-start | bytes 1769480 | tf_op jit(solution)/shard_map/ppermute | solution.py:576
  331.8 13.5 %collective-permute-start.23 = (bf16[208,1536]{1,0:T(8,128)(2,1)S(1)}, bf16[208,1536]{1,0:T(8,128)(2,1)S(1)}, u32[]{:S(2)}, u32[]{:S(2)}) collective-permute-start(bf16[208,1536]{1,0:T(8,128)(2,1)S(1)} %slice.979), channel_id=1, source_target_pairs={{0,1},{1,0},{2,3},{3,2},{4,5},{5,4},{6,7},{7,6},{8,9},{9,8},{10,11... | collective-permute-start | bytes 1916936 | tf_op jit(solution)/shard_map/ppermute | solution.py:576
  348.0 15.7 %collective-permute-start.24 = (bf16[208,1536]{1,0:T(8,128)(2,1)S(1)}, bf16[208,1536]{1,0:T(8,128)(2,1)S(1)}, u32[]{:S(2)}, u32[]{:S(2)}) collective-permute-start(bf16[208,1536]{1,0:T(8,128)(2,1)S(1)} %multiply_convert_fusion.4), channel_id=1, source_target_pairs={{0,1},{1,0},{2,3},{3,2},{4,5},{5,4},{6,7},{7,6},{8,9},{9,8},{10,11... | collective-permute-start | bytes 1916936 | tf_op jit(solution)/shard_map/ppermute | solution.py:576
  363.8 22.5 %collective-permute-start.25 = (bf16[192,1536]{1,0:T(8,128)(2,1)S(1)}, bf16[192,1536]{1,0:T(8,128)(2,1)}, u32[]{:S(2)}, u32[]{:S(2)}) collective-permute-start(bf16[192,1536]{1,0:T(8,128)(2,1)S(1)} %slice.981), channel_id=1, source_target_pairs={{0,1},{1,0},{2,3},{3,2},{4,5},{5,4},{6,7},{7,6},{8,9},{9,8},{10,11... | collective-permute-start | bytes 1769480 | tf_op jit(solution)/shard_map/ppermute | solution.py:576
  386.4 391.4 %reduce-scatter.5.cloned.1.call-start = ((), (), s32[]{:S(2)}) async-start(), calls=%async_computation.5 | async-start | bytes 14622720 | tf_op jit(solution)/shard_map/reduce_scatter | solution.py:837
  408.5 14.8 %collective-permute-start.26 = (bf16[192,1536]{1,0:T(8,128)(2,1)S(1)}, bf16[192,1536]{1,0:T(8,128)(2,1)S(1)}, u32[]{:S(2)}, u32[]{:S(2)}) collective-permute-start(bf16[192,1536]{1,0:T(8,128)(2,1)S(1)} %get-tuple-element.211.refs_13_), channel_id=1, source_target_pairs={{0,1},{1,0},{2,3},{3,2},{4,5},{5,4},{6,7},{7,6},{8,9},{9,8},{10,11... | collective-permute-start | bytes 1769480 | tf_op jit(solution)/shard_map/ppermute | solution.py:576
  423.4 21.5 %collective-permute-start.27 = (bf16[208,1536]{1,0:T(8,128)(2,1)S(1)}, bf16[208,1536]{1,0:T(8,128)(2,1)S(1)}, u32[]{:S(2)}, u32[]{:S(2)}) collective-permute-start(bf16[208,1536]{1,0:T(8,128)(2,1)S(1)} %slice.978), channel_id=1, source_target_pairs={{0,1},{1,0},{2,3},{3,2},{4,5},{5,4},{6,7},{7,6},{8,9},{9,8},{10,11... | collective-permute-start | bytes 1916936 | tf_op jit(solution)/shard_map/ppermute | solution.py:576
  448.2 11.9 %collective-permute-start.28 = (bf16[208,1536]{1,0:T(8,128)(2,1)S(1)}, bf16[208,1536]{1,0:T(8,128)(2,1)S(1)}, u32[]{:S(2)}, u32[]{:S(2)}) collective-permute-start(bf16[208,1536]{1,0:T(8,128)(2,1)S(1)} %get-tuple-element.217.refs_10_), channel_id=1, source_target_pairs={{0,1},{1,0},{2,3},{3,2},{4,5},{5,4},{6,7},{7,6},{8,9},{9,8},{10,11... | collective-permute-start | bytes 1916936 | tf_op jit(solution)/shard_map/ppermute | solution.py:576
  472.0 16.6 %collective-permute-start.30 = (bf16[192,1536]{1,0:T(8,128)(2,1)}, bf16[192,1536]{1,0:T(8,128)(2,1)}, u32[]{:S(2)}, u32[]{:S(2)}) collective-permute-start(bf16[192,1536]{1,0:T(8,128)(2,1)} %slice.980), channel_id=1, source_target_pairs={{0,1},{1,0},{2,3},{3,2},{4,5},{5,4},{6,7},{7,6},{8,9},{9,8},{10,11... | collective-permute-start | bytes 1769480 | tf_op jit(solution)/shard_map/ppermute | solution.py:576
  500.5 10.7 %collective-permute-start.32 = (bf16[208,1536]{1,0:T(8,128)(2,1)S(1)}, bf16[208,1536]{1,0:T(8,128)(2,1)S(1)}, u32[]{:S(2)}, u32[]{:S(2)}) collective-permute-start(bf16[208,1536]{1,0:T(8,128)(2,1)S(1)} %slice.977), channel_id=1, source_target_pairs={{0,1},{1,0},{2,3},{3,2},{4,5},{5,4},{6,7},{7,6},{8,9},{9,8},{10,11... | collective-permute-start | bytes 1916936 | tf_op jit(solution)/shard_map/ppermute | solution.py:576
  504.9 25.1 %collective-permute-start.34 = (bf16[192,1536]{1,0:T(8,128)(2,1)S(1)}, bf16[192,1536]{1,0:T(8,128)(2,1)S(1)}, u32[]{:S(2)}, u32[]{:S(2)}) collective-permute-start(bf16[192,1536]{1,0:T(8,128)(2,1)S(1)} %get-tuple-element.381.refs_3_), channel_id=1, source_target_pairs={{0,1},{1,0},{2,3},{3,2},{4,5},{5,4},{6,7},{7,6},{8,9},{9,8},{10,11... | collective-permute-start | bytes 1769480 | tf_op jit(solution)/shard_map/ppermute | solution.py:576
  513.7 16.3 %collective-permute-start.33 = (bf16[208,1536]{1,0:T(8,128)(2,1)S(1)}, bf16[208,1536]{1,0:T(8,128)(2,1)S(1)}, u32[]{:S(2)}, u32[]{:S(2)}) collective-permute-start(bf16[208,1536]{1,0:T(8,128)(2,1)S(1)} %get-tuple-element.378.refs_0_), channel_id=1, source_target_pairs={{0,1},{1,0},{2,3},{3,2},{4,5},{5,4},{6,7},{7,6},{8,9},{9,8},{10,11... | collective-permute-start | bytes 1916936 | tf_op jit(solution)/shard_map/ppermute | solution.py:576
  557.2 43.3 %collective-permute-start.38 = (bf16[256,1536]{1,0:T(8,128)(2,1)}, bf16[256,1536]{1,0:T(8,128)(2,1)}, u32[]{:S(2)}, u32[]{:S(2)}) collective-permute-start(bf16[256,1536]{1,0:T(8,128)(2,1)} %slice.976), channel_id=1, source_target_pairs={{0,1},{1,0},{2,3},{3,2},{4,5},{5,4},{6,7},{7,6},{8,9},{9,8},{10,11... | collective-permute-start | bytes 2359304 | tf_op jit(solution)/shard_map/ppermute | solution.py:576
  (234 other events, 2414.6 us)
Sparse Core Ops, SparseCore 0:
  10.1 104.6 all-gather.2
  116.9 139.6 all-gather.4
  386.5 143.1 reduce-scatter.2
  536.0 154.9 reduce-scatter.4

commit v7 on v5

--- a/solution.py
+++ b/solution.py
@@ -619,7 +619,7 @@
 
 
 def chunks_of(padded):
-    first = (padded // 2 + 15) // 16 * 16
+    first = padded // 2 // 16 * 16
     return [(0, first), (first, padded)]
 
 

time: 804 us -> 813 us (1.011)
    unnamed x436 -> x434, local copies, waits for them, and re-layouts: 33.1 us -> 30.5 us
  transfers between devices with their start and end apart: 43 -> 43, of which waited for: 19 -> 19; matrix products, arithmetic and copies ran while one was open for 38% -> 39% of each run, Pallas kernels for 32% -> 32%
where the time goes in v7:
time: 813 us; the launch traced here: 800 us
  Pallas kernels  252 us (31%)
  matrix products  188 us (23%)
  waiting for transfers between devices  132 us (16%)
  other arithmetic  93.8 us (12%)
  local copies, waits for them, and re-layouts  67.2 us (8%)
  starting transfers between devices  44.7 us (5%)
  between operations  20.7 us (3%)
    pallas_call x1, Pallas kernels, tail(): pl.pallas_call(functools.partial(tail_kernel, ndp, counts, nc), in_specs=...  132 us
    dot_general x17, matrix products, dot_nn(): lax.dot_general(a, b, (((1,), (0,)), ((), ())), preferred_element_type=F32)  97.6 us
    ppermute x35, waiting for transfers between devices, swap(): return lax.ppermute(values, 'mp', SWAP)  67.1 us
    all_gather x2, waiting for transfers between devices, whole(): return lax.all_gather(shards, 'dp', axis=1, tiled=True)  53.2 us
    dot_general x8, matrix products, dot_nt(): lax.dot_general(a, b, (((1,), (1,)), ((), ())), preferred_element_type=F32)  50.6 us
    dot_general x2, matrix products, dot_tn(): lax.dot_general(a, b, (((0,), (0,)), ((), ())), preferred_element_type=F32)  40.2 us
    pallas_call x4, Pallas kernels, attend(): pl.pallas_call(functools.partial(attend_kernel, mask is not None), grid=(...  38.3 us
    ppermute x35, starting transfers between devices, swap(): return lax.ppermute(values, 'mp', SWAP)  38.2 us
  transfers between devices with their start and end apart: 43, of which 19 were waited for; matrix products, arithmetic and copies ran while one was open for 39% of the time, Pallas kernels for 32%

profile of v7, /device:TPU:0, one launch (start us, length us, event | category | flops | bytes accessed | tf_op | source)
XLA Modules:
  0.0 799.6 jit_solution(1563273982940286509)
XLA Ops:
  35.6 5.5 collective-permute-done.4
  61.6 53.2 %all-gather.3.cloned.1.call-done.refs_3_.refs_4_ = bf16[8,1536,768]{2,1,0:T(8,128)(2,1)} async-done(((bf16[8,96,768]{2,1,0:T(8,128)(2,1)}), bf16[8,1536,768]{2,1,0:T(8,128)(2,1)}) %all-gather.3.cloned.1.call-update) | async-done | bytes 18874384 | tf_op jit(solution)/shard_map/all_gather | solution.py:677
  141.4 6.8 rope_prep.1
  148.4 10.8 %attend_fwd.4 = (bf16[416,768]{1,0:T(8,128)(2,1)S(1)}, f32[6,1,416]{2,1,0:T(1,128)S(1)}, f32[208,1536]{1,0:T(8,128)S(1)}, bf16[208,1536]{1,0:T(8,128)(2,1)S(1)}) custom-call(bf16[416,768]{1,0:T(8,128)(2,1)S(1)} %slice.551.refs_0_, bf16[800,768]{1,0:T(8,128)(2,1)S(1)} %get-tuple-element.149.refs_1_, bf16[800,768]{1,0:T(8,128)(2,1)S(1)} %pad_maximum_fusion.5.refs_2_, ...), custom_call_target="tpu_custom_call" | custom-call | flops 3067084800 | bytes 3735552 | tf_op jit(solution)/shard_map/attend_fwd/pallas_call | solution.py:125
  176.0 9.3 %attend_fwd.5 = (bf16[384,768]{1,0:T(8,128)(2,1)S(1)}, f32[6,1,384]{2,1,0:T(1,128)S(1)}, f32[192,1536]{1,0:T(8,128)S(1)}, bf16[192,1536]{1,0:T(8,128)(2,1)S(1)}) custom-call(bf16[384,768]{1,0:T(8,128)(2,1)S(1)} %slice.553.refs_0_, bf16[800,768]{1,0:T(8,128)(2,1)S(1)} %copy-done.6, bf16[800,768]{1,0:T(8,128)(2,1)S(1)} %pad_maximum_fusion.5.refs_2_, ...), custom_call_target="tpu_custom_call" | custom-call | flops 2831155200 | bytes 3637248 | tf_op jit(solution)/shard_map/attend_fwd/pallas_call | solution.py:125
  190.7 11.1 %collective-permute-done.10 = bf16[192,1536]{1,0:T(8,128)(2,1)S(1)} collective-permute-done((bf16[192,1536]{1,0:T(8,128)(2,1)S(1)}, bf16[192,1536]{1,0:T(8,128)(2,1)S(1)}, u32[]{:S(2)}, u32[]{:S(2)}) %collective-permute-start.10) | collective-permute-done | bytes 589856 | tf_op jit(solution)/shard_map/ppermute | solution.py:571
  208.6 4.4 fusion.114
  222.9 8.2 %collective-permute-done.14 = f32[416,1]{1,0:T(8,128)S(1)} collective-permute-done((f32[416,1]{1,0:T(8,128)S(1)}, f32[416,1]{1,0:T(8,128)S(1)}, u32[]{:S(2)}, u32[]{:S(2)}) %collective-permute-start.14) | collective-permute-done | bytes 1696 | tf_op jit(solution)/shard_map/ppermute | solution.py:571
  232.8 9.6 %attend_fwd.6 = (bf16[416,768]{1,0:T(8,128)(2,1)S(1)}, f32[6,1,416]{2,1,0:T(1,128)S(1)}, f32[208,1536]{1,0:T(8,128)S(1)}, bf16[208,1536]{1,0:T(8,128)(2,1)}) custom-call(bf16[416,768]{1,0:T(8,128)(2,1)S(1)} %multiply_convert_fusion.5.refs_0_, bf16[512,768]{1,0:T(8,128)(2,1)S(1)} %multiply_convert_fusion.2.refs_1_, bf16[512,768]{1,0:T(8,128)(2,1)S(1)} %copy-done.9, ...), custom_call_target="tpu_custom_call" | custom-call | flops 1962934272 | bytes 2850816 | tf_op jit(solution)/shard_map/attend_fwd/pallas_call | solution.py:125
  248.3 11.3 %collective-permute-done.16 = bf16[208,1536]{1,0:T(8,128)(2,1)} collective-permute-done((bf16[208,1536]{1,0:T(8,128)(2,1)}, bf16[208,1536]{1,0:T(8,128)(2,1)}, u32[]{:S(2)}, u32[]{:S(2)}) %collective-permute-start.16) | collective-permute-done | bytes 639008 | tf_op jit(solution)/shard_map/ppermute | solution.py:571
  268.3 8.6 %attend_fwd.7 = (bf16[384,768]{1,0:T(8,128)(2,1)S(1)}, f32[6,1,384]{2,1,0:T(1,128)S(1)}, f32[192,1536]{1,0:T(8,128)S(1)}, bf16[192,1536]{1,0:T(8,128)(2,1)}) custom-call(bf16[384,768]{1,0:T(8,128)(2,1)S(1)} %multiply_convert_fusion.8.refs_0_, bf16[512,768]{1,0:T(8,128)(2,1)S(1)} %multiply_convert_fusion.2.refs_1_, bf16[512,768]{1,0:T(8,128)(2,1)S(1)} %copy-done.10, ...), custom_call_target="tpu_custom_call" | custom-call | flops 1811939328 | bytes 2752512 | tf_op jit(solution)/shard_map/attend_fwd/pallas_call | solution.py:125
  281.6 12.8 %multiply_convert_fusion = (bf16[416,4480]{1,0:T(8,128)(2,1)S(1)}, f32[416,4480]{1,0:T(8,128)}) fusion(f32[4480]{0:T(1024)S(1)} %reduce.26, bf16[2,1536,4480]{2,1,0:T(8,128)(2,1)} %all-gather.5.cloned.1.call-done, bf16[208,1536]{1,0:T(8,128)(2,1)} %collective-permute-done.18, bf16[208,1536]{1,0:T(8,128)(2,1)} %add_convert_fusion.2), kind=kOutput, calls=%fused_computation.26 | convolution fusion | flops 5746417664 | bytes 26240512 | tf_op jit(solution)/shard_map/dot_general | solution.py:38
  298.6 9.0 %fusion.7 = f32[416,1536]{1,0:T(8,128)S(1)} fusion(bf16[416,4480]{1,0:T(8,128)(2,1)S(1)} %get-tuple-element.190, bf16[2,1536,4480]{2,1,0:T(8,128)(2,1)} %all-gather.5.cloned.1.call-done), kind=kOutput, calls=%fused_computation.15 | convolution fusion | flops 5725224960 | bytes 20045824 | tf_op jit(solution)/shard_map/dot_general | solution.py:42
  311.5 12.3 %multiply_convert_fusion.1 = (bf16[384,4480]{1,0:T(8,128)(2,1)S(1)}, f32[384,4480]{1,0:T(8,128)}) fusion(f32[4480]{0:T(1024)S(1)} %reduce.26, bf16[2,1536,4480]{2,1,0:T(8,128)(2,1)} %all-gather.5.cloned.1.call-done, bf16[192,1536]{1,0:T(8,128)(2,1)S(1)} %collective-permute-done.20, bf16[192,1536]{1,0:T(8,128)(2,1)S(1)} %add_convert_fusion.5), kind=kOutput, calls=%fused_computation.45 | convolution fusion | flops 5304385536 | bytes 25282048 | tf_op jit(solution)/shard_map/dot_general | solution.py:38
  328.0 8.8 %fusion.6 = f32[384,1536]{1,0:T(8,128)S(1)} fusion(bf16[384,4480]{1,0:T(8,128)(2,1)S(1)} %get-tuple-element.198, bf16[2,1536,4480]{2,1,0:T(8,128)(2,1)} %all-gather.5.cloned.1.call-done), kind=kOutput, calls=%fused_computation.14 | convolution fusion | flops 5284823040 | bytes 19562496 | tf_op jit(solution)/shard_map/dot_general | solution.py:42
  336.9 4.9 collective-permute-done.22
  344.4 13.3 %fusion.25 = bf16[416,4480]{1,0:T(8,128)(2,1)S(1)} fusion(bf16[2,1536,4480]{2,1,0:T(8,128)(2,1)} %all-gather.5.cloned.1.call-done, f32[416,4480]{1,0:T(8,128)} %get-tuple-element.490, bf16[208,1536]{1,0:T(8,128)(2,1)S(1)} %collective-permute-done.22, bf16[208,1536]{1,0:T(8,128)(2,1)S(1)} %multiply_convert_fusion.4), kind=kOutput, calls=%fused_computation.35 | convolution fusion | flops 5766918144 | bytes 26222592 | tf_op jit(solution)/shard_map/dot_general | solution.py:38
  360.7 9.0 %fusion.1 = f32[416,1536]{1,0:T(8,128)S(1)} fusion(bf16[416,4480]{1,0:T(8,128)(2,1)S(1)} %fusion.25, bf16[2,1536,4480]{2,1,0:T(8,128)(2,1)} %all-gather.5.cloned.1.call-done), kind=kOutput, calls=%fused_computation.9 | convolution fusion | flops 5725224960 | bytes 20045824 | tf_op jit(solution)/shard_map/dot_general | solution.py:42
  369.7 4.8 collective-permute-done.24
  376.4 20.5 %convolution_convert_fusion.1 = bf16[1536,4480]{1,0:T(8,128)(2,1)} fusion(bf16[384,4480]{1,0:T(8,128)(2,1)} %copy-done.213, bf16[416,4480]{1,0:T(8,128)(2,1)} %copy-done.212, bf16[192,1536]{1,0:T(8,128)(2,1)S(1)} %collective-permute-done.24, bf16[192,1536]{1,0:T(8,128)(2,1)S(1)} %multiply_convert_fusion.7, ...), kind=kOutput, calls=%fused_computation.1 | convolution fusion | flops 11041095680 | bytes 23388160 | tf_op jit(solution)/shard_map/dot_general | solution.py:46
  405.2 14.2 %fusion.26 = bf16[384,4480]{1,0:T(8,128)(2,1)S(1)} fusion(bf16[384,1536]{1,0:T(8,128)(2,1)S(1)} %copy-done.118, bf16[2,1536,4480]{2,1,0:T(8,128)(2,1)} %all-gather.5.cloned.1.call-done, f32[384,4480]{1,0:T(8,128)} %get-tuple-element.492), kind=kOutput, calls=%fused_computation.36 | convolution fusion | flops 5320949760 | bytes 25264128 | tf_op jit(solution)/shard_map/dot_general | solution.py:38
  419.6 10.9 %fusion = f32[384,1536]{1,0:T(8,128)S(1)} fusion(bf16[384,4480]{1,0:T(8,128)(2,1)S(1)} %fusion.26, bf16[2,1536,4480]{2,1,0:T(8,128)(2,1)} %all-gather.5.cloned.1.call-done), kind=kOutput, calls=%fused_computation.8 | convolution fusion | flops 5284823040 | bytes 19562496 | tf_op jit(solution)/shard_map/dot_general | solution.py:42
  433.5 19.7 %convolution_convert_fusion = bf16[1536,4480]{1,0:T(8,128)(2,1)} fusion(bf16[384,4480]{1,0:T(8,128)(2,1)S(1)} %fusion.26, bf16[416,4480]{1,0:T(8,128)(2,1)S(1)} %copy-done.101, bf16[192,1536]{1,0:T(8,128)(2,1)} %copy-done.209, bf16[192,1536]{1,0:T(8,128)(2,1)} %copy-done.123, bf16[208,1536]{1,0:T(8,128)(2,1)} %collective-permute-done.18, ...), kind=kOutput, calls=%fused_computation | convolution fusion | flops 11041095680 | bytes 23388160 | tf_op jit(solution)/shard_map/dot_general | solution.py:46
  462.5 9.5 %attend_bwd_cross.2 = (f32[416,768]{1,0:T(8,128)S(1)}, f32[512,768]{1,0:T(8,128)}, f32[512,768]{1,0:T(8,128)}, f32[416,1]{1,0:T(8,128)S(1)}, f32[1,768]{1,0:T(1,128)S(1)}) custom-call(bf16[416,768]{1,0:T(8,128)(2,1)S(1)} %copy-done.13, bf16[512,768]{1,0:T(8,128)(2,1)S(1)} %multiply_convert_fusion.2.refs_1_, bf16[512,768]{1,0:T(8,128)(2,1)S(1)} %copy-done.11, ...), custom_call_target="tpu_custom_call" | custom-call | flops 4907335680 | bytes 8552448 | tf_op jit(solution)/shard_map/attend_bwd_cross/pallas_call | solution.py:219
  483.8 8.3 %attend_bwd_cross.3 = (f32[384,768]{1,0:T(8,128)S(1)}, f32[512,768]{1,0:T(8,128)}, f32[512,768]{1,0:T(8,128)}, f32[384,1]{1,0:T(8,128)S(1)}, f32[1,768]{1,0:T(1,128)S(1)}) custom-call(bf16[384,768]{1,0:T(8,128)(2,1)S(1)} %copy-done.18, bf16[512,768]{1,0:T(8,128)(2,1)S(1)} %multiply_convert_fusion.2.refs_1_, bf16[512,768]{1,0:T(8,128)(2,1)S(1)} %copy-done.11, ...), custom_call_target="tpu_custom_call" | custom-call | flops 4529848320 | bytes 8257536 | tf_op jit(solution)/shard_map/attend_bwd_cross/pallas_call | solution.py:219
  500.8 5.9 collective-permute-done.31
  513.9 7.7 collective-permute-done.32
  526.7 12.9 %head_grads.3 = bf16[4,1536,768]{2,1,0:T(8,128)(2,1)} custom-call(bf16[192,1536]{1,0:T(8,128)(2,1)S(1)} %copy-done.41, bf16[384,768]{1,0:T(8,128)(2,1)S(1)} %get-tuple-element.384.refs_1_, bf16[192,1536]{1,0:T(8,128)(2,1)} %collective-permute-done.11.refs_2_, bf16[208,1536]{1,0:T(8,128)(2,1)S(1)} %copy-done.37, ...), custom_call_target="tpu_custom_call" | custom-call | flops 6190792704 | bytes 19955712 | tf_op jit(solution)/shard_map/head_grads/pallas_call | solution.py:328
  543.8 4.8 fusion.101.refs_3_
  579.1 22.7 %attend_bwd_self.1 = (f32[800,768]{1,0:T(8,128)}, f32[800,768]{1,0:T(8,128)}, bf16[800,768]{1,0:T(8,128)(2,1)S(1)}, f32[800,1]{1,0:T(8,128)S(1)}, f32[800,1]{1,0...) custom-call(bf16[800,768]{1,0:T(8,128)(2,1)S(1)} %copy-done.29, bf16[800,768]{1,0:T(8,128)(2,1)} %copy-done.5, ...), custom_call_target="tpu_custom_call" | custom-call | flops 14745600000 | bytes 15974400 | tf_op jit(solution)/shard_map/attend_bwd_self/pallas_call | solution.py:198
  621.7 19.0 %self_back.1 = (bf16[3,1536,768]{2,1,0:T(8,128)(2,1)}, f32[400,1536]{1,0:T(8,128)}, bf16[400,1536]{1,0:T(8,128)(2,1)S(1)}) custom-call(bf16[192,1536]{1,0:T(8,128)(2,1)S(1)} %copy-done.39, bf16[192,1536]{1,0:T(8,128)(2,1)} %collective-permute-done.5.refs_1_, bf16[208,1536]{1,0:T(8,128)(2,1)S(1)} %copy-done.35, bf16[208,1536]{1,0:T(8,128)(2,1)S(1)} %copy-done.52, ...), custom_call_target="tpu_custom_call" | custom-call | flops 11324620800 | bytes 30000000 | tf_op jit(solution)/shard_map/self_back/pallas_call | solution.py:285
  641.7 132.1 %tail_sums.1 = (f32[8,96,768]{2,1,0:T(8,128)}, f32[400,1536]{1,0:T(8,128)}, f32[24,1536]{1,0:T(8,128)}) custom-call(bf16[3,8,2,96,768]{4,3,2,1,0:T(8,128)(2,1)} %bitcast.261, bf16[1,8,2,96,768]{4,3,2,1,0:T(8,128)(2,1)} %bitcast.253, bf16[4,8,2,96,768]{4,3,2,1,0:T(8,128)(2,1)} %bitcast.260, f32[192,1536]{1,0:T(8,128)} %get-tuple-element.393.refs_3_, ...), custom_call_target="tpu_custom_call" | custom-call | flops 1000000 | bytes 1000000 | tf_op jit(solution)/shard_map/tail_sums/pallas_call | solution.py:520
  (812 shorter events, 277.2 us)
Async XLA Ops:
  7.2 107.6 %all-gather.3.cloned.1.call-start = ((), (), s32[]{:S(2)}) async-start(), calls=%async_computation.2 | async-start | bytes 20054016 | tf_op jit(solution)/shard_map/all_gather | solution.py:677
  9.8 271.8 %all-gather.5.cloned.1.call-start = ((), (), s32[]{:S(2)}) async-start(), calls=%async_computation.3 | async-start | bytes 29245440 | tf_op jit(solution)/shard_map/all_gather | solution.py:677
  11.4 537.2 %reduce-scatter.3.cloned.1.call-start = ((), (), s32[]{:S(2)}) async-start(), calls=%async_computation.4 | async-start | bytes 14622720 | tf_op jit(solution)/shard_map/reduce_scatter | solution.py:832
  15.9 146.1 %collective-permute-start.12 = (bf16[256,1536]{1,0:T(8,128)(2,1)}, bf16[256,1536]{1,0:T(8,128)(2,1)}, u32[]{:S(2)}, u32[]{:S(2)}) collective-permute-start(bf16[256,1536]{1,0:T(8,128)(2,1)} %bitcast.39.refs_6_), channel_id=1, source_target_pairs={{0,1},{1,0},{2,3},{3,2},{4,5},{5,4},{6,7},{7,6},{8,9},{9,8},{10,11... | collective-permute-start | bytes 2359304 | tf_op jit(solution)/shard_map/ppermute | solution.py:571
  44.8 70.0 %collective-permute-start.5 = (bf16[192,1536]{1,0:T(8,128)(2,1)S(1)}, bf16[192,1536]{1,0:T(8,128)(2,1)}, u32[]{:S(2)}, u32[]{:S(2)}) collective-permute-start(bf16[192,1536]{1,0:T(8,128)(2,1)S(1)} %get-tuple-element.426.refs_0_), channel_id=1, source_target_pairs={{0,1},{1,0},{2,3},{3,2},{4,5},{5,4},{6,7},{7,6},{8,9},{9,8},{10,11... | collective-permute-start | bytes 1769480 | tf_op jit(solution)/shard_map/ppermute | solution.py:571
  59.1 64.3 %collective-permute-start.6 = (bf16[208,1536]{1,0:T(8,128)(2,1)S(1)}, bf16[208,1536]{1,0:T(8,128)(2,1)S(1)}, u32[]{:S(2)}, u32[]{:S(2)}) collective-permute-start(bf16[208,1536]{1,0:T(8,128)(2,1)S(1)} %get-tuple-element.424.refs_2_), channel_id=1, source_target_pairs={{0,1},{1,0},{2,3},{3,2},{4,5},{5,4},{6,7},{7,6},{8,9},{9,8},{10,11... | collective-permute-start | bytes 1916936 | tf_op jit(solution)/shard_map/ppermute | solution.py:571
  122.0 18.8 %collective-permute-start.7 = (f32[384,2]{0,1:T(2,128)S(1)}, f32[384,2]{0,1:T(2,128)S(1)}, u32[]{:S(2)}, u32[]{:S(2)}) collective-permute-start(f32[384,2]{0,1:T(2,128)S(1)} %pad_maximum_fusion.32), channel_id=1, source_target_pairs={{0,1},{1,0},{2,3},{3,2},{4,5},{5,4},{6,7},{7,6},{8,9},{9,8},{10,11... | collective-permute-start | bytes 9224 | tf_op jit(solution)/shard_map/ppermute | solution.py:571
  130.4 10.5 %collective-permute-start.8 = (f32[416,2]{0,1:T(2,128)S(1)}, f32[416,2]{0,1:T(2,128)S(1)}, u32[]{:S(2)}, u32[]{:S(2)}) collective-permute-start(f32[416,2]{0,1:T(2,128)S(1)} %pad_maximum_fusion.25), channel_id=1, source_target_pairs={{0,1},{1,0},{2,3},{3,2},{4,5},{5,4},{6,7},{7,6},{8,9},{9,8},{10,11... | collective-permute-start | bytes 9992 | tf_op jit(solution)/shard_map/ppermute | solution.py:571
  160.6 25.5 %collective-permute-start.9 = (bf16[208,1536]{1,0:T(8,128)(2,1)S(1)}, bf16[208,1536]{1,0:T(8,128)(2,1)}, u32[]{:S(2)}, u32[]{:S(2)}) collective-permute-start(bf16[208,1536]{1,0:T(8,128)(2,1)S(1)} %get-tuple-element.152), channel_id=1, source_target_pairs={{0,1},{1,0},{2,3},{3,2},{4,5},{5,4},{6,7},{7,6},{8,9},{9,8},{10,11... | collective-permute-start | bytes 1916936 | tf_op jit(solution)/shard_map/ppermute | solution.py:571
  185.4 16.3 %collective-permute-start.10 = (bf16[192,1536]{1,0:T(8,128)(2,1)S(1)}, bf16[192,1536]{1,0:T(8,128)(2,1)S(1)}, u32[]{:S(2)}, u32[]{:S(2)}) collective-permute-start(bf16[192,1536]{1,0:T(8,128)(2,1)S(1)} %get-tuple-element.155), channel_id=1, source_target_pairs={{0,1},{1,0},{2,3},{3,2},{4,5},{5,4},{6,7},{7,6},{8,9},{9,8},{10,11... | collective-permute-start | bytes 1769480 | tf_op jit(solution)/shard_map/ppermute | solution.py:571
  189.2 26.3 %collective-permute-start.13 = (bf16[208,1536]{1,0:T(8,128)(2,1)S(1)}, bf16[208,1536]{1,0:T(8,128)(2,1)S(1)}, u32[]{:S(2)}, u32[]{:S(2)}) collective-permute-start(bf16[208,1536]{1,0:T(8,128)(2,1)S(1)} %add_convert_fusion.3.refs_3_), channel_id=1, source_target_pairs={{0,1},{1,0},{2,3},{3,2},{4,5},{5,4},{6,7},{7,6},{8,9},{9,8},{10,11... | collective-permute-start | bytes 1916936 | tf_op jit(solution)/shard_map/ppermute | solution.py:571
  203.6 39.6 %collective-permute-start.11 = (bf16[192,1536]{1,0:T(8,128)(2,1)S(1)}, bf16[192,1536]{1,0:T(8,128)(2,1)}, u32[]{:S(2)}, u32[]{:S(2)}) collective-permute-start(bf16[192,1536]{1,0:T(8,128)(2,1)S(1)} %add_convert_fusion.6.refs_0_), channel_id=1, source_target_pairs={{0,1},{1,0},{2,3},{3,2},{4,5},{5,4},{6,7},{7,6},{8,9},{9,8},{10,11... | collective-permute-start | bytes 1769480 | tf_op jit(solution)/shard_map/ppermute | solution.py:571
  219.0 12.1 %collective-permute-start.14 = (f32[416,1]{1,0:T(8,128)S(1)}, f32[416,1]{1,0:T(8,128)S(1)}, u32[]{:S(2)}, u32[]{:S(2)}) collective-permute-start(f32[416,1]{1,0:T(8,128)S(1)} %copy.136), channel_id=1, source_target_pairs={{0,1},{1,0},{2,3},{3,2},{4,5},{5,4},{6,7},{7,6},{8,9},{9,8},{10,11... | collective-permute-start | bytes 5000 | tf_op jit(solution)/shard_map/ppermute | solution.py:571
  221.4 10.1 %collective-permute-start.15 = (f32[512,1]{0,1:T(1,128)S(1)}, f32[512,1]{0,1:T(1,128)S(1)}, u32[]{:S(2)}, u32[]{:S(2)}) collective-permute-start(f32[512,1]{0,1:T(1,128)S(1)} %pad_maximum_fusion.35), channel_id=1, source_target_pairs={{0,1},{1,0},{2,3},{3,2},{4,5},{5,4},{6,7},{7,6},{8,9},{9,8},{10,11... | collective-permute-start | bytes 6152 | tf_op jit(solution)/shard_map/ppermute | solution.py:571
  244.3 15.3 %collective-permute-start.16 = (bf16[208,1536]{1,0:T(8,128)(2,1)}, bf16[208,1536]{1,0:T(8,128)(2,1)}, u32[]{:S(2)}, u32[]{:S(2)}) collective-permute-start(bf16[208,1536]{1,0:T(8,128)(2,1)} %get-tuple-element.171), channel_id=1, source_target_pairs={{0,1},{1,0},{2,3},{3,2},{4,5},{5,4},{6,7},{7,6},{8,9},{9,8},{10,11... | collective-permute-start | bytes 1916936 | tf_op jit(solution)/shard_map/ppermute | solution.py:571
  266.3 14.1 %collective-permute-start.18 = (bf16[208,1536]{1,0:T(8,128)(2,1)}, bf16[208,1536]{1,0:T(8,128)(2,1)}, u32[]{:S(2)}, u32[]{:S(2)}) collective-permute-start(bf16[208,1536]{1,0:T(8,128)(2,1)} %add_convert_fusion.2), channel_id=1, source_target_pairs={{0,1},{1,0},{2,3},{3,2},{4,5},{5,4},{6,7},{7,6},{8,9},{9,8},{10,11... | collective-permute-start | bytes 1916936 | tf_op jit(solution)/shard_map/ppermute | solution.py:571
  280.4 13.9 %collective-permute-start.19 = (bf16[192,1536]{1,0:T(8,128)(2,1)}, bf16[192,1536]{1,0:T(8,128)(2,1)S(1)}, u32[]{:S(2)}, u32[]{:S(2)}) collective-permute-start(bf16[192,1536]{1,0:T(8,128)(2,1)} %get-tuple-element.183), channel_id=1, source_target_pairs={{0,1},{1,0},{2,3},{3,2},{4,5},{5,4},{6,7},{7,6},{8,9},{9,8},{10,11... | collective-permute-start | bytes 1769480 | tf_op jit(solution)/shard_map/ppermute | solution.py:571
  297.8 13.3 %collective-permute-start.20 = (bf16[192,1536]{1,0:T(8,128)(2,1)S(1)}, bf16[192,1536]{1,0:T(8,128)(2,1)S(1)}, u32[]{:S(2)}, u32[]{:S(2)}) collective-permute-start(bf16[192,1536]{1,0:T(8,128)(2,1)S(1)} %add_convert_fusion.5), channel_id=1, source_target_pairs={{0,1},{1,0},{2,3},{3,2},{4,5},{5,4},{6,7},{7,6},{8,9},{9,8},{10,11... | collective-permute-start | bytes 1769480 | tf_op jit(solution)/shard_map/ppermute | solution.py:571
  311.2 12.5 %collective-permute-start.21 = (bf16[208,1536]{1,0:T(8,128)(2,1)S(1)}, bf16[208,1536]{1,0:T(8,128)(2,1)S(1)}, u32[]{:S(2)}, u32[]{:S(2)}) collective-permute-start(bf16[208,1536]{1,0:T(8,128)(2,1)S(1)} %slice.984), channel_id=1, source_target_pairs={{0,1},{1,0},{2,3},{3,2},{4,5},{5,4},{6,7},{7,6},{8,9},{9,8},{10,11... | collective-permute-start | bytes 1916936 | tf_op jit(solution)/shard_map/ppermute | solution.py:571
  326.4 15.4 %collective-permute-start.22 = (bf16[208,1536]{1,0:T(8,128)(2,1)S(1)}, bf16[208,1536]{1,0:T(8,128)(2,1)S(1)}, u32[]{:S(2)}, u32[]{:S(2)}) collective-permute-start(bf16[208,1536]{1,0:T(8,128)(2,1)S(1)} %multiply_convert_fusion.4), channel_id=1, source_target_pairs={{0,1},{1,0},{2,3},{3,2},{4,5},{5,4},{6,7},{7,6},{8,9},{9,8},{10,11... | collective-permute-start | bytes 1916936 | tf_op jit(solution)/shard_map/ppermute | solution.py:571
  341.8 15.8 %collective-permute-start.23 = (bf16[192,1536]{1,0:T(8,128)(2,1)S(1)}, bf16[192,1536]{1,0:T(8,128)(2,1)S(1)}, u32[]{:S(2)}, u32[]{:S(2)}) collective-permute-start(bf16[192,1536]{1,0:T(8,128)(2,1)S(1)} %slice.987), channel_id=1, source_target_pairs={{0,1},{1,0},{2,3},{3,2},{4,5},{5,4},{6,7},{7,6},{8,9},{9,8},{10,11... | collective-permute-start | bytes 1769480 | tf_op jit(solution)/shard_map/ppermute | solution.py:571
  360.1 14.4 %collective-permute-start.24 = (bf16[192,1536]{1,0:T(8,128)(2,1)S(1)}, bf16[192,1536]{1,0:T(8,128)(2,1)S(1)}, u32[]{:S(2)}, u32[]{:S(2)}) collective-permute-start(bf16[192,1536]{1,0:T(8,128)(2,1)S(1)} %multiply_convert_fusion.7), channel_id=1, source_target_pairs={{0,1},{1,0},{2,3},{3,2},{4,5},{5,4},{6,7},{7,6},{8,9},{9,8},{10,11... | collective-permute-start | bytes 1769480 | tf_op jit(solution)/shard_map/ppermute | solution.py:571
  374.6 23.4 %collective-permute-start.25 = (bf16[208,1536]{1,0:T(8,128)(2,1)S(1)}, bf16[208,1536]{1,0:T(8,128)(2,1)S(1)}, u32[]{:S(2)}, u32[]{:S(2)}) collective-permute-start(bf16[208,1536]{1,0:T(8,128)(2,1)S(1)} %slice.983), channel_id=1, source_target_pairs={{0,1},{1,0},{2,3},{3,2},{4,5},{5,4},{6,7},{7,6},{8,9},{9,8},{10,11... | collective-permute-start | bytes 1916936 | tf_op jit(solution)/shard_map/ppermute | solution.py:571
  398.1 391.1 %reduce-scatter.5.cloned.1.call-start = ((), (), s32[]{:S(2)}) async-start(), calls=%async_computation.5 | async-start | bytes 14622720 | tf_op jit(solution)/shard_map/reduce_scatter | solution.py:832
  419.5 11.0 %collective-permute-start.26 = (bf16[208,1536]{1,0:T(8,128)(2,1)S(1)}, bf16[208,1536]{1,0:T(8,128)(2,1)S(1)}, u32[]{:S(2)}, u32[]{:S(2)}) collective-permute-start(bf16[208,1536]{1,0:T(8,128)(2,1)S(1)} %get-tuple-element.210.refs_13_), channel_id=1, source_target_pairs={{0,1},{1,0},{2,3},{3,2},{4,5},{5,4},{6,7},{7,6},{8,9},{9,8},{10,11... | collective-permute-start | bytes 1916936 | tf_op jit(solution)/shard_map/ppermute | solution.py:571
  432.2 21.0 %collective-permute-start.27 = (bf16[192,1536]{1,0:T(8,128)(2,1)}, bf16[192,1536]{1,0:T(8,128)(2,1)}, u32[]{:S(2)}, u32[]{:S(2)}) collective-permute-start(bf16[192,1536]{1,0:T(8,128)(2,1)} %slice.986), channel_id=1, source_target_pairs={{0,1},{1,0},{2,3},{3,2},{4,5},{5,4},{6,7},{7,6},{8,9},{9,8},{10,11... | collective-permute-start | bytes 1769480 | tf_op jit(solution)/shard_map/ppermute | solution.py:571
  458.4 13.7 %collective-permute-start.28 = (bf16[192,1536]{1,0:T(8,128)(2,1)S(1)}, bf16[192,1536]{1,0:T(8,128)(2,1)S(1)}, u32[]{:S(2)}, u32[]{:S(2)}) collective-permute-start(bf16[192,1536]{1,0:T(8,128)(2,1)S(1)} %get-tuple-element.216.refs_10_), channel_id=1, source_target_pairs={{0,1},{1,0},{2,3},{3,2},{4,5},{5,4},{6,7},{7,6},{8,9},{9,8},{10,11... | collective-permute-start | bytes 1769480 | tf_op jit(solution)/shard_map/ppermute | solution.py:571
  483.0 15.7 %collective-permute-start.30 = (bf16[208,1536]{1,0:T(8,128)(2,1)}, bf16[208,1536]{1,0:T(8,128)(2,1)S(1)}, u32[]{:S(2)}, u32[]{:S(2)}) collective-permute-start(bf16[208,1536]{1,0:T(8,128)(2,1)} %slice.982), channel_id=1, source_target_pairs={{0,1},{1,0},{2,3},{3,2},{4,5},{5,4},{6,7},{7,6},{8,9},{9,8},{10,11... | collective-permute-start | bytes 1916936 | tf_op jit(solution)/shard_map/ppermute | solution.py:571
  510.1 11.5 %collective-permute-start.32 = (bf16[192,1536]{1,0:T(8,128)(2,1)S(1)}, bf16[192,1536]{1,0:T(8,128)(2,1)S(1)}, u32[]{:S(2)}, u32[]{:S(2)}) collective-permute-start(bf16[192,1536]{1,0:T(8,128)(2,1)S(1)} %slice.985), channel_id=1, source_target_pairs={{0,1},{1,0},{2,3},{3,2},{4,5},{5,4},{6,7},{7,6},{8,9},{9,8},{10,11... | collective-permute-start | bytes 1769480 | tf_op jit(solution)/shard_map/ppermute | solution.py:571
  513.1 26.5 %collective-permute-start.34 = (bf16[208,1536]{1,0:T(8,128)(2,1)S(1)}, bf16[208,1536]{1,0:T(8,128)(2,1)S(1)}, u32[]{:S(2)}, u32[]{:S(2)}) collective-permute-start(bf16[208,1536]{1,0:T(8,128)(2,1)S(1)} %get-tuple-element.395.refs_3_), channel_id=1, source_target_pairs={{0,1},{1,0},{2,3},{3,2},{4,5},{5,4},{6,7},{7,6},{8,9},{9,8},{10,11... | collective-permute-start | bytes 1916936 | tf_op jit(solution)/shard_map/ppermute | solution.py:571
  524.0 15.6 %collective-permute-start.33 = (bf16[192,1536]{1,0:T(8,128)(2,1)S(1)}, bf16[192,1536]{1,0:T(8,128)(2,1)S(1)}, u32[]{:S(2)}, u32[]{:S(2)}) collective-permute-start(bf16[192,1536]{1,0:T(8,128)(2,1)S(1)} %get-tuple-element.392.refs_0_), channel_id=1, source_target_pairs={{0,1},{1,0},{2,3},{3,2},{4,5},{5,4},{6,7},{7,6},{8,9},{9,8},{10,11... | collective-permute-start | bytes 1769480 | tf_op jit(solution)/shard_map/ppermute | solution.py:571
  572.0 39.4 %collective-permute-start.38 = (bf16[256,1536]{1,0:T(8,128)(2,1)}, bf16[256,1536]{1,0:T(8,128)(2,1)}, u32[]{:S(2)}, u32[]{:S(2)}) collective-permute-start(bf16[256,1536]{1,0:T(8,128)(2,1)} %slice.981), channel_id=1, source_target_pairs={{0,1},{1,0},{2,3},{3,2},{4,5},{5,4},{6,7},{7,6},{8,9},{9,8},{10,11... | collective-permute-start | bytes 2359304 | tf_op jit(solution)/shard_map/ppermute | solution.py:571
  (225 other events, 1992.5 us)
Sparse Core Ops, SparseCore 0:
  10.1 104.5 all-gather.2
  116.9 139.7 all-gather.4
  398.2 143.1 reduce-scatter.2
  548.8 154.4 reduce-scatter.4
